TPU v7x, 32 devices: a whole 2x2x4 slice. The times are simulated.
32 devices in a mesh: batch: 8 (over z, core), seq: 4 (over y, x).
Axes of the slice: x: 2, y: 2, z: 4, core: 2. Of those that a mesh axis runs over, the one named last changes fastest.
Arguments:
- inputs: bfloat16 [16, 2080, 1152], P('batch', 'seq'), may hold values from -6 to 6
- skip_inputs: bfloat16 [16, 2080, 1152], P('batch', 'seq'), may hold values from -6 to 6
- out_cotangent: bfloat16 [16, 2080, 1152], P('batch', 'seq'), may hold values from -6 to 6
- segments: int32 [16, 2080], P('batch'), may hold values from 0 to 8, as said below
- occupied: int32 [16, 2080], P('batch'), may hold values from 0 to 1, as said below
- skip_weight: bfloat16 [2304, 1152], P('batch', 'seq'), may hold values from -0.125 to 0.125
- skip_bias: bfloat16 [1152], P('seq'), may hold values from -3 to 3
- first_gain: bfloat16 [1152], P('seq'), may hold values from 0.25 to 1.75
- first_shift: bfloat16 [1152], P('seq'), may hold values from -3 to 3
- qkv_weight: bfloat16 [1152, 3456], P('batch', 'seq'), may hold values from -0.25 to 0.25
- proj_weight: bfloat16 [1152, 1152], P('batch', 'seq'), may hold values from -1.5 to 1.5
- proj_bias: bfloat16 [1152], P('seq'), may hold values from -3 to 3
- second_gain: bfloat16 [1152], P('seq'), may hold values from 0.25 to 1.75
- second_shift: bfloat16 [1152], P('seq'), may hold values from -3 to 3
- hidden_weight: bfloat16 [1152, 4608], P('batch', 'seq'), may hold values from -0.1875 to 0.1875
- hidden_bias: bfloat16 [4608], P('seq'), may hold values from -3 to 3
- down_weight: bfloat16 [4608, 1152], P('batch', 'seq'), may hold values from -0.125 to 0.125
- down_bias: bfloat16 [1152], P('seq'), may hold values from -3 to 3
Outputs:
- output: bfloat16 [16, 2080, 1152], P('batch', 'seq')
- input_grad: float32 [16, 2080, 1152], P('batch', 'seq')
- skip_grad: float32 [16, 2080, 1152], P('batch', 'seq')
- skip_weight_grad: float32 [2304, 1152], P('batch', 'seq')
- skip_bias_grad: float32 [1152], P('seq')
- first_gain_grad: float32 [1152], P('seq')
- first_shift_grad: float32 [1152], P('seq')
- qkv_weight_grad: float32 [1152, 3456], P('batch', 'seq')
- proj_weight_grad: float32 [1152, 1152], P('batch', 'seq')
- proj_bias_grad: float32 [1152], P('seq')
- second_gain_grad: float32 [1152], P('seq')
- second_shift_grad: float32 [1152], P('seq')
- hidden_weight_grad: float32 [1152, 4608], P('batch', 'seq')
- hidden_bias_grad: float32 [4608], P('seq')
- down_weight_grad: float32 [4608, 1152], P('batch', 'seq')
- down_bias_grad: float32 [1152], P('seq')
Inputs may be any that keep to these rules, and one draw needn't show every extreme that they name: `segments`: each row holds whole items numbered 0, 1, 2, ... in order from slot 0: eight items of 258 slots, two of 1026, one of 1026 then four of 258, or one of 1026 then one of 258; each of these four kinds is some row's. The slots after the last item have id 8. `occupied`: 1 exactly on the slots of items, 0 on the slots after them.
All inputs are finite; a program needn't handle non-finite values.
Results may differ from a plain program's by a relative error of at most 0.02.
Values may be sent and summed in bfloat16 or wider, within the bound.
No kernel may reach another device: no remote copies, remote signals or barrier semaphores. Data moves between devices by JAX's collectives and lax.ppermute only.
A program may use at most 384 MiB of HBM per device.

v0:
```python
import jax
import jax.numpy as jnp
from jax import lax
from jax.sharding import PartitionSpec as P

HEADS = 16
HEAD_DIM = 72
QBLOCK = 520


epsilon = 1e-05
masked_score = -1e30
matrix_slots = (0, 4, 5, 9, 11)
vector_slots = (1, 2, 3, 6, 7, 8, 10, 12)


def layer_norm(stream, norm_gain, norm_shift):
    centred = stream - jnp.mean(stream, axis=-1, keepdims=True)
    spread = jnp.mean(centred * centred, axis=-1, keepdims=True)
    return centred * lax.rsqrt(spread + epsilon) * norm_gain + norm_shift


def gelu_exact(pre_act):
    return jax.nn.gelu(pre_act, approximate=False)


def mat_dot(left_side, right_side):
    return jnp.dot(left_side, right_side, preferred_element_type=jnp.float32)


def outer_dot(left_side, right_side):
    return lax.dot_general(
        left_side, right_side, (((0,), (0,)), ((), ())), preferred_element_type=jnp.float32
    )


def back_dot(left_side, right_side):
    return lax.dot_general(
        left_side, right_side, (((1,), (1,)), ((), ())), preferred_element_type=jnp.float32
    )


def whole_matrix(gathered, piece_shape, batch_count, seq_count):
    piece_rows, piece_cols = piece_shape
    return (
        gathered.reshape(batch_count, seq_count, piece_rows, piece_cols)
        .transpose(0, 2, 1, 3)
        .reshape(batch_count * piece_rows, seq_count * piece_cols)
    )


def whole_vector(gathered, seq_count):
    return gathered[:seq_count].reshape(-1).astype(jnp.float32)


def unpack_weights(gathered, weight_args, batch_count, seq_count):
    result_list = []
    for slot_number in range(len(weight_args)):
        if slot_number in matrix_slots:
            result_list.append(
                whole_matrix(
                    gathered[slot_number], weight_args[slot_number].shape, batch_count, seq_count
                )
            )
        else:
            result_list.append(whole_vector(gathered[slot_number], seq_count))
    return tuple(result_list)


def regroup(matrix_parts, vector_parts):
    result_list = [None] * 13
    for place, slot_number in enumerate(matrix_slots):
        result_list[slot_number] = matrix_parts[place]
    for place, slot_number in enumerate(vector_slots):
        result_list[slot_number] = vector_parts[place]
    return tuple(result_list)


def reduce_end(grads):
    parts = (
        lax.psum_scatter(
            grads[0].astype(jnp.bfloat16), "seq", scatter_dimension=1, tiled=True
        ).astype(jnp.float32),
        lax.psum_scatter(
            grads[1].astype(jnp.bfloat16), "seq", scatter_dimension=0, tiled=True
        ).astype(jnp.float32),
        lax.psum_scatter(
            grads[2].astype(jnp.bfloat16), "seq", scatter_dimension=0, tiled=True
        ).astype(jnp.float32),
        lax.psum_scatter(
            grads[3].astype(jnp.bfloat16), "seq", scatter_dimension=0, tiled=True
        ).astype(jnp.float32),
        lax.psum_scatter(
            grads[4].astype(jnp.bfloat16), "seq", scatter_dimension=1, tiled=True
        ).astype(jnp.float32),
        lax.psum_scatter(
            grads[5].astype(jnp.bfloat16), "seq", scatter_dimension=1, tiled=True
        ).astype(jnp.float32),
        lax.psum_scatter(
            grads[6].astype(jnp.bfloat16), "seq", scatter_dimension=0, tiled=True
        ).astype(jnp.float32),
        lax.psum_scatter(
            grads[7].astype(jnp.bfloat16), "seq", scatter_dimension=0, tiled=True
        ).astype(jnp.float32),
        lax.psum_scatter(
            grads[8].astype(jnp.bfloat16), "seq", scatter_dimension=0, tiled=True
        ).astype(jnp.float32),
        lax.psum_scatter(
            grads[9].astype(jnp.bfloat16), "seq", scatter_dimension=1, tiled=True
        ).astype(jnp.float32),
        lax.psum_scatter(
            grads[10].astype(jnp.bfloat16), "seq", scatter_dimension=0, tiled=True
        ).astype(jnp.float32),
        lax.psum_scatter(
            grads[11].astype(jnp.bfloat16), "seq", scatter_dimension=1, tiled=True
        ).astype(jnp.float32),
        lax.psum_scatter(
            grads[12].astype(jnp.bfloat16), "seq", scatter_dimension=0, tiled=True
        ).astype(jnp.float32),
    )
    matrix_parts = (
        lax.psum_scatter(
            parts[0].astype(jnp.bfloat16), "batch", scatter_dimension=0, tiled=True
        ).astype(jnp.float32),
        lax.psum_scatter(
            parts[4].astype(jnp.bfloat16), "batch", scatter_dimension=0, tiled=True
        ).astype(jnp.float32),
        lax.psum_scatter(
            parts[5].astype(jnp.bfloat16), "batch", scatter_dimension=0, tiled=True
        ).astype(jnp.float32),
        lax.psum_scatter(
            parts[9].astype(jnp.bfloat16), "batch", scatter_dimension=0, tiled=True
        ).astype(jnp.float32),
        lax.psum_scatter(
            parts[11].astype(jnp.bfloat16), "batch", scatter_dimension=0, tiled=True
        ).astype(jnp.float32),
    )
    vector_parts = lax.psum(
        (parts[1], parts[2], parts[3], parts[6], parts[7], parts[8], parts[10], parts[12]), "batch"
    )
    return regroup(matrix_parts, vector_parts)


def block_mask(segment_row, occupied_row, block_start, block_rows):
    slot_count = segment_row.shape[0]
    query_slots = block_start + lax.iota(jnp.int32, block_rows)
    key_slots = lax.iota(jnp.int32, slot_count)
    query_segments = lax.dynamic_slice_in_dim(segment_row, block_start, block_rows)
    same_item = (query_segments[:, None] == segment_row[None, :]) & (occupied_row[None, :] > 0)
    return same_item | (query_slots[:, None] == key_slots[None, :])


def block_scores(query_block, key_heads, segment_row, occupied_row, block_start):
    scores = jnp.einsum(
        "hqd,hkd->hqk", query_block, key_heads, preferred_element_type=jnp.float32
    ) * HEAD_DIM ** (-0.5)
    allowed = block_mask(segment_row, occupied_row, block_start, query_block.shape[1])
    return jnp.where(allowed[None], scores, masked_score)


def attend_row(packed, segment_row, occupied_row):
    query_heads = packed[:, 0].transpose(1, 0, 2)
    key_heads = packed[:, 1].transpose(1, 0, 2)
    value_heads = packed[:, 2].transpose(1, 0, 2)
    slot_count = packed.shape[0]

    def one_block(block_start):
        query_block = lax.dynamic_slice_in_dim(query_heads, block_start, QBLOCK, 1)
        scores = block_scores(query_block, key_heads, segment_row, occupied_row, block_start)
        row_top = jnp.max(scores, axis=-1, keepdims=True)
        exp_scores = jnp.exp(scores - row_top)
        row_total = jnp.sum(exp_scores, axis=-1, keepdims=True)
        soft_low = (exp_scores / row_total).astype(jnp.bfloat16)
        attended = jnp.einsum(
            "hqk,hkd->hqd", soft_low, value_heads, preferred_element_type=jnp.float32
        ).astype(jnp.bfloat16)
        return (attended, (row_top + jnp.log(row_total))[..., 0])

    block_starts = jnp.arange(slot_count // QBLOCK, dtype=jnp.int32) * QBLOCK
    attended, log_total = lax.map(one_block, block_starts)
    heads_local = attended.shape[1]
    attended = attended.transpose(0, 2, 1, 3).reshape(slot_count, heads_local, attended.shape[3])
    return (attended, log_total)


def attend_back(packed, grad_row, log_total, segment_row, occupied_row):
    query_heads = packed[:, 0].transpose(1, 0, 2)
    key_heads = packed[:, 1].transpose(1, 0, 2)
    value_heads = packed[:, 2].transpose(1, 0, 2)
    grad_heads = grad_row.transpose(1, 0, 2)
    heads_local, slot_count, head_width = query_heads.shape
    score_scale = HEAD_DIM ** (-0.5)

    def one_step(carry, block_index):
        key_acc, value_acc = carry
        block_start = block_index * QBLOCK
        query_block = lax.dynamic_slice_in_dim(query_heads, block_start, QBLOCK, 1)
        grad_block = lax.dynamic_slice_in_dim(grad_heads, block_start, QBLOCK, 1)
        scores = block_scores(query_block, key_heads, segment_row, occupied_row, block_start)
        soft = jnp.exp(scores - log_total[block_index][..., None])
        grad_soft = jnp.einsum(
            "hqd,hkd->hqk", grad_block, value_heads, preferred_element_type=jnp.float32
        )
        row_dot = jnp.sum(soft * grad_soft, axis=-1, keepdims=True)
        grad_scores = (soft * (grad_soft - row_dot)).astype(jnp.bfloat16)
        query_grad = (
            jnp.einsum("hqk,hkd->hqd", grad_scores, key_heads, preferred_element_type=jnp.float32)
            * score_scale
        )
        key_acc = (
            key_acc
            + jnp.einsum(
                "hqk,hqd->hkd", grad_scores, query_block, preferred_element_type=jnp.float32
            )
            * score_scale
        )
        value_acc = value_acc + jnp.einsum(
            "hqk,hqd->hkd",
            soft.astype(jnp.bfloat16),
            grad_block,
            preferred_element_type=jnp.float32,
        )
        return ((key_acc, value_acc), query_grad)

    zero_acc = jnp.zeros((heads_local, slot_count, head_width), jnp.float32)
    (key_acc, value_acc), query_blocks = lax.scan(
        one_step, (zero_acc, zero_acc), jnp.arange(slot_count // QBLOCK, dtype=jnp.int32)
    )
    query_grad = query_blocks.transpose(1, 0, 2, 3).reshape(heads_local, slot_count, head_width)
    stacked = jnp.stack([query_grad, key_acc, value_acc], axis=0).astype(jnp.bfloat16)
    return stacked.transpose(2, 0, 1, 3)


def micro_batch(full, row_parts, seq_index):
    (
        skip_full,
        skip_bias_full,
        gain_one,
        shift_one,
        qkv_full,
        proj_full,
        proj_bias_full,
        gain_two,
        shift_two,
        hidden_full,
        hidden_bias_full,
        down_full,
        down_bias_full,
    ) = full
    row_input, row_skip, row_cotangent, segment_row, occupied_row = row_parts
    tok_local, feature_width = row_input.shape
    joined = jnp.concatenate([row_input, row_skip], axis=-1)
    stream = mat_dot(joined, skip_full) + skip_bias_full
    first_norm, first_pull = jax.vjp(layer_norm, stream, gain_one, shift_one)
    first_low = first_norm.astype(jnp.bfloat16)
    qkv_tokens = (
        mat_dot(first_low, qkv_full).astype(jnp.bfloat16).reshape(tok_local, 3, HEADS, HEAD_DIM)
    )
    qkv_heads = lax.all_to_all(qkv_tokens, "seq", split_axis=2, concat_axis=0, tiled=True)
    attended_heads, log_total = attend_row(qkv_heads, segment_row, occupied_row)
    attended_tokens = lax.all_to_all(
        attended_heads, "seq", split_axis=0, concat_axis=1, tiled=True
    ).reshape(tok_local, feature_width)
    middle = stream + mat_dot(attended_tokens, proj_full) + proj_bias_full
    second_norm, second_pull = jax.vjp(layer_norm, middle, gain_two, shift_two)
    second_low = second_norm.astype(jnp.bfloat16)
    pre_act = mat_dot(second_low, hidden_full) + hidden_bias_full
    activated, gelu_pull = jax.vjp(gelu_exact, pre_act)
    act_low = activated.astype(jnp.bfloat16)
    result = middle + mat_dot(act_low, down_full) + down_bias_full
    output_row = result.astype(jnp.bfloat16)
    local_occupied = lax.dynamic_slice_in_dim(occupied_row, seq_index * tok_local, tok_local, 0)
    grad_out = row_cotangent.astype(jnp.float32) * local_occupied[:, None].astype(jnp.float32)
    grad_branch = grad_out.astype(jnp.bfloat16)
    down_grad = outer_dot(act_low, grad_branch)
    down_bias_grad = jnp.sum(grad_branch.astype(jnp.float32), axis=0)
    grad_act = back_dot(grad_branch, down_full)
    grad_pre = gelu_pull(grad_act)[0].astype(jnp.bfloat16)
    hidden_grad = outer_dot(second_low, grad_pre)
    hidden_bias_grad = jnp.sum(grad_pre.astype(jnp.float32), axis=0)
    grad_middle_norm, gain_two_grad, shift_two_grad = second_pull(back_dot(grad_pre, hidden_full))
    grad_middle = grad_out + grad_middle_norm
    grad_proj = grad_middle.astype(jnp.bfloat16)
    proj_grad = outer_dot(attended_tokens, grad_proj)
    proj_bias_grad = jnp.sum(grad_proj.astype(jnp.float32), axis=0)
    grad_attended = (
        back_dot(grad_proj, proj_full).astype(jnp.bfloat16).reshape(tok_local, HEADS, HEAD_DIM)
    )
    grad_heads = lax.all_to_all(grad_attended, "seq", split_axis=1, concat_axis=0, tiled=True)
    grad_qkv_heads = attend_back(qkv_heads, grad_heads, log_total, segment_row, occupied_row)
    grad_qkv = lax.all_to_all(
        grad_qkv_heads, "seq", split_axis=0, concat_axis=2, tiled=True
    ).reshape(tok_local, 3 * feature_width)
    qkv_grad = outer_dot(first_low, grad_qkv)
    grad_stream_norm, gain_one_grad, shift_one_grad = first_pull(back_dot(grad_qkv, qkv_full))
    grad_stream = (grad_middle + grad_stream_norm).astype(jnp.bfloat16)
    skip_grad_weight = outer_dot(joined, grad_stream)
    skip_bias_grad = jnp.sum(grad_stream.astype(jnp.float32), axis=0)
    grad_joined = back_dot(grad_stream, skip_full)
    input_grad_row = grad_joined[:, :feature_width]
    skip_grad_row = grad_joined[:, feature_width:]
    grads = (
        skip_grad_weight,
        skip_bias_grad,
        gain_one_grad,
        shift_one_grad,
        qkv_grad,
        proj_grad,
        proj_bias_grad,
        gain_two_grad,
        shift_two_grad,
        hidden_grad,
        hidden_bias_grad,
        down_grad,
        down_bias_grad,
    )
    return ((output_row, input_grad_row, skip_grad_row), grads)


def add_pair(first_sum, second_sum):
    return first_sum + second_sum


def body(
    inputs,
    skip_inputs,
    out_cotangent,
    segments,
    occupied,
    skip_weight,
    skip_bias,
    first_gain,
    first_shift,
    qkv_weight,
    proj_weight,
    proj_bias,
    second_gain,
    second_shift,
    hidden_weight,
    hidden_bias,
    down_weight,
    down_bias,
):
    batch_count = lax.axis_size("batch")
    seq_count = lax.axis_size("seq")
    seq_index = lax.axis_index("seq")
    weight_args = (
        skip_weight,
        skip_bias,
        first_gain,
        first_shift,
        qkv_weight,
        proj_weight,
        proj_bias,
        second_gain,
        second_shift,
        hidden_weight,
        hidden_bias,
        down_weight,
        down_bias,
    )
    gathered_once = (
        lax.all_gather(skip_weight.reshape(1, -1), ("batch", "seq"), axis=0, tiled=True),
        lax.all_gather(skip_bias.reshape(1, -1), ("batch", "seq"), axis=0, tiled=True),
        lax.all_gather(first_gain.reshape(1, -1), ("batch", "seq"), axis=0, tiled=True),
        lax.all_gather(first_shift.reshape(1, -1), ("batch", "seq"), axis=0, tiled=True),
        lax.all_gather(qkv_weight.reshape(1, -1), ("batch", "seq"), axis=0, tiled=True),
        lax.all_gather(proj_weight.reshape(1, -1), ("batch", "seq"), axis=0, tiled=True),
        lax.all_gather(proj_bias.reshape(1, -1), ("batch", "seq"), axis=0, tiled=True),
        lax.all_gather(second_gain.reshape(1, -1), ("batch", "seq"), axis=0, tiled=True),
        lax.all_gather(second_shift.reshape(1, -1), ("batch", "seq"), axis=0, tiled=True),
        lax.all_gather(hidden_weight.reshape(1, -1), ("batch", "seq"), axis=0, tiled=True),
        lax.all_gather(hidden_bias.reshape(1, -1), ("batch", "seq"), axis=0, tiled=True),
        lax.all_gather(down_weight.reshape(1, -1), ("batch", "seq"), axis=0, tiled=True),
        lax.all_gather(down_bias.reshape(1, -1), ("batch", "seq"), axis=0, tiled=True),
    )
    fixed_full = unpack_weights(gathered_once, weight_args, batch_count, seq_count)
    start_sums = tuple(
        (
            (
                jnp.zeros(
                    (weight_arg.shape[0] * batch_count, weight_arg.shape[1] * seq_count),
                    jnp.float32,
                )
                if slot_number in matrix_slots
                else jnp.zeros((weight_arg.shape[0] * seq_count,), jnp.float32)
            )
            for slot_number, weight_arg in enumerate(weight_args)
        )
    )

    def step(sums, row_parts):
        row_outs, grads = micro_batch(fixed_full, row_parts, seq_index)
        sums = jax.tree.map(add_pair, sums, grads)
        return (sums, row_outs)

    sums, (output, input_grad, skip_grad) = lax.scan(
        step, start_sums, (inputs, skip_inputs, out_cotangent, segments, occupied)
    )
    shards = reduce_end(sums)
    return (
        output,
        input_grad,
        skip_grad,
        shards[0],
        shards[1],
        shards[2],
        shards[3],
        shards[4],
        shards[5],
        shards[6],
        shards[7],
        shards[8],
        shards[9],
        shards[10],
        shards[11],
        shards[12],
    )


def solution(mesh):
    return jax.shard_map(
        body,
        mesh=mesh,
        in_specs=(
            P("batch", "seq", None),
            P("batch", "seq", None),
            P("batch", "seq", None),
            P("batch", None),
            P("batch", None),
            P("batch", "seq"),
            P("seq"),
            P("seq"),
            P("seq"),
            P("batch", "seq"),
            P("batch", "seq"),
            P("seq"),
            P("seq"),
            P("seq"),
            P("batch", "seq"),
            P("seq"),
            P("batch", "seq"),
            P("seq"),
        ),
        out_specs=(
            P("batch", "seq", None),
            P("batch", "seq", None),
            P("batch", "seq", None),
            P("batch", "seq"),
            P("seq"),
            P("seq"),
            P("seq"),
            P("batch", "seq"),
            P("batch", "seq"),
            P("seq"),
            P("seq"),
            P("seq"),
            P("batch", "seq"),
            P("seq"),
            P("batch", "seq"),
            P("seq"),
        ),
        check_vma=False,
    )
```

profile of v0, /device:TPU:0, one launch (start us, length us, event | category | flops | bytes accessed | tf_op | source)
XLA Modules:
  0.0 3393.0 jit_solution(7731522021588461248)
XLA Ops:
  24.6 70.7 %all-gather.12 = bf16[32,1,1152]{2,1,0:T(2,128)(2,1)S(1)} all-gather(bf16[1,1,1152]{2,1,0:T(2,128)(2,1)S(1)} %reshape.509), channel_id=8, replica_groups=mesh['batch'=8,'seq'=4] {'batch','seq'}, dimensions={0}, use_global_device_ids=true | all-gather | bytes 76032 | tf_op jit(solution)/shard_map/all_gather | solution.py:373
  96.0 47.2 %all-reduce.20.cloned.1.call-done = (bf16[9216]{0:T(1024)(128)(2,1)}, bf16[9216]{0:T(1024)(128)(2,1)}, bf16[9216]{0:T(1024)(128)(2,1)}, bf16[9216]{0:T(1024)(128...) async-done(((bf16[9216]{0:T(1024)(128)(2,1)}, bf16[9216]{0:T(1024)(128)(2,1)}, bf16[9216]{0:T(1024)(128)(2,1)}, ...) | async-done | bytes 129040
  147.7 64.2 %all-gather.24.cloned.1.call-done = bf16[32,1,41472]{2,1,0:T(2,128)(2,1)} async-done(((bf16[1,1,41472]{2,1,0:T(2,128)(2,1)}), bf16[32,1,41472]{2,1,0:T(2,128)(2,1)}) %all-gather.24.cloned.1.call-update) | async-done | bytes 2654224 | tf_op jit(solution)/shard_map/all_gather | solution.py:368
  211.9 48.6 %reduce.5 = bf16[32,41472]{1,0:T(8,128)(2,1)} reduce(bf16[32,1,41472]{2,1,0:T(2,128)(2,1)} %all-gather.24.cloned.1.call-done, bf16[]{:T(256)} %constant.430), dimensions={1}, to_apply=%all-gather.10.reduce_sub_computation | reduce | bytes 5308418 | tf_op jit(solution)/shard_map/all_gather | solution.py:368
  276.1 25.9 all-gather.20.cloned.1.call-done
  302.0 114.5 %reduce.3 = bf16[32,82944]{1,0:T(8,128)(2,1)} reduce(bf16[32,1,82944]{2,1,0:T(2,128)(2,1)} %all-gather.20.cloned.1.call-done, bf16[]{:T(256)} %constant.430), dimensions={1}, to_apply=%all-gather.8.reduce_sub_computation | reduce | bytes 10616834 | tf_op jit(solution)/shard_map/all_gather | solution.py:363
  416.5 13.0 reshape.424
  451.1 167.3 %reduce.4 = bf16[32,124416]{1,0:T(8,128)(2,1)} reduce(bf16[32,1,124416]{2,1,0:T(2,128)(2,1)} %all-gather.22.cloned.1.call-done, bf16[]{:T(256)} %constant.430), dimensions={1}, to_apply=%all-gather.9.reduce_sub_computation | reduce | bytes 15925250 | tf_op jit(solution)/shard_map/all_gather | solution.py:367
  618.3 15.3 reshape.430
  641.9 14.8 reshape.431
  656.6 225.4 %reduce.8 = bf16[32,165888]{1,0:T(8,128)(2,1)} reduce(bf16[32,1,165888]{2,1,0:T(2,128)(2,1)} %all-gather.28.cloned.1.call-done, bf16[]{:T(256)} %constant.430), dimensions={1}, to_apply=%all-gather.13.reduce_sub_computation | reduce | bytes 21233666 | tf_op jit(solution)/shard_map/all_gather | solution.py:374
  882.1 24.5 reshape.443
  906.6 29.6 copy.95
  936.2 22.3 reshape.533
  958.5 225.9 %reduce.6 = bf16[32,165888]{1,0:T(8,128)(2,1)} reduce(bf16[32,1,165888]{2,1,0:T(2,128)(2,1)} %all-gather.26.cloned.1.call-done, bf16[]{:T(256)} %constant.430), dimensions={1}, to_apply=%all-gather.11.reduce_sub_computation | reduce | bytes 21233666 | tf_op jit(solution)/shard_map/all_gather | solution.py:372
  1204.3 1579.3 %while.111 = (s32[]{:T(128)}, f32[2304,1152]{1,0:T(8,128)}, f32[1152]{0:T(1024)}, f32[1152]{0:T(1024)}, f32[1152]{0:T(1024)}, /*index=5*/f32[1152,3456]{1,0:T(8,...) while((s32[]{:T(128)}, f32[2304,1152]{1,0:T(8,128)}, ...), condition=%wide.region_24.25_spmd.clone, body=%wide.region_0.24_spmd.clone.sunk | while | flops 62737883136 | bytes 1102064128 | solution.py:397
  1239.0 49.8 %all-to-all-done = bf16[520,3,16,72]{0,3,1,2:T(8,128)(2,1)} async-done(((bf16[520,3,16,72]{0,3,1,2:T(8,128)(2,1)}), bf16[520,3,16,72]{0,3,1,2:T(8,128)(2,1)}, u32[]{:S(2)}, u32[]{:S(2)}) %all-to-all-start) | async-done | bytes 3594272 | tf_op jit(solution)/shard_map/while/body/eval_jaxpr/all_to_all | solution.py:259
  1307.4 97.2 %while.112 = (s32[]{:T(128)}, bf16[4,4,520,72]{2,3,1,0:T(8,128)(2,1)}, f32[4,4,520]{2,1,0:T(4,128)}, s32[4]{0:T(128)S(1)}, s32[2080]{0:T(1024)S(1)}, /*index=5*/...) while((s32[]{:T(128)}, ...), condition=%wide.region_6.6_spmd, body=%wide.region_3.5_spmd.sunk | while | flops 1302396672 | bytes 59588112 | solution.py:180
  1414.3 24.4 all-to-all-done.1
  1448.2 28.5 multiply_convert_fusion.4
  1476.7 18.6 convert_reduce_fusion.10
  1495.2 12.7 multiply_reduce_fusion.14
  1521.8 14.6 convolution_add_fusion.16
  1558.4 272.4 %while.113 = (s32[]{:T(128)}, f32[4,2080,72]{1,2,0:T(8,128)}, f32[4,2080,72]{1,2,0:T(8,128)}, bf16[4,4,520,72]{2,3,1,0:T(8,128)(2,1)}, s32[4]{0:T(128)S(1)}, /*i...) while((s32[]{:T(128)}, f32[4,2080,72]{1,2,0:T(8,128)}, ...), condition=%wide.region_13.13_spmd.clone, body=%wide.region_11.12_spmd.clone.sunk | while | flops 3161417472 | bytes 194342864 | solution.py:226
  1574.6 14.9 multiply_reduce_fusion.16
  1589.5 15.8 multiply_convert_fusion.5
  1641.4 14.9 multiply_reduce_fusion.16
  1656.3 15.8 multiply_convert_fusion.5
  1709.8 14.9 multiply_reduce_fusion.16
  1724.7 15.8 multiply_convert_fusion.5
  1778.2 14.8 multiply_reduce_fusion.16
  1793.0 15.8 multiply_convert_fusion.5
  1859.6 16.6 convolution_add_fusion.17
  1876.2 53.6 %all-to-all-done.3 = bf16[2080,3,4,72]{3,2,1,0:T(4,128)(2,1)} async-done(((bf16[2080,3,4,72]{3,2,1,0:T(4,128)(2,1)}), bf16[2080,3,4,72]{3,2,1,0:T(4,128)(2,1)}, u32[]{:S(2)}, u32[]{:S(2)}) %all-to-all-start.3) | async-done | bytes 3594272 | tf_op jit(solution)/shard_map/while/body/eval_jaxpr/all_to_all | solution.py:291
  2019.3 48.5 %all-to-all-done = bf16[520,3,16,72]{0,3,1,2:T(8,128)(2,1)} async-done(((bf16[520,3,16,72]{0,3,1,2:T(8,128)(2,1)}), bf16[520,3,16,72]{0,3,1,2:T(8,128)(2,1)}, u32[]{:S(2)}, u32[]{:S(2)}) %all-to-all-start) | async-done | bytes 3594272 | tf_op jit(solution)/shard_map/while/body/eval_jaxpr/all_to_all | solution.py:259
  2086.4 97.1 %while.112 = (s32[]{:T(128)}, bf16[4,4,520,72]{2,3,1,0:T(8,128)(2,1)}, f32[4,4,520]{2,1,0:T(4,128)}, s32[4]{0:T(128)S(1)}, s32[2080]{0:T(1024)S(1)}, /*index=5*/...) while((s32[]{:T(128)}, ...), condition=%wide.region_6.6_spmd, body=%wide.region_3.5_spmd.sunk | while | flops 1302396672 | bytes 59588112 | solution.py:180
  2193.2 23.9 all-to-all-done.1
  2226.6 28.5 multiply_convert_fusion.4
  2255.1 18.6 convert_reduce_fusion.10
  2300.2 21.5 convolution_add_fusion.16
  2346.3 272.4 %while.113 = (s32[]{:T(128)}, f32[4,2080,72]{1,2,0:T(8,128)}, f32[4,2080,72]{1,2,0:T(8,128)}, bf16[4,4,520,72]{2,3,1,0:T(8,128)(2,1)}, s32[4]{0:T(128)S(1)}, /*i...) while((s32[]{:T(128)}, f32[4,2080,72]{1,2,0:T(8,128)}, ...), condition=%wide.region_13.13_spmd.clone, body=%wide.region_11.12_spmd.clone.sunk | while | flops 3161417472 | bytes 194342864 | solution.py:226
  2362.4 14.9 multiply_reduce_fusion.16
  2377.3 15.8 multiply_convert_fusion.5
  2429.3 14.9 multiply_reduce_fusion.16
  2444.1 15.8 multiply_convert_fusion.5
  2497.6 14.9 multiply_reduce_fusion.16
  2512.5 15.8 multiply_convert_fusion.5
  2566.0 14.8 multiply_reduce_fusion.16
  2580.8 15.8 multiply_convert_fusion.5
  2647.4 22.6 convolution_add_fusion.17
  2670.1 47.6 %all-to-all-done.3 = bf16[2080,3,4,72]{3,2,1,0:T(4,128)(2,1)} async-done(((bf16[2080,3,4,72]{3,2,1,0:T(4,128)(2,1)}), bf16[2080,3,4,72]{3,2,1,0:T(4,128)(2,1)}, u32[]{:S(2)}, u32[]{:S(2)}) %all-to-all-start.3) | async-done | bytes 3594272 | tf_op jit(solution)/shard_map/while/body/eval_jaxpr/all_to_all | solution.py:291
  2740.7 16.8 convolution_add_fusion.14
  2825.5 17.8 copy.93
  2856.0 15.0 copy.103
  2873.5 19.7 reduce-scatter.31.cloned.1.call-done
  2895.9 84.0 %reduce-scatter.33.cloned.1.call-done = bf16[864,1152]{1,0:T(8,128)(2,1)} async-done(((bf16[3456,1152]{1,0:T(8,128)(2,1)}), bf16[864,1152]{1,0:T(8,128)(2,1)}) %reduce-scatter.33.cloned.1.call-update) | async-done | bytes 1990672
  2984.1 103.4 %reduce-scatter.29.cloned.1.call-done = bf16[4608,288]{0,1:T(8,128)(2,1)} async-done(((bf16[4608,1152]{0,1:T(8,128)(2,1)}), bf16[4608,288]{0,1:T(8,128)(2,1)}) %reduce-scatter.29.cloned.1.call-update) | async-done | bytes 2654224 | tf_op jit(solution)/shard_map/reduce_scatter | solution.py:114
  3092.2 103.0 %reduce-scatter.37.cloned.1.call-done = bf16[1152,1152]{1,0:T(8,128)(2,1)} async-done(((bf16[4608,1152]{1,0:T(8,128)(2,1)}), bf16[1152,1152]{1,0:T(8,128)(2,1)}) %reduce-scatter.37.cloned.1.call-update) | async-done | bytes 2654224
  3202.7 15.8 all-reduce.17
  3219.1 26.8 all-reduce.15
  3247.6 17.2 reduce-scatter.21.cloned.1.call-done
  3266.5 34.5 %reduce-scatter.23.cloned.1.call-done = bf16[144,864]{1,0:T(8,128)(2,1)} async-done(((bf16[1152,864]{1,0:T(8,128)(2,1)}), bf16[144,864]{1,0:T(8,128)(2,1)}) %reduce-scatter.23.cloned.1.call-update) | async-done | bytes 248848 | tf_op jit(solution)/shard_map/reduce_scatter | solution.py:125
  3302.8 43.1 %reduce-scatter.39.cloned.1.call-done = bf16[576,288]{1,0:T(8,128)(2,1)} async-done(((bf16[4608,288]{1,0:T(8,128)(2,1)}), bf16[576,288]{1,0:T(8,128)(2,1)}) %reduce-scatter.39.cloned.1.call-update) | async-done | bytes 331792
  3348.0 36.5 %reduce-scatter.27.cloned.1.call-done = bf16[144,1152]{1,0:T(8,128)(2,1)} async-done(((bf16[1152,1152]{1,0:T(8,128)(2,1)}), bf16[144,1152]{1,0:T(8,128)(2,1)}) %reduce-scatter.27.cloned.1.call-update) | async-done | bytes 331792 | tf_op jit(solution)/shard_map/reduce_scatter | solution.py:131
  (790 shorter events, 1012.4 us)
Async XLA Ops:
  7.2 16.2 copy-start.46
  7.2 17.4 copy-start.86
  7.2 135.9 %all-reduce.20.cloned.1.call-start = ((), (), s32[]{:S(2)}) async-start(), calls=%async_computation.29 | async-start | bytes 258048
  14.1 197.8 %all-gather.24.cloned.1.call-start = ((), (), s32[]{:S(2)}) async-start(), calls=%async_computation.21 | async-start | bytes 5474304 | tf_op jit(solution)/shard_map/all_gather | solution.py:368
  15.9 286.1 %all-gather.20.cloned.1.call-start = ((), (), s32[]{:S(2)}) async-start(), calls=%async_computation.19 | async-start | bytes 10948608 | tf_op jit(solution)/shard_map/all_gather | solution.py:363
  18.1 433.0 %all-gather.22.cloned.1.call-start = ((), (), s32[]{:S(2)}) async-start(), calls=%async_computation.20 | async-start | bytes 16422912 | tf_op jit(solution)/shard_map/all_gather | solution.py:367
  20.3 636.3 %all-gather.28.cloned.1.call-start = ((), (), s32[]{:S(2)}) async-start(), calls=%async_computation.23 | async-start | bytes 21897216 | tf_op jit(solution)/shard_map/all_gather | solution.py:374
  23.3 935.2 %all-gather.26.cloned.1.call-start = ((), (), s32[]{:S(2)}) async-start(), calls=%async_computation.22 | async-start | bytes 21897216 | tf_op jit(solution)/shard_map/all_gather | solution.py:372
  24.3 2846.7 %reduce-scatter.35.cloned.1.call-start = ((), (), s32[]{:S(2)}) async-start(), calls=%async_computation.26 | async-start | bytes 3317760
  1233.3 55.5 %all-to-all-start = ((bf16[520,3,16,72]{0,3,1,2:T(8,128)(2,1)}), bf16[520,3,16,72]{0,3,1,2:T(8,128)(2,1)}, u32[]{:S(2)}, u32[]{:S(2)}) async-start(bf16[520,3,16,72]{0,3,1,2:T(8,128)(2,1)} %copy.123), calls=%async_computation | async-start | bytes 8847360 | tf_op jit(solution)/shard_map/while/body/eval_jaxpr/all_to_all | solution.py:259
  1408.9 34.0 %copy-start.4 = (f32[520,1152]{1,0:T(8,128)S(1)}, f32[520,1152]{1,0:T(8,128)}, u32[]{:S(2)}) copy-start(f32[520,1152]{1,0:T(8,128)} %copy-done.3) | copy-start | bytes 7188484 | tf_op jit(solution)/shard_map/while
  1408.9 34.0 %copy-start.31 = (f32[1152]{0:T(1024)S(1)}, f32[1152]{0:T(1024)}, u32[]{:S(2)}) copy-start(f32[1152]{0:T(1024)} %get-tuple-element.1835) | copy-start | bytes 13828 | tf_op jit(solution)/shard_map/while
  1408.9 29.8 all-to-all-start.1
  1414.3 94.4 %copy-start.34 = (f32[520]{0:T(1024)}, f32[520]{0:T(1024)S(1)}, u32[]{:S(2)}) copy-start(f32[520]{0:T(1024)S(1)} %convert_reduce_fusion.9) | copy-start | bytes 6244 | tf_op jit(solution)/shard_map/while
  1447.4 29.3 copy-start.6
  1476.7 18.6 copy-start.7
  1517.4 36.9 %all-to-all-start.2 = ((bf16[520,16,72]{0,2,1:T(8,128)(2,1)}), bf16[520,16,72]{0,2,1:T(8,128)(2,1)}, u32[]{:S(2)}, u32[]{:S(2)}) async-start(bf16[520,16,72]{0,2,1:T(8,128)(2,1)} %bitcast.259), calls=%async_computation.2 | async-start | bytes 2949120 | tf_op jit(solution)/shard_map/while/body/eval_jaxpr/all_to_all | solution.py:289
  1521.8 14.6 copy-start.65
  1521.8 14.6 copy-start.82
  1536.4 12.5 copy-start.66
  1536.4 12.5 copy-start.53
  1536.4 12.5 copy-start.68
  1536.4 13.1 copy-start.10
  1536.4 13.1 copy-start.13
  1683.2 10.9 copy-start.24
  1751.6 10.9 copy-start.24
  1819.9 10.8 copy-start.24
  1854.1 75.8 %all-to-all-start.3 = ((bf16[2080,3,4,72]{3,2,1,0:T(4,128)(2,1)}), bf16[2080,3,4,72]{3,2,1,0:T(4,128)(2,1)}, u32[]{:S(2)}, u32[]{:S(2)}) async-start(bf16[2080,3,4,72]{3,2,1,0:T(4,128)(2,1)} %copy.130), calls=%async_computation.3 | async-start | bytes 12779520 | tf_op jit(solution)/shard_map/while/body/eval_jaxpr/all_to_all | solution.py:291
  1859.5 16.7 copy-start.51
  1859.5 16.7 copy-start.41
  1940.3 12.5 copy-start.14
  1940.3 12.5 copy-start.81
  2013.6 54.2 %all-to-all-start = ((bf16[520,3,16,72]{0,3,1,2:T(8,128)(2,1)}), bf16[520,3,16,72]{0,3,1,2:T(8,128)(2,1)}, u32[]{:S(2)}, u32[]{:S(2)}) async-start(bf16[520,3,16,72]{0,3,1,2:T(8,128)(2,1)} %copy.123), calls=%async_computation | async-start | bytes 8847360 | tf_op jit(solution)/shard_map/while/body/eval_jaxpr/all_to_all | solution.py:259
  2187.8 33.5 copy-start.4
  2187.8 33.5 copy-start.31
  2187.8 29.3 all-to-all-start.1
  2193.2 93.9 %copy-start.34 = (f32[520]{0:T(1024)}, f32[520]{0:T(1024)S(1)}, u32[]{:S(2)}) copy-start(f32[520]{0:T(1024)S(1)} %convert_reduce_fusion.9) | copy-start | bytes 6244 | tf_op jit(solution)/shard_map/while
  2225.8 29.3 copy-start.6
  2255.1 18.6 copy-start.7
  2295.8 46.4 %all-to-all-start.2 = ((bf16[520,16,72]{0,2,1:T(8,128)(2,1)}), bf16[520,16,72]{0,2,1:T(8,128)(2,1)}, u32[]{:S(2)}, u32[]{:S(2)}) async-start(bf16[520,16,72]{0,2,1:T(8,128)(2,1)} %bitcast.259), calls=%async_computation.2 | async-start | bytes 2949120 | tf_op jit(solution)/shard_map/while/body/eval_jaxpr/all_to_all | solution.py:289
  2300.2 21.5 copy-start.65
  2300.2 21.5 copy-start.82
  2321.7 12.5 copy-start.66
  2321.7 12.5 copy-start.53
  2321.7 12.5 copy-start.68
  2321.7 13.1 copy-start.10
  2321.7 13.1 copy-start.13
  2471.0 10.9 copy-start.24
  2539.4 10.9 copy-start.24
  2641.9 75.8 %all-to-all-start.3 = ((bf16[2080,3,4,72]{3,2,1,0:T(4,128)(2,1)}), bf16[2080,3,4,72]{3,2,1,0:T(4,128)(2,1)}, u32[]{:S(2)}, u32[]{:S(2)}) async-start(bf16[2080,3,4,72]{3,2,1,0:T(4,128)(2,1)} %copy.130), calls=%async_computation.3 | async-start | bytes 12779520 | tf_op jit(solution)/shard_map/while/body/eval_jaxpr/all_to_all | solution.py:291
  2647.3 22.7 copy-start.51
  2647.4 22.7 copy-start.41
  2728.2 12.5 copy-start.14
  2728.2 12.5 copy-start.81
  2740.7 16.8 copy-start.39
  2789.7 103.5 %reduce-scatter.31.cloned.1.call-start = ((), (), s32[]{:S(2)}) async-start(), calls=%async_computation.24 | async-start | bytes 6635520
  2805.3 174.6 %reduce-scatter.33.cloned.1.call-start = ((), (), s32[]{:S(2)}) async-start(), calls=%async_computation.25 | async-start | bytes 9953280
  2825.4 262.0 %reduce-scatter.29.cloned.1.call-start = ((), (), s32[]{:S(2)}) async-start(), calls=%async_computation.18 | async-start | bytes 13271040 | tf_op jit(solution)/shard_map/reduce_scatter | solution.py:114
  2843.3 351.9 %reduce-scatter.37.cloned.1.call-start = ((), (), s32[]{:S(2)}) async-start(), calls=%async_computation.27 | async-start | bytes 13271040
  2871.0 375.0 %reduce-scatter.25.cloned.1.call-start = ((), (), s32[]{:S(2)}) async-start(), calls=%async_computation.16 | async-start | bytes 995328 | tf_op jit(solution)/shard_map/reduce_scatter | solution.py:128
  2873.4 391.4 %reduce-scatter.21.cloned.1.call-start = ((), (), s32[]{:S(2)}) async-start(), calls=%async_computation.14 | async-start | bytes 1990656 | tf_op jit(solution)/shard_map/reduce_scatter | solution.py:122
  2895.9 405.2 %reduce-scatter.23.cloned.1.call-start = ((), (), s32[]{:S(2)}) async-start(), calls=%async_computation.15 | async-start | bytes 2322432 | tf_op jit(solution)/shard_map/reduce_scatter | solution.py:125
  2984.0 361.9 %reduce-scatter.39.cloned.1.call-start = ((), (), s32[]{:S(2)}) async-start(), calls=%async_computation.28 | async-start | bytes 3981312
  3092.2 292.3 %reduce-scatter.27.cloned.1.call-start = ((), (), s32[]{:S(2)}) async-start(), calls=%async_computation.17 | async-start | bytes 2985984 | tf_op jit(solution)/shard_map/reduce_scatter | solution.py:131
  (149 other events, 804.9 us)
Sparse Core Ops, SparseCore 0:
  14.5 128.6 all-reduce.19
  147.1 64.7 all-gather.23
  215.7 86.2 all-gather.19
  305.8 109.4 all-gather.21
  419.0 133.9 all-gather.27
  556.8 133.9 all-gather.25
  2789.8 38.0 reduce-scatter.34
  2831.2 61.9 reduce-scatter.30
  2896.6 83.2 reduce-scatter.32
  2982.9 104.5 reduce-scatter.28
  3090.6 104.6 reduce-scatter.36
  3197.4 31.9 reduce-scatter.24
  3231.8 32.9 reduce-scatter.20
  3267.1 33.9 reduce-scatter.22
  3303.3 42.4 reduce-scatter.38
  3348.0 36.3 reduce-scatter.26
where the time goes:
time: 3410 us; the launch traced here: 3390 us
  other arithmetic  1050 us (31%)
  matrix products  830 us (24%)
  waiting for transfers between devices  827 us (24%)
  local copies, waits for them, and re-layouts  473 us (14%)
  blocking collectives  113 us (3%)
  loops' own time  47 us (1%)
  starting transfers between devices  39.1 us (1%)
    unnamed x22, waiting for transfers between devices  297 us
    all_gather x1, other arithmetic, body(): lax.all_gather(hidden_weight.reshape(1, -1), ('batch', 'seq'), axis=0, ti...  226 us
    all_gather x1, other arithmetic, body(): lax.all_gather(down_weight.reshape(1, -1), ('batch', 'seq'), axis=0, tile...  225 us
    all_gather x1, other arithmetic, body(): lax.all_gather(qkv_weight.reshape(1, -1), ('batch', 'seq'), axis=0, tiled...  167 us
    dot_general x16, matrix products, block_scores(): jnp.einsum('hqd,hkd->hqk', query_block, key_heads, preferred_element_type...  165 us
    unnamed x76, local copies, waits for them, and re-layouts  161 us
    dot_general x10, matrix products, outer_dot(): lax.dot_general(left_side, right_side, (((0,), (0,)), ((), ())), preferre...  128 us
    convert_element_type x8, other arithmetic, one_step(): grad_scores = (soft * (grad_soft - row_dot)).astype(jnp.bfloat16)  126 us
  transfers between devices with their start and end apart: 24, of which 17 were waited for; matrix products, arithmetic and copies ran while one was open for 28% of the time, Pallas kernels for 0%

commit v1 on v0

v1 whole, which is shorter than its diff:
```python
import jax
import jax.numpy as jnp
from jax import lax
from jax.experimental import pallas as pl
from jax.experimental.pallas import tpu as pltpu
from jax.sharding import PartitionSpec as P

HEADS = 16
HEAD_DIM = 72
LANES = 128
epsilon = 1e-05
masked_score = -1e30
VMEM_BYTES = 60 * 1024 * 1024
def nt_dot(left_side, right_side):
    return lax.dot_general(
        left_side, right_side, (((1,), (1,)), ((), ())), preferred_element_type=jnp.float32
    )


def tn_dot(left_side, right_side):
    return lax.dot_general(
        left_side, right_side, (((0,), (0,)), ((), ())), preferred_element_type=jnp.float32
    )


def nn_dot(left_side, right_side):
    return lax.dot_general(
        left_side, right_side, (((1,), (0,)), ((), ())), preferred_element_type=jnp.float32
    )


def split_heads(wide, head_ref, start=0):
    rows = wide.shape[0]
    pad = jnp.zeros((rows, LANES - HEAD_DIM), wide.dtype)
    for head in range(HEADS):
        piece = wide[:, head * HEAD_DIM : (head + 1) * HEAD_DIM]
        head_ref[head, start : start + rows] = jnp.concatenate([piece, pad], axis=1)


def split_keys(own_ref, far_ref, kh, vh):
    features = own_ref.shape[2] // 2
    start = 0
    for ref in (own_ref, far_ref):
        split_heads(ref[0, :, :features], kh, start)
        split_heads(ref[0, :, features:], vh, start)
        start += ref.shape[1]


def join_heads(head_ref):
    return jnp.concatenate([head_ref[head][:, :HEAD_DIM] for head in range(HEADS)], axis=1)


def chunk_of(rows):
    for count in (4, 2, 1):
        if rows % (count * 16) == 0:
            return rows // count
    return rows


def attend_kernel(
    q_ref, own_ref, far_ref, qid_ref, kid_ref, old_out, old_lse, out_ref, lse_ref,
    qh, kh, vh, score, prob,
):
    split_heads(q_ref[0], qh)
    split_keys(own_ref, far_ref, kh, vh)
    key_rows = kh.shape[1]
    step = chunk_of(key_rows)
    scale = HEAD_DIM ** (-0.5)
    query_ids = qid_ref[0]

    def one_head(head, carry):
        query = qh[head]
        top = jnp.full((1, query.shape[0]), masked_score, jnp.float32)
        for start in range(0, key_rows, step):
            part = nt_dot(kh[head, start : start + step], query) * scale
            part = jnp.where(kid_ref[0, start : start + step] == query_ids, part, masked_score)
            score[start : start + step] = part
            top = jnp.maximum(top, jnp.max(part, axis=0, keepdims=True))
        total = jnp.zeros_like(top)
        for start in range(0, key_rows, step):
            part = jnp.exp(score[start : start + step] - top)
            total = total + jnp.sum(part, axis=0, keepdims=True)
            prob[start : start + step] = part.astype(jnp.bfloat16)
        mixed = tn_dot(vh[head], prob[...]) / total
        qh[head] = mixed.T.astype(jnp.bfloat16)
        lse_ref[0, pl.ds(head, 1)] = top + jnp.log(total)
        return carry

    lax.fori_loop(0, HEADS, one_head, 0)
    out_ref[0] = join_heads(qh)


def attend(query, own, far, query_ids, key_ids, row, out, level):
    rows, width, features = query.shape
    far_rows = far.shape[1]
    key_rows = width + far_rows
    here = lambda i: (row, 0, 0)
    only = lambda i: (0, 0, 0)
    wide = pl.BlockSpec((1, width, features), here)
    levels = pl.BlockSpec((1, HEADS, width), here)
    return pl.pallas_call(
        attend_kernel,
        grid=(1,),
        in_specs=[
            wide,
            pl.BlockSpec((1, width, 2 * features), here),
            pl.BlockSpec((1, far_rows, 2 * features), only),
            pl.BlockSpec((1, 1, width), here),
            pl.BlockSpec((1, key_rows, 1), here),
            pl.BlockSpec(memory_space=pl.ANY),
            pl.BlockSpec(memory_space=pl.ANY),
        ],
        out_specs=[wide, levels],
        out_shape=[
            jax.ShapeDtypeStruct((rows, width, features), jnp.bfloat16),
            jax.ShapeDtypeStruct((rows, HEADS, width), jnp.float32),
        ],
        scratch_shapes=[
            pltpu.VMEM((HEADS, width, LANES), jnp.bfloat16),
            pltpu.VMEM((HEADS, key_rows, LANES), jnp.bfloat16),
            pltpu.VMEM((HEADS, key_rows, LANES), jnp.bfloat16),
            pltpu.VMEM((key_rows, width), jnp.float32),
            pltpu.VMEM((key_rows, width), jnp.bfloat16),
        ],
        input_output_aliases={5: 0, 6: 1},
        compiler_params=pltpu.CompilerParams(vmem_limit_bytes=VMEM_BYTES),
        cost_estimate=pl.CostEstimate(
            flops=4 * HEADS * width * key_rows * LANES,
            transcendentals=HEADS * width * key_rows,
            bytes_accessed=4 * features * (width + key_rows),
        ),
        name="attend",
    )(query, own, far, query_ids[:, None, :], key_ids[:, :, None], out, level)


def attend_back_kernel(
    q_ref, own_ref, far_ref, o_ref, g_ref, lse_ref, qid_ref, kid_ref, old_dq, old_dkv,
    dq_ref, dkv_ref, qh, kh, vh, oh, gh, prob, slope,
):
    split_heads(q_ref[0], qh)
    features = q_ref.shape[2]
    split_keys(own_ref, far_ref, kh, vh)
    split_heads(o_ref[0], oh)
    split_heads(g_ref[0], gh)
    key_rows = kh.shape[1]
    step = chunk_of(key_rows)
    scale = HEAD_DIM ** (-0.5)
    query_ids = qid_ref[0]

    def one_head(head, carry):
        query = qh[head]
        grad = gh[head]
        level = lse_ref[0, pl.ds(head, 1)]
        overlap = oh[head].astype(jnp.float32) * grad.astype(jnp.float32)
        row_dot = jnp.sum(overlap.T, axis=0, keepdims=True)
        for start in range(0, key_rows, step):
            part = nt_dot(kh[head, start : start + step], query) * scale
            part = jnp.where(kid_ref[0, start : start + step] == query_ids, part, masked_score)
            soft = jnp.exp(part - level)
            prob[start : start + step] = soft.astype(jnp.bfloat16)
            turn = nt_dot(vh[head, start : start + step], grad)
            slope[start : start + step] = (soft * (turn - row_dot)).astype(jnp.bfloat16)
        value_grad = nn_dot(prob[...], grad)
        query_grad = tn_dot(kh[head], slope[...]) * scale
        key_grad = nn_dot(slope[...], query) * scale
        vh[head] = value_grad.astype(jnp.bfloat16)
        kh[head] = key_grad.astype(jnp.bfloat16)
        qh[head] = query_grad.T.astype(jnp.bfloat16)
        return carry

    lax.fori_loop(0, HEADS, one_head, 0)
    dq_ref[0] = join_heads(qh)
    dkv_ref[0, :, :features] = join_heads(kh)
    dkv_ref[0, :, features:] = join_heads(vh)


def attend_back(
    query, own, far, mixed, grad, level, query_ids, key_ids, row, query_grad, both_grad
):
    rows, width, features = query.shape
    far_rows = far.shape[1]
    key_rows = width + far_rows
    here = lambda i: (row, 0, 0)
    only = lambda i: (0, 0, 0)
    wide = pl.BlockSpec((1, width, features), here, pipeline_mode=pl.Buffered(1))
    return pl.pallas_call(
        attend_back_kernel,
        grid=(1,),
        in_specs=[
            wide,
            pl.BlockSpec((1, width, 2 * features), here, pipeline_mode=pl.Buffered(1)),
            pl.BlockSpec((1, far_rows, 2 * features), only, pipeline_mode=pl.Buffered(1)),
            wide,
            wide,
            pl.BlockSpec((1, HEADS, width), here),
            pl.BlockSpec((1, 1, width), here),
            pl.BlockSpec((1, key_rows, 1), here),
            pl.BlockSpec(memory_space=pl.ANY),
            pl.BlockSpec(memory_space=pl.ANY),
        ],
        out_specs=[
            pl.BlockSpec((1, width, features), here),
            pl.BlockSpec((1, key_rows, 2 * features), here),
        ],
        out_shape=[
            jax.ShapeDtypeStruct((rows, width, features), jnp.bfloat16),
            jax.ShapeDtypeStruct((rows, key_rows, 2 * features), jnp.bfloat16),
        ],
        scratch_shapes=[
            pltpu.VMEM((HEADS, width, LANES), jnp.bfloat16),
            pltpu.VMEM((HEADS, key_rows, LANES), jnp.bfloat16),
            pltpu.VMEM((HEADS, key_rows, LANES), jnp.bfloat16),
            pltpu.VMEM((HEADS, width, LANES), jnp.bfloat16),
            pltpu.VMEM((HEADS, width, LANES), jnp.bfloat16),
            pltpu.VMEM((key_rows, width), jnp.bfloat16),
            pltpu.VMEM((key_rows, width), jnp.bfloat16),
        ],
        input_output_aliases={8: 0, 9: 1},
        compiler_params=pltpu.CompilerParams(vmem_limit_bytes=VMEM_BYTES),
        cost_estimate=pl.CostEstimate(
            flops=10 * HEADS * width * key_rows * LANES,
            transcendentals=HEADS * width * key_rows,
            bytes_accessed=8 * features * (width + key_rows),
        ),
        name="attend_back",
    )(
        query,
        own,
        far,
        mixed,
        grad,
        level,
        query_ids[:, None, :],
        key_ids[:, :, None],
        query_grad,
        both_grad,
    )


def weight_grad_kernel(outer, here_ref, left_ref, right_ref, keep_ref, give_ref, total):
    total[...] = tn_dot(left_ref[...], right_ref[...]).astype(jnp.bfloat16)
    inner = total.shape[0] // (2 * outer)
    here = here_ref[0]
    for group in range(outer):
        start = group * 2 * inner
        mine = pl.multiple_of(start + here * inner, 16)
        other = pl.multiple_of(start + (1 - here) * inner, 16)
        span = slice(group * inner, (group + 1) * inner)
        keep_ref[span] = total[pl.ds(mine, inner)]
        give_ref[span] = total[pl.ds(other, inner)]


def weight_grad(left, right, here, outer, row_blocks, column_blocks, name):
    tokens = left.shape[0]
    model = left.shape[1] // row_blocks
    width = right.shape[1] // column_blocks
    half = jax.ShapeDtypeStruct((left.shape[1] // 2, right.shape[1]), jnp.bfloat16)
    spec = pl.BlockSpec((model // 2, width), lambda i, j, here: (i, j))
    return pl.pallas_call(
        lambda *refs: weight_grad_kernel(outer, *refs),
        grid_spec=pltpu.PrefetchScalarGridSpec(
            num_scalar_prefetch=1,
            grid=(row_blocks, column_blocks),
            in_specs=[
                pl.BlockSpec((tokens, model), lambda i, j, here: (0, i)),
                pl.BlockSpec((tokens, width), lambda i, j, here: (0, j)),
            ],
            out_specs=[spec, spec],
            scratch_shapes=[pltpu.VMEM((model, width), jnp.bfloat16)],
        ),
        out_shape=[half, half],
        compiler_params=pltpu.CompilerParams(vmem_limit_bytes=VMEM_BYTES),
        cost_estimate=pl.CostEstimate(
            flops=2 * tokens * left.shape[1] * right.shape[1],
            transcendentals=0,
            bytes_accessed=2 * (tokens + right.shape[1]) * (left.shape[1] + right.shape[1]),
        ),
        name=name,
    )(here.astype(jnp.int32).reshape(1), left, right)


def column_chunks(width):
    cut = width // 256 // 2 * 256
    return ((0, cut), (cut, width)) if cut else ((0, width),)


def middle_kernel(
    stream_ref, att_ref, cot_ref, used_ref, proj_ref, hidden_ref, down_ref,
    proj_bias_ref, gain_ref, shift_ref, hidden_bias_ref, down_bias_ref,
    out_ref, second_ref, act_ref, pre_ref, middle_grad_ref, proj_grad_ref, att_grad_ref,
    hidden_sum_ref, sums_ref,
    low, normal, scale, branch, total, back,
):
    step = pl.program_id(1)
    steps = pl.num_programs(1)

    @pl.when(step == 0)
    def _():
        middle = stream_ref[...] + nn_dot(att_ref[...], proj_ref[...]) + proj_bias_ref[...]
        centred = middle - jnp.mean(middle, axis=-1, keepdims=True)
        inverse = lax.rsqrt(jnp.mean(centred * centred, axis=-1, keepdims=True) + epsilon)
        unit = centred * inverse
        normal[...] = unit
        scale[...] = inverse
        second = (unit * gain_ref[...] + shift_ref[...]).astype(jnp.bfloat16)
        low[...] = second
        second_ref[...] = second
        branch[...] = (cot_ref[...].astype(jnp.float32) * used_ref[...]).astype(jnp.bfloat16)
        total[...] = middle + down_bias_ref[...]
        back[...] = jnp.zeros_like(back)

    for start, stop in column_chunks(hidden_ref.shape[2]):
        pre_act = nn_dot(low[...], hidden_ref[0, :, start:stop]) + hidden_bias_ref[0, :, start:stop]
        grad_act = nt_dot(branch[...], down_ref[0, start:stop])
        below = 0.5 + 0.5 * lax.erf(pre_act * (0.5**0.5))
        density = jnp.exp(-0.5 * pre_act * pre_act) * ((2.0 * jnp.pi) ** -0.5)
        act = (pre_act * below).astype(jnp.bfloat16)
        grad_pre = (grad_act * (below + pre_act * density)).astype(jnp.bfloat16)
        act_ref[:, start:stop] = act
        pre_ref[:, start:stop] = grad_pre
        hidden_sum_ref[0, 0, :, start:stop] = jnp.sum(
            grad_pre.astype(jnp.float32), axis=0, keepdims=True
        )
        total[...] += nn_dot(act, down_ref[0, start:stop])
        back[...] += nt_dot(grad_pre, hidden_ref[0, :, start:stop])

    @pl.when(step == steps - 1)
    def _():
        out_ref[...] = total[...].astype(jnp.bfloat16)
        grad = back[...]
        unit = normal[...]
        part = grad * gain_ref[...]
        mean_part = jnp.mean(part, axis=-1, keepdims=True)
        mean_both = jnp.mean(part * unit, axis=-1, keepdims=True)
        grad_out = cot_ref[...].astype(jnp.float32) * used_ref[...]
        grad_middle = grad_out + (part - mean_part - unit * mean_both) * scale[...]
        middle_grad_ref[...] = grad_middle
        grad_low = grad_middle.astype(jnp.bfloat16)
        proj_grad_ref[...] = grad_low
        att_grad_ref[...] = nt_dot(grad_low, proj_ref[...]).astype(jnp.bfloat16)
        sums_ref[0, 0:1] = jnp.sum(grad * unit, axis=0, keepdims=True)
        sums_ref[0, 1:2] = jnp.sum(grad, axis=0, keepdims=True)
        sums_ref[0, 2:3] = jnp.sum(grad_low.astype(jnp.float32), axis=0, keepdims=True)
        sums_ref[0, 3:4] = jnp.sum(grad_out, axis=0, keepdims=True)


def token_block(tokens):
    return tokens // 4 if tokens % 64 == 0 else tokens


def middle_block(
    stream, attended, cotangent, used, proj, hidden, down, proj_bias, gain, shift, hidden_bias,
    down_bias,
):
    tokens, model = stream.shape
    steps = hidden.shape[0]
    rows = token_block(tokens)
    blocks = tokens // rows
    by_rows = pl.BlockSpec((rows, model), lambda i, s: (i, 0))
    by_step = pl.BlockSpec((rows, model), lambda i, s: (i, s))
    vector = pl.BlockSpec((1, model), lambda i, s: (0, 0))
    low_rows = jax.ShapeDtypeStruct((tokens, model), jnp.bfloat16)
    low_steps = jax.ShapeDtypeStruct((tokens, steps * model), jnp.bfloat16)
    flops = 2 * tokens * model * model * (4 * steps + 2)
    return pl.pallas_call(
        middle_kernel,
        grid=(blocks, steps),
        in_specs=[
            by_rows,
            by_rows,
            by_rows,
            pl.BlockSpec((rows, 1), lambda i, s: (i, 0)),
            pl.BlockSpec((model, model), lambda i, s: (0, 0), pipeline_mode=pl.Buffered(1)),
            pl.BlockSpec((1, model, model), lambda i, s: (s, 0, 0)),
            pl.BlockSpec((1, model, model), lambda i, s: (s, 0, 0)),
            vector,
            vector,
            vector,
            pl.BlockSpec((1, 1, model), lambda i, s: (s, 0, 0)),
            vector,
        ],
        out_specs=[
            by_rows,
            by_rows,
            by_step,
            by_step,
            by_rows,
            by_rows,
            by_rows,
            pl.BlockSpec((1, 1, 1, model), lambda i, s: (i, s, 0, 0)),
            pl.BlockSpec((1, 4, model), lambda i, s: (i, 0, 0)),
        ],
        out_shape=[
            low_rows,
            low_rows,
            low_steps,
            low_steps,
            jax.ShapeDtypeStruct((tokens, model), jnp.float32),
            low_rows,
            low_rows,
            jax.ShapeDtypeStruct((blocks, steps, 1, model), jnp.float32),
            jax.ShapeDtypeStruct((blocks, 4, model), jnp.float32),
        ],
        scratch_shapes=[
            pltpu.VMEM((rows, model), jnp.bfloat16),
            pltpu.VMEM((rows, model), jnp.float32),
            pltpu.VMEM((rows, 1), jnp.float32),
            pltpu.VMEM((rows, model), jnp.bfloat16),
            pltpu.VMEM((rows, model), jnp.float32),
            pltpu.VMEM((rows, model), jnp.float32),
        ],
        compiler_params=pltpu.CompilerParams(vmem_limit_bytes=VMEM_BYTES),
        cost_estimate=pl.CostEstimate(
            flops=flops,
            transcendentals=2 * tokens * model * steps,
            bytes_accessed=2 * tokens * model * (2 * steps + 12) + 4 * model * model * steps * blocks,
        ),
        name="middle_block",
    )(
        stream,
        attended,
        cotangent,
        used,
        proj,
        hidden,
        down,
        proj_bias[None],
        gain[None],
        shift[None],
        hidden_bias.reshape(steps, 1, model),
        down_bias[None],
    )


def layer_norm(stream, norm_gain, norm_shift):
    centred = stream - jnp.mean(stream, axis=-1, keepdims=True)
    scale = lax.rsqrt(jnp.mean(centred * centred, axis=-1, keepdims=True) + epsilon)
    normal = centred * scale
    return (normal * norm_gain + norm_shift).astype(jnp.bfloat16), normal, scale


def layer_norm_back(grad, normal, scale, norm_gain):
    part = grad * norm_gain
    mean_part = jnp.mean(part, axis=-1, keepdims=True)
    mean_both = jnp.mean(part * normal, axis=-1, keepdims=True)
    gain_grad = jnp.sum(grad * normal, axis=(0, 1))
    shift_grad = jnp.sum(grad, axis=(0, 1))
    return (part - mean_part - normal * mean_both) * scale, gain_grad, shift_grad


def outer_dot(left_side, right_side):
    return lax.dot_general(
        left_side, right_side, (((0,), (0,)), ((), ())), preferred_element_type=jnp.bfloat16
    )


def dot_last(left_side, right_side):
    return lax.dot_general(
        left_side, right_side, (((2,), (0,)), ((), ())), preferred_element_type=jnp.float32
    )


def dot_back(left_side, right_side):
    return lax.dot_general(
        left_side, right_side, (((2,), (1,)), ((), ())), preferred_element_type=jnp.float32
    )


def dot_tokens(left_side, right_side):
    return lax.dot_general(
        left_side, right_side, (((0, 1), (0, 1)), ((), ())), preferred_element_type=jnp.bfloat16
    )


class Grid:
    def __init__(self):
        self.batch_count = lax.axis_size("batch")
        self.seq_count = lax.axis_size("seq")
        self.seq_index = lax.axis_index("seq")
        batch_index = lax.axis_index("batch")
        self.outer_count = self.batch_count // 2
        self.square = self.seq_count == 4 and self.outer_count == 4
        self.at = {
            "z": batch_index // 2,
            "c": batch_index % 2,
            "y": self.seq_index // 2,
            "x": self.seq_index % 2,
        }

    def index(self, z, c, s):
        return (z * 2 + c) * self.seq_count + s

    def send(self, value, axis, turn=1):
        pairs = []
        for z in range(self.outer_count):
            for c in range(2):
                for s in range(self.seq_count):
                    far_z, far_c, far_s = z, c, s
                    if axis == "z":
                        far_z = (z + turn) % self.outer_count
                    elif axis == "c":
                        far_c = 1 - c
                    elif axis == "y":
                        far_s = s ^ 2
                    else:
                        far_s = s ^ 1
                    pairs.append((self.index(z, c, s), self.index(far_z, far_c, far_s)))
        return lax.ppermute(value, ("batch", "seq"), pairs)

    def shift(self, value, source, target):
        pairs = [
            (b * self.seq_count + source, b * self.seq_count + target)
            for b in range(self.batch_count)
        ]
        return lax.ppermute(value, ("batch", "seq"), pairs)


def tie(value, *others):
    return lax.optimization_barrier((value, others))[0]


def square_gather(grid, shard):
    over_x = grid.send(shard, "x")
    found = jnp.stack([shard, over_x, grid.send(shard, "y"), grid.send(over_x, "y")])
    return jnp.stack(
        [
            lax.dynamic_index_in_dim(found, grid.seq_index ^ place, 0, keepdims=False)
            for place in range(4)
        ]
    )


def pack_lanes(shard):
    rows, columns = shard.shape
    whole = columns // LANES
    rest = columns - whole * LANES
    pieces = [shard[:, k * LANES : (k + 1) * LANES] for k in range(whole)]
    if rest:
        fold = LANES // rest
        step = rows // fold
        last = [shard[k * step : (k + 1) * step, whole * LANES :] for k in range(fold)]
        pieces.append(jnp.concatenate(last, axis=1))
    return jnp.concatenate(pieces, axis=0)


def unpack_lanes(packed, rows, columns):
    whole = columns // LANES
    rest = columns - whole * LANES
    pieces = [packed[k * rows : (k + 1) * rows] for k in range(whole)]
    if rest:
        fold = LANES // rest
        last = packed[whole * rows : whole * rows + rows // fold]
        pieces.append(
            jnp.concatenate([last[:, k * rest : (k + 1) * rest] for k in range(fold)], axis=0)
        )
    return jnp.concatenate(pieces, axis=1)


def rows_kernel(rows, columns, turn_ref, to_ref, *refs):
    blocks, out_ref, found = refs[:8], refs[8], refs[9]
    for block in range(8):
        found[to_ref[block]] = blocks[block][...]
    for core in range(2):
        wide = [unpack_lanes(found[core * 4 + place], rows, columns) for place in range(4)]
        out_ref[core * rows : (core + 1) * rows] = jnp.concatenate(wide, axis=1)


def mixed_kernel(columns, turn_ref, to_ref, *refs):
    blocks, query_ref, both_ref, proj_ref, found = refs[:8], refs[8], refs[9], refs[10], refs[11]
    rows, model = found.shape[1:]
    for block in range(8):
        found[to_ref[block]] = blocks[block][...]
    for core in range(2):
        span = slice(core * rows, (core + 1) * rows)
        parts = [found[core * 4 + place] for place in range(4)]
        wide = jnp.concatenate([part[:, :columns] for part in parts], axis=1)
        query_ref[span] = wide[:, :model]
        both_ref[span] = wide[:, model:]
        proj_ref[span] = jnp.concatenate([part[:, columns:] for part in parts], axis=1)


def assemble(grid, blocks, piece, kernel, widths, rows, name):
    outer = grid.outer_count
    turns = jnp.stack([(grid.at["z"] - z + outer) % outer for z in range(outer)])
    places = [
        (grid.at["c"] ^ (block >> 2)) * 4 + (grid.seq_index ^ (block & 3)) for block in range(8)
    ]
    shapes = [jax.ShapeDtypeStruct((outer * 2 * rows, w), jnp.bfloat16) for w in widths]
    result = pl.pallas_call(
        kernel,
        grid_spec=pltpu.PrefetchScalarGridSpec(
            num_scalar_prefetch=2,
            grid=(outer,),
            in_specs=[pl.BlockSpec(piece, lambda z, turn, to: (turn[z], 0))] * 8,
            out_specs=[pl.BlockSpec((2 * rows, w), lambda z, turn, to: (z, 0)) for w in widths],
            scratch_shapes=[pltpu.VMEM((8,) + piece, jnp.bfloat16)],
        ),
        out_shape=shapes,
        compiler_params=pltpu.CompilerParams(vmem_limit_bytes=VMEM_BYTES),
        cost_estimate=pl.CostEstimate(
            flops=0,
            transcendentals=0,
            bytes_accessed=8 * outer * rows * sum(widths),
        ),
        name=name,
    )(turns.astype(jnp.int32), jnp.stack(places).astype(jnp.int32), *blocks)
    return result


def place_kernel(block_count, outer_count, to_ref, *refs):
    blocks, out_ref, sems = refs[:block_count], refs[block_count], refs[block_count + 1]
    rows = out_ref.shape[1]
    copies = []
    for block in range(block_count):
        for turn in range(outer_count):
            slot = block * outer_count + turn
            copies.append(
                pltpu.make_async_copy(
                    blocks[block].at[pl.ds(turn * rows, rows)], out_ref.at[to_ref[slot]], sems.at[slot]
                )
            )
    for copy in copies:
        copy.start()
    for copy in copies:
        copy.wait()


def place_blocks(grid, blocks):
    outer = grid.outer_count
    rows, columns = blocks[0].shape[0] // outer, blocks[0].shape[1]
    slots = []
    for block in range(8):
        core, place = grid.at["c"] ^ (block >> 2), grid.seq_index ^ (block & 3)
        for turn in range(outer):
            far = (grid.at["z"] - turn + outer) % outer
            slots.append((place * outer + far) * 2 + core)
    count = 8 * outer
    return pl.pallas_call(
        lambda *refs: place_kernel(8, outer, *refs),
        grid_spec=pltpu.PrefetchScalarGridSpec(
            num_scalar_prefetch=1,
            grid=(1,),
            in_specs=[pl.BlockSpec(memory_space=pl.ANY)] * 8,
            out_specs=pl.BlockSpec((count, rows, columns), lambda i, to: (0, 0, 0)),
            scratch_shapes=[pltpu.SemaphoreType.DMA((count,))],
        ),
        compiler_params=pltpu.CompilerParams(vmem_limit_bytes=VMEM_BYTES),
        out_shape=jax.ShapeDtypeStruct((count, rows, columns), blocks[0].dtype),
        cost_estimate=pl.CostEstimate(
            flops=0, transcendentals=0, bytes_accessed=4 * count * rows * columns
        ),
        name="place_blocks",
    )(jnp.stack(slots).astype(jnp.int32), *blocks)


def column_gather(grid, piece, *extra):
    parts = [piece] + [grid.send(piece, "z", turn) for turn in range(1, grid.outer_count)]
    return jnp.concatenate(parts + list(extra), axis=0)


def seq_gather(grid, column, first):
    if first == "x":
        over_x = grid.send(column, "x")
        return [column, over_x, grid.send(column, "y"), grid.send(over_x, "y")]
    over_y = grid.send(column, "y")
    return [column, grid.send(column, "x"), over_y, grid.send(over_y, "x")]


def core_gather(grid, blocks):
    return blocks + [grid.send(block, "c") for block in blocks]


def columns_of_seq(grid, piece):
    rows, columns = piece.shape
    split = piece.reshape(rows, 4, columns // 4).transpose(1, 0, 2)
    mixed = lax.all_to_all(split, "seq", 0, 0)
    return mixed.reshape(4 * rows, columns // 4)


def split_vectors(joint, widths):
    result, start = [], 0
    for width in widths:
        result.append(joint[:, start : start + width].reshape(-1).astype(jnp.float32))
        start += width
    return result


def gather_all(grid, matrices, vectors):
    skip_weight, qkv_weight, proj_weight, hidden_weight, down_weight = matrices
    widths = [vector.shape[0] for vector in vectors]
    joint = jnp.concatenate(vectors)
    if not grid.square:
        wide = [
            lax.all_gather(
                lax.all_gather(shard, "batch", axis=0, tiled=True), "seq", axis=1, tiled=True
            )
            for shard in matrices
        ]
        skip_full, qkv_full, proj_full, hidden_full, down_full = wide
        model = skip_full.shape[1]
        hidden_blocks = jnp.stack(jnp.split(hidden_full, hidden_full.shape[1] // model, axis=1))
        down_blocks = down_full.reshape(-1, model, model)
        joint = lax.all_gather(joint, "seq", axis=0)
        return (
            split_vectors(joint, widths),
            skip_full,
            qkv_full[:, :model],
            qkv_full[:, model:],
            proj_full,
            hidden_blocks,
            down_blocks,
        )
    model = proj_weight.shape[1] * 4
    short = -joint.shape[0] % (8 * LANES)
    extra = jnp.pad(joint, (0, short)).reshape(-1, LANES)
    skip_rows, skip_columns = skip_weight.shape
    skip_piece = pack_lanes(skip_weight)
    skip_column = column_gather(grid, skip_piece, extra)
    skip_blocks = seq_gather(grid, skip_column, "x")
    found = jnp.stack([block[-extra.shape[0] :].reshape(-1) for block in skip_blocks])
    joint = jnp.stack(
        [
            lax.dynamic_index_in_dim(found, grid.seq_index ^ place, 0, keepdims=False)
            for place in range(4)
        ]
    )
    (skip_full,) = assemble(
        grid,
        core_gather(grid, skip_blocks),
        skip_piece.shape,
        lambda *refs: rows_kernel(skip_rows, skip_columns, *refs),
        [model],
        skip_rows,
        "join_skip",
    )
    mixed_piece = jnp.concatenate([qkv_weight, proj_weight], axis=1)
    mixed_piece = tie(mixed_piece, skip_blocks[1], skip_blocks[2])
    mixed_column = column_gather(grid, mixed_piece)
    mixed_blocks = seq_gather(grid, mixed_column, "x")
    query_full, both_full, proj_full = assemble(
        grid,
        core_gather(grid, mixed_blocks),
        mixed_piece.shape,
        lambda *refs: mixed_kernel(qkv_weight.shape[1], *refs),
        [model, 2 * model, model],
        mixed_piece.shape[0],
        "join_mixed",
    )
    hidden_piece = tie(hidden_weight, mixed_column)
    hidden_column = column_gather(grid, hidden_piece)
    hidden_blocks = seq_gather(grid, hidden_column, "y")
    hidden_full = place_blocks(grid, core_gather(grid, hidden_blocks)).reshape(4, -1, model)
    down_rows, down_columns = down_weight.shape
    down_piece = tie(pack_lanes(down_weight), hidden_column)
    down_blocks = seq_gather(grid, column_gather(grid, down_piece), "x")
    (down_full,) = assemble(
        grid,
        core_gather(grid, down_blocks),
        down_piece.shape,
        lambda *refs: rows_kernel(down_rows, down_columns, *refs),
        [model],
        down_rows,
        "join_down",
    )
    return (
        split_vectors(joint, widths),
        skip_full,
        query_full,
        both_full,
        proj_full,
        hidden_full,
        down_full.reshape(-1, model, model),
    )


def add_low(mine, other):
    return (mine.astype(jnp.float32) + other.astype(jnp.float32)).astype(jnp.bfloat16)


class Scatter:
    def __init__(self, grid, keep, give):
        self.grid, self.mine, self.sent = grid, keep, give
        self.got = [grid.send(value, "c") for value in give]

    def push(self, axis, choose):
        here = self.grid.at[axis]
        self.mine = choose(self.values, here)
        self.sent = choose(self.values, 1 - here)
        self.got = [self.grid.send(value, axis) for value in self.sent]

    def pull(self, *after):
        mine, got = self.mine, self.got
        if after:
            mine = tie(mine, *after)
        self.values = [add_low(m, g) for m, g in zip(mine, got, strict=True)]

    def push_outer(self):
        grid = self.grid
        (value,) = self.values
        pick = lambda at: lax.dynamic_index_in_dim(value, at, 0, keepdims=False)
        self.mine = pick(grid.at["z"])
        self.sent = [
            pick((grid.at["z"] + turn) % grid.outer_count) for turn in range(1, grid.outer_count)
        ]
        self.got = [grid.send(value, "z", turn + 1) for turn, value in enumerate(self.sent)]

    def pull_outer(self, *after):
        mine = tie(self.mine, *after) if after else self.mine
        total = mine.astype(jnp.float32)
        for value in self.got:
            total = total + value.astype(jnp.float32)
        return total


def choose_dim(dim):
    return lambda values, at: [
        lax.dynamic_index_in_dim(value, at, dim, keepdims=False) for value in values
    ]


def choose_lanes(values, at):
    half = values[0].shape[-1] // 2
    return [lax.dynamic_slice_in_dim(value, at * half, half, value.ndim - 1) for value in values]


def choose_pair(values, at):
    half = len(values) // 2
    return [jnp.where(at == 0, values[k], values[half + k]) for k in range(half)]


def mixed_shards(grid, part):
    part = part.astype(jnp.bfloat16)
    rows, columns = part.shape
    whole = square_gather(grid, part).reshape(4, rows, 4, columns // 4)
    whole = whole.transpose(0, 2, 1, 3).reshape(16, rows, columns // 4)
    qkv = lax.dynamic_slice_in_dim(whole, 3 * grid.seq_index, 3, 0)
    qkv = qkv.transpose(1, 0, 2).reshape(rows, 3 * columns // 4)
    proj = lax.dynamic_index_in_dim(whole, 12 + grid.seq_index, 0, keepdims=False)
    return qkv.astype(jnp.float32), proj.astype(jnp.float32)


def seq_scatter(value):
    value = lax.psum_scatter(value, "seq", scatter_dimension=1, tiled=True)
    return lax.psum_scatter(value, "batch", scatter_dimension=0, tiled=True).astype(jnp.float32)


def scatter_vectors(grid, vectors):
    if not grid.square:
        totals = lax.psum(tuple(vectors), ("batch", "seq"))
    else:
        sizes = [vector.shape[0] for vector in vectors]
        joint = jnp.concatenate(vectors).reshape(-1, LANES)
        for axis in ("c", "x", "y"):
            joint = joint + grid.send(joint, axis)
        others = [grid.send(joint, "z", turn) for turn in range(1, grid.outer_count)]
        for other in others:
            joint = joint + other
        joint = joint.reshape(-1)
        totals, start = [], 0
        for size in sizes:
            totals.append(joint[start : start + size])
            start += size
    return [
        lax.dynamic_slice_in_dim(
            total, grid.seq_index * (total.shape[0] // grid.seq_count), total.shape[0] // grid.seq_count
        )
        for total in totals
    ]


class Items:
    def __init__(self, grid, segments, occupied, own_rows, all_rows):
        self.grid = grid
        self.segments, self.occupied = segments, occupied
        self.own_rows, self.all_rows = own_rows, all_rows
        self.halo_rows = all_rows - own_rows
        self.border = own_rows * (grid.seq_count // 2)
        tail = slice(self.border - self.halo_rows, self.border)
        self.moved = (segments[:, tail] == segments[:, self.border : self.border + 1]) & (
            occupied[:, tail] > 0
        )

    def of(self, seq_index):
        half = self.grid.seq_count // 2
        start = seq_index * self.own_rows
        rows = self.segments.shape[0]
        segment = lax.dynamic_slice(self.segments, (0, start), (rows, self.own_rows))
        used = lax.dynamic_slice(self.occupied, (0, start), (rows, self.own_rows)) > 0
        gone = jnp.pad(self.moved, ((0, 0), (self.own_rows - self.halo_rows, 0)))
        used = used & ~(gone & (seq_index == half - 1))
        halo_used = self.moved & (seq_index == half)
        halo_segment = self.segments[:, self.border - self.halo_rows : self.border]
        segment = jnp.concatenate([segment, halo_segment], axis=1)
        used = jnp.concatenate([used, halo_used], axis=1)
        alone = 1024 + seq_index * self.all_rows + jnp.arange(self.all_rows, dtype=jnp.int32)
        return jnp.where(used, segment, alone[None]), used


def far_gather(grid, value):
    rows, width, features = value.shape
    half = grid.seq_count // 2
    if half == 2:
        return [grid.send(value[row : row + 1], "x") for row in range(rows)]
    whole = lax.all_gather(value, "seq", axis=0)
    start = grid.seq_index // half * half
    whole = lax.dynamic_slice_in_dim(whole, start, half, 0)
    whole = whole.transpose(1, 0, 2, 3).reshape(rows, half * width, features)
    return [whole[row : row + 1] for row in range(rows)]


def far_ids(grid, items):
    half = grid.seq_count // 2
    if half == 2:
        return items.of(grid.seq_index ^ 1)[0]
    start = grid.seq_index // half * half
    ids = [
        jnp.where(start + part == grid.seq_index, -1, items.of(start + part)[0])
        for part in range(half)
    ]
    return jnp.concatenate(ids, axis=1)


def far_reduce(grid, value):
    half = grid.seq_count // 2
    value = value.astype(jnp.bfloat16)
    if half == 2:
        return grid.send(value, "x").astype(jnp.float32)
    split = value.reshape(half, -1, value.shape[2])
    whole = jnp.zeros((grid.seq_count,) + split.shape[1:], jnp.bfloat16)
    start = grid.seq_index // half * half
    whole = lax.dynamic_update_slice_in_dim(whole, split, start, 0)
    return lax.psum_scatter(whole, "seq", scatter_dimension=0).astype(jnp.float32)[None]


def body(
    inputs,
    skip_inputs,
    out_cotangent,
    segments,
    occupied,
    skip_weight,
    skip_bias,
    first_gain,
    first_shift,
    qkv_weight,
    proj_weight,
    proj_bias,
    second_gain,
    second_shift,
    hidden_weight,
    hidden_bias,
    down_weight,
    down_bias,
):
    grid = Grid()
    own_rows, model = inputs.shape[1], inputs.shape[2]
    all_rows = -(-(own_rows + 16) // 32) * 32
    halo_rows = all_rows - own_rows
    half = grid.seq_count // 2
    vectors, skip_full, query_full, both_full, proj_full, hidden_blocks, down_blocks = gather_all(
        grid,
        [skip_weight, qkv_weight, proj_weight, hidden_weight, down_weight],
        [
            skip_bias,
            first_gain,
            first_shift,
            proj_bias,
            second_gain,
            second_shift,
            hidden_bias,
            down_bias,
        ],
    )
    (
        skip_bias_full,
        gain_one,
        shift_one,
        proj_bias_full,
        gain_two,
        shift_two,
        hidden_bias_full,
        down_bias_full,
    ) = vectors
    items = Items(grid, segments, occupied, own_rows, all_rows)
    query_ids, used = items.of(grid.seq_index)
    key_ids = jnp.concatenate([query_ids, far_ids(grid, items)], axis=1)
    tails = jnp.stack([v[:, own_rows - halo_rows :] for v in (inputs, skip_inputs, out_cotangent)])
    halo = grid.shift(tails, half - 1, half)
    first_tokens = jnp.concatenate([inputs, halo[0]], axis=1)
    second_tokens = jnp.concatenate([skip_inputs, halo[1]], axis=1)
    joined = jnp.concatenate([first_tokens, second_tokens], axis=2)
    cotangent = jnp.concatenate([out_cotangent, halo[2]], axis=1)

    stream = dot_last(joined, skip_full) + skip_bias_full
    first_low, first_normal, first_scale = layer_norm(stream, gain_one, shift_one)
    rows = inputs.shape[0]
    first_far = far_gather(grid, first_low)
    query = dot_last(first_low, query_full).astype(jnp.bfloat16)
    own = dot_last(first_low, both_full).astype(jnp.bfloat16)
    attended = jnp.zeros(query.shape, jnp.bfloat16)
    level = jnp.zeros((rows, HEADS, all_rows), jnp.float32)
    far = []
    for row in range(rows):
        far.append(dot_last(first_far[row], both_full).astype(jnp.bfloat16))
        attended, level = attend(
            query, own, far[row], query_ids, key_ids, row, attended, level
        )
    used_rows = used.astype(jnp.float32).reshape(-1, 1)
    flat = (-1, model)
    (
        output,
        second_low,
        act_low,
        grad_pre,
        grad_middle,
        grad_proj,
        grad_attended,
        hidden_sums,
        middle_sums,
    ) = middle_block(
        stream.reshape(flat),
        attended.reshape(flat),
        cotangent.reshape(flat),
        used_rows,
        proj_full,
        hidden_blocks,
        down_blocks,
        proj_bias_full,
        gain_two,
        shift_two,
        hidden_bias_full,
        down_bias_full,
    )
    hidden_bias_grad = jnp.sum(hidden_sums, axis=0).reshape(-1)
    middle_sums = jnp.sum(middle_sums, axis=0)
    gain_two_grad, shift_two_grad = middle_sums[0], middle_sums[1]
    proj_bias_grad, down_bias_grad = middle_sums[2], middle_sums[3]
    grad_branch = jnp.where(used[..., None], cotangent, 0).reshape(flat)
    here, outer = grid.at["c"], grid.outer_count
    core_rows = lambda value, *lead: value.reshape((outer,) + lead + (-1, value.shape[-1]))
    if grid.square:
        keep, give = weight_grad(act_low, grad_branch, here, outer // 4, 4, 1, "down_weight_grad")
        down_way = Scatter(
            grid, [core_rows(keep, 2, 2)], [core_rows(give, 2, 2)]
        )
        second_low = tie(second_low, give)
        keep, give = weight_grad(second_low, grad_pre, here, outer, 1, 4, "hidden_weight_grad")
        hidden_way = Scatter(grid, [core_rows(keep)], [core_rows(give)])
        down_way.pull(give)
        down_way.push("x", choose_dim(2))
        hidden_way.pull(*down_way.sent)
        hidden_way.push("y", choose_lanes)
        grad_attended = tie(grad_attended, *hidden_way.sent)
    else:
        down_grad = outer_dot(act_low, grad_branch)
        hidden_grad = outer_dot(second_low, grad_pre)
    output = output.reshape(stream.shape)
    grad_middle = grad_middle.reshape(stream.shape)
    grad_attended = grad_attended.reshape(stream.shape)

    query_grad = jnp.zeros(query.shape, jnp.bfloat16)
    both_grad = jnp.zeros((rows, key_ids.shape[1], 2 * model), jnp.bfloat16)
    grad_far = []
    for row in range(rows):
        query_grad, both_grad = attend_back(
            query,
            own,
            far[row],
            attended,
            grad_attended,
            level,
            query_ids,
            key_ids,
            row,
            query_grad,
            both_grad,
        )
        share = dot_back(both_grad[row : row + 1, all_rows:], both_full).astype(jnp.bfloat16)
        grad_far.append(far_reduce(grid, share))
        if row == 0 and grid.square:
            down_way.pull(share)
            down_way.push("y", choose_dim(1))
            hidden_way.pull(*down_way.sent)
            hidden_way.push("x", choose_lanes)
            both_grad = tie(both_grad, share, *hidden_way.sent)
    if grid.square:
        down_way.pull(share)
        down_way.push_outer()
        hidden_way.pull(*down_way.sent)
        hidden_way.push_outer()
        both_grad = tie(both_grad, *hidden_way.sent)
    both_flat = both_grad.reshape(-1, 2 * model)
    first_all = [jnp.concatenate([first_low[row], first_far[row][0]]) for row in range(rows)]
    first_all = jnp.concatenate(first_all)
    query_flat = query_grad.reshape(flat)
    if grid.square:
        both_keep, both_give = weight_grad(
            first_all, both_flat, here, outer, 1, 2, "both_weight_grad"
        )
        query_keep, query_give = weight_grad(
            first_low.reshape(flat), query_flat, here, outer, 1, 1, "query_weight_grad"
        )
        proj_keep, proj_give = weight_grad(
            attended.reshape(flat), grad_proj, here, outer, 1, 1, "proj_weight_grad"
        )
        mixed_way = Scatter(
            grid,
            [core_rows(value) for value in (query_keep, both_keep, proj_keep)],
            [core_rows(value) for value in (query_give, both_give, proj_give)],
        )
        query_grad = tie(query_grad, query_give, both_give, proj_give)
    else:
        both_weight_grad = outer_dot(first_all, both_flat)
        query_weight_grad = outer_dot(first_low.reshape(flat), query_flat)
        proj_grad = outer_dot(attended.reshape(flat), grad_proj)
    grad_first = dot_back(both_grad[:, :all_rows], both_full) + dot_back(query_grad, query_full)
    if grid.square:
        mixed_way.pull(grad_first)
        query_part, both_part, proj_part = mixed_way.values
        mixed_way.values = [
            query_part, both_part[..., :model], both_part[..., model:], proj_part
        ]
        mixed_way.push("y", choose_pair)
        grad_first = tie(grad_first, *mixed_way.sent)
    grad_first = grad_first + jnp.concatenate(grad_far)
    grad_norm, gain_one_grad, shift_one_grad = layer_norm_back(
        grad_first, first_normal, first_scale, gain_one
    )
    grad_stream = (grad_middle + grad_norm).astype(jnp.bfloat16)
    skip_bias_grad = jnp.sum(grad_stream.astype(jnp.float32), axis=(0, 1))
    joined_flat, stream_flat = joined.reshape(-1, 2 * model), grad_stream.reshape(flat)
    if grid.square:
        keep, give = weight_grad(joined_flat, stream_flat, here, outer // 2, 2, 1, "skip_weight_grad")
        skip_way = Scatter(grid, [core_rows(keep, 2, 2)], [core_rows(give, 2, 2)])
        grad_stream = tie(grad_stream, give)
    else:
        skip_weight_grad = outer_dot(joined_flat, stream_flat)
    input_grad = dot_back(grad_stream, skip_full[:model])
    if grid.square:
        skip_way.pull(input_grad)
        skip_way.push("x", choose_dim(2))
        grad_stream = tie(grad_stream, *skip_way.sent)
    skip_grad = dot_back(grad_stream, skip_full[model:])
    if grid.square:
        skip_way.pull(skip_grad)
        skip_way.push("y", choose_dim(1))
        mixed_way.pull(*skip_way.sent)
        mixed_way.push("x", choose_pair)
        skip_way.pull(*mixed_way.sent)
        skip_way.push_outer()
        mixed_way.pull(*skip_way.sent)
        mixed_way.push_outer()
        down_shard = columns_of_seq(grid, down_way.pull_outer().astype(jnp.bfloat16))
        down_shard = down_shard.astype(jnp.float32)
        hidden_shard = hidden_way.pull_outer()
        skip_shard = columns_of_seq(grid, skip_way.pull_outer().astype(jnp.bfloat16))
        skip_shard = skip_shard.astype(jnp.float32)
        qkv_shard, proj_shard = mixed_shards(grid, mixed_way.pull_outer())
    else:
        down_shard = seq_scatter(down_grad)
        hidden_shard = seq_scatter(hidden_grad)
        skip_shard = seq_scatter(skip_weight_grad)
        proj_shard = seq_scatter(proj_grad)
        qkv_shard = seq_scatter(jnp.concatenate([query_weight_grad, both_weight_grad], axis=1))

    moved = items.moved[..., None] & (grid.seq_index == half - 1)

    def settle(value):
        own, far = value[:, :own_rows], grid.shift(value[:, own_rows:], half, half - 1)
        tail = jnp.where(moved, far, own[:, own_rows - halo_rows :])
        return lax.dynamic_update_slice_in_dim(own, tail, own_rows - halo_rows, 1)

    vectors = scatter_vectors(
        grid,
        [
            skip_bias_grad,
            gain_one_grad,
            shift_one_grad,
            proj_bias_grad,
            gain_two_grad,
            shift_two_grad,
            hidden_bias_grad,
            down_bias_grad,
        ],
    )
    return (
        settle(output),
        settle(input_grad),
        settle(skip_grad),
        skip_shard,
        vectors[0],
        vectors[1],
        vectors[2],
        qkv_shard,
        proj_shard,
        vectors[3],
        vectors[4],
        vectors[5],
        hidden_shard,
        vectors[6],
        down_shard,
        vectors[7],
    )


def solution(mesh):
    return jax.shard_map(
        body,
        mesh=mesh,
        in_specs=(
            P("batch", "seq", None),
            P("batch", "seq", None),
            P("batch", "seq", None),
            P("batch", None),
            P("batch", None),
            P("batch", "seq"),
            P("seq"),
            P("seq"),
            P("seq"),
            P("batch", "seq"),
            P("batch", "seq"),
            P("seq"),
            P("seq"),
            P("seq"),
            P("batch", "seq"),
            P("seq"),
            P("batch", "seq"),
            P("seq"),
        ),
        out_specs=(
            P("batch", "seq", None),
            P("batch", "seq", None),
            P("batch", "seq", None),
            P("batch", "seq"),
            P("seq"),
            P("seq"),
            P("seq"),
            P("batch", "seq"),
            P("batch", "seq"),
            P("seq"),
            P("seq"),
            P("seq"),
            P("batch", "seq"),
            P("seq"),
            P("batch", "seq"),
            P("seq"),
        ),
        check_vma=False,
    )
```

time: 3410 us -> 1070 us (0.31)
  other arithmetic: 1050 us -> 74.5 us
  matrix products: 830 us -> 90.9 us
  waiting for transfers between devices: 827 us -> 243 us
  local copies, waits for them, and re-layouts: 473 us -> 93.4 us
  Pallas kernels: 0 us -> 378 us
  starting transfers between devices: 39.1 us -> 180 us
  blocking collectives: 113 us -> 0 us
  loops' own time: 47 us -> 0 us
    all_gather x5 -> x0, other arithmetic: 782 us -> none  [the longest x1 226 us: body(): lax.all_gather(hidden_weight.reshape(1, -1), ('batch', 'seq'), axis=0, ti...]
    dot_general x86 -> x11, matrix products: 830 us -> 90.9 us  [the longest x6 52 us: dot_back(): lax.dot_general(left_side, right_side, (((2,), (1,)), ((), ())), preferre...]
    pallas_call x0 -> x15, Pallas kernels: none -> 378 us  [the longest x2 100 us: attend_back(): pl.pallas_call(attend_back_kernel, grid=(1,), in_specs=[wide, pl.BlockSpe...]
    unnamed x22 -> x0, waiting for transfers between devices: 297 us -> none
    all_to_all x8 -> x2, waiting for transfers between devices: 248 us -> 1.36 us  [columns_of_seq(): mixed = lax.all_to_all(split, 'seq', 0, 0)]
    ppermute x0 -> x84, waiting for transfers between devices: none -> 242 us  [the longest x80 242 us: send(): return lax.ppermute(value, ('batch', 'seq'), pairs)]
    reduce_scatter x5 -> x0, waiting for transfers between devices: 192 us -> none  [the longest x1 103 us: reduce_end(): lax.psum_scatter(grads[11].astype(jnp.bfloat16), 'seq', scatter_dimension...]
    ppermute x0 -> x84, starting transfers between devices: none -> 172 us  [the longest x80 169 us: send(): return lax.ppermute(value, ('batch', 'seq'), pairs)]
  transfers between devices with their start and end apart: 24 -> 86, of which waited for: 17 -> 21; matrix products, arithmetic and copies ran while one was open for 28% -> 21% of each run, Pallas kernels for 0% -> 22%
where the time goes in v1:
time: 1070 us; the launch traced here: 1060 us
  Pallas kernels  378 us (35%)
  waiting for transfers between devices  243 us (23%)
  starting transfers between devices  180 us (17%)
  local copies, waits for them, and re-layouts  93.4 us (9%)
  matrix products  90.9 us (8%)
  other arithmetic  74.5 us (7%)
    ppermute x80, waiting for transfers between devices, send(): return lax.ppermute(value, ('batch', 'seq'), pairs)  242 us
    ppermute x80, starting transfers between devices, send(): return lax.ppermute(value, ('batch', 'seq'), pairs)  169 us
    pallas_call x2, Pallas kernels, attend_back(): pl.pallas_call(attend_back_kernel, grid=(1,), in_specs=[wide, pl.BlockSpe...  100 us
    pallas_call x6, Pallas kernels, weight_grad(): pl.pallas_call(lambda *refs: weight_grad_kernel(outer, *refs), grid_spec=...  90.2 us
    pallas_call x1, Pallas kernels, middle_block(): pl.pallas_call(middle_kernel, grid=(blocks, steps), in_specs=[by_rows, by...  83.8 us
    pallas_call x2, Pallas kernels, attend(): pl.pallas_call(attend_kernel, grid=(1,), in_specs=[wide, pl.BlockSpec((1,...  66.4 us
    dot_general x6, matrix products, dot_back(): lax.dot_general(left_side, right_side, (((2,), (1,)), ((), ())), preferre...  52 us
    dot_general x5, matrix products, dot_last(): lax.dot_general(left_side, right_side, (((2,), (0,)), ((), ())), preferre...  39 us
  transfers between devices with their start and end apart: 86, of which 21 were waited for; matrix products, arithmetic and copies ran while one was open for 21% of the time, Pallas kernels for 22%

profile of v1, /device:TPU:0, one launch (start us, length us, event | category | flops | bytes accessed | tf_op | source)
XLA Modules:
  0.0 1062.3 jit_solution(16368190877737121860)
XLA Ops:
  25.3 4.3 collective-permute-start.4
  31.0 12.6 %collective-permute-done.4.refs_3_ = bf16[2624,128]{1,0:T(8,128)(2,1)S(1)} collective-permute-done((bf16[2624,128]{1,0:T(8,128)(2,1)S(1)}, bf16[2624,128]{1,0:T(8,128)(2,1)S(1)}, u32[]{:S(2)}, u32[]{:S(2)}) %collective-permute-start.4) | collective-permute-done | bytes 671776 | tf_op jit(solution)/shard_map/ppermute | solution.py:508
  49.7 8.1 collective-permute-done.11
  58.5 10.0 collective-permute-done.12
  70.0 13.9 %collective-permute-start.23 = (bf16[144,1152]{1,0:T(8,128)(2,1)S(1)}, bf16[144,1152]{1,0:T(8,128)(2,1)S(1)}, u32[]{:S(2)}, u32[]{:S(2)}) collective-permute-start(bf16[144,1152]{1,0:T(8,128)(2,1)S(1)} %copy-done.36), channel_id=1, source_target_pairs={{0,8},{1,9},{2,10},{3,11},{4,12},{5,13},{6,14},{7,15},{8,16},{9,17... | collective-permute-start | bytes 995336 | tf_op jit(solution)/shard_map/ppermute | solution.py:508
  86.0 6.0 collective-permute-done.23
  93.0 10.1 collective-permute-done.24
  103.8 4.1 collective-permute-done.25
  113.3 5.9 collective-permute-start.33
  122.6 7.5 join_skip.1
  130.1 10.0 fusion.52
  143.3 7.2 collective-permute-start.35
  151.0 21.7 %collective-permute-done.16.refs_5_ = bf16[576,1152]{1,0:T(8,128)(2,1)S(1)} collective-permute-done((bf16[576,1152]{1,0:T(8,128)(2,1)}, bf16[576,1152]{1,0:T(8,128)(2,1)S(1)}, u32[]{:S(2)}, u32[]{:S(2)}) %collective-permute-start.16) | collective-permute-done | bytes 1327136 | tf_op jit(solution)/shard_map/ppermute | solution.py:508
  180.3 24.4 %collective-permute-done.22 = bf16[1,544,1152]{2,1,0:T(8,128)(2,1)S(1)} collective-permute-done((bf16[1,544,1152]{2,1,0:T(8,128)(2,1)S(1)}, bf16[1,544,1152]{2,1,0:T(8,128)(2,1)S(1)}, u32[]{:S(2)}, u32[]{:S(2)}) %collective-permute-start.22) | collective-permute-done | bytes 1253408 | tf_op jit(solution)/shard_map/ppermute | solution.py:508
  213.0 10.2 join_mixed.1
  223.2 7.9 fusion.15.far_ref
  232.5 4.6 collective-permute-done.26.refs_2_
  238.4 27.0 %collective-permute-done.36.refs_3_ = bf16[5184,128]{1,0:T(8,128)(2,1)} collective-permute-done((bf16[5184,128]{1,0:T(8,128)(2,1)}, bf16[5184,128]{1,0:T(8,128)(2,1)}, u32[]{:S(2)}, u32[]{:S(2)}) %collective-permute-start.36) | collective-permute-done | bytes 1327136 | tf_op jit(solution)/shard_map/ppermute | solution.py:508
  266.1 4.9 convolution_convert_fusion.3.q_ref
  271.0 8.3 convolution_convert_fusion.own_ref
  279.4 12.9 %collective-permute-done.21 = bf16[1,544,1152]{2,1,0:T(8,128)(2,1)S(1)} collective-permute-done((bf16[1,544,1152]{2,1,0:T(8,128)(2,1)S(1)}, bf16[1,544,1152]{2,1,0:T(8,128)(2,1)S(1)}, u32[]{:S(2)}, u32[]{:S(2)}) %collective-permute-start.21) | collective-permute-done | bytes 1253408 | tf_op jit(solution)/shard_map/ppermute | solution.py:508
  292.2 27.1 %collective-permute-done.28.refs_4_ = bf16[576,1152]{1,0:T(8,128)(2,1)} collective-permute-done((bf16[576,1152]{1,0:T(8,128)(2,1)}, bf16[576,1152]{1,0:T(8,128)(2,1)}, u32[]{:S(2)}, u32[]{:S(2)}) %collective-permute-start.28) | collective-permute-done | bytes 1327136 | tf_op jit(solution)/shard_map/ppermute | solution.py:508
  322.8 33.4 %attend.2 = (bf16[2,544,1152]{2,1,0:T(8,128)(2,1)}, f32[2,16,544]{2,1,0:T(8,128)}) custom-call(bf16[2,544,1152]{2,1,0:T(8,128)(2,1)} %convolution_convert_fusion.3.q_ref, bf16[2,544,2304]{2,1,0:T(8,128)(2,1)} %convolution_convert_fusion.own_ref, bf16[1,544,2304]{2,1,0:T(8,128)(2,1)} %fusion.15.far_ref, ...), custom_call_target="tpu_custom_call", output_to_operand_aliasing={{0}: (5, {}), {1}: (6, {})} | custom-call | flops 4848615424 | bytes 7520256 | tf_op jit(solution)/shard_map/attend/pallas_call | solution.py:101
  356.3 7.8 fusion.14.far_ref
  364.1 33.0 %attend.3 = (bf16[2,544,1152]{2,1,0:T(8,128)(2,1)}, f32[2,16,544]{2,1,0:T(8,128)}) custom-call(bf16[2,544,1152]{2,1,0:T(8,128)(2,1)} %convolution_convert_fusion.3.q_ref, bf16[2,544,2304]{2,1,0:T(8,128)(2,1)} %convolution_convert_fusion.own_ref, bf16[1,544,2304]{2,1,0:T(8,128)(2,1)} %fusion.14.far_ref, ...), custom_call_target="tpu_custom_call", output_to_operand_aliasing={{0}: (5, {}), {1}: (6, {})} | custom-call | flops 4848615424 | bytes 7520256 | tf_op jit(solution)/shard_map/attend/pallas_call | solution.py:101
  397.1 8.9 place_blocks.1
  408.0 11.0 %join_down.1 = bf16[4608,1152]{1,0:T(8,128)(2,1)} custom-call(s32[4]{0:T(128)} %pad_add_fusion.3.refs_0_, s32[8]{0:T(128)} %stack.230.refs_1_, bf16[5184,128]{1,0:T(8,128)(2,1)} %constant_dynamic-update-slice_fusion.15.refs_2_, bf16[5184,128]{1,0:T(8,128)(2,1)} %collective-permute-done.36.refs_3_, bf16[5184,128]{1,0:T(8,128)(2,1)} %collective-permute-done.37.refs_4_, ...), custom_call_target="tpu_custom_call" | custom-call | bytes 21233664 | tf_op jit(solution)/shard_map/join_down/pallas_call | solution.py:589
  419.0 83.8 %middle_block.1 = (bf16[1088,1152]{1,0:T(8,128)(2,1)}, bf16[1088,1152]{1,0:T(8,128)(2,1)}, bf16[1088,4608]{1,0:T(8,128)(2,1)}, bf16[1088,4608]{1,0:T(8,128)(2,1)...) custom-call(f32[1088,1152]{1,0:T(8,128)} %bitcast.258, ...), custom_call_target="tpu_custom_call" | custom-call | flops 51980009472 | bytes 135069696 | tf_op jit(solution)/shard_map/middle_block/pallas_call | solution.py:365
  502.8 20.8 %down_weight_grad.1 = (bf16[2304,1152]{1,0:T(8,128)(2,1)}, bf16[2304,1152]{1,0:T(8,128)(2,1)}) custom-call(s32[1]{0:T(128)} %bitcast.70.refs_0_, bf16[1088,4608]{1,0:T(8,128)(2,1)} %get-tuple-element.87.refs_1_, bf16[1088,1152]{1,0:T(8,128)(2,1)} %broadcast_select_fusion.refs_2_), custom_call_target="tpu_custom_call" | custom-call | flops 11551113216 | bytes 25804800 | tf_op jit(solution)/shard_map/down_weight_grad/pallas_call | solution.py:259
  523.6 5.2 copy.125
  528.9 20.8 %hidden_weight_grad.1 = (bf16[576,4608]{1,0:T(8,128)(2,1)}, bf16[576,4608]{1,0:T(8,128)(2,1)}) custom-call(s32[1]{0:T(128)} %bitcast.70.refs_0_, bf16[1088,1152]{1,0:T(8,128)(2,1)} %get-tuple-element.89.refs_1_, bf16[1088,4608]{1,0:T(8,128)(2,1)} %get-tuple-element.90.refs_2_), custom_call_target="tpu_custom_call" | custom-call | flops 11551113216 | bytes 65617920 | tf_op jit(solution)/shard_map/hidden_weight_grad/pallas_call | solution.py:259
  550.2 8.2 maximum_maximum_fusion
  562.7 3.8 add_convert_fusion.1
  569.9 5.4 add_convert_fusion
  578.6 4.4 broadcast_in_dim.87.old_dkv
  584.6 50.1 %attend_back.2 = (bf16[2,544,1152]{2,1,0:T(8,128)(2,1)}, bf16[2,1088,2304]{2,1,0:T(8,128)(2,1)}) custom-call(bf16[2,544,1152]{2,1,0:T(8,128)(2,1)} %convolution_convert_fusion.3.q_ref, bf16[2,544,2304]{2,1,0:T(8,128)(2,1)} %convolution_convert_fusion.own_ref, bf16[1,544,2304]{2,1,0:T(8,128)(2,1)} %fusion.15.far_ref, ...), custom_call_target="tpu_custom_call", output_to_operand_aliasing={{0}: (8, {}), {1}: (9, {})} | custom-call | flops 12121538560 | bytes 15040512 | tf_op jit(solution)/shard_map/attend_back/pallas_call | solution.py:186
  634.7 7.8 fusion.16
  651.6 50.2 %attend_back.3 = (bf16[2,544,1152]{2,1,0:T(8,128)(2,1)}, bf16[2,1088,2304]{2,1,0:T(8,128)(2,1)}) custom-call(bf16[2,544,1152]{2,1,0:T(8,128)(2,1)} %convolution_convert_fusion.3.q_ref, bf16[2,544,2304]{2,1,0:T(8,128)(2,1)} %convolution_convert_fusion.own_ref, bf16[1,544,2304]{2,1,0:T(8,128)(2,1)} %fusion.14.far_ref, ...), custom_call_target="tpu_custom_call", output_to_operand_aliasing={{0}: (8, {}), {1}: (9, {})} | custom-call | flops 12121538560 | bytes 15040512 | tf_op jit(solution)/shard_map/attend_back/pallas_call | solution.py:186
  701.8 7.7 fusion.17
  714.8 20.3 %both_weight_grad.1 = (bf16[576,2304]{1,0:T(8,128)(2,1)}, bf16[576,2304]{1,0:T(8,128)(2,1)}) custom-call(s32[1]{0:T(128)} %bitcast.70.refs_0_, bf16[2176,1152]{1,0:T(8,128)(2,1)} %pad_maximum_fusion.refs_1_, bf16[2176,2304]{1,0:T(8,128)(2,1)} %bitcast.263), custom_call_target="tpu_custom_call" | custom-call | flops 11551113216 | bytes 30965760 | tf_op jit(solution)/shard_map/both_weight_grad/pallas_call | solution.py:259
  735.1 8.1 proj_weight_grad.1
  745.7 8.0 query_weight_grad.1
  753.8 8.6 fusion.20
  762.5 10.6 fusion.6
  775.9 5.4 broadcast_select_fusion.2
  781.3 19.1 %collective-permute-done.54 = bf16[1,544,1152]{2,1,0:T(8,128)(2,1)} collective-permute-done((bf16[1,544,1152]{2,1,0:T(8,128)(2,1)}, bf16[1,544,1152]{2,1,0:T(8,128)(2,1)}, u32[]{:S(2)}, u32[]{:S(2)}) %collective-permute-start.54) | collective-permute-done | bytes 1253408 | tf_op jit(solution)/shard_map/ppermute | solution.py:508
  800.4 5.0 multiply_reduce_fusion
  805.4 5.3 convert_reduce_fusion
  810.7 12.2 %skip_weight_grad.1 = (bf16[1152,1152]{1,0:T(8,128)(2,1)}, bf16[1152,1152]{1,0:T(8,128)(2,1)}) custom-call(s32[1]{0:T(128)} %bitcast.70.refs_0_, bf16[1088,2304]{1,0:T(8,128)(2,1)} %bitcast.278, bf16[1088,1152]{1,0:T(8,128)(2,1)} %bitcast.287), custom_call_target="tpu_custom_call" | custom-call | flops 5775556608 | bytes 15482880 | tf_op jit(solution)/shard_map/skip_weight_grad/pallas_call | solution.py:259
  836.8 5.9 collective-permute-start.81
  848.3 8.6 fusion.19
  863.3 7.8 collective-permute-start.66
  871.1 5.5 collective-permute-start.58
  878.0 4.1 all-to-all-start.1
  884.2 8.6 fusion.18
  892.8 14.0 %collective-permute-done.58 = bf16[4,2,72,1152]{3,2,1,0:T(8,128)(2,1)} collective-permute-done((bf16[4,2,72,1152]{3,2,1,0:T(8,128)(2,1)}, bf16[4,2,72,1152]{3,2,1,0:T(8,128)(2,1)}, u32[]{:S(2)}, u32[]{:S(2)}) %collective-permute-start.58) | collective-permute-done | bytes 1327136 | tf_op jit(solution)/shard_map/ppermute | solution.py:508
  906.8 6.4 collective-permute-start.80
  919.1 27.5 %collective-permute-done.60 = bf16[4,144,1152]{2,1,0:T(8,128)(2,1)S(1)} collective-permute-done((bf16[4,144,1152]{2,1,0:T(8,128)(2,1)}, bf16[4,144,1152]{2,1,0:T(8,128)(2,1)S(1)}, u32[]{:S(2)}, u32[]{:S(2)}) %collective-permute-start.60) | collective-permute-done | bytes 1327136 | tf_op jit(solution)/shard_map/ppermute | solution.py:508
  952.5 19.8 %collective-permute-start.68 = (f32[99,128]{1,0:T(8,128)S(1)}, f32[99,128]{1,0:T(8,128)S(1)}, u32[]{:S(2)}, u32[]{:S(2)}) collective-permute-start(f32[99,128]{1,0:T(8,128)S(1)} %add.730), channel_id=1, source_target_pairs={{0,8},{1,9},{2,10},{3,11},{4,12},{5,13},{6,14},{7,15},{8,16},{9,17... | collective-permute-start | bytes 152072 | tf_op jit(solution)/shard_map/ppermute | solution.py:508
  977.0 5.0 slice.317
  987.5 12.7 %collective-permute-start.72 = (bf16[144,1152]{1,0:T(8,128)(2,1)S(1)}, bf16[144,1152]{1,0:T(8,128)(2,1)S(1)}, u32[]{:S(2)}, u32[]{:S(2)}) collective-permute-start(bf16[144,1152]{1,0:T(8,128)(2,1)S(1)} %get-tuple-element.240), channel_id=1, source_target_pairs={{0,8},{1,9},{2,10},{3,11},{4,12},{5,13},{6,14},{7,15},{8,16},{9,17... | collective-permute-start | bytes 995336 | tf_op jit(solution)/shard_map/ppermute | solution.py:508
  1011.3 9.3 collective-permute-start.62
  1023.1 14.8 %collective-permute-start.64 = (bf16[72,1152]{1,0:T(8,128)(2,1)S(1)}, bf16[72,1152]{1,0:T(8,128)(2,1)S(1)}, u32[]{:S(2)}, u32[]{:S(2)}) collective-permute-start(bf16[72,1152]{1,0:T(8,128)(2,1)S(1)} %get-tuple-element.252), channel_id=1, source_target_pairs={{0,24},{1,25},{2,26},{3,27},{4,28},{5,29},{6,30},{7,31},{8,0},{9,1... | collective-permute-start | bytes 497672 | tf_op jit(solution)/shard_map/ppermute | solution.py:508
  1054.9 3.6 collective-permute-done.77
  (461 shorter events, 192.8 us)
Async XLA Ops:
  2.6 22.5 %collective-permute-start.1 = (bf16[648,128]{1,0:T(8,128)(2,1)S(1)}, bf16[648,128]{1,0:T(8,128)(2,1)S(1)}, u32[]{:S(2)}, u32[]{:S(2)}) collective-permute-start(bf16[648,128]{1,0:T(8,128)(2,1)S(1)} %maximum_maximum_fusion.2), channel_id=1, source_target_pairs={{0,8},{1,9},{2,10},{3,11},{4,12},{5,13},{6,14},{7,15},{8,16},{9,17... | collective-permute-start | bytes 497672 | tf_op jit(solution)/shard_map/ppermute | solution.py:508
  30.3 82.2 %collective-permute-start.7 = (bf16[2624,128]{1,0:T(8,128)(2,1)S(1)}, bf16[2624,128]{1,0:T(8,128)(2,1)}, u32[]{:S(2)}, u32[]{:S(2)}) collective-permute-start(bf16[2624,128]{1,0:T(8,128)(2,1)S(1)} %constant_dynamic-update-slice_fusion.refs_2_), channel_id=1, source_target_pairs={{0,4},{1,5},{2,6},{3,7},{4,0},{5,1},{6,2},{7,3},{8,12},{9,13},{10,... | collective-permute-start | bytes 2015240 | tf_op jit(solution)/shard_map/ppermute | solution.py:508
  46.5 21.9 %collective-permute-start.12 = (bf16[144,1152]{1,0:T(8,128)(2,1)S(1)}, bf16[144,1152]{1,0:T(8,128)(2,1)S(1)}, u32[]{:S(2)}, u32[]{:S(2)}) collective-permute-start(bf16[144,1152]{1,0:T(8,128)(2,1)S(1)} %pad_maximum_fusion.6), channel_id=1, source_target_pairs={{0,16},{1,17},{2,18},{3,19},{4,20},{5,21},{6,22},{7,23},{8,24},{9,... | collective-permute-start | bytes 995336 | tf_op jit(solution)/shard_map/ppermute | solution.py:508
  46.9 22.4 %collective-permute-start.13 = (bf16[144,1152]{1,0:T(8,128)(2,1)S(1)}, bf16[144,1152]{1,0:T(8,128)(2,1)S(1)}, u32[]{:S(2)}, u32[]{:S(2)}) collective-permute-start(bf16[144,1152]{1,0:T(8,128)(2,1)S(1)} %pad_maximum_fusion.6), channel_id=1, source_target_pairs={{0,24},{1,25},{2,26},{3,27},{4,28},{5,29},{6,30},{7,31},{8,0},{9,1... | collective-permute-start | bytes 995336 | tf_op jit(solution)/shard_map/ppermute | solution.py:508
  70.0 22.1 %collective-permute-start.23 = (bf16[144,1152]{1,0:T(8,128)(2,1)S(1)}, bf16[144,1152]{1,0:T(8,128)(2,1)S(1)}, u32[]{:S(2)}, u32[]{:S(2)}) collective-permute-start(bf16[144,1152]{1,0:T(8,128)(2,1)S(1)} %copy-done.36), channel_id=1, source_target_pairs={{0,8},{1,9},{2,10},{3,11},{4,12},{5,13},{6,14},{7,15},{8,16},{9,17... | collective-permute-start | bytes 995336 | tf_op jit(solution)/shard_map/ppermute | solution.py:508
  84.7 24.6 %collective-permute-start.6 = (bf16[2624,128]{1,0:T(8,128)(2,1)S(1)}, bf16[2624,128]{1,0:T(8,128)(2,1)}, u32[]{:S(2)}, u32[]{:S(2)}) collective-permute-start(bf16[2624,128]{1,0:T(8,128)(2,1)S(1)} %collective-permute-done.4.refs_3_), channel_id=1, source_target_pairs={{0,2},{1,3},{2,0},{3,1},{4,6},{5,7},{6,4},{7,5},{8,10},{9,11},{10,... | collective-permute-start | bytes 2015240 | tf_op jit(solution)/shard_map/ppermute | solution.py:508
  85.3 27.8 %collective-permute-start.8 = (bf16[2624,128]{1,0:T(8,128)(2,1)S(1)}, bf16[2624,128]{1,0:T(8,128)(2,1)}, u32[]{:S(2)}, u32[]{:S(2)}) collective-permute-start(bf16[2624,128]{1,0:T(8,128)(2,1)S(1)} %collective-permute-done.4.refs_3_), channel_id=1, source_target_pairs={{0,4},{1,5},{2,6},{3,7},{4,0},{5,1},{6,2},{7,3},{8,12},{9,13},{10,... | collective-permute-start | bytes 2015240 | tf_op jit(solution)/shard_map/ppermute | solution.py:508
  107.9 32.3 %collective-permute-start.14 = (bf16[576,1152]{1,0:T(8,128)(2,1)}, bf16[576,1152]{1,0:T(8,128)(2,1)}, u32[]{:S(2)}, u32[]{:S(2)}) collective-permute-start(bf16[576,1152]{1,0:T(8,128)(2,1)} %constant_dynamic-update-slice_fusion.7.refs_2_), channel_id=1, source_target_pairs={{0,1},{1,0},{2,3},{3,2},{4,5},{5,4},{6,7},{7,6},{8,9},{9,8},{10,11... | collective-permute-start | bytes 3981320 | tf_op jit(solution)/shard_map/ppermute | solution.py:508
  112.4 38.0 %collective-permute-start.15 = (bf16[576,1152]{1,0:T(8,128)(2,1)}, bf16[576,1152]{1,0:T(8,128)(2,1)}, u32[]{:S(2)}, u32[]{:S(2)}) collective-permute-start(bf16[576,1152]{1,0:T(8,128)(2,1)} %constant_dynamic-update-slice_fusion.7.refs_2_), channel_id=1, source_target_pairs={{0,2},{1,3},{2,0},{3,1},{4,6},{5,7},{6,4},{7,5},{8,10},{9,11},{10,... | collective-permute-start | bytes 3981320 | tf_op jit(solution)/shard_map/ppermute | solution.py:508
  113.1 66.6 %collective-permute-start.17 = (bf16[576,1152]{1,0:T(8,128)(2,1)}, bf16[576,1152]{1,0:T(8,128)(2,1)}, u32[]{:S(2)}, u32[]{:S(2)}) collective-permute-start(bf16[576,1152]{1,0:T(8,128)(2,1)} %constant_dynamic-update-slice_fusion.7.refs_2_), channel_id=1, source_target_pairs={{0,4},{1,5},{2,6},{3,7},{4,0},{5,1},{6,2},{7,3},{8,12},{9,13},{10,... | collective-permute-start | bytes 3981320 | tf_op jit(solution)/shard_map/ppermute | solution.py:508
  113.3 30.0 %collective-permute-start.33 = (bf16[1296,128]{1,0:T(8,128)(2,1)S(1)}, bf16[1296,128]{1,0:T(8,128)(2,1)S(1)}, u32[]{:S(2)}, u32[]{:S(2)}) collective-permute-start(bf16[1296,128]{1,0:T(8,128)(2,1)S(1)} %maximum_maximum_fusion.1), channel_id=1, source_target_pairs={{0,8},{1,9},{2,10},{3,11},{4,12},{5,13},{6,14},{7,15},{8,16},{9,17... | collective-permute-start | bytes 995336 | tf_op jit(solution)/shard_map/ppermute | solution.py:508
  119.2 31.3 %collective-permute-start.34 = (bf16[1296,128]{1,0:T(8,128)(2,1)S(1)}, bf16[1296,128]{1,0:T(8,128)(2,1)S(1)}, u32[]{:S(2)}, u32[]{:S(2)}) collective-permute-start(bf16[1296,128]{1,0:T(8,128)(2,1)S(1)} %maximum_maximum_fusion.1), channel_id=1, source_target_pairs={{0,16},{1,17},{2,18},{3,19},{4,20},{5,21},{6,22},{7,23},{8,24},{9,... | collective-permute-start | bytes 995336 | tf_op jit(solution)/shard_map/ppermute | solution.py:508
  140.2 32.5 %collective-permute-start.16 = (bf16[576,1152]{1,0:T(8,128)(2,1)}, bf16[576,1152]{1,0:T(8,128)(2,1)S(1)}, u32[]{:S(2)}, u32[]{:S(2)}) collective-permute-start(bf16[576,1152]{1,0:T(8,128)(2,1)} %collective-permute-done.14.refs_3_), channel_id=1, source_target_pairs={{0,2},{1,3},{2,0},{3,1},{4,6},{5,7},{6,4},{7,5},{8,10},{9,11},{10,... | collective-permute-start | bytes 3981320 | tf_op jit(solution)/shard_map/ppermute | solution.py:508
  143.3 31.6 %collective-permute-start.35 = (bf16[1296,128]{1,0:T(8,128)(2,1)S(1)}, bf16[1296,128]{1,0:T(8,128)(2,1)S(1)}, u32[]{:S(2)}, u32[]{:S(2)}) collective-permute-start(bf16[1296,128]{1,0:T(8,128)(2,1)S(1)} %maximum_maximum_fusion.1), channel_id=1, source_target_pairs={{0,24},{1,25},{2,26},{3,27},{4,28},{5,29},{6,30},{7,31},{8,0},{9,1... | collective-permute-start | bytes 995336 | tf_op jit(solution)/shard_map/ppermute | solution.py:508
  150.5 55.6 %collective-permute-start.18 = (bf16[576,1152]{1,0:T(8,128)(2,1)}, bf16[576,1152]{1,0:T(8,128)(2,1)S(1)}, u32[]{:S(2)}, u32[]{:S(2)}) collective-permute-start(bf16[576,1152]{1,0:T(8,128)(2,1)} %collective-permute-done.14.refs_3_), channel_id=1, source_target_pairs={{0,4},{1,5},{2,6},{3,7},{4,0},{5,1},{6,2},{7,3},{8,12},{9,13},{10,... | collective-permute-start | bytes 3981320 | tf_op jit(solution)/shard_map/ppermute | solution.py:508
  150.5 55.6 %collective-permute-start.19 = (bf16[576,1152]{1,0:T(8,128)(2,1)}, bf16[576,1152]{1,0:T(8,128)(2,1)S(1)}, u32[]{:S(2)}, u32[]{:S(2)}) collective-permute-start(bf16[576,1152]{1,0:T(8,128)(2,1)} %collective-permute-done.15.refs_4_), channel_id=1, source_target_pairs={{0,4},{1,5},{2,6},{3,7},{4,0},{5,1},{6,2},{7,3},{8,12},{9,13},{10,... | collective-permute-start | bytes 3981320 | tf_op jit(solution)/shard_map/ppermute | solution.py:508
  172.7 34.1 %collective-permute-start.20 = (bf16[576,1152]{1,0:T(8,128)(2,1)S(1)}, bf16[576,1152]{1,0:T(8,128)(2,1)S(1)}, u32[]{:S(2)}, u32[]{:S(2)}) collective-permute-start(bf16[576,1152]{1,0:T(8,128)(2,1)S(1)} %collective-permute-done.16.refs_5_), channel_id=1, source_target_pairs={{0,4},{1,5},{2,6},{3,7},{4,0},{5,1},{6,2},{7,3},{8,12},{9,13},{10,... | collective-permute-start | bytes 3981320 | tf_op jit(solution)/shard_map/ppermute | solution.py:508
  174.9 29.7 %collective-permute-start.22 = (bf16[1,544,1152]{2,1,0:T(8,128)(2,1)S(1)}, bf16[1,544,1152]{2,1,0:T(8,128)(2,1)S(1)}, u32[]{:S(2)}, u32[]{:S(2)}) collective-permute-start(bf16[1,544,1152]{2,1,0:T(8,128)(2,1)S(1)} %get-tuple-element.230), channel_id=1, source_target_pairs={{0,1},{1,0},{2,3},{3,2},{4,5},{5,4},{6,7},{7,6},{8,9},{9,8},{10,11... | collective-permute-start | bytes 3760136 | tf_op jit(solution)/shard_map/ppermute | solution.py:508
  179.7 51.3 %collective-permute-start.27 = (bf16[576,1152]{1,0:T(8,128)(2,1)}, bf16[576,1152]{1,0:T(8,128)(2,1)}, u32[]{:S(2)}, u32[]{:S(2)}) collective-permute-start(bf16[576,1152]{1,0:T(8,128)(2,1)} %constant_dynamic-update-slice_fusion.11.refs_1_), channel_id=1, source_target_pairs={{0,2},{1,3},{2,0},{3,1},{4,6},{5,7},{6,4},{7,5},{8,10},{9,11},{10,... | collective-permute-start | bytes 3981320 | tf_op jit(solution)/shard_map/ppermute | solution.py:508
  204.7 32.4 %collective-permute-start.26 = (bf16[576,1152]{1,0:T(8,128)(2,1)}, bf16[576,1152]{1,0:T(8,128)(2,1)}, u32[]{:S(2)}, u32[]{:S(2)}) collective-permute-start(bf16[576,1152]{1,0:T(8,128)(2,1)} %constant_dynamic-update-slice_fusion.11.refs_1_), channel_id=1, source_target_pairs={{0,1},{1,0},{2,3},{3,2},{4,5},{5,4},{6,7},{7,6},{8,9},{9,8},{10,11... | collective-permute-start | bytes 3981320 | tf_op jit(solution)/shard_map/ppermute | solution.py:508
  206.1 32.4 %collective-permute-start.29 = (bf16[576,1152]{1,0:T(8,128)(2,1)}, bf16[576,1152]{1,0:T(8,128)(2,1)}, u32[]{:S(2)}, u32[]{:S(2)}) collective-permute-start(bf16[576,1152]{1,0:T(8,128)(2,1)} %constant_dynamic-update-slice_fusion.11.refs_1_), channel_id=1, source_target_pairs={{0,4},{1,5},{2,6},{3,7},{4,0},{5,1},{6,2},{7,3},{8,12},{9,13},{10,... | collective-permute-start | bytes 3981320 | tf_op jit(solution)/shard_map/ppermute | solution.py:508
  206.1 59.4 %collective-permute-start.36 = (bf16[5184,128]{1,0:T(8,128)(2,1)}, bf16[5184,128]{1,0:T(8,128)(2,1)}, u32[]{:S(2)}, u32[]{:S(2)}) collective-permute-start(bf16[5184,128]{1,0:T(8,128)(2,1)} %constant_dynamic-update-slice_fusion.15.refs_2_), channel_id=1, source_target_pairs={{0,1},{1,0},{2,3},{3,2},{4,5},{5,4},{6,7},{7,6},{8,9},{9,8},{10,11... | collective-permute-start | bytes 3981320 | tf_op jit(solution)/shard_map/ppermute | solution.py:508
  206.8 58.7 %collective-permute-start.37 = (bf16[5184,128]{1,0:T(8,128)(2,1)}, bf16[5184,128]{1,0:T(8,128)(2,1)}, u32[]{:S(2)}, u32[]{:S(2)}) collective-permute-start(bf16[5184,128]{1,0:T(8,128)(2,1)} %constant_dynamic-update-slice_fusion.15.refs_2_), channel_id=1, source_target_pairs={{0,2},{1,3},{2,0},{3,1},{4,6},{5,7},{6,4},{7,5},{8,10},{9,11},{10,... | collective-permute-start | bytes 3981320 | tf_op jit(solution)/shard_map/ppermute | solution.py:508
  231.1 61.2 %collective-permute-start.21 = (bf16[1,544,1152]{2,1,0:T(8,128)(2,1)S(1)}, bf16[1,544,1152]{2,1,0:T(8,128)(2,1)S(1)}, u32[]{:S(2)}, u32[]{:S(2)}) collective-permute-start(bf16[1,544,1152]{2,1,0:T(8,128)(2,1)S(1)} %copy-done.24), channel_id=1, source_target_pairs={{0,1},{1,0},{2,3},{3,2},{4,5},{5,4},{6,7},{7,6},{8,9},{9,8},{10,11... | collective-permute-start | bytes 3760136 | tf_op jit(solution)/shard_map/ppermute | solution.py:508
  237.1 82.3 %collective-permute-start.28 = (bf16[576,1152]{1,0:T(8,128)(2,1)}, bf16[576,1152]{1,0:T(8,128)(2,1)}, u32[]{:S(2)}, u32[]{:S(2)}) collective-permute-start(bf16[576,1152]{1,0:T(8,128)(2,1)} %collective-permute-done.27.refs_3_), channel_id=1, source_target_pairs={{0,1},{1,0},{2,3},{3,2},{4,5},{5,4},{6,7},{7,6},{8,9},{9,8},{10,11... | collective-permute-start | bytes 3981320 | tf_op jit(solution)/shard_map/ppermute | solution.py:508
  238.4 81.4 %collective-permute-start.31 = (bf16[576,1152]{1,0:T(8,128)(2,1)}, bf16[576,1152]{1,0:T(8,128)(2,1)}, u32[]{:S(2)}, u32[]{:S(2)}) collective-permute-start(bf16[576,1152]{1,0:T(8,128)(2,1)} %collective-permute-done.27.refs_3_), channel_id=1, source_target_pairs={{0,4},{1,5},{2,6},{3,7},{4,0},{5,1},{6,2},{7,3},{8,12},{9,13},{10,... | collective-permute-start | bytes 3981320 | tf_op jit(solution)/shard_map/ppermute | solution.py:508
  265.5 53.9 %collective-permute-start.30 = (bf16[576,1152]{1,0:T(8,128)(2,1)}, bf16[576,1152]{1,0:T(8,128)(2,1)}, u32[]{:S(2)}, u32[]{:S(2)}) collective-permute-start(bf16[576,1152]{1,0:T(8,128)(2,1)} %collective-permute-done.26.refs_2_), channel_id=1, source_target_pairs={{0,4},{1,5},{2,6},{3,7},{4,0},{5,1},{6,2},{7,3},{8,12},{9,13},{10,... | collective-permute-start | bytes 3981320 | tf_op jit(solution)/shard_map/ppermute | solution.py:508
  265.5 54.5 %collective-permute-start.38 = (bf16[5184,128]{1,0:T(8,128)(2,1)}, bf16[5184,128]{1,0:T(8,128)(2,1)}, u32[]{:S(2)}, u32[]{:S(2)}) collective-permute-start(bf16[5184,128]{1,0:T(8,128)(2,1)} %collective-permute-done.36.refs_3_), channel_id=1, source_target_pairs={{0,2},{1,3},{2,0},{3,1},{4,6},{5,7},{6,4},{7,5},{8,10},{9,11},{10,... | collective-permute-start | bytes 3981320 | tf_op jit(solution)/shard_map/ppermute | solution.py:508
  292.2 113.8 %collective-permute-start.39 = (bf16[5184,128]{1,0:T(8,128)(2,1)}, bf16[5184,128]{1,0:T(8,128)(2,1)S(1)}, u32[]{:S(2)}, u32[]{:S(2)}) collective-permute-start(bf16[5184,128]{1,0:T(8,128)(2,1)} %constant_dynamic-update-slice_fusion.15.refs_2_), channel_id=1, source_target_pairs={{0,4},{1,5},{2,6},{3,7},{4,0},{5,1},{6,2},{7,3},{8,12},{9,13},{10,... | collective-permute-start | bytes 3981320 | tf_op jit(solution)/shard_map/ppermute | solution.py:508
  319.4 86.7 %collective-permute-start.40 = (bf16[5184,128]{1,0:T(8,128)(2,1)}, bf16[5184,128]{1,0:T(8,128)(2,1)S(1)}, u32[]{:S(2)}, u32[]{:S(2)}) collective-permute-start(bf16[5184,128]{1,0:T(8,128)(2,1)} %collective-permute-done.36.refs_3_), channel_id=1, source_target_pairs={{0,4},{1,5},{2,6},{3,7},{4,0},{5,1},{6,2},{7,3},{8,12},{9,13},{10,... | collective-permute-start | bytes 3981320 | tf_op jit(solution)/shard_map/ppermute | solution.py:508
  319.4 86.7 %collective-permute-start.41 = (bf16[5184,128]{1,0:T(8,128)(2,1)}, bf16[5184,128]{1,0:T(8,128)(2,1)S(1)}, u32[]{:S(2)}, u32[]{:S(2)}) collective-permute-start(bf16[5184,128]{1,0:T(8,128)(2,1)} %collective-permute-done.37.refs_4_), channel_id=1, source_target_pairs={{0,4},{1,5},{2,6},{3,7},{4,0},{5,1},{6,2},{7,3},{8,12},{9,13},{10,... | collective-permute-start | bytes 3981320 | tf_op jit(solution)/shard_map/ppermute | solution.py:508
  319.9 77.2 %collective-permute-start.32 = (bf16[576,1152]{1,0:T(8,128)(2,1)}, bf16[576,1152]{1,0:T(8,128)(2,1)}, u32[]{:S(2)}, u32[]{:S(2)}) collective-permute-start(bf16[576,1152]{1,0:T(8,128)(2,1)} %collective-permute-done.28.refs_4_), channel_id=1, source_target_pairs={{0,4},{1,5},{2,6},{3,7},{4,0},{5,1},{6,2},{7,3},{8,12},{9,13},{10,... | collective-permute-start | bytes 3981320 | tf_op jit(solution)/shard_map/ppermute | solution.py:508
  320.0 86.1 %collective-permute-start.42 = (bf16[5184,128]{1,0:T(8,128)(2,1)}, bf16[5184,128]{1,0:T(8,128)(2,1)}, u32[]{:S(2)}, u32[]{:S(2)}) collective-permute-start(bf16[5184,128]{1,0:T(8,128)(2,1)} %collective-permute-done.38.refs_5_), channel_id=1, source_target_pairs={{0,4},{1,5},{2,6},{3,7},{4,0},{5,1},{6,2},{7,3},{8,12},{9,13},{10,... | collective-permute-start | bytes 3981320 | tf_op jit(solution)/shard_map/ppermute | solution.py:508
  528.8 32.9 %collective-permute-start.44 = (bf16[4,2,2,144,1152]{4,3,1,0,2:T(8,128)(2,1)}, bf16[4,2,2,144,1152]{4,3,1,0,2:T(8,128)(2,1)}, u32[]{:S(2)}, u32[]{:S(2)}) collective-permute-start(bf16[4,2,2,144,1152]{4,3,1,0,2:T(8,128)(2,1)} %copy.125), channel_id=1, source_target_pairs={{0,4},{1,5},{2,6},{3,7},{4,0},{5,1},{6,2},{7,3},{8,12},{9,13},{10,... | collective-permute-start | bytes 15925256 | tf_op jit(solution)/shard_map/ppermute | solution.py:508
  568.5 74.0 %collective-permute-start.46 = (bf16[4,2,144,1152]{3,2,1,0:T(8,128)(2,1)}, bf16[4,2,144,1152]{3,2,1,0:T(8,128)(2,1)}, u32[]{:S(2)}, u32[]{:S(2)}) collective-permute-start(bf16[4,2,144,1152]{3,2,1,0:T(8,128)(2,1)} %get-tuple-element.217), channel_id=1, source_target_pairs={{0,1},{1,0},{2,3},{3,2},{4,5},{5,4},{6,7},{7,6},{8,9},{9,8},{10,11... | collective-permute-start | bytes 7962632 | tf_op jit(solution)/shard_map/ppermute | solution.py:508
  578.1 68.7 %collective-permute-start.47 = (bf16[4,144,2304]{2,1,0:T(8,128)(2,1)}, bf16[4,144,2304]{2,1,0:T(8,128)(2,1)}, u32[]{:S(2)}, u32[]{:S(2)}) collective-permute-start(bf16[4,144,2304]{2,1,0:T(8,128)(2,1)} %get-tuple-element.219), channel_id=1, source_target_pairs={{0,2},{1,3},{2,0},{3,1},{4,6},{5,7},{6,4},{7,5},{8,10},{9,11},{10,... | collective-permute-start | bytes 7962632 | tf_op jit(solution)/shard_map/ppermute | solution.py:508
  645.2 64.4 %collective-permute-start.48 = (bf16[4,144,1152]{2,1,0:T(8,128)(2,1)S(1)}, bf16[4,144,1152]{2,1,0:T(8,128)(2,1)}, u32[]{:S(2)}, u32[]{:S(2)}) collective-permute-start(bf16[4,144,1152]{2,1,0:T(8,128)(2,1)S(1)} %get-tuple-element.225), channel_id=1, source_target_pairs={{0,2},{1,3},{2,0},{3,1},{4,6},{5,7},{6,4},{7,5},{8,10},{9,11},{10,... | collective-permute-start | bytes 3981320 | tf_op jit(solution)/shard_map/ppermute | solution.py:508
  650.9 61.2 %collective-permute-start.49 = (bf16[4,144,1152]{2,1,0:T(8,128)(2,1)}, bf16[4,144,1152]{2,1,0:T(8,128)(2,1)}, u32[]{:S(2)}, u32[]{:S(2)}) collective-permute-start(bf16[4,144,1152]{2,1,0:T(8,128)(2,1)} %get-tuple-element.227), channel_id=1, source_target_pairs={{0,1},{1,0},{2,3},{3,2},{4,5},{5,4},{6,7},{7,6},{8,9},{9,8},{10,11... | collective-permute-start | bytes 3981320 | tf_op jit(solution)/shard_map/ppermute | solution.py:508
  735.0 38.1 %collective-permute-start.51 = (bf16[4,144,2304]{2,1,0:T(8,128)(2,1)}, bf16[4,144,2304]{2,1,0:T(8,128)(2,1)}, u32[]{:S(2)}, u32[]{:S(2)}) collective-permute-start(bf16[4,144,2304]{2,1,0:T(8,128)(2,1)} %bitcast.311), channel_id=1, source_target_pairs={{0,4},{1,5},{2,6},{3,7},{4,0},{5,1},{6,2},{7,3},{8,12},{9,13},{10,... | collective-permute-start | bytes 7962632 | tf_op jit(solution)/shard_map/ppermute | solution.py:508
  743.2 32.6 %collective-permute-start.52 = (bf16[4,144,1152]{2,1,0:T(8,128)(2,1)}, bf16[4,144,1152]{2,1,0:T(8,128)(2,1)}, u32[]{:S(2)}, u32[]{:S(2)}) collective-permute-start(bf16[4,144,1152]{2,1,0:T(8,128)(2,1)} %bitcast.312), channel_id=1, source_target_pairs={{0,4},{1,5},{2,6},{3,7},{4,0},{5,1},{6,2},{7,3},{8,12},{9,13},{10,... | collective-permute-start | bytes 3981320 | tf_op jit(solution)/shard_map/ppermute | solution.py:508
  743.7 37.6 %collective-permute-start.53 = (bf16[1,544,1152]{2,1,0:T(8,128)(2,1)}, bf16[1,544,1152]{2,1,0:T(8,128)(2,1)}, u32[]{:S(2)}, u32[]{:S(2)}) collective-permute-start(bf16[1,544,1152]{2,1,0:T(8,128)(2,1)} %fusion.16), channel_id=1, source_target_pairs={{0,1},{1,0},{2,3},{3,2},{4,5},{5,4},{6,7},{7,6},{8,9},{9,8},{10,11... | collective-permute-start | bytes 3760136 | tf_op jit(solution)/shard_map/ppermute | solution.py:508
  744.9 55.4 %collective-permute-start.54 = (bf16[1,544,1152]{2,1,0:T(8,128)(2,1)}, bf16[1,544,1152]{2,1,0:T(8,128)(2,1)}, u32[]{:S(2)}, u32[]{:S(2)}) collective-permute-start(bf16[1,544,1152]{2,1,0:T(8,128)(2,1)} %fusion.17), channel_id=1, source_target_pairs={{0,1},{1,0},{2,3},{3,2},{4,5},{5,4},{6,7},{7,6},{8,9},{9,8},{10,11... | collective-permute-start | bytes 3760136 | tf_op jit(solution)/shard_map/ppermute | solution.py:508
  753.8 22.1 %collective-permute-start.50 = (bf16[4,144,1152]{2,1,0:T(8,128)(2,1)}, bf16[4,144,1152]{2,1,0:T(8,128)(2,1)}, u32[]{:S(2)}, u32[]{:S(2)}) collective-permute-start(bf16[4,144,1152]{2,1,0:T(8,128)(2,1)} %bitcast.313), channel_id=1, source_target_pairs={{0,4},{1,5},{2,6},{3,7},{4,0},{5,1},{6,2},{7,3},{8,12},{9,13},{10,... | collective-permute-start | bytes 3981320 | tf_op jit(solution)/shard_map/ppermute | solution.py:508
  826.4 32.6 %collective-permute-start.56 = (bf16[4,2,2,72,1152]{4,3,1,0,2:T(8,128)(2,1)}, bf16[4,2,2,72,1152]{4,3,1,0,2:T(8,128)(2,1)}, u32[]{:S(2)}, u32[]{:S(2)}) collective-permute-start(bf16[4,2,2,72,1152]{4,3,1,0,2:T(8,128)(2,1)} %copy.129), channel_id=1, source_target_pairs={{0,4},{1,5},{2,6},{3,7},{4,0},{5,1},{6,2},{7,3},{8,12},{9,13},{10,... | collective-permute-start | bytes 7962632 | tf_op jit(solution)/shard_map/ppermute | solution.py:508
  836.8 26.4 %collective-permute-start.81 = (bf16[144,1152]{1,0:T(8,128)(2,1)}, bf16[144,1152]{1,0:T(8,128)(2,1)S(1)}, u32[]{:S(2)}, u32[]{:S(2)}) collective-permute-start(bf16[144,1152]{1,0:T(8,128)(2,1)} %get-tuple-element.250), channel_id=1, source_target_pairs={{0,8},{1,9},{2,10},{3,11},{4,12},{5,13},{6,14},{7,15},{8,16},{9,17... | collective-permute-start | bytes 995336 | tf_op jit(solution)/shard_map/ppermute | solution.py:508
  842.7 28.4 %collective-permute-start.82 = (bf16[144,1152]{1,0:T(8,128)(2,1)S(1)}, bf16[144,1152]{1,0:T(8,128)(2,1)S(1)}, u32[]{:S(2)}, u32[]{:S(2)}) collective-permute-start(bf16[144,1152]{1,0:T(8,128)(2,1)S(1)} %get-tuple-element.249), channel_id=1, source_target_pairs={{0,16},{1,17},{2,18},{3,19},{4,20},{5,21},{6,22},{7,23},{8,24},{9,... | collective-permute-start | bytes 995336 | tf_op jit(solution)/shard_map/ppermute | solution.py:508
  846.1 30.5 %collective-permute-start.83 = (bf16[144,1152]{1,0:T(8,128)(2,1)S(1)}, bf16[144,1152]{1,0:T(8,128)(2,1)S(1)}, u32[]{:S(2)}, u32[]{:S(2)}) collective-permute-start(bf16[144,1152]{1,0:T(8,128)(2,1)S(1)} %get-tuple-element.248), channel_id=1, source_target_pairs={{0,24},{1,25},{2,26},{3,27},{4,28},{5,29},{6,30},{7,31},{8,0},{9,1... | collective-permute-start | bytes 995336 | tf_op jit(solution)/shard_map/ppermute | solution.py:508
  856.9 91.8 %collective-permute-start.78 = (bf16[144,1152]{1,0:T(8,128)(2,1)}, bf16[144,1152]{1,0:T(8,128)(2,1)}, u32[]{:S(2)}, u32[]{:S(2)}) collective-permute-start(bf16[144,1152]{1,0:T(8,128)(2,1)} %get-tuple-element.247), channel_id=1, source_target_pairs={{0,8},{1,9},{2,10},{3,11},{4,12},{5,13},{6,14},{7,15},{8,16},{9,17... | collective-permute-start | bytes 995336 | tf_op jit(solution)/shard_map/ppermute | solution.py:508
  859.0 91.4 %collective-permute-start.79 = (bf16[144,1152]{1,0:T(8,128)(2,1)}, bf16[144,1152]{1,0:T(8,128)(2,1)}, u32[]{:S(2)}, u32[]{:S(2)}) collective-permute-start(bf16[144,1152]{1,0:T(8,128)(2,1)} %get-tuple-element.246), channel_id=1, source_target_pairs={{0,16},{1,17},{2,18},{3,19},{4,20},{5,21},{6,22},{7,23},{8,24},{9,... | collective-permute-start | bytes 995336 | tf_op jit(solution)/shard_map/ppermute | solution.py:508
  863.3 20.8 %collective-permute-start.66 = (f32[99,128]{1,0:T(8,128)S(1)}, f32[99,128]{1,0:T(8,128)S(1)}, u32[]{:S(2)}, u32[]{:S(2)}) collective-permute-start(f32[99,128]{1,0:T(8,128)S(1)} %bitcast_add_fusion), channel_id=1, source_target_pairs={{0,1},{1,0},{2,3},{3,2},{4,5},{5,4},{6,7},{7,6},{8,9},{9,8},{10,11... | collective-permute-start | bytes 152072 | tf_op jit(solution)/shard_map/ppermute | solution.py:508
  871.1 35.7 %collective-permute-start.58 = (bf16[4,2,72,1152]{3,2,1,0:T(8,128)(2,1)}, bf16[4,2,72,1152]{3,2,1,0:T(8,128)(2,1)}, u32[]{:S(2)}, u32[]{:S(2)}) collective-permute-start(bf16[4,2,72,1152]{3,2,1,0:T(8,128)(2,1)} %get-tuple-element.223), channel_id=1, source_target_pairs={{0,1},{1,0},{2,3},{3,2},{4,5},{5,4},{6,7},{7,6},{8,9},{9,8},{10,11... | collective-permute-start | bytes 3981320 | tf_op jit(solution)/shard_map/ppermute | solution.py:508
  878.0 96.8 %all-to-all-start.1 = ((bf16[4,144,288]{2,1,0:T(8,128)(2,1)}), bf16[4,144,288]{2,1,0:T(8,128)(2,1)}, u32[]{:S(2)}, u32[]{:S(2)}) async-start(bf16[4,144,288]{2,1,0:T(8,128)(2,1)} %copy.132), calls=%async_computation.1 | async-start | bytes 884736 | tf_op jit(solution)/shard_map/all_to_all | solution.py:676
  882.1 37.0 %collective-permute-start.59 = (bf16[4,144,1152]{2,1,0:T(8,128)(2,1)}, bf16[4,144,1152]{2,1,0:T(8,128)(2,1)S(1)}, u32[]{:S(2)}, u32[]{:S(2)}) collective-permute-start(bf16[4,144,1152]{2,1,0:T(8,128)(2,1)} %get-tuple-element.220), channel_id=1, source_target_pairs={{0,2},{1,3},{2,0},{3,1},{4,6},{5,7},{6,4},{7,5},{8,10},{9,11},{10,... | collective-permute-start | bytes 3981320 | tf_op jit(solution)/shard_map/ppermute | solution.py:508
  884.1 62.5 %collective-permute-start.60 = (bf16[4,144,1152]{2,1,0:T(8,128)(2,1)}, bf16[4,144,1152]{2,1,0:T(8,128)(2,1)S(1)}, u32[]{:S(2)}, u32[]{:S(2)}) collective-permute-start(bf16[4,144,1152]{2,1,0:T(8,128)(2,1)} %get-tuple-element.213), channel_id=1, source_target_pairs={{0,2},{1,3},{2,0},{3,1},{4,6},{5,7},{6,4},{7,5},{8,10},{9,11},{10,... | collective-permute-start | bytes 3981320 | tf_op jit(solution)/shard_map/ppermute | solution.py:508
  906.8 43.6 %collective-permute-start.80 = (bf16[144,1152]{1,0:T(8,128)(2,1)}, bf16[144,1152]{1,0:T(8,128)(2,1)S(1)}, u32[]{:S(2)}, u32[]{:S(2)}) collective-permute-start(bf16[144,1152]{1,0:T(8,128)(2,1)} %get-tuple-element.245), channel_id=1, source_target_pairs={{0,24},{1,25},{2,26},{3,27},{4,28},{5,29},{6,30},{7,31},{8,0},{9,1... | collective-permute-start | bytes 995336 | tf_op jit(solution)/shard_map/ppermute | solution.py:508
  919.1 33.4 %collective-permute-start.67 = (f32[99,128]{1,0:T(8,128)S(1)}, f32[99,128]{1,0:T(8,128)S(1)}, u32[]{:S(2)}, u32[]{:S(2)}) collective-permute-start(f32[99,128]{1,0:T(8,128)S(1)} %fusion.62), channel_id=1, source_target_pairs={{0,2},{1,3},{2,0},{3,1},{4,6},{5,7},{6,4},{7,5},{8,10},{9,11},{10,... | collective-permute-start | bytes 152072 | tf_op jit(solution)/shard_map/ppermute | solution.py:508
  946.5 37.9 %collective-permute-start.61 = (bf16[4,72,1152]{2,1,0:T(8,128)(2,1)}, bf16[4,72,1152]{2,1,0:T(8,128)(2,1)}, u32[]{:S(2)}, u32[]{:S(2)}) collective-permute-start(bf16[4,72,1152]{2,1,0:T(8,128)(2,1)} %get-tuple-element.244), channel_id=1, source_target_pairs={{0,2},{1,3},{2,0},{3,1},{4,6},{5,7},{6,4},{7,5},{8,10},{9,11},{10,... | collective-permute-start | bytes 1990664 | tf_op jit(solution)/shard_map/ppermute | solution.py:508
  948.7 37.0 %collective-permute-start.71 = (bf16[4,144,1152]{2,1,0:T(8,128)(2,1)}, bf16[4,144,1152]{2,1,0:T(8,128)(2,1)}, u32[]{:S(2)}, u32[]{:S(2)}) collective-permute-start(bf16[4,144,1152]{2,1,0:T(8,128)(2,1)} %get-tuple-element.211), channel_id=1, source_target_pairs={{0,1},{1,0},{2,3},{3,2},{4,5},{5,4},{6,7},{7,6},{8,9},{9,8},{10,11... | collective-permute-start | bytes 3981320 | tf_op jit(solution)/shard_map/ppermute | solution.py:508
  952.5 31.2 %collective-permute-start.68 = (f32[99,128]{1,0:T(8,128)S(1)}, f32[99,128]{1,0:T(8,128)S(1)}, u32[]{:S(2)}, u32[]{:S(2)}) collective-permute-start(f32[99,128]{1,0:T(8,128)S(1)} %add.730), channel_id=1, source_target_pairs={{0,8},{1,9},{2,10},{3,11},{4,12},{5,13},{6,14},{7,15},{8,16},{9,17... | collective-permute-start | bytes 152072 | tf_op jit(solution)/shard_map/ppermute | solution.py:508
  983.7 64.7 %collective-permute-start.55 = (f32[2,24,1152]{2,1,0:T(8,128)}, f32[2,24,1152]{2,1,0:T(8,128)S(1)}, u32[]{:S(2)}, u32[]{:S(2)}) collective-permute-start(f32[2,24,1152]{2,1,0:T(8,128)} %slice.318), channel_id=1, source_target_pairs={{2,1},{6,5},{10,9},{14,13},{18,17},{22,21},{26,25},{30,29}} | collective-permute-start | bytes 663560 | tf_op jit(solution)/shard_map/ppermute | solution.py:515
  987.5 23.8 %collective-permute-start.72 = (bf16[144,1152]{1,0:T(8,128)(2,1)S(1)}, bf16[144,1152]{1,0:T(8,128)(2,1)S(1)}, u32[]{:S(2)}, u32[]{:S(2)}) collective-permute-start(bf16[144,1152]{1,0:T(8,128)(2,1)S(1)} %get-tuple-element.240), channel_id=1, source_target_pairs={{0,8},{1,9},{2,10},{3,11},{4,12},{5,13},{6,14},{7,15},{8,16},{9,17... | collective-permute-start | bytes 995336 | tf_op jit(solution)/shard_map/ppermute | solution.py:508
  1000.2 22.9 %collective-permute-start.74 = (bf16[144,1152]{1,0:T(8,128)(2,1)S(1)}, bf16[144,1152]{1,0:T(8,128)(2,1)S(1)}, u32[]{:S(2)}, u32[]{:S(2)}) collective-permute-start(bf16[144,1152]{1,0:T(8,128)(2,1)S(1)} %get-tuple-element.241), channel_id=1, source_target_pairs={{0,24},{1,25},{2,26},{3,27},{4,28},{5,29},{6,30},{7,31},{8,0},{9,1... | collective-permute-start | bytes 995336 | tf_op jit(solution)/shard_map/ppermute | solution.py:508
  1010.6 37.8 %collective-permute-start.57 = (f32[2,24,1152]{2,1,0:T(8,128)S(1)}, f32[2,24,1152]{2,1,0:T(8,128)S(1)}, u32[]{:S(2)}, u32[]{:S(2)}) collective-permute-start(f32[2,24,1152]{2,1,0:T(8,128)S(1)} %slice.322), channel_id=1, source_target_pairs={{2,1},{6,5},{10,9},{14,13},{18,17},{22,21},{26,25},{30,29}} | collective-permute-start | bytes 663560 | tf_op jit(solution)/shard_map/ppermute | solution.py:515
  1011.3 26.8 %collective-permute-start.62 = (bf16[72,1152]{1,0:T(8,128)(2,1)S(1)}, bf16[72,1152]{1,0:T(8,128)(2,1)S(1)}, u32[]{:S(2)}, u32[]{:S(2)}) collective-permute-start(bf16[72,1152]{1,0:T(8,128)(2,1)S(1)} %get-tuple-element.251), channel_id=1, source_target_pairs={{0,8},{1,9},{2,10},{3,11},{4,12},{5,13},{6,14},{7,15},{8,16},{9,17... | collective-permute-start | bytes 497672 | tf_op jit(solution)/shard_map/ppermute | solution.py:508
  (95 other events, 1746.5 us)

commit v2 on v1

--- a/solution.py
+++ b/solution.py
@@ -58,9 +58,9 @@
 
 
 def attend_kernel(
-    q_ref, own_ref, far_ref, qid_ref, kid_ref, old_out, old_lse, out_ref, lse_ref,
-    qh, kh, vh, score, prob,
+    q_ref, own_ref, far_ref, qid_ref, kid_ref, *refs
 ):
+    out_ref, lse_ref, qh, kh, vh, score, prob = refs[-7:]
     split_heads(q_ref[0], qh)
     split_keys(own_ref, far_ref, kh, vh)
     key_rows = kh.shape[1]
@@ -90,7 +90,7 @@
     out_ref[0] = join_heads(qh)
 
 
-def attend(query, own, far, query_ids, key_ids, row, out, level):
+def attend(query, own, far, query_ids, key_ids, row, *old):
     rows, width, features = query.shape
     far_rows = far.shape[1]
     key_rows = width + far_rows
@@ -107,9 +107,8 @@
             pl.BlockSpec((1, far_rows, 2 * features), only),
             pl.BlockSpec((1, 1, width), here),
             pl.BlockSpec((1, key_rows, 1), here),
-            pl.BlockSpec(memory_space=pl.ANY),
-            pl.BlockSpec(memory_space=pl.ANY),
-        ],
+        ]
+        + [pl.BlockSpec(memory_space=pl.ANY)] * len(old),
         out_specs=[wide, levels],
         out_shape=[
             jax.ShapeDtypeStruct((rows, width, features), jnp.bfloat16),
@@ -122,7 +121,7 @@
             pltpu.VMEM((key_rows, width), jnp.float32),
             pltpu.VMEM((key_rows, width), jnp.bfloat16),
         ],
-        input_output_aliases={5: 0, 6: 1},
+        input_output_aliases={5: 0, 6: 1} if old else {},
         compiler_params=pltpu.CompilerParams(vmem_limit_bytes=VMEM_BYTES),
         cost_estimate=pl.CostEstimate(
             flops=4 * HEADS * width * key_rows * LANES,
@@ -130,13 +129,13 @@
             bytes_accessed=4 * features * (width + key_rows),
         ),
         name="attend",
-    )(query, own, far, query_ids[:, None, :], key_ids[:, :, None], out, level)
+    )(query, own, far, query_ids[:, None, :], key_ids[:, :, None], *old)
 
 
 def attend_back_kernel(
-    q_ref, own_ref, far_ref, o_ref, g_ref, lse_ref, qid_ref, kid_ref, old_dq, old_dkv,
-    dq_ref, dkv_ref, qh, kh, vh, oh, gh, prob, slope,
+    q_ref, own_ref, far_ref, o_ref, g_ref, lse_ref, qid_ref, kid_ref, *refs
 ):
+    dq_ref, dkv_ref, qh, kh, vh, oh, gh, prob, slope = refs[-9:]
     split_heads(q_ref[0], qh)
     features = q_ref.shape[2]
     split_keys(own_ref, far_ref, kh, vh)
@@ -175,7 +174,7 @@
 
 
 def attend_back(
-    query, own, far, mixed, grad, level, query_ids, key_ids, row, query_grad, both_grad
+    query, own, far, mixed, grad, level, query_ids, key_ids, row, *old
 ):
     rows, width, features = query.shape
     far_rows = far.shape[1]
@@ -195,9 +194,8 @@
             pl.BlockSpec((1, HEADS, width), here),
             pl.BlockSpec((1, 1, width), here),
             pl.BlockSpec((1, key_rows, 1), here),
-            pl.BlockSpec(memory_space=pl.ANY),
-            pl.BlockSpec(memory_space=pl.ANY),
-        ],
+        ]
+        + [pl.BlockSpec(memory_space=pl.ANY)] * len(old),
         out_specs=[
             pl.BlockSpec((1, width, features), here),
             pl.BlockSpec((1, key_rows, 2 * features), here),
@@ -215,7 +213,7 @@
             pltpu.VMEM((key_rows, width), jnp.bfloat16),
             pltpu.VMEM((key_rows, width), jnp.bfloat16),
         ],
-        input_output_aliases={8: 0, 9: 1},
+        input_output_aliases={8: 0, 9: 1} if old else {},
         compiler_params=pltpu.CompilerParams(vmem_limit_bytes=VMEM_BYTES),
         cost_estimate=pl.CostEstimate(
             flops=10 * HEADS * width * key_rows * LANES,
@@ -232,51 +230,176 @@
         level,
         query_ids[:, None, :],
         key_ids[:, :, None],
-        query_grad,
-        both_grad,
-    )
-
-
-def weight_grad_kernel(outer, here_ref, left_ref, right_ref, keep_ref, give_ref, total):
-    total[...] = tn_dot(left_ref[...], right_ref[...]).astype(jnp.bfloat16)
-    inner = total.shape[0] // (2 * outer)
-    here = here_ref[0]
+        *old,
+    )
+
+
+def split_rows(total_ref, here, outer, keep_ref, give_ref):
+    inner = total_ref.shape[0] // (2 * outer)
     for group in range(outer):
         start = group * 2 * inner
-        mine = pl.multiple_of(start + here * inner, 16)
-        other = pl.multiple_of(start + (1 - here) * inner, 16)
         span = slice(group * inner, (group + 1) * inner)
-        keep_ref[span] = total[pl.ds(mine, inner)]
-        give_ref[span] = total[pl.ds(other, inner)]
-
-
-def weight_grad(left, right, here, outer, row_blocks, column_blocks, name):
-    tokens = left.shape[0]
-    model = left.shape[1] // row_blocks
-    width = right.shape[1] // column_blocks
-    half = jax.ShapeDtypeStruct((left.shape[1] // 2, right.shape[1]), jnp.bfloat16)
-    spec = pl.BlockSpec((model // 2, width), lambda i, j, here: (i, j))
+        keep_ref[span] = total_ref[pl.ds(pl.multiple_of(start + here * inner, 16), inner)]
+        give_ref[span] = total_ref[pl.ds(pl.multiple_of(start + (1 - here) * inner, 16), inner)]
+
+
+def wide_grad_kernel(outer, here_ref, left_ref, right_ref, keep_ref, give_ref, total):
+    total[...] = tn_dot(left_ref[...], right_ref[...]).astype(jnp.bfloat16)
+    split_rows(total, here_ref[0], outer, keep_ref, give_ref)
+
+
+def wide_grad(left, right, here, outer, name):
+    tokens, rows = left.shape
+    blocks = right.shape[1] // rows
+    half = jax.ShapeDtypeStruct((rows // 2, right.shape[1]), jnp.bfloat16)
+    spec = pl.BlockSpec((rows // 2, rows), lambda j, here: (0, j))
     return pl.pallas_call(
-        lambda *refs: weight_grad_kernel(outer, *refs),
+        lambda *refs: wide_grad_kernel(outer, *refs),
         grid_spec=pltpu.PrefetchScalarGridSpec(
             num_scalar_prefetch=1,
-            grid=(row_blocks, column_blocks),
+            grid=(blocks,),
             in_specs=[
-                pl.BlockSpec((tokens, model), lambda i, j, here: (0, i)),
-                pl.BlockSpec((tokens, width), lambda i, j, here: (0, j)),
+                pl.BlockSpec((tokens, rows), lambda j, here: (0, 0)),
+                pl.BlockSpec((tokens, rows), lambda j, here: (0, j)),
             ],
             out_specs=[spec, spec],
-            scratch_shapes=[pltpu.VMEM((model, width), jnp.bfloat16)],
+            scratch_shapes=[pltpu.VMEM((rows, rows), jnp.bfloat16)],
         ),
         out_shape=[half, half],
         compiler_params=pltpu.CompilerParams(vmem_limit_bytes=VMEM_BYTES),
         cost_estimate=pl.CostEstimate(
-            flops=2 * tokens * left.shape[1] * right.shape[1],
+            flops=2 * tokens * rows * right.shape[1],
             transcendentals=0,
-            bytes_accessed=2 * (tokens + right.shape[1]) * (left.shape[1] + right.shape[1]),
+            bytes_accessed=2 * (tokens + right.shape[1]) * rows,
         ),
         name=name,
-    )(here.astype(jnp.int32).reshape(1), left, right)
+    )(here, left, right)
+
+
+def tall_grad_kernel(groups, here_ref, left_ref, right_ref, keep_ref, give_ref, total):
+    total[...] = tn_dot(left_ref[...], right_ref[...]).astype(jnp.bfloat16)
+    here = here_ref[0]
+    inner = total.shape[0] // (2 * groups)
+    columns = total.shape[1] // 4
+    for group in range(groups):
+        start = group * 2 * inner
+        for core, out_ref in ((here, keep_ref), (1 - here, give_ref)):
+            rows = total[pl.ds(pl.multiple_of(start + core * inner, 16), inner)]
+            for place in range(4):
+                out_ref[group, place] = pack_lanes(rows[:, place * columns : (place + 1) * columns])
+
+
+def tall_grad(left, right, here, outer, name):
+    tokens, model = right.shape
+    blocks = left.shape[1] // model
+    groups = outer // blocks
+    packed = left.shape[1] // (2 * outer) * (model // 4) // LANES
+    half = jax.ShapeDtypeStruct((outer, 4, packed, LANES), jnp.bfloat16)
+    spec = pl.BlockSpec((groups, 4, packed, LANES), lambda i, here: (i, 0, 0, 0))
+    return pl.pallas_call(
+        lambda *refs: tall_grad_kernel(groups, *refs),
+        grid_spec=pltpu.PrefetchScalarGridSpec(
+            num_scalar_prefetch=1,
+            grid=(blocks,),
+            in_specs=[
+                pl.BlockSpec((tokens, model), lambda i, here: (0, i)),
+                pl.BlockSpec((tokens, model), lambda i, here: (0, 0)),
+            ],
+            out_specs=[spec, spec],
+            scratch_shapes=[pltpu.VMEM((model, model), jnp.bfloat16)],
+        ),
+        out_shape=[half, half],
+        compiler_params=pltpu.CompilerParams(vmem_limit_bytes=VMEM_BYTES),
+        cost_estimate=pl.CostEstimate(
+            flops=2 * tokens * model * left.shape[1],
+            transcendentals=0,
+            bytes_accessed=2 * (tokens + model) * left.shape[1],
+        ),
+        name=name,
+    )(here, left, right)
+
+
+def mixed_grad_kernel(
+    outer, here_ref, first_ref, far_a, far_b, att_ref, query_ref, both_ref, proj_ref,
+    keep_ref, give_ref, total, sums,
+):
+    step = pl.program_id(0)
+    width = far_a.shape[0]
+    span = far_a.shape[0] + first_ref.shape[0] // 2
+    own = first_ref.shape[0] // 2
+
+    @pl.when(step == 0)
+    def _():
+        total[0] = tn_dot(first_ref[...], query_ref[...]).astype(jnp.bfloat16)
+
+    @pl.when((step == 1) | (step == 2))
+    def _():
+        sums[...] = tn_dot(first_ref[0:own], both_ref[0:own])
+        sums[...] += tn_dot(far_a[...], both_ref[own:span])
+        sums[...] += tn_dot(first_ref[own:], both_ref[span : span + own])
+        total[step] = (sums[...] + tn_dot(far_b[...], both_ref[span + own :])).astype(jnp.bfloat16)
+
+    @pl.when(step == 3)
+    def _():
+        total[3] = tn_dot(att_ref[...], proj_ref[...]).astype(jnp.bfloat16)
+        here = here_ref[0]
+        model = total.shape[2]
+        inner = model // (2 * outer)
+        cut = model * 3 // 4
+        for group in range(outer):
+            rows = slice(group * inner, (group + 1) * inner)
+            for core, out_ref in ((here, keep_ref), (1 - here, give_ref)):
+                start = pl.multiple_of((group * 2 + core) * inner, 16)
+                wide = jnp.concatenate([total[k, pl.ds(start, inner)] for k in range(3)], axis=1)
+                last = total[3, pl.ds(start, inner)]
+                for place in range(4):
+                    out_ref[rows, place * model : (place + 1) * model] = jnp.concatenate(
+                        [
+                            wide[:, place * cut : (place + 1) * cut],
+                            last[:, place * (model - cut) : (place + 1) * (model - cut)],
+                        ],
+                        axis=1,
+                    )
+
+
+def mixed_grad(first, far, attended, query_grad, both_grad, proj_grad, here, outer):
+    tokens, model = first.shape
+    half = jax.ShapeDtypeStruct((model // 2, 4 * model), jnp.bfloat16)
+    fixed = lambda *shape: pl.BlockSpec(
+        shape, lambda j, here: (0, 0), pipeline_mode=pl.Buffered(1)
+    )
+    return pl.pallas_call(
+        lambda *refs: mixed_grad_kernel(outer, *refs),
+        grid_spec=pltpu.PrefetchScalarGridSpec(
+            num_scalar_prefetch=1,
+            grid=(4,),
+            in_specs=[
+                fixed(tokens, model),
+                fixed(*far[0].shape),
+                fixed(*far[1].shape),
+                fixed(tokens, model),
+                fixed(tokens, model),
+                pl.BlockSpec(
+                    (both_grad.shape[0], model),
+                    lambda j, here: (0, jnp.minimum(jnp.maximum(j - 1, 0), 1)),
+                ),
+                fixed(tokens, model),
+            ],
+            out_specs=[fixed(model // 2, 4 * model), fixed(model // 2, 4 * model)],
+            scratch_shapes=[
+                pltpu.VMEM((4, model, model), jnp.bfloat16),
+                pltpu.VMEM((model, model), jnp.float32),
+            ],
+        ),
+        out_shape=[half, half],
+        compiler_params=pltpu.CompilerParams(vmem_limit_bytes=VMEM_BYTES),
+        cost_estimate=pl.CostEstimate(
+            flops=2 * model * model * (2 * tokens + 2 * both_grad.shape[0]),
+            transcendentals=0,
+            bytes_accessed=2 * model * (6 * tokens + 2 * both_grad.shape[0] + 4 * model),
+        ),
+        name="mixed_weight_grad",
+    )(here, first, far[0], far[1], attended, query_grad, both_grad, proj_grad)
 
 
 def column_chunks(width):
@@ -490,14 +613,14 @@
     def index(self, z, c, s):
         return (z * 2 + c) * self.seq_count + s
 
-    def send(self, value, axis, turn=1):
+    def send(self, value, axis, turn=0):
         pairs = []
         for z in range(self.outer_count):
             for c in range(2):
                 for s in range(self.seq_count):
                     far_z, far_c, far_s = z, c, s
                     if axis == "z":
-                        far_z = (z + turn) % self.outer_count
+                        far_z = z ^ turn
                     elif axis == "c":
                         far_c = 1 - c
                     elif axis == "y":
@@ -516,7 +639,7 @@
 
 
 def tie(value, *others):
-    return lax.optimization_barrier((value, others))[0]
+    return lax.optimization_barrier((value, *others))[0]
 
 
 def square_gather(grid, shard):
@@ -579,14 +702,17 @@
         proj_ref[span] = jnp.concatenate([part[:, columns:] for part in parts], axis=1)
 
 
-def assemble(grid, blocks, piece, kernel, widths, rows, name):
+def assemble(grid, blocks, order, piece, kernel, widths, rows, name):
     outer = grid.outer_count
-    turns = jnp.stack([(grid.at["z"] - z + outer) % outer for z in range(outer)])
+    spots = jnp.array([order.index(turn) for turn in range(outer)], jnp.int32)
+    turns = jnp.stack(
+        [lax.dynamic_index_in_dim(spots, grid.at["z"] ^ z, keepdims=False) for z in range(outer)]
+    )
     places = [
         (grid.at["c"] ^ (block >> 2)) * 4 + (grid.seq_index ^ (block & 3)) for block in range(8)
     ]
     shapes = [jax.ShapeDtypeStruct((outer * 2 * rows, w), jnp.bfloat16) for w in widths]
-    result = pl.pallas_call(
+    return pl.pallas_call(
         kernel,
         grid_spec=pltpu.PrefetchScalarGridSpec(
             num_scalar_prefetch=2,
@@ -604,7 +730,6 @@
         ),
         name=name,
     )(turns.astype(jnp.int32), jnp.stack(places).astype(jnp.int32), *blocks)
-    return result
 
 
 def place_kernel(block_count, outer_count, to_ref, *refs):
@@ -625,15 +750,14 @@
         copy.wait()
 
 
-def place_blocks(grid, blocks):
+def place_blocks(grid, blocks, order):
     outer = grid.outer_count
     rows, columns = blocks[0].shape[0] // outer, blocks[0].shape[1]
     slots = []
     for block in range(8):
         core, place = grid.at["c"] ^ (block >> 2), grid.seq_index ^ (block & 3)
-        for turn in range(outer):
-            far = (grid.at["z"] - turn + outer) % outer
-            slots.append((place * outer + far) * 2 + core)
+        for turn in order:
+            slots.append((place * outer + (grid.at["z"] ^ turn)) * 2 + core)
     count = 8 * outer
     return pl.pallas_call(
         lambda *refs: place_kernel(8, outer, *refs),
@@ -653,28 +777,37 @@
     )(jnp.stack(slots).astype(jnp.int32), *blocks)
 
 
-def column_gather(grid, piece, *extra):
-    parts = [piece] + [grid.send(piece, "z", turn) for turn in range(1, grid.outer_count)]
-    return jnp.concatenate(parts + list(extra), axis=0)
-
-
-def seq_gather(grid, column, first):
-    if first == "x":
-        over_x = grid.send(column, "x")
-        return [column, over_x, grid.send(column, "y"), grid.send(over_x, "y")]
-    over_y = grid.send(column, "y")
-    return [column, grid.send(column, "x"), over_y, grid.send(over_y, "x")]
-
-
-def core_gather(grid, blocks):
-    return blocks + [grid.send(block, "c") for block in blocks]
-
-
-def columns_of_seq(grid, piece):
-    rows, columns = piece.shape
-    split = piece.reshape(rows, 4, columns // 4).transpose(1, 0, 2)
-    mixed = lax.all_to_all(split, "seq", 0, 0)
-    return mixed.reshape(4 * rows, columns // 4)
+class Gather:
+    def __init__(self, grid, piece, *extra, direct=False):
+        self.grid = grid
+        if direct:
+            self.order = [0, 1, 2, 3]
+            parts = [piece] + [grid.send(piece, "z", turn) for turn in (1, 2, 3)]
+        else:
+            self.order = [0, 2, 1, 3]
+            self.pair = jnp.concatenate([piece, grid.send(piece, "z", 2)], axis=0)
+            parts = [self.pair, grid.send(self.pair, "z", 1)]
+        self.column = jnp.concatenate(parts + list(extra), axis=0)
+
+    def spread(self):
+        self.over_x = self.grid.send(self.column, "x")
+        self.over_y = self.grid.send(self.column, "y")
+
+    def forward(self, axis, *after):
+        value = self.over_x if axis == "y" else self.over_y
+        if after:
+            value = tie(value, *after)
+            if axis == "y":
+                self.over_x = value
+            else:
+                self.over_y = value
+        self.blocks = [self.column, self.over_x, self.over_y, self.grid.send(value, axis)]
+
+    def core(self, *after):
+        blocks = list(self.blocks)
+        if after:
+            blocks[3] = tie(blocks[3], *after)
+        return blocks + [self.grid.send(block, "c") for block in blocks]
 
 
 def split_vectors(joint, widths):
@@ -685,39 +818,31 @@
     return result
 
 
-def gather_all(grid, matrices, vectors):
-    skip_weight, qkv_weight, proj_weight, hidden_weight, down_weight = matrices
-    widths = [vector.shape[0] for vector in vectors]
+def gather_plain(matrices, vectors):
+    joint = lax.all_gather(jnp.concatenate(vectors), "seq", axis=0)
+    wide = [
+        lax.all_gather(
+            lax.all_gather(shard, "batch", axis=0, tiled=True), "seq", axis=1, tiled=True
+        )
+        for shard in matrices
+    ]
+    return split_vectors(joint, [vector.shape[0] for vector in vectors]), wide
+
+
+def hidden_columns(hidden_full, model):
+    return jnp.stack(jnp.split(hidden_full, hidden_full.shape[1] // model, axis=1))
+
+
+def gather_skip(grid, skip_weight, vectors):
     joint = jnp.concatenate(vectors)
-    if not grid.square:
-        wide = [
-            lax.all_gather(
-                lax.all_gather(shard, "batch", axis=0, tiled=True), "seq", axis=1, tiled=True
-            )
-            for shard in matrices
-        ]
-        skip_full, qkv_full, proj_full, hidden_full, down_full = wide
-        model = skip_full.shape[1]
-        hidden_blocks = jnp.stack(jnp.split(hidden_full, hidden_full.shape[1] // model, axis=1))
-        down_blocks = down_full.reshape(-1, model, model)
-        joint = lax.all_gather(joint, "seq", axis=0)
-        return (
-            split_vectors(joint, widths),
-            skip_full,
-            qkv_full[:, :model],
-            qkv_full[:, model:],
-            proj_full,
-            hidden_blocks,
-            down_blocks,
-        )
-    model = proj_weight.shape[1] * 4
     short = -joint.shape[0] % (8 * LANES)
     extra = jnp.pad(joint, (0, short)).reshape(-1, LANES)
-    skip_rows, skip_columns = skip_weight.shape
-    skip_piece = pack_lanes(skip_weight)
-    skip_column = column_gather(grid, skip_piece, extra)
-    skip_blocks = seq_gather(grid, skip_column, "x")
-    found = jnp.stack([block[-extra.shape[0] :].reshape(-1) for block in skip_blocks])
+    rows, columns = skip_weight.shape
+    piece = pack_lanes(skip_weight)
+    way = Gather(grid, piece, extra, direct=True)
+    way.spread()
+    way.forward("y")
+    found = jnp.stack([block[-extra.shape[0] :].reshape(-1) for block in way.blocks])
     joint = jnp.stack(
         [
             lax.dynamic_index_in_dim(found, grid.seq_index ^ place, 0, keepdims=False)
@@ -726,51 +851,43 @@
     )
     (skip_full,) = assemble(
         grid,
-        core_gather(grid, skip_blocks),
-        skip_piece.shape,
-        lambda *refs: rows_kernel(skip_rows, skip_columns, *refs),
-        [model],
-        skip_rows,
+        way.core(),
+        way.order,
+        piece.shape,
+        lambda *refs: rows_kernel(rows, columns, *refs),
+        [4 * columns],
+        rows,
         "join_skip",
     )
-    mixed_piece = jnp.concatenate([qkv_weight, proj_weight], axis=1)
-    mixed_piece = tie(mixed_piece, skip_blocks[1], skip_blocks[2])
-    mixed_column = column_gather(grid, mixed_piece)
-    mixed_blocks = seq_gather(grid, mixed_column, "x")
-    query_full, both_full, proj_full = assemble(
+    return way, split_vectors(joint, [vector.shape[0] for vector in vectors]), skip_full
+
+
+def join_mixed(grid, blocks, order, rows, columns, model):
+    return assemble(
         grid,
-        core_gather(grid, mixed_blocks),
-        mixed_piece.shape,
-        lambda *refs: mixed_kernel(qkv_weight.shape[1], *refs),
+        blocks,
+        order,
+        (rows, model),
+        lambda *refs: mixed_kernel(columns, *refs),
         [model, 2 * model, model],
-        mixed_piece.shape[0],
+        rows,
         "join_mixed",
     )
-    hidden_piece = tie(hidden_weight, mixed_column)
-    hidden_column = column_gather(grid, hidden_piece)
-    hidden_blocks = seq_gather(grid, hidden_column, "y")
-    hidden_full = place_blocks(grid, core_gather(grid, hidden_blocks)).reshape(4, -1, model)
-    down_rows, down_columns = down_weight.shape
-    down_piece = tie(pack_lanes(down_weight), hidden_column)
-    down_blocks = seq_gather(grid, column_gather(grid, down_piece), "x")
-    (down_full,) = assemble(
+
+
+def join_down(grid, blocks, order, rows, columns):
+    packed = rows * columns // LANES
+    (full,) = assemble(
         grid,
-        core_gather(grid, down_blocks),
-        down_piece.shape,
-        lambda *refs: rows_kernel(down_rows, down_columns, *refs),
-        [model],
-        down_rows,
+        blocks,
+        order,
+        (packed, LANES),
+        lambda *refs: rows_kernel(rows, columns, *refs),
+        [4 * columns],
+        rows,
         "join_down",
     )
-    return (
-        split_vectors(joint, widths),
-        skip_full,
-        query_full,
-        both_full,
-        proj_full,
-        hidden_full,
-        down_full.reshape(-1, model, model),
-    )
+    return full.reshape(-1, 4 * columns, 4 * columns)
 
 
 def add_low(mine, other):
@@ -778,65 +895,61 @@
 
 
 class Scatter:
-    def __init__(self, grid, keep, give):
-        self.grid, self.mine, self.sent = grid, keep, give
-        self.got = [grid.send(value, "c") for value in give]
-
-    def push(self, axis, choose):
+    def __init__(self, grid, keep, give, view):
+        self.grid, self.mine, self.sent, self.view = grid, keep, give, view
+        self.got = grid.send(give, "c")
+
+    def push(self, axis, choose, turn=0):
         here = self.grid.at[axis]
-        self.mine = choose(self.values, here)
-        self.sent = choose(self.values, 1 - here)
-        self.got = [self.grid.send(value, axis) for value in self.sent]
+        if turn:
+            here = here // turn % 2
+        self.mine, self.sent = choose(self.value, here), choose(self.value, 1 - here)
+        self.got = self.grid.send(self.sent, axis, turn)
 
     def pull(self, *after):
-        mine, got = self.mine, self.got
-        if after:
-            mine = tie(mine, *after)
-        self.values = [add_low(m, g) for m, g in zip(mine, got, strict=True)]
-
-    def push_outer(self):
-        grid = self.grid
-        (value,) = self.values
-        pick = lambda at: lax.dynamic_index_in_dim(value, at, 0, keepdims=False)
-        self.mine = pick(grid.at["z"])
-        self.sent = [
-            pick((grid.at["z"] + turn) % grid.outer_count) for turn in range(1, grid.outer_count)
-        ]
-        self.got = [grid.send(value, "z", turn + 1) for turn, value in enumerate(self.sent)]
-
-    def pull_outer(self, *after):
         mine = tie(self.mine, *after) if after else self.mine
-        total = mine.astype(jnp.float32)
-        for value in self.got:
-            total = total + value.astype(jnp.float32)
-        return total
+        self.value = add_low(mine, self.got)
+        if self.view is not None:
+            self.value, self.view = self.value.reshape(self.view), None
+        return self.value
+
+
+def fork(way):
+    rows = way.value.shape[1] // 2
+    ways = []
+    for part in range(2):
+        branch = object.__new__(Scatter)
+        branch.grid, branch.view = way.grid, None
+        branch.value = way.value[:, part * rows : (part + 1) * rows]
+        ways.append(branch)
+    return ways
 
 
 def choose_dim(dim):
-    return lambda values, at: [
-        lax.dynamic_index_in_dim(value, at, dim, keepdims=False) for value in values
+    return lambda value, at: lax.dynamic_index_in_dim(value, at, dim, keepdims=False)
+
+
+def choose_half(value, at):
+    half = value.shape[0] // 2
+    return lax.dynamic_slice_in_dim(value, at * half, half, 0)
+
+
+def choose_odd(value, at):
+    pairs = value.reshape((2, 2) + value.shape[1:])
+    return lax.dynamic_index_in_dim(pairs, at, 1, keepdims=False)
+
+
+def choose_lanes(value, at):
+    half = value.shape[-1] // 2
+    return lax.dynamic_slice_in_dim(value, at * half, half, value.ndim - 1)
+
+
+def choose_odd_lanes(value, at):
+    part = value.shape[-1] // 4
+    pieces = [
+        lax.dynamic_slice_in_dim(value, (2 * k + at) * part, part, value.ndim - 1) for k in range(2)
     ]
-
-
-def choose_lanes(values, at):
-    half = values[0].shape[-1] // 2
-    return [lax.dynamic_slice_in_dim(value, at * half, half, value.ndim - 1) for value in values]
-
-
-def choose_pair(values, at):
-    half = len(values) // 2
-    return [jnp.where(at == 0, values[k], values[half + k]) for k in range(half)]
-
-
-def mixed_shards(grid, part):
-    part = part.astype(jnp.bfloat16)
-    rows, columns = part.shape
-    whole = square_gather(grid, part).reshape(4, rows, 4, columns // 4)
-    whole = whole.transpose(0, 2, 1, 3).reshape(16, rows, columns // 4)
-    qkv = lax.dynamic_slice_in_dim(whole, 3 * grid.seq_index, 3, 0)
-    qkv = qkv.transpose(1, 0, 2).reshape(rows, 3 * columns // 4)
-    proj = lax.dynamic_index_in_dim(whole, 12 + grid.seq_index, 0, keepdims=False)
-    return qkv.astype(jnp.float32), proj.astype(jnp.float32)
+    return jnp.concatenate(pieces, axis=-1)
 
 
 def seq_scatter(value):
@@ -845,27 +958,22 @@
 
 
 def scatter_vectors(grid, vectors):
-    if not grid.square:
-        totals = lax.psum(tuple(vectors), ("batch", "seq"))
+    joint = jnp.concatenate(vectors)
+    if grid.square:
+        joint = lax.all_gather(joint.reshape(-1, LANES), ("batch", "seq"))
     else:
-        sizes = [vector.shape[0] for vector in vectors]
-        joint = jnp.concatenate(vectors).reshape(-1, LANES)
-        for axis in ("c", "x", "y"):
-            joint = joint + grid.send(joint, axis)
-        others = [grid.send(joint, "z", turn) for turn in range(1, grid.outer_count)]
-        for other in others:
-            joint = joint + other
-        joint = joint.reshape(-1)
-        totals, start = [], 0
-        for size in sizes:
-            totals.append(joint[start : start + size])
-            start += size
-    return [
-        lax.dynamic_slice_in_dim(
-            total, grid.seq_index * (total.shape[0] // grid.seq_count), total.shape[0] // grid.seq_count
-        )
-        for total in totals
-    ]
+        joint = lax.psum(joint, ("batch", "seq"))[None]
+    return lambda *after: own_columns(grid, tie(joint, *after), vectors)
+
+
+def own_columns(grid, joint, vectors):
+    joint = jnp.sum(joint, axis=0).reshape(-1)
+    result, start = [], 0
+    for vector in vectors:
+        width = vector.shape[0] // grid.seq_count
+        result.append(lax.dynamic_slice_in_dim(joint, start + grid.seq_index * width, width))
+        start += vector.shape[0]
+    return result
 
 
 class Items:
@@ -920,16 +1028,15 @@
     return jnp.concatenate(ids, axis=1)
 
 
-def far_reduce(grid, value):
+def far_send(grid, value):
     half = grid.seq_count // 2
-    value = value.astype(jnp.bfloat16)
     if half == 2:
-        return grid.send(value, "x").astype(jnp.float32)
+        return grid.send(value, "x")
     split = value.reshape(half, -1, value.shape[2])
     whole = jnp.zeros((grid.seq_count,) + split.shape[1:], jnp.bfloat16)
     start = grid.seq_index // half * half
     whole = lax.dynamic_update_slice_in_dim(whole, split, start, 0)
-    return lax.psum_scatter(whole, "seq", scatter_dimension=0).astype(jnp.float32)[None]
+    return lax.psum_scatter(whole, "seq", scatter_dimension=0)[None]
 
 
 def body(
@@ -957,20 +1064,30 @@
     all_rows = -(-(own_rows + 16) // 32) * 32
     halo_rows = all_rows - own_rows
     half = grid.seq_count // 2
-    vectors, skip_full, query_full, both_full, proj_full, hidden_blocks, down_blocks = gather_all(
-        grid,
-        [skip_weight, qkv_weight, proj_weight, hidden_weight, down_weight],
-        [
-            skip_bias,
-            first_gain,
-            first_shift,
-            proj_bias,
-            second_gain,
-            second_shift,
-            hidden_bias,
-            down_bias,
-        ],
-    )
+    vectors = [
+        skip_bias,
+        first_gain,
+        first_shift,
+        proj_bias,
+        second_gain,
+        second_shift,
+        hidden_bias,
+        down_bias,
+    ]
+    if grid.square:
+        skip_way, vectors, skip_full = gather_skip(grid, skip_weight, vectors)
+        mixed_piece = jnp.concatenate([qkv_weight, proj_weight], axis=1)
+        mixed_way = Gather(grid, tie(mixed_piece, skip_way.column))
+        mixed_way.spread()
+        mixed_way.forward("y")
+    else:
+        vectors, wide = gather_plain(
+            [skip_weight, qkv_weight, proj_weight, hidden_weight, down_weight], vectors
+        )
+        skip_full, qkv_full, proj_full, hidden_full, down_full = wide
+        query_full, both_full = qkv_full[:, :model], qkv_full[:, model:]
+        hidden_blocks = hidden_columns(hidden_full, model)
+        down_blocks = down_full.reshape(-1, model, model)
     (
         skip_bias_full,
         gain_one,
@@ -981,30 +1098,54 @@
         hidden_bias_full,
         down_bias_full,
     ) = vectors
+    joined_inputs = inputs
+    if grid.square:
+        joined_inputs = tie(inputs, skip_way.over_x, skip_way.over_y)
     items = Items(grid, segments, occupied, own_rows, all_rows)
     query_ids, used = items.of(grid.seq_index)
     key_ids = jnp.concatenate([query_ids, far_ids(grid, items)], axis=1)
     tails = jnp.stack([v[:, own_rows - halo_rows :] for v in (inputs, skip_inputs, out_cotangent)])
     halo = grid.shift(tails, half - 1, half)
-    first_tokens = jnp.concatenate([inputs, halo[0]], axis=1)
+    first_tokens = jnp.concatenate([joined_inputs, halo[0]], axis=1)
     second_tokens = jnp.concatenate([skip_inputs, halo[1]], axis=1)
-    joined = jnp.concatenate([first_tokens, second_tokens], axis=2)
+    joined = tie(jnp.concatenate([first_tokens, second_tokens], axis=2))
     cotangent = jnp.concatenate([out_cotangent, halo[2]], axis=1)
 
     stream = dot_last(joined, skip_full) + skip_bias_full
     first_low, first_normal, first_scale = layer_norm(stream, gain_one, shift_one)
     rows = inputs.shape[0]
     first_far = far_gather(grid, first_low)
+    if grid.square:
+        hidden_way = Gather(grid, tie(hidden_weight, mixed_way.column, stream))
+        down_way = Gather(grid, tie(pack_lanes(down_weight), hidden_way.pair))
+        hidden_way.column = tie(hidden_way.column, mixed_way.blocks[3])
+        hidden_way.spread()
+        mixed_blocks = mixed_way.core(first_far[0], hidden_way.column, down_way.column)
+        query_full, both_full, proj_full = join_mixed(
+            grid, mixed_blocks, mixed_way.order, *qkv_weight.shape, model
+        )
+        query_full = tie(query_full, first_far[1])
+        both_full = tie(both_full, first_far[1])
     query = dot_last(first_low, query_full).astype(jnp.bfloat16)
     own = dot_last(first_low, both_full).astype(jnp.bfloat16)
-    attended = jnp.zeros(query.shape, jnp.bfloat16)
-    level = jnp.zeros((rows, HEADS, all_rows), jnp.float32)
-    far = []
+    if grid.square:
+        down_way.spread()
+        hidden_way.forward("y")
+        first_far[0] = tie(first_far[0], query, own, hidden_way.over_x, hidden_way.over_y)
+    far, done = [], ()
     for row in range(rows):
         far.append(dot_last(first_far[row], both_full).astype(jnp.bfloat16))
-        attended, level = attend(
-            query, own, far[row], query_ids, key_ids, row, attended, level
-        )
+        done = attend(query, own, far[row], query_ids, key_ids, row, *done)
+        if row == 0 and grid.square:
+            down_way.forward("y", done[0])
+            first_far[1] = tie(
+                first_far[1], *hidden_way.blocks, down_way.over_x, down_way.over_y
+            )
+    attended, level = done
+    if grid.square:
+        hidden_blocks = place_blocks(grid, hidden_way.core(), hidden_way.order)
+        hidden_blocks = hidden_blocks.reshape(-1, model, model)
+        down_blocks = join_down(grid, down_way.core(attended), down_way.order, *down_weight.shape)
     used_rows = used.astype(jnp.float32).reshape(-1, 1)
     flat = (-1, model)
     (
@@ -1036,21 +1177,18 @@
     gain_two_grad, shift_two_grad = middle_sums[0], middle_sums[1]
     proj_bias_grad, down_bias_grad = middle_sums[2], middle_sums[3]
     grad_branch = jnp.where(used[..., None], cotangent, 0).reshape(flat)
-    here, outer = grid.at["c"], grid.outer_count
-    core_rows = lambda value, *lead: value.reshape((outer,) + lead + (-1, value.shape[-1]))
+    here, outer = grid.at["c"].astype(jnp.int32).reshape(1), grid.outer_count
     if grid.square:
-        keep, give = weight_grad(act_low, grad_branch, here, outer // 4, 4, 1, "down_weight_grad")
-        down_way = Scatter(
-            grid, [core_rows(keep, 2, 2)], [core_rows(give, 2, 2)]
-        )
+        keep, give = tall_grad(act_low, grad_branch, here, outer, "down_weight_grad")
+        down_way = Scatter(grid, keep, give, (outer, 2, 2) + keep.shape[2:])
         second_low = tie(second_low, give)
-        keep, give = weight_grad(second_low, grad_pre, here, outer, 1, 4, "hidden_weight_grad")
-        hidden_way = Scatter(grid, [core_rows(keep)], [core_rows(give)])
+        keep, give = wide_grad(second_low, grad_pre, here, outer, "hidden_weight_grad")
+        hidden_way = Scatter(grid, keep, give, (outer, -1, keep.shape[1]))
         down_way.pull(give)
         down_way.push("x", choose_dim(2))
-        hidden_way.pull(*down_way.sent)
+        hidden_way.pull(down_way.sent)
         hidden_way.push("y", choose_lanes)
-        grad_attended = tie(grad_attended, *hidden_way.sent)
+        grad_attended = tie(grad_attended, hidden_way.sent)
     else:
         down_grad = outer_dot(act_low, grad_branch)
         hidden_grad = outer_dot(second_low, grad_pre)
@@ -1058,11 +1196,9 @@
     grad_middle = grad_middle.reshape(stream.shape)
     grad_attended = grad_attended.reshape(stream.shape)
 
-    query_grad = jnp.zeros(query.shape, jnp.bfloat16)
-    both_grad = jnp.zeros((rows, key_ids.shape[1], 2 * model), jnp.bfloat16)
-    grad_far = []
+    grad_far, done = [], ()
     for row in range(rows):
-        query_grad, both_grad = attend_back(
+        done = attend_back(
             query,
             own,
             far[row],
@@ -1072,57 +1208,56 @@
             query_ids,
             key_ids,
             row,
-            query_grad,
-            both_grad,
+            *done,
         )
+        both_grad = done[1]
+        if grid.square:
+            down_way.pull(both_grad)
+            hidden_way.pull(down_way.value)
+            if row == 0:
+                down_way.push("y", choose_dim(1))
+                hidden_way.push("x", choose_lanes)
+            else:
+                down_way.push("z", choose_half, 2)
+                hidden_way.push("z", choose_odd, 1)
+            both_grad = tie(both_grad, down_way.sent, hidden_way.sent, *grad_far)
         share = dot_back(both_grad[row : row + 1, all_rows:], both_full).astype(jnp.bfloat16)
-        grad_far.append(far_reduce(grid, share))
-        if row == 0 and grid.square:
-            down_way.pull(share)
-            down_way.push("y", choose_dim(1))
-            hidden_way.pull(*down_way.sent)
-            hidden_way.push("x", choose_lanes)
-            both_grad = tie(both_grad, share, *hidden_way.sent)
-    if grid.square:
-        down_way.pull(share)
-        down_way.push_outer()
-        hidden_way.pull(*down_way.sent)
-        hidden_way.push_outer()
-        both_grad = tie(both_grad, *hidden_way.sent)
+        grad_far.append(far_send(grid, share))
+        done = (done[0], tie(both_grad, share))
+    query_grad, both_grad = done
     both_flat = both_grad.reshape(-1, 2 * model)
-    first_all = [jnp.concatenate([first_low[row], first_far[row][0]]) for row in range(rows)]
-    first_all = jnp.concatenate(first_all)
     query_flat = query_grad.reshape(flat)
     if grid.square:
-        both_keep, both_give = weight_grad(
-            first_all, both_flat, here, outer, 1, 2, "both_weight_grad"
+        keep, give = mixed_grad(
+            first_low.reshape(flat),
+            [value[0] for value in first_far],
+            attended.reshape(flat),
+            query_flat,
+            both_flat,
+            grad_proj,
+            here,
+            outer,
         )
-        query_keep, query_give = weight_grad(
-            first_low.reshape(flat), query_flat, here, outer, 1, 1, "query_weight_grad"
-        )
-        proj_keep, proj_give = weight_grad(
-            attended.reshape(flat), grad_proj, here, outer, 1, 1, "proj_weight_grad"
-        )
-        mixed_way = Scatter(
-            grid,
-            [core_rows(value) for value in (query_keep, both_keep, proj_keep)],
-            [core_rows(value) for value in (query_give, both_give, proj_give)],
-        )
-        query_grad = tie(query_grad, query_give, both_give, proj_give)
+        mixed_way = Scatter(grid, keep, give, (outer, -1, keep.shape[1]))
+        down_way.pull(give)
+        down_way.push("z", choose_half, 1)
+        hidden_way.pull(give)
+        hidden_way.push("z", choose_half, 2)
+        query_grad = tie(query_grad, hidden_way.sent, down_way.sent, *grad_far)
+        both_grad = tie(both_grad, hidden_way.sent, down_way.sent, *grad_far)
     else:
-        both_weight_grad = outer_dot(first_all, both_flat)
+        first_all = [jnp.concatenate([first_low[row], first_far[row][0]]) for row in range(rows)]
+        both_weight_grad = outer_dot(jnp.concatenate(first_all), both_flat)
         query_weight_grad = outer_dot(first_low.reshape(flat), query_flat)
         proj_grad = outer_dot(attended.reshape(flat), grad_proj)
-    grad_first = dot_back(both_grad[:, :all_rows], both_full) + dot_back(query_grad, query_full)
+    grad_first = dot_back(query_grad, query_full) + dot_back(both_grad[:, :all_rows], both_full)
     if grid.square:
         mixed_way.pull(grad_first)
-        query_part, both_part, proj_part = mixed_way.values
-        mixed_way.values = [
-            query_part, both_part[..., :model], both_part[..., model:], proj_part
-        ]
-        mixed_way.push("y", choose_pair)
-        grad_first = tie(grad_first, *mixed_way.sent)
-    grad_first = grad_first + jnp.concatenate(grad_far)
+        way_a, way_b = fork(mixed_way)
+        way_a.push("y", choose_lanes)
+        way_b.push("x", choose_odd_lanes)
+        grad_first = tie(grad_first, way_a.sent, way_b.sent)
+    grad_first = grad_first + jnp.concatenate(grad_far).astype(jnp.float32)
     grad_norm, gain_one_grad, shift_one_grad = layer_norm_back(
         grad_first, first_normal, first_scale, gain_one
     )
@@ -1130,46 +1265,11 @@
     skip_bias_grad = jnp.sum(grad_stream.astype(jnp.float32), axis=(0, 1))
     joined_flat, stream_flat = joined.reshape(-1, 2 * model), grad_stream.reshape(flat)
     if grid.square:
-        keep, give = weight_grad(joined_flat, stream_flat, here, outer // 2, 2, 1, "skip_weight_grad")
-        skip_way = Scatter(grid, [core_rows(keep, 2, 2)], [core_rows(give, 2, 2)])
+        keep, give = tall_grad(joined_flat, stream_flat, here, outer, "skip_weight_grad")
+        skip_way = Scatter(grid, keep, give, (outer, 2, 2) + keep.shape[2:])
         grad_stream = tie(grad_stream, give)
     else:
         skip_weight_grad = outer_dot(joined_flat, stream_flat)
-    input_grad = dot_back(grad_stream, skip_full[:model])
-    if grid.square:
-        skip_way.pull(input_grad)
-        skip_way.push("x", choose_dim(2))
-        grad_stream = tie(grad_stream, *skip_way.sent)
-    skip_grad = dot_back(grad_stream, skip_full[model:])
-    if grid.square:
-        skip_way.pull(skip_grad)
-        skip_way.push("y", choose_dim(1))
-        mixed_way.pull(*skip_way.sent)
-        mixed_way.push("x", choose_pair)
-        skip_way.pull(*mixed_way.sent)
-        skip_way.push_outer()
-        mixed_way.pull(*skip_way.sent)
-        mixed_way.push_outer()
-        down_shard = columns_of_seq(grid, down_way.pull_outer().astype(jnp.bfloat16))
-        down_shard = down_shard.astype(jnp.float32)
-        hidden_shard = hidden_way.pull_outer()
-        skip_shard = columns_of_seq(grid, skip_way.pull_outer().astype(jnp.bfloat16))
-        skip_shard = skip_shard.astype(jnp.float32)
-        qkv_shard, proj_shard = mixed_shards(grid, mixed_way.pull_outer())
-    else:
-        down_shard = seq_scatter(down_grad)
-        hidden_shard = seq_scatter(hidden_grad)
-        skip_shard = seq_scatter(skip_weight_grad)
-        proj_shard = seq_scatter(proj_grad)
-        qkv_shard = seq_scatter(jnp.concatenate([query_weight_grad, both_weight_grad], axis=1))
-
-    moved = items.moved[..., None] & (grid.seq_index == half - 1)
-
-    def settle(value):
-        own, far = value[:, :own_rows], grid.shift(value[:, own_rows:], half, half - 1)
-        tail = jnp.where(moved, far, own[:, own_rows - halo_rows :])
-        return lax.dynamic_update_slice_in_dim(own, tail, own_rows - halo_rows, 1)
-
     vectors = scatter_vectors(
         grid,
         [
@@ -1183,10 +1283,67 @@
             down_bias_grad,
         ],
     )
+    input_grad = dot_back(grad_stream, skip_full[:model])
+    if grid.square:
+        skip_way.pull(input_grad)
+        skip_way.push("x", choose_dim(2))
+        grad_stream = tie(grad_stream, skip_way.sent)
+    skip_grad = dot_back(grad_stream, skip_full[model:])
+    if grid.square:
+        way_a.pull(skip_grad)
+        way_b.pull(skip_grad)
+        way_a.push("x", choose_lanes)
+        way_b.push("y", choose_lanes)
+        skip_way.pull(way_a.sent, way_b.sent)
+        skip_way.push("y", choose_dim(1))
+        way_a.pull(skip_way.sent)
+        way_b.pull(skip_way.sent)
+        mixed_way.value = jnp.concatenate([way_a.value, way_b.value], axis=1)
+        mixed_way.push("z", choose_half, 2)
+        skip_way.pull(mixed_way.sent)
+        skip_way.push("z", choose_odd, 1)
+        mixed_way.pull(skip_way.sent)
+        mixed_way.push("z", choose_half, 1)
+        skip_way.pull(mixed_way.sent)
+        skip_way.push("z", choose_half, 2)
+        vectors = vectors(skip_way.sent)
+
+        def tall_shard(way, shape):
+            total = way.mine.astype(jnp.float32) + way.got.astype(jnp.float32)
+            return unpack_lanes(total[0], *shape)
+
+        def wide_shard(way):
+            return (way.mine.astype(jnp.float32) + way.got.astype(jnp.float32))[0]
+
+        down_shard = tall_shard(down_way, down_weight.shape)
+        hidden_shard = wide_shard(hidden_way)
+        skip_shard = tall_shard(skip_way, skip_weight.shape)
+        mixed_shard = wide_shard(mixed_way)
+        qkv_shard = mixed_shard[:, : qkv_weight.shape[1]]
+        proj_shard = mixed_shard[:, qkv_weight.shape[1] :]
+    else:
+        down_shard = seq_scatter(down_grad)
+        hidden_shard = seq_scatter(hidden_grad)
+        skip_shard = seq_scatter(skip_weight_grad)
+        proj_shard = seq_scatter(proj_grad)
+        qkv_shard = seq_scatter(jnp.concatenate([query_weight_grad, both_weight_grad], axis=1))
+        vectors = vectors()
+
+    moved = items.moved[..., None] & (grid.seq_index == half - 1)
+    results = [output, input_grad, skip_grad]
+    tails = jnp.stack([value[:, own_rows:].astype(jnp.float32) for value in results])
+    tails = grid.shift(tails, half, half - 1)
+
+    def settle(place):
+        own = results[place][:, :own_rows]
+        tail = own[:, own_rows - halo_rows :]
+        tail = jnp.where(moved, tails[place].astype(own.dtype), tail)
+        return lax.dynamic_update_slice_in_dim(own, tail, own_rows - halo_rows, 1)
+
     return (
-        settle(output),
-        settle(input_grad),
-        settle(skip_grad),
+        settle(0),
+        settle(1),
+        settle(2),
         skip_shard,
         vectors[0],
         vectors[1],

time: 1070 us -> 909 us (0.85)
  starting transfers between devices: 180 us -> 72.2 us
  local copies, waits for them, and re-layouts: 93.4 us -> 52 us
  waiting for transfers between devices: 243 us -> 217 us
  between operations: 2.44 us -> 15.9 us
  matrix products: 90.9 us -> 78.2 us
  Pallas kernels: 378 us -> 389 us
    ppermute x80 -> x63, starting transfers between devices: 169 us -> 69.9 us  [send(): return lax.ppermute(value, ('batch', 'seq'), pairs)]
    ppermute x80 -> x63, waiting for transfers between devices: 242 us -> 217 us  [send(): return lax.ppermute(value, ('batch', 'seq'), pairs)]
    dot_general x6, matrix products: 52 us -> 38.5 us  [dot_back(): lax.dot_general(left_side, right_side, (((2,), (1,)), ((), ())), preferre...]
    pallas_call x6 -> x4, Pallas kernels: 90.2 us -> 101 us  [the longest x2 40.8 us: tall_grad(): pl.pallas_call(lambda *refs: tall_grad_kernel(groups, *refs), grid_spec=p...]
    convert_element_type x11 -> x18, other arithmetic: 27.1 us -> 33.5 us  [add_low(): (mine.astype(jnp.float32) + other.astype(jnp.float32)).astype(jnp.bfloat16)]
  transfers between devices with their start and end apart: 86 -> 66, of which waited for: 21 -> 22; matrix products, arithmetic and copies ran while one was open for 21% -> 20% of each run, Pallas kernels for 22% -> 28%
where the time goes in v2:
time: 909 us; the launch traced here: 898 us
  Pallas kernels  389 us (43%)
  waiting for transfers between devices  217 us (24%)
  matrix products  78.2 us (9%)
  other arithmetic  72.9 us (8%)
  starting transfers between devices  72.2 us (8%)
  local copies, waits for them, and re-layouts  52 us (6%)
  between operations  15.9 us (2%)
    ppermute x63, waiting for transfers between devices, send(): return lax.ppermute(value, ('batch', 'seq'), pairs)  217 us
    pallas_call x2, Pallas kernels, attend_back(): pl.pallas_call(attend_back_kernel, grid=(1,), in_specs=[wide, pl.BlockSpe...  100 us
    pallas_call x1, Pallas kernels, middle_block(): pl.pallas_call(middle_kernel, grid=(blocks, steps), in_specs=[by_rows, by...  83.7 us
    ppermute x63, starting transfers between devices, send(): return lax.ppermute(value, ('batch', 'seq'), pairs)  69.9 us
    pallas_call x2, Pallas kernels, attend(): pl.pallas_call(attend_kernel, grid=(1,), in_specs=[wide, pl.BlockSpec((1,...  66.1 us
    pallas_call x2, Pallas kernels, tall_grad(): pl.pallas_call(lambda *refs: tall_grad_kernel(groups, *refs), grid_spec=p...  40.8 us
    dot_general x5, matrix products, dot_last(): lax.dot_general(left_side, right_side, (((2,), (0,)), ((), ())), preferre...  39.7 us
    pallas_call x1, Pallas kernels, mixed_grad(): pl.pallas_call(lambda *refs: mixed_grad_kernel(outer, *refs), grid_spec=p...  39.5 us
  transfers between devices with their start and end apart: 66, of which 22 were waited for; matrix products, arithmetic and copies ran while one was open for 20% of the time, Pallas kernels for 28%

profile of v2, /device:TPU:0, one launch (start us, length us, event | category | flops | bytes accessed | tf_op | source)
XLA Modules:
  0.0 897.8 jit_solution(3772469843880132392)
XLA Ops:
  9.3 3.1 collective-permute-start
  12.4 2.6 collective-permute-start.1
  27.7 2.9 collective-permute-start.3
  30.7 3.7 collective-permute-start.11
  36.8 13.1 %collective-permute-done.11 = bf16[144,1152]{1,0:T(8,128)(2,1)S(1)} collective-permute-done((bf16[144,1152]{1,0:T(8,128)(2,1)S(1)}, bf16[144,1152]{1,0:T(8,128)(2,1)S(1)}, u32[]{:S(2)}, u32[]{:S(2)}) %collective-permute-start.11) | collective-permute-done | bytes 331808 | tf_op jit(solution)/shard_map/ppermute | solution.py:631
  52.2 8.3 maximum_maximum_fusion
  61.2 5.7 collective-permute-done.12
  71.5 7.4 join_skip.1
  79.0 10.4 %fusion.45 = (f32[2,544]{1,0:T(2,128)S(1)}, f32[2,544,1152]{2,1,0:T(8,128)S(1)}) fusion(f32[1152]{0:T(1024)S(1)} %reshape.366, bf16[2,544,2304]{2,1,0:T(8,128)(2,1)} %maximum_maximum_fusion, bf16[2304,1152]{1,0:T(8,128)(2,1)} %join_skip.1), kind=kOutput, calls=%fused_computation.227 | convolution fusion | flops 5778062336 | bytes 15344384 | tf_op jit(solution)/shard_map/dot_general | solution.py:581
  89.4 3.2 collective-permute-start.17
  94.8 13.2 %collective-permute-done.17 = bf16[144,1152]{1,0:T(8,128)(2,1)S(1)} collective-permute-done((bf16[144,1152]{1,0:T(8,128)(2,1)S(1)}, bf16[144,1152]{1,0:T(8,128)(2,1)S(1)}, u32[]{:S(2)}, u32[]{:S(2)}) %collective-permute-start.17) | collective-permute-done | bytes 331808 | tf_op jit(solution)/shard_map/ppermute | solution.py:631
  108.1 2.9 collective-permute-start.19
  113.7 16.0 %collective-permute-done.19 = bf16[1296,128]{1,0:T(8,128)(2,1)S(1)} collective-permute-done((bf16[1296,128]{1,0:T(8,128)(2,1)S(1)}, bf16[1296,128]{1,0:T(8,128)(2,1)S(1)}, u32[]{:S(2)}, u32[]{:S(2)}) %collective-permute-start.19) | collective-permute-done | bytes 331808 | tf_op jit(solution)/shard_map/ppermute | solution.py:631
  136.3 11.4 %collective-permute-done.20 = bf16[2592,128]{1,0:T(8,128)(2,1)S(1)} collective-permute-done((bf16[2592,128]{1,0:T(8,128)(2,1)S(1)}, bf16[2592,128]{1,0:T(8,128)(2,1)S(1)}, u32[]{:S(2)}, u32[]{:S(2)}) %collective-permute-start.20) | collective-permute-done | bytes 663584 | tf_op jit(solution)/shard_map/ppermute | solution.py:631
  147.7 2.4 collective-permute-start.25
  151.0 9.3 %collective-permute-done.15.refs_5_ = bf16[576,1152]{1,0:T(8,128)(2,1)} collective-permute-done((bf16[576,1152]{1,0:T(8,128)(2,1)}, bf16[576,1152]{1,0:T(8,128)(2,1)}, u32[]{:S(2)}, u32[]{:S(2)}) %collective-permute-start.15) | collective-permute-done | bytes 1327136 | tf_op jit(solution)/shard_map/ppermute | solution.py:631
  166.4 3.2 pad_add_fusion.4.refs_0_
  172.5 9.9 %join_mixed.1 = (bf16[1152,1152]{1,0:T(8,128)(2,1)}, bf16[1152,2304]{1,0:T(8,128)(2,1)}, bf16[1152,1152]{1,0:T(8,128)(2,1)}) custom-call(s32[4]{0:T(128)} %pad_add_fusion.4.refs_0_, s32[8]{0:T(128)} %stack.215.refs_1_, bf16[576,1152]{1,0:T(8,128)(2,1)} %constant_dynamic-update-slice_fusion.7.refs_2_, bf16[576,1152]{1,0:T(8,128)(2,1)} %collective-permute-done.13.refs_3_, ...), custom_call_target="tpu_custom_call" | custom-call | bytes 21233664 | tf_op jit(solution)/shard_map/join_mixed/pallas_call | solution.py:715
  183.6 9.0 %collective-permute-done.30.refs_4_ = bf16[5184,128]{1,0:T(8,128)(2,1)} collective-permute-done((bf16[5184,128]{1,0:T(8,128)(2,1)}, bf16[5184,128]{1,0:T(8,128)(2,1)}, u32[]{:S(2)}, u32[]{:S(2)}) %collective-permute-start.30) | collective-permute-done | bytes 1327136 | tf_op jit(solution)/shard_map/ppermute | solution.py:631
  192.6 11.6 %convolution_convert_fusion.own_ref = bf16[2,544,2304]{2,1,0:T(8,128)(2,1)} fusion(bf16[2,544,1152]{2,1,0:T(8,128)(2,1)S(1)} %add_convert_fusion.7, bf16[1152,2304]{1,0:T(8,128)(2,1)} %get-tuple-element.95), kind=kOutput, calls=%fused_computation.3 | convolution fusion | flops 5778063360 | bytes 12828672 | tf_op jit(solution)/shard_map/dot_general | solution.py:581
  204.2 5.0 convolution_convert_fusion.3.q_ref
  209.2 24.5 %collective-permute-done.26.refs_2_ = bf16[576,1152]{1,0:T(8,128)(2,1)} collective-permute-done((bf16[576,1152]{1,0:T(8,128)(2,1)}, bf16[576,1152]{1,0:T(8,128)(2,1)}, u32[]{:S(2)}, u32[]{:S(2)}) %collective-permute-start.26) | collective-permute-done | bytes 1327136 | tf_op jit(solution)/shard_map/ppermute | solution.py:631
  234.8 4.7 fusion.9.far_ref
  239.5 33.2 %attend.2 = (bf16[2,544,1152]{2,1,0:T(8,128)(2,1)}, f32[2,16,544]{2,1,0:T(8,128)}) custom-call(bf16[2,544,1152]{2,1,0:T(8,128)(2,1)} %convolution_convert_fusion.3.q_ref, bf16[2,544,2304]{2,1,0:T(8,128)(2,1)} %convolution_convert_fusion.own_ref, bf16[1,544,2304]{2,1,0:T(8,128)(2,1)} %fusion.9.far_ref, s32[2,1,544]{2,1,0:T(1,128)} %add_select_fusion.qid_ref, ...), custom_call_target="tpu_custom_call" | custom-call | flops 4848615424 | bytes 7520256 | tf_op jit(solution)/shard_map/attend/pallas_call | solution.py:101
  276.1 8.1 fusion.10.far_ref
  284.2 32.9 %attend.3 = (bf16[2,544,1152]{2,1,0:T(8,128)(2,1)}, f32[2,16,544]{2,1,0:T(8,128)}) custom-call(bf16[2,544,1152]{2,1,0:T(8,128)(2,1)} %convolution_convert_fusion.3.q_ref, bf16[2,544,2304]{2,1,0:T(8,128)(2,1)} %convolution_convert_fusion.own_ref, bf16[1,544,2304]{2,1,0:T(8,128)(2,1)} %fusion.10.far_ref, ...), custom_call_target="tpu_custom_call", output_to_operand_aliasing={{0}: (5, {}), {1}: (6, {})} | custom-call | flops 4848615424 | bytes 7520256 | tf_op jit(solution)/shard_map/attend/pallas_call | solution.py:101
  324.6 11.4 %join_down.1 = bf16[4608,1152]{1,0:T(8,128)(2,1)} custom-call(s32[4]{0:T(128)} %pad_add_fusion.4.refs_0_, s32[8]{0:T(128)} %stack.215.refs_1_, bf16[5184,128]{1,0:T(8,128)(2,1)} %constant_dynamic-update-slice_fusion.12.refs_2_, bf16[5184,128]{1,0:T(8,128)(2,1)} %collective-permute-done.29.refs_3_, bf16[5184,128]{1,0:T(8,128)(2,1)} %collective-permute-done.30.refs_4_, ...), custom_call_target="tpu_custom_call" | custom-call | bytes 21233664 | tf_op jit(solution)/shard_map/join_down/pallas_call | solution.py:715
  336.0 8.9 place_blocks.1
  344.9 83.7 %middle_block.1 = (bf16[1088,1152]{1,0:T(8,128)(2,1)}, bf16[1088,1152]{1,0:T(8,128)(2,1)}, bf16[1088,4608]{1,0:T(8,128)(2,1)}, bf16[1088,4608]{1,0:T(8,128)(2,1)...) custom-call(f32[1088,1152]{1,0:T(8,128)} %bitcast.234, ...), custom_call_target="tpu_custom_call" | custom-call | flops 51980009472 | bytes 135069696 | tf_op jit(solution)/shard_map/middle_block/pallas_call | solution.py:488
  428.6 25.7 %down_weight_grad.1 = (bf16[4,4,1296,128]{3,2,1,0:T(8,128)(2,1)}, bf16[4,4,1296,128]{3,2,1,0:T(8,128)(2,1)}) custom-call(s32[1]{0:T(128)} %bitcast.71.refs_0_, bf16[1088,4608]{1,0:T(8,128)(2,1)} %get-tuple-element.108.refs_1_, bf16[1088,1152]{1,0:T(8,128)(2,1)} %broadcast_select_fusion.refs_2_), custom_call_target="tpu_custom_call" | custom-call | flops 11551113216 | bytes 20643840 | tf_op jit(solution)/shard_map/down_weight_grad/pallas_call | solution.py:299
  454.7 21.0 %hidden_weight_grad.1 = (bf16[576,4608]{1,0:T(8,128)(2,1)}, bf16[576,4608]{1,0:T(8,128)(2,1)}) custom-call(s32[1]{0:T(128)} %bitcast.71.refs_0_, bf16[1088,1152]{1,0:T(8,128)(2,1)} %get-tuple-element.110.refs_1_, bf16[1088,4608]{1,0:T(8,128)(2,1)} %get-tuple-element.111.refs_2_), custom_call_target="tpu_custom_call" | custom-call | flops 11551113216 | bytes 13123584 | tf_op jit(solution)/shard_map/hidden_weight_grad/pallas_call | solution.py:256
  477.8 5.5 add_convert_fusion.2
  486.9 5.4 add_convert_fusion.1
  492.3 2.8 constant_dynamic-slice_fusion.18
  497.8 50.1 %attend_back.2 = (bf16[2,544,1152]{2,1,0:T(8,128)(2,1)}, bf16[2,1088,2304]{2,1,0:T(8,128)(2,1)}) custom-call(bf16[2,544,1152]{2,1,0:T(8,128)(2,1)} %convolution_convert_fusion.3.q_ref, bf16[2,544,2304]{2,1,0:T(8,128)(2,1)} %convolution_convert_fusion.own_ref, bf16[1,544,2304]{2,1,0:T(8,128)(2,1)} %fusion.9.far_ref, ...), custom_call_target="tpu_custom_call" | custom-call | flops 12121538560 | bytes 15040512 | tf_op jit(solution)/shard_map/attend_back/pallas_call | solution.py:185
  548.0 2.4 add_convert_fusion.5
  552.6 2.7 collective-permute-done.43
  555.3 2.5 add_convert_fusion.4
  559.3 6.2 fusion.11
  567.2 50.4 %attend_back.3 = (bf16[2,544,1152]{2,1,0:T(8,128)(2,1)}, bf16[2,1088,2304]{2,1,0:T(8,128)(2,1)}) custom-call(bf16[2,544,1152]{2,1,0:T(8,128)(2,1)} %convolution_convert_fusion.3.q_ref, bf16[2,544,2304]{2,1,0:T(8,128)(2,1)} %convolution_convert_fusion.own_ref, bf16[1,544,2304]{2,1,0:T(8,128)(2,1)} %fusion.10.far_ref, ...), custom_call_target="tpu_custom_call", output_to_operand_aliasing={{0}: (8, {}), {1}: (9, {})} | custom-call | flops 12121538560 | bytes 15040512 | tf_op jit(solution)/shard_map/attend_back/pallas_call | solution.py:185
  622.0 8.2 fusion.12
  630.2 39.5 %mixed_weight_grad.1 = (bf16[576,4608]{1,0:T(8,128)(2,1)}, bf16[576,4608]{1,0:T(8,128)(2,1)}) custom-call(s32[1]{0:T(128)} %bitcast.71.refs_0_, bf16[1088,1152]{1,0:T(8,128)(2,1)} %bitcast.243, bf16[544,1152]{1,0:T(8,128)(2,1)} %bitcast.270, bf16[544,1152]{1,0:T(8,128)(2,1)} %bitcast.29.refs_3_, bf16[1088,1152]{1,0:T(8,128)(2,1)} %bitcast.276, ...), custom_call_target="tpu_custom_call" | custom-call | flops 17326669824 | bytes 35684352 | tf_op jit(solution)/shard_map/mixed_weight_grad/pallas_call | solution.py:371
  669.8 2.4 collective-permute-start.47
  674.0 14.1 %collective-permute-done.47 = bf16[2,144,1152]{2,1,0:T(8,128)(2,1)S(1)} collective-permute-done((bf16[2,144,1152]{2,1,0:T(8,128)(2,1)S(1)}, bf16[2,144,1152]{2,1,0:T(8,128)(2,1)S(1)}, u32[]{:S(2)}, u32[]{:S(2)}) %collective-permute-start.47) | collective-permute-done | bytes 663584 | tf_op jit(solution)/shard_map/ppermute | solution.py:631
  688.2 2.5 collective-permute-start.63
  690.7 9.3 %collective-permute-done.64 = bf16[1,1296,128]{2,1,0:T(8,128)(2,1)S(1)} collective-permute-done((bf16[1,1296,128]{2,1,0:T(8,128)(2,1)S(1)}, bf16[1,1296,128]{2,1,0:T(8,128)(2,1)S(1)}, u32[]{:S(2)}, u32[]{:S(2)}) %collective-permute-start.64) | collective-permute-done | bytes 331808 | tf_op jit(solution)/shard_map/ppermute | solution.py:631
  700.8 5.0 collective-permute-done.63
  706.8 10.3 %fusion = f32[2,544,1152]{2,1,0:T(8,128)S(1)} fusion(bf16[1152,2304]{1,0:T(8,128)(2,1)} %get-tuple-element.95, bf16[2,1088,2304]{2,1,0:T(8,128)(2,1)} %get-tuple-element.136), kind=kOutput, calls=%fused_computation.4 | convolution fusion | flops 5775556608 | bytes 15335424 | tf_op jit(solution)/shard_map/dot_general | solution.py:587
  717.1 3.8 convolution_add_fusion
  721.0 5.4 add_convert_fusion
  731.2 3.2 multiply_reduce_fusion
  734.5 4.6 convert_reduce_fusion
  739.0 15.0 %skip_weight_grad.1 = (bf16[4,4,648,128]{3,2,1,0:T(8,128)(2,1)}, bf16[4,4,648,128]{3,2,1,0:T(8,128)(2,1)}) custom-call(s32[1]{0:T(128)} %bitcast.71.refs_0_, bf16[1088,2304]{1,0:T(8,128)(2,1)} %bitcast.250, bf16[1088,1152]{1,0:T(8,128)(2,1)} %bitcast.258), custom_call_target="tpu_custom_call" | custom-call | flops 5775556608 | bytes 10321920 | tf_op jit(solution)/shard_map/skip_weight_grad/pallas_call | solution.py:299
  757.7 6.2 fusion.14
  764.0 2.2 copy-done.4
  769.3 2.6 add_convert_fusion.3
  773.7 3.8 fusion.13
  777.5 10.7 %collective-permute-done.54 = bf16[4,72,2304]{2,1,0:T(8,128)(2,1)} collective-permute-done((bf16[4,72,2304]{2,1,0:T(8,128)(2,1)}, bf16[4,72,2304]{2,1,0:T(8,128)(2,1)}, u32[]{:S(2)}, u32[]{:S(2)}) %collective-permute-start.54) | collective-permute-done | bytes 1327136 | tf_op jit(solution)/shard_map/ppermute | solution.py:631
  796.4 24.6 %collective-permute-done.55 = bf16[4,2,648,128]{3,2,1,0:T(8,128)(2,1)S(1)} collective-permute-done((bf16[4,2,648,128]{3,2,1,0:T(8,128)(2,1)S(1)}, bf16[4,2,648,128]{3,2,1,0:T(8,128)(2,1)S(1)}, u32[]{:S(2)}, u32[]{:S(2)}) %collective-permute-start.55) | collective-permute-done | bytes 1327136 | tf_op jit(solution)/shard_map/ppermute | solution.py:631
  821.6 15.7 %collective-permute-start.58 = (bf16[4,648,128]{2,1,0:T(8,128)(2,1)S(1)}, bf16[4,648,128]{2,1,0:T(8,128)(2,1)S(1)}, u32[]{:S(2)}, u32[]{:S(2)}) collective-permute-start(bf16[4,648,128]{2,1,0:T(8,128)(2,1)S(1)} %get-tuple-element.277), channel_id=1, source_target_pairs={{0,2},{1,3},{2,0},{3,1},{4,6},{5,7},{6,4},{7,5},{8,10},{9,11},{10,... | collective-permute-start | bytes 1990664 | tf_op jit(solution)/shard_map/ppermute | solution.py:631
  839.5 12.2 %collective-permute-done.58 = bf16[4,648,128]{2,1,0:T(8,128)(2,1)S(1)} collective-permute-done((bf16[4,648,128]{2,1,0:T(8,128)(2,1)S(1)}, bf16[4,648,128]{2,1,0:T(8,128)(2,1)S(1)}, u32[]{:S(2)}, u32[]{:S(2)}) %collective-permute-start.58) | collective-permute-done | bytes 663584 | tf_op jit(solution)/shard_map/ppermute | solution.py:631
  852.0 16.9 %collective-permute-done.59 = bf16[2,144,1152]{2,1,0:T(8,128)(2,1)S(1)} collective-permute-done((bf16[2,144,1152]{2,1,0:T(8,128)(2,1)S(1)}, bf16[2,144,1152]{2,1,0:T(8,128)(2,1)S(1)}, u32[]{:S(2)}, u32[]{:S(2)}) %collective-permute-start.59) | collective-permute-done | bytes 663584 | tf_op jit(solution)/shard_map/ppermute | solution.py:631
  869.2 6.9 collective-permute-done.60
  876.2 8.9 collective-permute-done.62
  (400 shorter events, 111.8 us)
Async XLA Ops:
  7.2 879.7 %all-gather.2.cloned.1.call-start = ((), (), s32[]{:S(2)}) async-start(), calls=%async_computation | async-start | bytes 1757184 | tf_op jit(solution)/shard_map/all_gather | solution.py:963
  9.3 16.6 %collective-permute-start = (bf16[648,128]{1,0:T(8,128)(2,1)S(1)}, bf16[648,128]{1,0:T(8,128)(2,1)S(1)}, u32[]{:S(2)}, u32[]{:S(2)}) collective-permute-start(bf16[648,128]{1,0:T(8,128)(2,1)S(1)} %maximum_maximum_fusion.4), channel_id=1, source_target_pairs={{0,8},{1,9},{2,10},{3,11},{4,12},{5,13},{6,14},{7,15},{8,0},{9,1},... | collective-permute-start | bytes 497672 | tf_op jit(solution)/shard_map/ppermute | solution.py:631
  12.4 15.2 %collective-permute-start.1 = (bf16[648,128]{1,0:T(8,128)(2,1)S(1)}, bf16[648,128]{1,0:T(8,128)(2,1)S(1)}, u32[]{:S(2)}, u32[]{:S(2)}) collective-permute-start(bf16[648,128]{1,0:T(8,128)(2,1)S(1)} %maximum_maximum_fusion.4), channel_id=1, source_target_pairs={{0,16},{1,17},{2,18},{3,19},{4,20},{5,21},{6,22},{7,23},{8,24},{9,... | collective-permute-start | bytes 497672 | tf_op jit(solution)/shard_map/ppermute | solution.py:631
  15.0 12.6 %collective-permute-start.2 = (bf16[648,128]{1,0:T(8,128)(2,1)S(1)}, bf16[648,128]{1,0:T(8,128)(2,1)S(1)}, u32[]{:S(2)}, u32[]{:S(2)}) collective-permute-start(bf16[648,128]{1,0:T(8,128)(2,1)S(1)} %maximum_maximum_fusion.4), channel_id=1, source_target_pairs={{0,24},{1,25},{2,26},{3,27},{4,28},{5,29},{6,30},{7,31},{8,16},{9,... | collective-permute-start | bytes 497672 | tf_op jit(solution)/shard_map/ppermute | solution.py:631
  16.9 18.2 %collective-permute-start.5 = (bf16[3,2,24,1152]{3,2,1,0:T(8,128)(2,1)S(1)}, bf16[3,2,24,1152]{3,2,1,0:T(8,128)(2,1)}, u32[]{:S(2)}, u32[]{:S(2)}) collective-permute-start(bf16[3,2,24,1152]{3,2,1,0:T(8,128)(2,1)S(1)} %pad_maximum_fusion.7), channel_id=1, source_target_pairs={{1,2},{5,6},{9,10},{13,14},{17,18},{21,22},{25,26},{29,30}} | collective-permute-start | bytes 995336 | tf_op jit(solution)/shard_map/ppermute | solution.py:638
  27.7 23.2 %collective-permute-start.3 = (bf16[2624,128]{1,0:T(8,128)(2,1)S(1)}, bf16[2624,128]{1,0:T(8,128)(2,1)S(1)}, u32[]{:S(2)}, u32[]{:S(2)}) collective-permute-start(bf16[2624,128]{1,0:T(8,128)(2,1)S(1)} %constant_dynamic-update-slice_fusion.refs_2_), channel_id=1, source_target_pairs={{0,1},{1,0},{2,3},{3,2},{4,5},{5,4},{6,7},{7,6},{8,9},{9,8},{10,11... | collective-permute-start | bytes 2015240 | tf_op jit(solution)/shard_map/ppermute | solution.py:631
  30.5 20.4 %collective-permute-start.4 = (bf16[2624,128]{1,0:T(8,128)(2,1)S(1)}, bf16[2624,128]{1,0:T(8,128)(2,1)S(1)}, u32[]{:S(2)}, u32[]{:S(2)}) collective-permute-start(bf16[2624,128]{1,0:T(8,128)(2,1)S(1)} %constant_dynamic-update-slice_fusion.refs_2_), channel_id=1, source_target_pairs={{0,2},{1,3},{2,0},{3,1},{4,6},{5,7},{6,4},{7,5},{8,10},{9,11},{10,... | collective-permute-start | bytes 2015240 | tf_op jit(solution)/shard_map/ppermute | solution.py:631
  30.7 39.5 %collective-permute-start.7 = (bf16[2624,128]{1,0:T(8,128)(2,1)S(1)}, bf16[2624,128]{1,0:T(8,128)(2,1)}, u32[]{:S(2)}, u32[]{:S(2)}) collective-permute-start(bf16[2624,128]{1,0:T(8,128)(2,1)S(1)} %constant_dynamic-update-slice_fusion.refs_2_), channel_id=1, source_target_pairs={{0,4},{1,5},{2,6},{3,7},{4,0},{5,1},{6,2},{7,3},{8,12},{9,13},{10,... | collective-permute-start | bytes 2015240 | tf_op jit(solution)/shard_map/ppermute | solution.py:631
  30.7 19.2 %collective-permute-start.11 = (bf16[144,1152]{1,0:T(8,128)(2,1)S(1)}, bf16[144,1152]{1,0:T(8,128)(2,1)S(1)}, u32[]{:S(2)}, u32[]{:S(2)}) collective-permute-start(bf16[144,1152]{1,0:T(8,128)(2,1)S(1)} %pad_maximum_fusion.8), channel_id=1, source_target_pairs={{0,16},{1,17},{2,18},{3,19},{4,20},{5,21},{6,22},{7,23},{8,24},{9,... | collective-permute-start | bytes 995336 | tf_op jit(solution)/shard_map/ppermute | solution.py:631
  50.0 16.8 %collective-permute-start.12 = (bf16[288,1152]{1,0:T(8,128)(2,1)S(1)}, bf16[288,1152]{1,0:T(8,128)(2,1)S(1)}, u32[]{:S(2)}, u32[]{:S(2)}) collective-permute-start(bf16[288,1152]{1,0:T(8,128)(2,1)S(1)} %pad_maximum_fusion.4), channel_id=1, source_target_pairs={{0,8},{1,9},{2,10},{3,11},{4,12},{5,13},{6,14},{7,15},{8,0},{9,1},... | collective-permute-start | bytes 1990664 | tf_op jit(solution)/shard_map/ppermute | solution.py:631
  50.9 17.3 %collective-permute-start.6 = (bf16[2624,128]{1,0:T(8,128)(2,1)S(1)}, bf16[2624,128]{1,0:T(8,128)(2,1)}, u32[]{:S(2)}, u32[]{:S(2)}) collective-permute-start(bf16[2624,128]{1,0:T(8,128)(2,1)S(1)} %collective-permute-done.3.refs_3_), channel_id=1, source_target_pairs={{0,2},{1,3},{2,0},{3,1},{4,6},{5,7},{6,4},{7,5},{8,10},{9,11},{10,... | collective-permute-start | bytes 2015240 | tf_op jit(solution)/shard_map/ppermute | solution.py:631
  60.6 10.5 %collective-permute-start.8 = (bf16[2624,128]{1,0:T(8,128)(2,1)S(1)}, bf16[2624,128]{1,0:T(8,128)(2,1)}, u32[]{:S(2)}, u32[]{:S(2)}) collective-permute-start(bf16[2624,128]{1,0:T(8,128)(2,1)S(1)} %collective-permute-done.3.refs_3_), channel_id=1, source_target_pairs={{0,4},{1,5},{2,6},{3,7},{4,0},{5,1},{6,2},{7,3},{8,12},{9,13},{10,... | collective-permute-start | bytes 2015240 | tf_op jit(solution)/shard_map/ppermute | solution.py:631
  60.7 10.6 %collective-permute-start.9 = (bf16[2624,128]{1,0:T(8,128)(2,1)S(1)}, bf16[2624,128]{1,0:T(8,128)(2,1)}, u32[]{:S(2)}, u32[]{:S(2)}) collective-permute-start(bf16[2624,128]{1,0:T(8,128)(2,1)S(1)} %collective-permute-done.4.refs_4_), channel_id=1, source_target_pairs={{0,4},{1,5},{2,6},{3,7},{4,0},{5,1},{6,2},{7,3},{8,12},{9,13},{10,... | collective-permute-start | bytes 2015240 | tf_op jit(solution)/shard_map/ppermute | solution.py:631
  67.7 44.5 %collective-permute-start.13 = (bf16[576,1152]{1,0:T(8,128)(2,1)}, bf16[576,1152]{1,0:T(8,128)(2,1)}, u32[]{:S(2)}, u32[]{:S(2)}) collective-permute-start(bf16[576,1152]{1,0:T(8,128)(2,1)} %constant_dynamic-update-slice_fusion.7.refs_2_), channel_id=1, source_target_pairs={{0,1},{1,0},{2,3},{3,2},{4,5},{5,4},{6,7},{7,6},{8,9},{9,8},{10,11... | collective-permute-start | bytes 3981320 | tf_op jit(solution)/shard_map/ppermute | solution.py:631
  70.2 80.7 %collective-permute-start.14 = (bf16[576,1152]{1,0:T(8,128)(2,1)}, bf16[576,1152]{1,0:T(8,128)(2,1)}, u32[]{:S(2)}, u32[]{:S(2)}) collective-permute-start(bf16[576,1152]{1,0:T(8,128)(2,1)} %constant_dynamic-update-slice_fusion.7.refs_2_), channel_id=1, source_target_pairs={{0,2},{1,3},{2,0},{3,1},{4,6},{5,7},{6,4},{7,5},{8,10},{9,11},{10,... | collective-permute-start | bytes 3981320 | tf_op jit(solution)/shard_map/ppermute | solution.py:631
  71.1 89.8 %collective-permute-start.21 = (bf16[576,1152]{1,0:T(8,128)(2,1)}, bf16[576,1152]{1,0:T(8,128)(2,1)}, u32[]{:S(2)}, u32[]{:S(2)}) collective-permute-start(bf16[576,1152]{1,0:T(8,128)(2,1)} %constant_dynamic-update-slice_fusion.7.refs_2_), channel_id=1, source_target_pairs={{0,4},{1,5},{2,6},{3,7},{4,0},{5,1},{6,2},{7,3},{8,12},{9,13},{10,... | collective-permute-start | bytes 3981320 | tf_op jit(solution)/shard_map/ppermute | solution.py:631
  89.4 18.6 %collective-permute-start.17 = (bf16[144,1152]{1,0:T(8,128)(2,1)S(1)}, bf16[144,1152]{1,0:T(8,128)(2,1)S(1)}, u32[]{:S(2)}, u32[]{:S(2)}) collective-permute-start(bf16[144,1152]{1,0:T(8,128)(2,1)S(1)} %copy-done.13), channel_id=1, source_target_pairs={{0,16},{1,17},{2,18},{3,19},{4,20},{5,21},{6,22},{7,23},{8,24},{9,... | collective-permute-start | bytes 995336 | tf_op jit(solution)/shard_map/ppermute | solution.py:631
  108.0 23.8 %collective-permute-start.18 = (bf16[288,1152]{1,0:T(8,128)(2,1)S(1)}, bf16[288,1152]{1,0:T(8,128)(2,1)S(1)}, u32[]{:S(2)}, u32[]{:S(2)}) collective-permute-start(bf16[288,1152]{1,0:T(8,128)(2,1)S(1)} %constant_dynamic-update-slice_fusion.10), channel_id=1, source_target_pairs={{0,8},{1,9},{2,10},{3,11},{4,12},{5,13},{6,14},{7,15},{8,0},{9,1},... | collective-permute-start | bytes 1990664 | tf_op jit(solution)/shard_map/ppermute | solution.py:631
  108.1 21.6 %collective-permute-start.19 = (bf16[1296,128]{1,0:T(8,128)(2,1)S(1)}, bf16[1296,128]{1,0:T(8,128)(2,1)S(1)}, u32[]{:S(2)}, u32[]{:S(2)}) collective-permute-start(bf16[1296,128]{1,0:T(8,128)(2,1)S(1)} %maximum_maximum_fusion.3), channel_id=1, source_target_pairs={{0,16},{1,17},{2,18},{3,19},{4,20},{5,21},{6,22},{7,23},{8,24},{9,... | collective-permute-start | bytes 995336 | tf_op jit(solution)/shard_map/ppermute | solution.py:631
  112.2 48.1 %collective-permute-start.16 = (bf16[1,544,1152]{2,1,0:T(8,128)(2,1)S(1)}, bf16[1,544,1152]{2,1,0:T(8,128)(2,1)S(1)}, u32[]{:S(2)}, u32[]{:S(2)}) collective-permute-start(bf16[1,544,1152]{2,1,0:T(8,128)(2,1)S(1)} %get-tuple-element.269), channel_id=1, source_target_pairs={{0,1},{1,0},{2,3},{3,2},{4,5},{5,4},{6,7},{7,6},{8,9},{9,8},{10,11... | collective-permute-start | bytes 3760136 | tf_op jit(solution)/shard_map/ppermute | solution.py:631
  129.7 30.6 %collective-permute-start.15 = (bf16[576,1152]{1,0:T(8,128)(2,1)}, bf16[576,1152]{1,0:T(8,128)(2,1)}, u32[]{:S(2)}, u32[]{:S(2)}) collective-permute-start(bf16[576,1152]{1,0:T(8,128)(2,1)} %collective-permute-done.13.refs_3_), channel_id=1, source_target_pairs={{0,2},{1,3},{2,0},{3,1},{4,6},{5,7},{6,4},{7,5},{8,10},{9,11},{10,... | collective-permute-start | bytes 3981320 | tf_op jit(solution)/shard_map/ppermute | solution.py:631
  131.8 15.8 %collective-permute-start.20 = (bf16[2592,128]{1,0:T(8,128)(2,1)S(1)}, bf16[2592,128]{1,0:T(8,128)(2,1)S(1)}, u32[]{:S(2)}, u32[]{:S(2)}) collective-permute-start(bf16[2592,128]{1,0:T(8,128)(2,1)S(1)} %pad_maximum_fusion.5), channel_id=1, source_target_pairs={{0,8},{1,9},{2,10},{3,11},{4,12},{5,13},{6,14},{7,15},{8,0},{9,1},... | collective-permute-start | bytes 1990664 | tf_op jit(solution)/shard_map/ppermute | solution.py:631
  147.7 34.8 %collective-permute-start.25 = (bf16[1,544,1152]{2,1,0:T(8,128)(2,1)}, bf16[1,544,1152]{2,1,0:T(8,128)(2,1)}, u32[]{:S(2)}, u32[]{:S(2)}) collective-permute-start(bf16[1,544,1152]{2,1,0:T(8,128)(2,1)} %get-tuple-element.268), channel_id=1, source_target_pairs={{0,1},{1,0},{2,3},{3,2},{4,5},{5,4},{6,7},{7,6},{8,9},{9,8},{10,11... | collective-permute-start | bytes 3760136 | tf_op jit(solution)/shard_map/ppermute | solution.py:631
  151.0 19.3 %collective-permute-start.22 = (bf16[576,1152]{1,0:T(8,128)(2,1)}, bf16[576,1152]{1,0:T(8,128)(2,1)}, u32[]{:S(2)}, u32[]{:S(2)}) collective-permute-start(bf16[576,1152]{1,0:T(8,128)(2,1)} %collective-permute-done.13.refs_3_), channel_id=1, source_target_pairs={{0,4},{1,5},{2,6},{3,7},{4,0},{5,1},{6,2},{7,3},{8,12},{9,13},{10,... | collective-permute-start | bytes 3981320 | tf_op jit(solution)/shard_map/ppermute | solution.py:631
  160.3 10.9 %collective-permute-start.23 = (bf16[576,1152]{1,0:T(8,128)(2,1)}, bf16[576,1152]{1,0:T(8,128)(2,1)}, u32[]{:S(2)}, u32[]{:S(2)}) collective-permute-start(bf16[576,1152]{1,0:T(8,128)(2,1)} %collective-permute-done.14.refs_4_), channel_id=1, source_target_pairs={{0,4},{1,5},{2,6},{3,7},{4,0},{5,1},{6,2},{7,3},{8,12},{9,13},{10,... | collective-permute-start | bytes 3981320 | tf_op jit(solution)/shard_map/ppermute | solution.py:631
  160.3 32.3 %collective-permute-start.30 = (bf16[5184,128]{1,0:T(8,128)(2,1)}, bf16[5184,128]{1,0:T(8,128)(2,1)}, u32[]{:S(2)}, u32[]{:S(2)}) collective-permute-start(bf16[5184,128]{1,0:T(8,128)(2,1)} %constant_dynamic-update-slice_fusion.12.refs_2_), channel_id=1, source_target_pairs={{0,2},{1,3},{2,0},{3,1},{4,6},{5,7},{6,4},{7,5},{8,10},{9,11},{10,... | collective-permute-start | bytes 3981320 | tf_op jit(solution)/shard_map/ppermute | solution.py:631
  160.9 10.5 %collective-permute-start.24 = (bf16[576,1152]{1,0:T(8,128)(2,1)}, bf16[576,1152]{1,0:T(8,128)(2,1)}, u32[]{:S(2)}, u32[]{:S(2)}) collective-permute-start(bf16[576,1152]{1,0:T(8,128)(2,1)} %collective-permute-done.15.refs_5_), channel_id=1, source_target_pairs={{0,4},{1,5},{2,6},{3,7},{4,0},{5,1},{6,2},{7,3},{8,12},{9,13},{10,... | collective-permute-start | bytes 3981320 | tf_op jit(solution)/shard_map/ppermute | solution.py:631
  170.3 102.4 %collective-permute-start.29 = (bf16[5184,128]{1,0:T(8,128)(2,1)}, bf16[5184,128]{1,0:T(8,128)(2,1)}, u32[]{:S(2)}, u32[]{:S(2)}) collective-permute-start(bf16[5184,128]{1,0:T(8,128)(2,1)} %constant_dynamic-update-slice_fusion.12.refs_2_), channel_id=1, source_target_pairs={{0,1},{1,0},{2,3},{3,2},{4,5},{5,4},{6,7},{7,6},{8,9},{9,8},{10,11... | collective-permute-start | bytes 3981320 | tf_op jit(solution)/shard_map/ppermute | solution.py:631
  171.2 146.6 %collective-permute-start.36 = (bf16[5184,128]{1,0:T(8,128)(2,1)}, bf16[5184,128]{1,0:T(8,128)(2,1)}, u32[]{:S(2)}, u32[]{:S(2)}) collective-permute-start(bf16[5184,128]{1,0:T(8,128)(2,1)} %constant_dynamic-update-slice_fusion.12.refs_2_), channel_id=1, source_target_pairs={{0,4},{1,5},{2,6},{3,7},{4,0},{5,1},{6,2},{7,3},{8,12},{9,13},{10,... | collective-permute-start | bytes 3981320 | tf_op jit(solution)/shard_map/ppermute | solution.py:631
  171.3 62.3 %collective-permute-start.26 = (bf16[576,1152]{1,0:T(8,128)(2,1)}, bf16[576,1152]{1,0:T(8,128)(2,1)}, u32[]{:S(2)}, u32[]{:S(2)}) collective-permute-start(bf16[576,1152]{1,0:T(8,128)(2,1)} %pad_maximum_fusion.1.refs_1_), channel_id=1, source_target_pairs={{0,1},{1,0},{2,3},{3,2},{4,5},{5,4},{6,7},{7,6},{8,9},{9,8},{10,11... | collective-permute-start | bytes 3981320 | tf_op jit(solution)/shard_map/ppermute | solution.py:631
  182.5 51.2 %collective-permute-start.27 = (bf16[576,1152]{1,0:T(8,128)(2,1)}, bf16[576,1152]{1,0:T(8,128)(2,1)}, u32[]{:S(2)}, u32[]{:S(2)}) collective-permute-start(bf16[576,1152]{1,0:T(8,128)(2,1)} %pad_maximum_fusion.1.refs_1_), channel_id=1, source_target_pairs={{0,2},{1,3},{2,0},{3,1},{4,6},{5,7},{6,4},{7,5},{8,10},{9,11},{10,... | collective-permute-start | bytes 3981320 | tf_op jit(solution)/shard_map/ppermute | solution.py:631
  192.6 125.2 %collective-permute-start.38 = (bf16[5184,128]{1,0:T(8,128)(2,1)}, bf16[5184,128]{1,0:T(8,128)(2,1)}, u32[]{:S(2)}, u32[]{:S(2)}) collective-permute-start(bf16[5184,128]{1,0:T(8,128)(2,1)} %collective-permute-done.30.refs_4_), channel_id=1, source_target_pairs={{0,4},{1,5},{2,6},{3,7},{4,0},{5,1},{6,2},{7,3},{8,12},{9,13},{10,... | collective-permute-start | bytes 3981320 | tf_op jit(solution)/shard_map/ppermute | solution.py:631
  233.7 41.8 %collective-permute-start.28 = (bf16[576,1152]{1,0:T(8,128)(2,1)}, bf16[576,1152]{1,0:T(8,128)(2,1)}, u32[]{:S(2)}, u32[]{:S(2)}) collective-permute-start(bf16[576,1152]{1,0:T(8,128)(2,1)} %collective-permute-done.26.refs_2_), channel_id=1, source_target_pairs={{0,2},{1,3},{2,0},{3,1},{4,6},{5,7},{6,4},{7,5},{8,10},{9,11},{10,... | collective-permute-start | bytes 3981320 | tf_op jit(solution)/shard_map/ppermute | solution.py:631
  272.7 44.4 %collective-permute-start.35 = (bf16[5184,128]{1,0:T(8,128)(2,1)}, bf16[5184,128]{1,0:T(8,128)(2,1)}, u32[]{:S(2)}, u32[]{:S(2)}) collective-permute-start(bf16[5184,128]{1,0:T(8,128)(2,1)} %collective-permute-done.29.refs_3_), channel_id=1, source_target_pairs={{0,2},{1,3},{2,0},{3,1},{4,6},{5,7},{6,4},{7,5},{8,10},{9,11},{10,... | collective-permute-start | bytes 3981320 | tf_op jit(solution)/shard_map/ppermute | solution.py:631
  273.6 44.6 %collective-permute-start.37 = (bf16[5184,128]{1,0:T(8,128)(2,1)}, bf16[5184,128]{1,0:T(8,128)(2,1)}, u32[]{:S(2)}, u32[]{:S(2)}) collective-permute-start(bf16[5184,128]{1,0:T(8,128)(2,1)} %collective-permute-done.29.refs_3_), channel_id=1, source_target_pairs={{0,4},{1,5},{2,6},{3,7},{4,0},{5,1},{6,2},{7,3},{8,12},{9,13},{10,... | collective-permute-start | bytes 3981320 | tf_op jit(solution)/shard_map/ppermute | solution.py:631
  275.5 60.4 %collective-permute-start.31 = (bf16[576,1152]{1,0:T(8,128)(2,1)S(1)}, bf16[576,1152]{1,0:T(8,128)(2,1)}, u32[]{:S(2)}, u32[]{:S(2)}) collective-permute-start(bf16[576,1152]{1,0:T(8,128)(2,1)S(1)} %copy-done.6), channel_id=1, source_target_pairs={{0,4},{1,5},{2,6},{3,7},{4,0},{5,1},{6,2},{7,3},{8,12},{9,13},{10,... | collective-permute-start | bytes 3981320 | tf_op jit(solution)/shard_map/ppermute | solution.py:631
  317.1 18.9 %collective-permute-start.32 = (bf16[576,1152]{1,0:T(8,128)(2,1)}, bf16[576,1152]{1,0:T(8,128)(2,1)}, u32[]{:S(2)}, u32[]{:S(2)}) collective-permute-start(bf16[576,1152]{1,0:T(8,128)(2,1)} %collective-permute-done.26.refs_2_), channel_id=1, source_target_pairs={{0,4},{1,5},{2,6},{3,7},{4,0},{5,1},{6,2},{7,3},{8,12},{9,13},{10,... | collective-permute-start | bytes 3981320 | tf_op jit(solution)/shard_map/ppermute | solution.py:631
  317.8 18.3 %collective-permute-start.33 = (bf16[576,1152]{1,0:T(8,128)(2,1)}, bf16[576,1152]{1,0:T(8,128)(2,1)}, u32[]{:S(2)}, u32[]{:S(2)}) collective-permute-start(bf16[576,1152]{1,0:T(8,128)(2,1)} %collective-permute-done.27.refs_3_), channel_id=1, source_target_pairs={{0,4},{1,5},{2,6},{3,7},{4,0},{5,1},{6,2},{7,3},{8,12},{9,13},{10,... | collective-permute-start | bytes 3981320 | tf_op jit(solution)/shard_map/ppermute | solution.py:631
  317.8 6.7 collective-permute-start.39
  318.3 17.7 %collective-permute-start.34 = (bf16[576,1152]{1,0:T(8,128)(2,1)}, bf16[576,1152]{1,0:T(8,128)(2,1)}, u32[]{:S(2)}, u32[]{:S(2)}) collective-permute-start(bf16[576,1152]{1,0:T(8,128)(2,1)} %collective-permute-done.28.refs_4_), channel_id=1, source_target_pairs={{0,4},{1,5},{2,6},{3,7},{4,0},{5,1},{6,2},{7,3},{8,12},{9,13},{10,... | collective-permute-start | bytes 3981320 | tf_op jit(solution)/shard_map/ppermute | solution.py:631
  454.3 23.5 %collective-permute-start.40 = (bf16[4,4,1296,128]{3,2,1,0:T(8,128)(2,1)}, bf16[4,4,1296,128]{3,2,1,0:T(8,128)(2,1)}, u32[]{:S(2)}, u32[]{:S(2)}) collective-permute-start(bf16[4,4,1296,128]{3,2,1,0:T(8,128)(2,1)} %get-tuple-element.109), channel_id=1, source_target_pairs={{0,4},{1,5},{2,6},{3,7},{4,0},{5,1},{6,2},{7,3},{8,12},{9,13},{10,... | collective-permute-start | bytes 15925256 | tf_op jit(solution)/shard_map/ppermute | solution.py:631
  475.7 11.2 %collective-permute-start.41 = (bf16[576,4608]{1,0:T(8,128)(2,1)}, bf16[576,4608]{1,0:T(8,128)(2,1)}, u32[]{:S(2)}, u32[]{:S(2)}) collective-permute-start(bf16[576,4608]{1,0:T(8,128)(2,1)} %get-tuple-element.114), channel_id=1, source_target_pairs={{0,4},{1,5},{2,6},{3,7},{4,0},{5,1},{6,2},{7,3},{8,12},{9,13},{10,... | collective-permute-start | bytes 15925256 | tf_op jit(solution)/shard_map/ppermute | solution.py:631
  485.1 62.9 %collective-permute-start.42 = (bf16[4,2,1296,128]{3,2,1,0:T(8,128)(2,1)}, bf16[4,2,1296,128]{3,2,1,0:T(8,128)(2,1)}, u32[]{:S(2)}, u32[]{:S(2)}) collective-permute-start(bf16[4,2,1296,128]{3,2,1,0:T(8,128)(2,1)} %get-tuple-element.255), channel_id=1, source_target_pairs={{0,1},{1,0},{2,3},{3,2},{4,5},{5,4},{6,7},{7,6},{8,9},{9,8},{10,11... | collective-permute-start | bytes 7962632 | tf_op jit(solution)/shard_map/ppermute | solution.py:631
  495.1 60.2 %collective-permute-start.43 = (bf16[4,144,2304]{2,1,0:T(8,128)(2,1)}, bf16[4,144,2304]{2,1,0:T(8,128)(2,1)}, u32[]{:S(2)}, u32[]{:S(2)}) collective-permute-start(bf16[4,144,2304]{2,1,0:T(8,128)(2,1)} %get-tuple-element.253), channel_id=1, source_target_pairs={{0,2},{1,3},{2,0},{3,1},{4,6},{5,7},{6,4},{7,5},{8,10},{9,11},{10,... | collective-permute-start | bytes 7962632 | tf_op jit(solution)/shard_map/ppermute | solution.py:631
  551.7 65.9 %collective-permute-start.44 = (bf16[4,1296,128]{2,1,0:T(8,128)(2,1)}, bf16[4,1296,128]{2,1,0:T(8,128)(2,1)}, u32[]{:S(2)}, u32[]{:S(2)}) collective-permute-start(bf16[4,1296,128]{2,1,0:T(8,128)(2,1)} %get-tuple-element.267), channel_id=1, source_target_pairs={{0,2},{1,3},{2,0},{3,1},{4,6},{5,7},{6,4},{7,5},{8,10},{9,11},{10,... | collective-permute-start | bytes 3981320 | tf_op jit(solution)/shard_map/ppermute | solution.py:631
  559.0 61.2 %collective-permute-start.45 = (bf16[4,144,1152]{2,1,0:T(8,128)(2,1)}, bf16[4,144,1152]{2,1,0:T(8,128)(2,1)}, u32[]{:S(2)}, u32[]{:S(2)}) collective-permute-start(bf16[4,144,1152]{2,1,0:T(8,128)(2,1)} %get-tuple-element.265), channel_id=1, source_target_pairs={{0,1},{1,0},{2,3},{3,2},{4,5},{5,4},{6,7},{7,6},{8,9},{9,8},{10,11... | collective-permute-start | bytes 3981320 | tf_op jit(solution)/shard_map/ppermute | solution.py:631
  565.5 56.6 %collective-permute-start.46 = (bf16[1,544,1152]{2,1,0:T(8,128)(2,1)}, bf16[1,544,1152]{2,1,0:T(8,128)(2,1)S(1)}, u32[]{:S(2)}, u32[]{:S(2)}) collective-permute-start(bf16[1,544,1152]{2,1,0:T(8,128)(2,1)} %fusion.11), channel_id=1, source_target_pairs={{0,1},{1,0},{2,3},{3,2},{4,5},{5,4},{6,7},{7,6},{8,9},{9,8},{10,11... | collective-permute-start | bytes 3760136 | tf_op jit(solution)/shard_map/ppermute | solution.py:631
  620.2 52.3 %collective-permute-start.48 = (bf16[2,1296,128]{2,1,0:T(8,128)(2,1)}, bf16[2,1296,128]{2,1,0:T(8,128)(2,1)}, u32[]{:S(2)}, u32[]{:S(2)}) collective-permute-start(bf16[2,1296,128]{2,1,0:T(8,128)(2,1)} %get-tuple-element.279), channel_id=1, source_target_pairs={{0,16},{1,17},{2,18},{3,19},{4,20},{5,21},{6,22},{7,23},{8,24},{9,... | collective-permute-start | bytes 1990664 | tf_op jit(solution)/shard_map/ppermute | solution.py:631
  669.7 51.3 %collective-permute-start.50 = (bf16[576,4608]{1,0:T(8,128)(2,1)}, bf16[576,4608]{1,0:T(8,128)(2,1)}, u32[]{:S(2)}, u32[]{:S(2)}) collective-permute-start(bf16[576,4608]{1,0:T(8,128)(2,1)} %get-tuple-element.132), channel_id=1, source_target_pairs={{0,4},{1,5},{2,6},{3,7},{4,0},{5,1},{6,2},{7,3},{8,12},{9,13},{10,... | collective-permute-start | bytes 15925256 | tf_op jit(solution)/shard_map/ppermute | solution.py:631
  669.8 18.2 %collective-permute-start.47 = (bf16[2,144,1152]{2,1,0:T(8,128)(2,1)S(1)}, bf16[2,144,1152]{2,1,0:T(8,128)(2,1)S(1)}, u32[]{:S(2)}, u32[]{:S(2)}) collective-permute-start(bf16[2,144,1152]{2,1,0:T(8,128)(2,1)S(1)} %get-tuple-element.281), channel_id=1, source_target_pairs={{0,8},{1,9},{2,10},{3,11},{4,12},{5,13},{6,14},{7,15},{8,0},{9,1},... | collective-permute-start | bytes 1990664 | tf_op jit(solution)/shard_map/ppermute | solution.py:631
  672.3 34.5 %collective-permute-start.49 = (bf16[1,544,1152]{2,1,0:T(8,128)(2,1)}, bf16[1,544,1152]{2,1,0:T(8,128)(2,1)}, u32[]{:S(2)}, u32[]{:S(2)}) collective-permute-start(bf16[1,544,1152]{2,1,0:T(8,128)(2,1)} %fusion.12), channel_id=1, source_target_pairs={{0,1},{1,0},{2,3},{3,2},{4,5},{5,4},{6,7},{7,6},{8,9},{9,8},{10,11... | collective-permute-start | bytes 3760136 | tf_op jit(solution)/shard_map/ppermute | solution.py:631
  673.8 26.2 %collective-permute-start.64 = (bf16[1,1296,128]{2,1,0:T(8,128)(2,1)S(1)}, bf16[1,1296,128]{2,1,0:T(8,128)(2,1)S(1)}, u32[]{:S(2)}, u32[]{:S(2)}) collective-permute-start(bf16[1,1296,128]{2,1,0:T(8,128)(2,1)S(1)} %constant_dynamic-slice_fusion.12), channel_id=1, source_target_pairs={{0,8},{1,9},{2,10},{3,11},{4,12},{5,13},{6,14},{7,15},{8,0},{9,1},... | collective-permute-start | bytes 995336 | tf_op jit(solution)/shard_map/ppermute | solution.py:631
  688.2 17.6 %collective-permute-start.63 = (bf16[1,144,1152]{2,1,0:T(8,128)(2,1)S(1)}, bf16[1,144,1152]{2,1,0:T(8,128)(2,1)S(1)}, u32[]{:S(2)}, u32[]{:S(2)}) collective-permute-start(bf16[1,144,1152]{2,1,0:T(8,128)(2,1)S(1)} %constant_dynamic-slice_fusion.14), channel_id=1, source_target_pairs={{0,16},{1,17},{2,18},{3,19},{4,20},{5,21},{6,22},{7,23},{8,24},{9,... | collective-permute-start | bytes 995336 | tf_op jit(solution)/shard_map/ppermute | solution.py:631
  754.1 15.2 %collective-permute-start.51 = (bf16[4,4,648,128]{3,2,1,0:T(8,128)(2,1)}, bf16[4,4,648,128]{3,2,1,0:T(8,128)(2,1)}, u32[]{:S(2)}, u32[]{:S(2)}) collective-permute-start(bf16[4,4,648,128]{3,2,1,0:T(8,128)(2,1)} %get-tuple-element.140), channel_id=1, source_target_pairs={{0,4},{1,5},{2,6},{3,7},{4,0},{5,1},{6,2},{7,3},{8,12},{9,13},{10,... | collective-permute-start | bytes 7962632 | tf_op jit(solution)/shard_map/ppermute | solution.py:631
  755.6 32.6 %collective-permute-start.54 = (bf16[4,72,2304]{2,1,0:T(8,128)(2,1)}, bf16[4,72,2304]{2,1,0:T(8,128)(2,1)}, u32[]{:S(2)}, u32[]{:S(2)}) collective-permute-start(bf16[4,72,2304]{2,1,0:T(8,128)(2,1)} %pad_maximum_fusion.2), channel_id=1, source_target_pairs={{0,1},{1,0},{2,3},{3,2},{4,5},{5,4},{6,7},{7,6},{8,9},{9,8},{10,11... | collective-permute-start | bytes 3981320 | tf_op jit(solution)/shard_map/ppermute | solution.py:631
  755.8 36.6 %collective-permute-start.53 = (bf16[4,72,2304]{2,1,0:T(8,128)(2,1)}, bf16[4,72,2304]{2,1,0:T(8,128)(2,1)}, u32[]{:S(2)}, u32[]{:S(2)}) collective-permute-start(bf16[4,72,2304]{2,1,0:T(8,128)(2,1)} %get-tuple-element.261), channel_id=1, source_target_pairs={{0,2},{1,3},{2,0},{3,1},{4,6},{5,7},{6,4},{7,5},{8,10},{9,11},{10,... | collective-permute-start | bytes 3981320 | tf_op jit(solution)/shard_map/ppermute | solution.py:631
  772.1 48.9 %collective-permute-start.55 = (bf16[4,2,648,128]{3,2,1,0:T(8,128)(2,1)S(1)}, bf16[4,2,648,128]{3,2,1,0:T(8,128)(2,1)S(1)}, u32[]{:S(2)}, u32[]{:S(2)}) collective-permute-start(bf16[4,2,648,128]{3,2,1,0:T(8,128)(2,1)S(1)} %get-tuple-element.263), channel_id=1, source_target_pairs={{0,1},{1,0},{2,3},{3,2},{4,5},{5,4},{6,7},{7,6},{8,9},{9,8},{10,11... | collective-permute-start | bytes 3981320 | tf_op jit(solution)/shard_map/ppermute | solution.py:631
  790.5 46.7 %collective-permute-start.57 = (bf16[4,72,1152]{2,1,0:T(8,128)(2,1)S(1)}, bf16[4,72,1152]{2,1,0:T(8,128)(2,1)S(1)}, u32[]{:S(2)}, u32[]{:S(2)}) collective-permute-start(bf16[4,72,1152]{2,1,0:T(8,128)(2,1)S(1)} %get-tuple-element.273), channel_id=1, source_target_pairs={{0,2},{1,3},{2,0},{3,1},{4,6},{5,7},{6,4},{7,5},{8,10},{9,11},{10,... | collective-permute-start | bytes 1990664 | tf_op jit(solution)/shard_map/ppermute | solution.py:631
  794.6 42.8 %collective-permute-start.56 = (bf16[4,72,1152]{2,1,0:T(8,128)(2,1)S(1)}, bf16[4,72,1152]{2,1,0:T(8,128)(2,1)S(1)}, u32[]{:S(2)}, u32[]{:S(2)}) collective-permute-start(bf16[4,72,1152]{2,1,0:T(8,128)(2,1)S(1)} %get-tuple-element.275), channel_id=1, source_target_pairs={{0,1},{1,0},{2,3},{3,2},{4,5},{5,4},{6,7},{7,6},{8,9},{9,8},{10,11... | collective-permute-start | bytes 1990664 | tf_op jit(solution)/shard_map/ppermute | solution.py:631
  821.6 30.1 %collective-permute-start.58 = (bf16[4,648,128]{2,1,0:T(8,128)(2,1)S(1)}, bf16[4,648,128]{2,1,0:T(8,128)(2,1)S(1)}, u32[]{:S(2)}, u32[]{:S(2)}) collective-permute-start(bf16[4,648,128]{2,1,0:T(8,128)(2,1)S(1)} %get-tuple-element.277), channel_id=1, source_target_pairs={{0,2},{1,3},{2,0},{3,1},{4,6},{5,7},{6,4},{7,5},{8,10},{9,11},{10,... | collective-permute-start | bytes 1990664 | tf_op jit(solution)/shard_map/ppermute | solution.py:631
  837.7 31.1 %collective-permute-start.59 = (bf16[2,144,1152]{2,1,0:T(8,128)(2,1)S(1)}, bf16[2,144,1152]{2,1,0:T(8,128)(2,1)S(1)}, u32[]{:S(2)}, u32[]{:S(2)}) collective-permute-start(bf16[2,144,1152]{2,1,0:T(8,128)(2,1)S(1)} %get-tuple-element.271), channel_id=1, source_target_pairs={{0,16},{1,17},{2,18},{3,19},{4,20},{5,21},{6,22},{7,23},{8,24},{9,... | collective-permute-start | bytes 1990664 | tf_op jit(solution)/shard_map/ppermute | solution.py:631
  851.9 24.1 %collective-permute-start.60 = (bf16[2,648,128]{2,1,0:T(8,128)(2,1)S(1)}, bf16[2,648,128]{2,1,0:T(8,128)(2,1)S(1)}, u32[]{:S(2)}, u32[]{:S(2)}) collective-permute-start(bf16[2,648,128]{2,1,0:T(8,128)(2,1)S(1)} %get-tuple-element.287), channel_id=1, source_target_pairs={{0,8},{1,9},{2,10},{3,11},{4,12},{5,13},{6,14},{7,15},{8,0},{9,1},... | collective-permute-start | bytes 995336 | tf_op jit(solution)/shard_map/ppermute | solution.py:631
  869.1 16.1 %collective-permute-start.62 = (bf16[1,144,1152]{2,1,0:T(8,128)(2,1)S(1)}, bf16[1,144,1152]{2,1,0:T(8,128)(2,1)S(1)}, u32[]{:S(2)}, u32[]{:S(2)}) collective-permute-start(bf16[1,144,1152]{2,1,0:T(8,128)(2,1)S(1)} %constant_dynamic-slice_fusion.1), channel_id=1, source_target_pairs={{0,8},{1,9},{2,10},{3,11},{4,12},{5,13},{6,14},{7,15},{8,0},{9,1},... | collective-permute-start | bytes 995336 | tf_op jit(solution)/shard_map/ppermute | solution.py:631
  876.2 13.6 %collective-permute-start.61 = (bf16[1,648,128]{2,1,0:T(8,128)(2,1)S(1)}, bf16[1,648,128]{2,1,0:T(8,128)(2,1)S(1)}, u32[]{:S(2)}, u32[]{:S(2)}) collective-permute-start(bf16[1,648,128]{2,1,0:T(8,128)(2,1)S(1)} %constant_dynamic-slice_fusion), channel_id=1, source_target_pairs={{0,16},{1,17},{2,18},{3,19},{4,20},{5,21},{6,22},{7,23},{8,24},{9,... | collective-permute-start | bytes 497672 | tf_op jit(solution)/shard_map/ppermute | solution.py:631
  (69 other events, 968.2 us)
Sparse Core Ops, SparseCore 0:
  767.1 58.2 all-gather.1

commit v3 on v2

--- a/solution.py
+++ b/solution.py
@@ -129,7 +129,7 @@
             bytes_accessed=4 * features * (width + key_rows),
         ),
         name="attend",
-    )(query, own, far, query_ids[:, None, :], key_ids[:, :, None], *old)
+    )(query, own, far, query_ids, key_ids, *old)
 
 
 def attend_back_kernel(
@@ -228,8 +228,8 @@
         mixed,
         grad,
         level,
-        query_ids[:, None, :],
-        key_ids[:, :, None],
+        query_ids,
+        key_ids,
         *old,
     )
 
@@ -702,15 +702,17 @@
         proj_ref[span] = jnp.concatenate([part[:, columns:] for part in parts], axis=1)
 
 
+def swap_bits(value):
+    return ((value & 1) << 1) | (value >> 1)
+
+
 def assemble(grid, blocks, order, piece, kernel, widths, rows, name):
     outer = grid.outer_count
-    spots = jnp.array([order.index(turn) for turn in range(outer)], jnp.int32)
-    turns = jnp.stack(
-        [lax.dynamic_index_in_dim(spots, grid.at["z"] ^ z, keepdims=False) for z in range(outer)]
-    )
-    places = [
-        (grid.at["c"] ^ (block >> 2)) * 4 + (grid.seq_index ^ (block & 3)) for block in range(8)
-    ]
+    turns = grid.at["z"] ^ jnp.arange(4, dtype=jnp.int32)
+    if order[1] == 2:
+        turns = swap_bits(turns)
+    block = jnp.arange(8, dtype=jnp.int32)
+    places = (grid.at["c"] ^ (block >> 2)) * 4 + (grid.seq_index ^ (block & 3))
     shapes = [jax.ShapeDtypeStruct((outer * 2 * rows, w), jnp.bfloat16) for w in widths]
     return pl.pallas_call(
         kernel,
@@ -729,7 +731,7 @@
             bytes_accessed=8 * outer * rows * sum(widths),
         ),
         name=name,
-    )(turns.astype(jnp.int32), jnp.stack(places).astype(jnp.int32), *blocks)
+    )(turns, places, *blocks)
 
 
 def place_kernel(block_count, outer_count, to_ref, *refs):
@@ -753,11 +755,12 @@
 def place_blocks(grid, blocks, order):
     outer = grid.outer_count
     rows, columns = blocks[0].shape[0] // outer, blocks[0].shape[1]
-    slots = []
-    for block in range(8):
-        core, place = grid.at["c"] ^ (block >> 2), grid.seq_index ^ (block & 3)
-        for turn in order:
-            slots.append((place * outer + (grid.at["z"] ^ turn)) * 2 + core)
+    spot = jnp.arange(8 * outer, dtype=jnp.int32)
+    core, place = grid.at["c"] ^ (spot >> 4), grid.seq_index ^ (spot >> 2 & 3)
+    turn = spot & 3
+    if order[1] == 2:
+        turn = swap_bits(turn)
+    slots = (place * outer + (grid.at["z"] ^ turn)) * 2 + core
     count = 8 * outer
     return pl.pallas_call(
         lambda *refs: place_kernel(8, outer, *refs),
@@ -774,20 +777,30 @@
             flops=0, transcendentals=0, bytes_accessed=4 * count * rows * columns
         ),
         name="place_blocks",
-    )(jnp.stack(slots).astype(jnp.int32), *blocks)
+    )(slots, *blocks)
 
 
 class Gather:
-    def __init__(self, grid, piece, *extra, direct=False):
-        self.grid = grid
-        if direct:
-            self.order = [0, 1, 2, 3]
-            parts = [piece] + [grid.send(piece, "z", turn) for turn in (1, 2, 3)]
-        else:
-            self.order = [0, 2, 1, 3]
-            self.pair = jnp.concatenate([piece, grid.send(piece, "z", 2)], axis=0)
-            parts = [self.pair, grid.send(self.pair, "z", 1)]
+    def __init__(self, grid, piece):
+        self.grid, self.piece, self.crossed = grid, piece, []
+
+    def direct(self, *extra):
+        self.order = [0, 1, 2, 3]
+        parts = [self.piece] + [self.grid.send(self.piece, "z", turn) for turn in (1, 2, 3)]
         self.column = jnp.concatenate(parts + list(extra), axis=0)
+
+    def first(self):
+        self.order = [0, 2, 1, 3]
+        self.far = self.grid.send(self.piece, "z", 2)
+
+    def second(self, *after):
+        piece = tie(self.piece, *after) if after else self.piece
+        self.pair = jnp.concatenate([piece, self.far], axis=0)
+        self.far = self.grid.send(self.pair, "z", 1)
+
+    def last(self, *after):
+        pair = tie(self.pair, *after) if after else self.pair
+        self.column = jnp.concatenate([pair, self.far], axis=0)
 
     def spread(self):
         self.over_x = self.grid.send(self.column, "x")
@@ -803,11 +816,14 @@
                 self.over_y = value
         self.blocks = [self.column, self.over_x, self.over_y, self.grid.send(value, axis)]
 
+    def cross(self, at, *after):
+        block = (self.column, self.over_x, self.over_y)[at]
+        block = tie(block, *after) if after else block
+        self.crossed.append(self.grid.send(block, "c"))
+
     def core(self, *after):
-        blocks = list(self.blocks)
-        if after:
-            blocks[3] = tie(blocks[3], *after)
-        return blocks + [self.grid.send(block, "c") for block in blocks]
+        block = tie(self.blocks[3], *self.crossed[1:], *after)
+        return self.blocks + self.crossed + [self.grid.send(block, "c")]
 
 
 def split_vectors(joint, widths):
@@ -839,9 +855,12 @@
     extra = jnp.pad(joint, (0, short)).reshape(-1, LANES)
     rows, columns = skip_weight.shape
     piece = pack_lanes(skip_weight)
-    way = Gather(grid, piece, extra, direct=True)
+    way = Gather(grid, piece)
+    way.direct(extra)
     way.spread()
     way.forward("y")
+    for at in range(3):
+        way.cross(at)
     found = jnp.stack([block[-extra.shape[0] :].reshape(-1) for block in way.blocks])
     joint = jnp.stack(
         [
@@ -914,13 +933,14 @@
         return self.value
 
 
-def fork(way):
-    rows = way.value.shape[1] // 2
+def fork(way, dim, align):
+    whole = way.value.shape[dim]
+    cut = -(-whole // (2 * align)) * align
     ways = []
-    for part in range(2):
+    for start, stop in ((0, cut), (cut, whole)):
         branch = object.__new__(Scatter)
         branch.grid, branch.view = way.grid, None
-        branch.value = way.value[:, part * rows : (part + 1) * rows]
+        branch.value = lax.slice_in_dim(way.value, start, stop, axis=dim)
         ways.append(branch)
     return ways
 
@@ -1078,8 +1098,13 @@
         skip_way, vectors, skip_full = gather_skip(grid, skip_weight, vectors)
         mixed_piece = jnp.concatenate([qkv_weight, proj_weight], axis=1)
         mixed_way = Gather(grid, tie(mixed_piece, skip_way.column))
+        mixed_way.first()
+        mixed_way.second()
+        mixed_way.last()
         mixed_way.spread()
         mixed_way.forward("y")
+        for at in range(3):
+            mixed_way.cross(at)
     else:
         vectors, wide = gather_plain(
             [skip_weight, qkv_weight, proj_weight, hidden_weight, down_weight], vectors
@@ -1101,6 +1126,7 @@
     joined_inputs = inputs
     if grid.square:
         joined_inputs = tie(inputs, skip_way.over_x, skip_way.over_y)
+        segments = tie(segments, skip_way.over_x, skip_way.over_y)
     items = Items(grid, segments, occupied, own_rows, all_rows)
     query_ids, used = items.of(grid.seq_index)
     key_ids = jnp.concatenate([query_ids, far_ids(grid, items)], axis=1)
@@ -1108,45 +1134,68 @@
     halo = grid.shift(tails, half - 1, half)
     first_tokens = jnp.concatenate([joined_inputs, halo[0]], axis=1)
     second_tokens = jnp.concatenate([skip_inputs, halo[1]], axis=1)
-    joined = tie(jnp.concatenate([first_tokens, second_tokens], axis=2))
+    query_ids, key_ids = query_ids[:, None, :], key_ids[:, :, None]
+    used_rows = used.astype(jnp.float32).reshape(-1, 1)
+    joined = jnp.concatenate([first_tokens, second_tokens], axis=2)
+    joined, query_ids, key_ids, used_rows = lax.optimization_barrier(
+        (joined, query_ids, key_ids, used_rows)
+    )
     cotangent = jnp.concatenate([out_cotangent, halo[2]], axis=1)
 
     stream = dot_last(joined, skip_full) + skip_bias_full
+    if grid.square:
+        stream = tie(stream, mixed_way.crossed[0])
     first_low, first_normal, first_scale = layer_norm(stream, gain_one, shift_one)
     rows = inputs.shape[0]
     first_far = far_gather(grid, first_low)
     if grid.square:
-        hidden_way = Gather(grid, tie(hidden_weight, mixed_way.column, stream))
+        hidden_way = Gather(grid, tie(hidden_weight, stream))
+        hidden_way.first()
+        mixed_blocks = mixed_way.core(first_far[0], hidden_way.far)
+        hidden_way.second(mixed_way.blocks[3])
         down_way = Gather(grid, tie(pack_lanes(down_weight), hidden_way.pair))
-        hidden_way.column = tie(hidden_way.column, mixed_way.blocks[3])
-        hidden_way.spread()
-        mixed_blocks = mixed_way.core(first_far[0], hidden_way.column, down_way.column)
+        down_way.first()
         query_full, both_full, proj_full = join_mixed(
             grid, mixed_blocks, mixed_way.order, *qkv_weight.shape, model
         )
-        query_full = tie(query_full, first_far[1])
-        both_full = tie(both_full, first_far[1])
-    query = dot_last(first_low, query_full).astype(jnp.bfloat16)
+        hidden_way.last(query_full)
+        hidden_way.spread()
+        down_way.second(query_full)
+        both_full = tie(both_full, hidden_way.column, down_way.pair)
     own = dot_last(first_low, both_full).astype(jnp.bfloat16)
     if grid.square:
+        query_full = tie(query_full, own, first_far[1])
+    query = dot_last(first_low, query_full).astype(jnp.bfloat16)
+    if grid.square:
+        down_way.last(query)
         down_way.spread()
-        hidden_way.forward("y")
-        first_far[0] = tie(first_far[0], query, own, hidden_way.over_x, hidden_way.over_y)
+        hidden_way.cross(0)
+        down_way.cross(0)
+        first_far[0] = tie(first_far[0], query, down_way.column, *hidden_way.crossed)
     far, done = [], ()
     for row in range(rows):
         far.append(dot_last(first_far[row], both_full).astype(jnp.bfloat16))
         done = attend(query, own, far[row], query_ids, key_ids, row, *done)
         if row == 0 and grid.square:
-            down_way.forward("y", done[0])
+            hidden_way.forward("y", done[0])
+            down_way.forward("x", done[0])
             first_far[1] = tie(
-                first_far[1], *hidden_way.blocks, down_way.over_x, down_way.over_y
+                first_far[1],
+                hidden_way.over_x,
+                hidden_way.over_y,
+                down_way.over_x,
+                down_way.over_y,
+                *down_way.crossed,
             )
+            hidden_way.cross(1)
+            hidden_way.cross(2)
     attended, level = done
     if grid.square:
-        hidden_blocks = place_blocks(grid, hidden_way.core(), hidden_way.order)
+        down_way.cross(1, attended, down_way.blocks[3])
+        down_way.cross(2, attended, down_way.blocks[3])
+        hidden_blocks = place_blocks(grid, hidden_way.core(attended), hidden_way.order)
         hidden_blocks = hidden_blocks.reshape(-1, model, model)
         down_blocks = join_down(grid, down_way.core(attended), down_way.order, *down_weight.shape)
-    used_rows = used.astype(jnp.float32).reshape(-1, 1)
     flat = (-1, model)
     (
         output,
@@ -1217,10 +1266,9 @@
             if row == 0:
                 down_way.push("y", choose_dim(1))
                 hidden_way.push("x", choose_lanes)
+                both_grad = tie(both_grad, down_way.sent, hidden_way.sent)
             else:
-                down_way.push("z", choose_half, 2)
-                hidden_way.push("z", choose_odd, 1)
-            both_grad = tie(both_grad, down_way.sent, hidden_way.sent, *grad_far)
+                both_grad = tie(both_grad, down_way.value, hidden_way.value, *grad_far)
         share = dot_back(both_grad[row : row + 1, all_rows:], both_full).astype(jnp.bfloat16)
         grad_far.append(far_send(grid, share))
         done = (done[0], tie(both_grad, share))
@@ -1238,13 +1286,14 @@
             here,
             outer,
         )
+        give = tie(give, *grad_far)
         mixed_way = Scatter(grid, keep, give, (outer, -1, keep.shape[1]))
-        down_way.pull(give)
-        down_way.push("z", choose_half, 1)
-        hidden_way.pull(give)
-        hidden_way.push("z", choose_half, 2)
-        query_grad = tie(query_grad, hidden_way.sent, down_way.sent, *grad_far)
-        both_grad = tie(both_grad, hidden_way.sent, down_way.sent, *grad_far)
+        down_way.value = tie(down_way.value, give)
+        hidden_way.value = tie(hidden_way.value, give)
+        down_way.push("z", choose_half, 2)
+        hidden_way.push("z", choose_odd, 1)
+        query_grad = tie(query_grad, give, *grad_far)
+        both_grad = tie(both_grad, give, *grad_far)
     else:
         first_all = [jnp.concatenate([first_low[row], first_far[row][0]]) for row in range(rows)]
         both_weight_grad = outer_dot(jnp.concatenate(first_all), both_flat)
@@ -1253,7 +1302,11 @@
     grad_first = dot_back(query_grad, query_full) + dot_back(both_grad[:, :all_rows], both_full)
     if grid.square:
         mixed_way.pull(grad_first)
-        way_a, way_b = fork(mixed_way)
+        down_way.pull(mixed_way.value)
+        down_way.push("z", choose_half, 1)
+        hidden_way.pull(mixed_way.value)
+        hidden_way.push("z", choose_half, 2)
+        way_a, way_b = fork(mixed_way, 1, 8)
         way_a.push("y", choose_lanes)
         way_b.push("x", choose_odd_lanes)
         grad_first = tie(grad_first, way_a.sent, way_b.sent)
@@ -1285,22 +1338,28 @@
     )
     input_grad = dot_back(grad_stream, skip_full[:model])
     if grid.square:
-        skip_way.pull(input_grad)
-        skip_way.push("x", choose_dim(2))
-        grad_stream = tie(grad_stream, skip_way.sent)
+        way_a.pull(input_grad)
+        way_b.pull(input_grad)
+        way_a.push("x", choose_lanes)
+        way_b.push("y", choose_lanes)
+        skip_way.pull(way_a.sent, way_b.sent)
+        skip_a, skip_b = fork(skip_way, 3, 8)
+        skip_a.push("x", choose_dim(2))
+        skip_b.push("y", choose_dim(1))
+        grad_stream = tie(grad_stream, skip_a.sent, skip_b.sent)
     skip_grad = dot_back(grad_stream, skip_full[model:])
     if grid.square:
         way_a.pull(skip_grad)
         way_b.pull(skip_grad)
-        way_a.push("x", choose_lanes)
-        way_b.push("y", choose_lanes)
-        skip_way.pull(way_a.sent, way_b.sent)
-        skip_way.push("y", choose_dim(1))
-        way_a.pull(skip_way.sent)
-        way_b.pull(skip_way.sent)
         mixed_way.value = jnp.concatenate([way_a.value, way_b.value], axis=1)
         mixed_way.push("z", choose_half, 2)
-        skip_way.pull(mixed_way.sent)
+        skip_a.pull(mixed_way.sent)
+        skip_b.pull(mixed_way.sent)
+        skip_a.push("y", choose_dim(1))
+        skip_b.push("x", choose_dim(1))
+        skip_a.pull()
+        skip_b.pull()
+        skip_way.value = jnp.concatenate([skip_a.value, skip_b.value], axis=1)
         skip_way.push("z", choose_odd, 1)
         mixed_way.pull(skip_way.sent)
         mixed_way.push("z", choose_half, 1)
@@ -1309,11 +1368,11 @@
         vectors = vectors(skip_way.sent)
 
         def tall_shard(way, shape):
-            total = way.mine.astype(jnp.float32) + way.got.astype(jnp.float32)
-            return unpack_lanes(total[0], *shape)
+            return unpack_lanes(wide_shard(way), *shape)
 
         def wide_shard(way):
-            return (way.mine.astype(jnp.float32) + way.got.astype(jnp.float32))[0]
+            mine = tie(way.mine, skip_way.sent, mixed_way.sent)
+            return (mine.astype(jnp.float32) + way.got.astype(jnp.float32))[0]
 
         down_shard = tall_shard(down_way, down_weight.shape)
         hidden_shard = wide_shard(hidden_way)
@@ -1330,7 +1389,7 @@
         vectors = vectors()
 
     moved = items.moved[..., None] & (grid.seq_index == half - 1)
-    results = [output, input_grad, skip_grad]
+    results = [tie(output, skip_grad), input_grad, skip_grad]
     tails = jnp.stack([value[:, own_rows:].astype(jnp.float32) for value in results])
     tails = grid.shift(tails, half, half - 1)
 

time: 909 us -> 841 us (0.925)
  waiting for transfers between devices: 217 us -> 131 us
  local copies, waits for them, and re-layouts: 52 us -> 62.1 us
    ppermute x63 -> x65, waiting for transfers between devices: 217 us -> 131 us  [send(): return lax.ppermute(value, ('batch', 'seq'), pairs)]
    unnamed x161 -> x182, local copies, waits for them, and re-layouts: 12.4 us -> 19.8 us
    ppermute x63 -> x65, starting transfers between devices: 69.9 us -> 68.6 us  [send(): return lax.ppermute(value, ('batch', 'seq'), pairs)]
    convert_element_type x18 -> x20, other arithmetic: 33.5 us -> 32.5 us  [add_low(): (mine.astype(jnp.float32) + other.astype(jnp.float32)).astype(jnp.bfloat16)]
  transfers between devices with their start and end apart: 66 -> 68, of which waited for: 22 -> 23; matrix products, arithmetic and copies ran while one was open for 20% -> 24% of each run, Pallas kernels for 28% -> 32%
where the time goes in v3:
time: 841 us; the launch traced here: 829 us
  Pallas kernels  389 us (46%)
  waiting for transfers between devices  131 us (16%)
  matrix products  81.8 us (10%)
  other arithmetic  78.2 us (9%)
  starting transfers between devices  71 us (8%)
  local copies, waits for them, and re-layouts  62.1 us (7%)
  between operations  16.1 us (2%)
    ppermute x65, waiting for transfers between devices, send(): return lax.ppermute(value, ('batch', 'seq'), pairs)  131 us
    pallas_call x2, Pallas kernels, attend_back(): pl.pallas_call(attend_back_kernel, grid=(1,), in_specs=[wide, pl.BlockSpe...  100 us
    pallas_call x1, Pallas kernels, middle_block(): pl.pallas_call(middle_kernel, grid=(blocks, steps), in_specs=[by_rows, by...  83.6 us
    ppermute x65, starting transfers between devices, send(): return lax.ppermute(value, ('batch', 'seq'), pairs)  68.6 us
    pallas_call x2, Pallas kernels, attend(): pl.pallas_call(attend_kernel, grid=(1,), in_specs=[wide, pl.BlockSpec((1,...  66.1 us
    dot_general x5, matrix products, dot_last(): lax.dot_general(left_side, right_side, (((2,), (0,)), ((), ())), preferre...  43.7 us
    pallas_call x2, Pallas kernels, tall_grad(): pl.pallas_call(lambda *refs: tall_grad_kernel(groups, *refs), grid_spec=p...  40.9 us
    pallas_call x1, Pallas kernels, mixed_grad(): pl.pallas_call(lambda *refs: mixed_grad_kernel(outer, *refs), grid_spec=p...  39.6 us
  transfers between devices with their start and end apart: 68, of which 23 were waited for; matrix products, arithmetic and copies ran while one was open for 24% of the time, Pallas kernels for 32%

profile of v3, /device:TPU:0, one launch (start us, length us, event | category | flops | bytes accessed | tf_op | source)
XLA Modules:
  0.0 829.5 jit_solution(16487960273347834978)
XLA Ops:
  9.8 3.0 collective-permute-start
  12.8 2.6 collective-permute-start.1
  24.0 4.3 collective-permute-done.1
  33.3 2.8 collective-permute-start.11
  38.5 13.1 %collective-permute-done.11 = bf16[144,1152]{1,0:T(8,128)(2,1)S(1)} collective-permute-done((bf16[144,1152]{1,0:T(8,128)(2,1)S(1)}, bf16[144,1152]{1,0:T(8,128)(2,1)S(1)}, u32[]{:S(2)}, u32[]{:S(2)}) %collective-permute-start.11) | collective-permute-done | bytes 331808 | tf_op jit(solution)/shard_map/ppermute | solution.py:631
  59.5 6.2 maximum_maximum_fusion
  69.5 2.0 constant_dynamic-update-slice_fusion.7.refs_2_
  71.5 11.1 %collective-permute-done.6.refs_5_ = bf16[2624,128]{1,0:T(8,128)(2,1)S(1)} collective-permute-done((bf16[2624,128]{1,0:T(8,128)(2,1)S(1)}, bf16[2624,128]{1,0:T(8,128)(2,1)S(1)}, u32[]{:S(2)}, u32[]{:S(2)}) %collective-permute-start.6) | collective-permute-done | bytes 671776 | tf_op jit(solution)/shard_map/ppermute | solution.py:631
  86.9 7.5 join_skip.1
  94.4 11.6 %fusion.6 = f32[2,544,1152]{2,1,0:T(8,128)} fusion(bf16[2,544,2304]{2,1,0:T(8,128)(2,1)} %maximum_maximum_fusion, bf16[2304,1152]{1,0:T(8,128)(2,1)} %join_skip.1, f32[1152]{0:T(1024)S(1)} %reshape.367), kind=kOutput, calls=%fused_computation.22 | convolution fusion | flops 5776809984 | bytes 15340032 | tf_op jit(solution)/shard_map/dot_general | solution.py:581
  106.0 3.2 reduce_sum.90
  109.2 3.7 collective-permute-done.14.refs_3_
  113.4 3.1 multiply_reduce_fusion.2
  121.8 15.6 %collective-permute-done.20 = bf16[144,1152]{1,0:T(8,128)(2,1)S(1)} collective-permute-done((bf16[144,1152]{1,0:T(8,128)(2,1)S(1)}, bf16[144,1152]{1,0:T(8,128)(2,1)S(1)}, u32[]{:S(2)}, u32[]{:S(2)}) %collective-permute-start.20) | collective-permute-done | bytes 331808 | tf_op jit(solution)/shard_map/ppermute | solution.py:631
  137.3 11.5 %collective-permute-done.19 = bf16[1,544,1152]{2,1,0:T(8,128)(2,1)S(1)} collective-permute-done((bf16[1,544,1152]{2,1,0:T(8,128)(2,1)S(1)}, bf16[1,544,1152]{2,1,0:T(8,128)(2,1)S(1)}, u32[]{:S(2)}, u32[]{:S(2)}) %collective-permute-start.19) | collective-permute-done | bytes 1253408 | tf_op jit(solution)/shard_map/ppermute | solution.py:631
  156.5 9.9 %join_mixed.1 = (bf16[1152,1152]{1,0:T(8,128)(2,1)}, bf16[1152,2304]{1,0:T(8,128)(2,1)}, bf16[1152,1152]{1,0:T(8,128)(2,1)}) custom-call(s32[4]{0:T(128)} %shift-right-arithmetic_or_fusion.refs_0_, s32[8]{0:T(128)} %xor_add_fusion.1.refs_1_, bf16[576,1152]{1,0:T(8,128)(2,1)} %constant_dynamic-update-slice_fusion.7.refs_2_, ...), custom_call_target="tpu_custom_call" | custom-call | bytes 21233664 | tf_op jit(solution)/shard_map/join_mixed/pallas_call | solution.py:717
  166.5 4.9 collective-permute-done.23
  173.4 6.6 collective-permute-done.22
  180.0 2.0 constant_dynamic-update-slice_fusion.12.refs_1_
  181.9 11.0 %convolution_convert_fusion.own_ref = bf16[2,544,2304]{2,1,0:T(8,128)(2,1)} fusion(bf16[2,544,1152]{2,1,0:T(8,128)(2,1)S(1)} %add_convert_fusion.7, bf16[1152,2304]{1,0:T(8,128)(2,1)} %get-tuple-element.122), kind=kOutput, calls=%fused_computation.3 | convolution fusion | flops 5778063360 | bytes 12828672 | tf_op jit(solution)/shard_map/dot_general | solution.py:581
  192.9 5.2 convolution_convert_fusion.3.q_ref
  203.8 7.8 fusion.9.far_ref
  211.6 33.2 %attend.2 = (bf16[2,544,1152]{2,1,0:T(8,128)(2,1)}, f32[2,16,544]{2,1,0:T(8,128)}) custom-call(bf16[2,544,1152]{2,1,0:T(8,128)(2,1)} %convolution_convert_fusion.3.q_ref, bf16[2,544,2304]{2,1,0:T(8,128)(2,1)} %convolution_convert_fusion.own_ref, bf16[1,544,2304]{2,1,0:T(8,128)(2,1)} %fusion.9.far_ref, s32[2,1,544]{2,1,0:T(1,128)} %add_select_fusion.qid_ref, ...), custom_call_target="tpu_custom_call" | custom-call | flops 4848615424 | bytes 7520256 | tf_op jit(solution)/shard_map/attend/pallas_call | solution.py:101
  247.8 11.0 %collective-permute-done.28.refs_3_ = bf16[576,1152]{1,0:T(8,128)(2,1)} collective-permute-done((bf16[576,1152]{1,0:T(8,128)(2,1)}, bf16[576,1152]{1,0:T(8,128)(2,1)}, u32[]{:S(2)}, u32[]{:S(2)}) %collective-permute-start.28) | collective-permute-done | bytes 1327136 | tf_op jit(solution)/shard_map/ppermute | solution.py:631
  258.8 3.2 collective-permute-done.29.refs_3_
  262.0 8.3 fusion.10.far_ref
  270.3 32.9 %attend.3 = (bf16[2,544,1152]{2,1,0:T(8,128)(2,1)}, f32[2,16,544]{2,1,0:T(8,128)}) custom-call(bf16[2,544,1152]{2,1,0:T(8,128)(2,1)} %convolution_convert_fusion.3.q_ref, bf16[2,544,2304]{2,1,0:T(8,128)(2,1)} %convolution_convert_fusion.own_ref, bf16[1,544,2304]{2,1,0:T(8,128)(2,1)} %fusion.10.far_ref, ...), custom_call_target="tpu_custom_call", output_to_operand_aliasing={{0}: (5, {}), {1}: (6, {})} | custom-call | flops 4848615424 | bytes 7520256 | tf_op jit(solution)/shard_map/attend/pallas_call | solution.py:101
  314.6 8.9 %place_blocks.1 = bf16[32,144,1152]{2,1,0:T(8,128)(2,1)} custom-call(s32[32]{0:T(128)} %xor_add_fusion.refs_0_, bf16[576,1152]{1,0:T(8,128)(2,1)} %constant_dynamic-update-slice_fusion.12.refs_1_, bf16[576,1152]{1,0:T(8,128)(2,1)} %collective-permute-done.25.refs_2_, bf16[576,1152]{1,0:T(8,128)(2,1)} %collective-permute-done.28.refs_3_, ...), custom_call_target="tpu_custom_call" | custom-call | bytes 21233664 | tf_op jit(solution)/shard_map/place_blocks/pallas_call | solution.py:765
  323.5 11.4 %join_down.1 = bf16[4608,1152]{1,0:T(8,128)(2,1)} custom-call(s32[4]{0:T(128)} %shift-right-arithmetic_or_fusion.refs_0_, s32[8]{0:T(128)} %xor_add_fusion.1.refs_1_, bf16[5184,128]{1,0:T(8,128)(2,1)} %copy-done.9, bf16[5184,128]{1,0:T(8,128)(2,1)} %collective-permute-done.29.refs_3_, bf16[5184,128]{1,0:T(8,128)(2,1)} %collective-permute-done.30.refs_4_, ...), custom_call_target="tpu_custom_call" | custom-call | bytes 21233664 | tf_op jit(solution)/shard_map/join_down/pallas_call | solution.py:717
  335.0 83.6 %middle_block.1 = (bf16[1088,1152]{1,0:T(8,128)(2,1)}, bf16[1088,1152]{1,0:T(8,128)(2,1)}, bf16[1088,4608]{1,0:T(8,128)(2,1)}, bf16[1088,4608]{1,0:T(8,128)(2,1)...) custom-call(f32[1088,1152]{1,0:T(8,128)} %bitcast.196, ...), custom_call_target="tpu_custom_call" | custom-call | flops 51980009472 | bytes 135069696 | tf_op jit(solution)/shard_map/middle_block/pallas_call | solution.py:488
  418.6 25.9 %down_weight_grad.1 = (bf16[4,4,1296,128]{3,2,1,0:T(8,128)(2,1)}, bf16[4,4,1296,128]{3,2,1,0:T(8,128)(2,1)}) custom-call(s32[1]{0:T(128)} %bitcast.26.refs_0_, bf16[1088,4608]{1,0:T(8,128)(2,1)} %get-tuple-element.144.refs_1_, bf16[1088,1152]{1,0:T(8,128)(2,1)} %broadcast_select_fusion.refs_2_), custom_call_target="tpu_custom_call" | custom-call | flops 11551113216 | bytes 20643840 | tf_op jit(solution)/shard_map/down_weight_grad/pallas_call | solution.py:299
  444.7 20.9 %hidden_weight_grad.1 = (bf16[576,4608]{1,0:T(8,128)(2,1)}, bf16[576,4608]{1,0:T(8,128)(2,1)}) custom-call(s32[1]{0:T(128)} %bitcast.26.refs_0_, bf16[1088,1152]{1,0:T(8,128)(2,1)} %get-tuple-element.146.refs_1_, bf16[1088,4608]{1,0:T(8,128)(2,1)} %get-tuple-element.147.refs_2_), custom_call_target="tpu_custom_call" | custom-call | flops 11551113216 | bytes 13123584 | tf_op jit(solution)/shard_map/hidden_weight_grad/pallas_call | solution.py:256
  466.0 5.5 add_convert_fusion.2
  474.9 3.8 add_convert_fusion.1
  478.8 2.7 constant_dynamic-slice_fusion.26
  482.0 50.3 %attend_back.2 = (bf16[2,544,1152]{2,1,0:T(8,128)(2,1)}, bf16[2,1088,2304]{2,1,0:T(8,128)(2,1)}) custom-call(bf16[2,544,1152]{2,1,0:T(8,128)(2,1)} %convolution_convert_fusion.3.q_ref, bf16[2,544,2304]{2,1,0:T(8,128)(2,1)} %convolution_convert_fusion.own_ref, bf16[1,544,2304]{2,1,0:T(8,128)(2,1)} %fusion.9.far_ref, ...), custom_call_target="tpu_custom_call" | custom-call | flops 12121538560 | bytes 15040512 | tf_op jit(solution)/shard_map/attend_back/pallas_call | solution.py:185
  533.2 2.4 add_convert_fusion.5
  536.6 5.7 collective-permute-done.43
  542.2 2.5 add_convert_fusion.4
  547.9 6.2 fusion.11
  554.6 50.0 %attend_back.3 = (bf16[2,544,1152]{2,1,0:T(8,128)(2,1)}, bf16[2,1088,2304]{2,1,0:T(8,128)(2,1)}) custom-call(bf16[2,544,1152]{2,1,0:T(8,128)(2,1)} %convolution_convert_fusion.3.q_ref, bf16[2,544,2304]{2,1,0:T(8,128)(2,1)} %convolution_convert_fusion.own_ref, bf16[1,544,2304]{2,1,0:T(8,128)(2,1)} %fusion.10.far_ref, ...), custom_call_target="tpu_custom_call", output_to_operand_aliasing={{0}: (8, {}), {1}: (9, {})} | custom-call | flops 12121538560 | bytes 15040512 | tf_op jit(solution)/shard_map/attend_back/pallas_call | solution.py:185
  608.1 7.7 fusion.12
  617.5 39.6 %mixed_weight_grad.1 = (bf16[576,4608]{1,0:T(8,128)(2,1)}, bf16[576,4608]{1,0:T(8,128)(2,1)}) custom-call(s32[1]{0:T(128)} %bitcast.26.refs_0_, bf16[1088,1152]{1,0:T(8,128)(2,1)} %bitcast.206, bf16[544,1152]{1,0:T(8,128)(2,1)} %bitcast.239, bf16[544,1152]{1,0:T(8,128)(2,1)} %bitcast.17.refs_3_, bf16[1088,1152]{1,0:T(8,128)(2,1)} %bitcast.245, ...), custom_call_target="tpu_custom_call" | custom-call | flops 17326669824 | bytes 35684352 | tf_op jit(solution)/shard_map/mixed_weight_grad/pallas_call | solution.py:371
  657.5 10.3 %fusion = f32[2,544,1152]{2,1,0:T(8,128)S(1)} fusion(bf16[1152,2304]{1,0:T(8,128)(2,1)} %get-tuple-element.122, bf16[2,1088,2304]{2,1,0:T(8,128)(2,1)} %get-tuple-element.171), kind=kOutput, calls=%fused_computation.4 | convolution fusion | flops 5775556608 | bytes 15335424 | tf_op jit(solution)/shard_map/dot_general | solution.py:587
  667.9 3.8 convolution_add_fusion
  674.0 2.5 collective-permute-start.63
  676.5 5.4 add_convert_fusion
  686.8 4.6 multiply_reduce_fusion
  691.5 4.7 convert_reduce_fusion
  696.2 15.0 %skip_weight_grad.1 = (bf16[4,4,648,128]{3,2,1,0:T(8,128)(2,1)}, bf16[4,4,648,128]{3,2,1,0:T(8,128)(2,1)}) custom-call(s32[1]{0:T(128)} %bitcast.26.refs_0_, bf16[1088,2304]{1,0:T(8,128)(2,1)} %bitcast.215, bf16[1088,1152]{1,0:T(8,128)(2,1)} %bitcast.225), custom_call_target="tpu_custom_call" | custom-call | flops 5775556608 | bytes 10321920 | tf_op jit(solution)/shard_map/skip_weight_grad/pallas_call | solution.py:299
  711.2 6.3 fusion.14
  717.5 2.2 copy-done.4
  725.2 2.4 collective-permute-start.64
  735.8 2.6 add_convert_fusion.3
  740.7 3.8 fusion.13
  744.8 2.2 copy-done.6
  749.7 2.8 collective-permute-done.53
  753.8 11.2 %collective-permute-done.57 = bf16[4,2,320,128]{3,2,0,1:T(8,128)(2,1)S(1)} collective-permute-done((bf16[4,2,320,128]{3,2,0,1:T(8,128)(2,1)S(1)}, bf16[4,2,320,128]{3,2,0,1:T(8,128)(2,1)S(1)}, u32[]{:S(2)}, u32[]{:S(2)}) %collective-permute-start.57) | collective-permute-done | bytes 655392 | tf_op jit(solution)/shard_map/ppermute | solution.py:631
  766.2 20.6 %collective-permute-start.58 = (bf16[4,320,128]{2,1,0:T(8,128)(2,1)S(1)}, bf16[4,320,128]{2,1,0:T(8,128)(2,1)S(1)}, u32[]{:S(2)}, u32[]{:S(2)}) collective-permute-start(bf16[4,320,128]{2,1,0:T(8,128)(2,1)S(1)} %dynamic-slice_bitcast_fusion.9), channel_id=1, source_target_pairs={{0,1},{1,0},{2,3},{3,2},{4,5},{5,4},{6,7},{7,6},{8,9},{9,8},{10,11... | collective-permute-start | bytes 983048 | tf_op jit(solution)/shard_map/ppermute | solution.py:631
  788.3 4.9 collective-permute-done.58
  793.3 3.0 collective-permute-done.56
  797.0 3.0 collective-permute-done.59
  800.3 6.9 collective-permute-done.60
  811.2 3.4 collective-permute-done.62
  (440 shorter events, 127.8 us)
Async XLA Ops:
  7.3 810.3 %all-gather.2.cloned.1.call-start = ((), (), s32[]{:S(2)}) async-start(), calls=%async_computation | async-start | bytes 1757184 | tf_op jit(solution)/shard_map/all_gather | solution.py:983
  9.8 13.2 %collective-permute-start = (bf16[648,128]{1,0:T(8,128)(2,1)}, bf16[648,128]{1,0:T(8,128)(2,1)}, u32[]{:S(2)}, u32[]{:S(2)}) collective-permute-start(bf16[648,128]{1,0:T(8,128)(2,1)} %maximum_maximum_fusion.4), channel_id=1, source_target_pairs={{0,8},{1,9},{2,10},{3,11},{4,12},{5,13},{6,14},{7,15},{8,0},{9,1},... | collective-permute-start | bytes 497672 | tf_op jit(solution)/shard_map/ppermute | solution.py:631
  12.8 15.5 %collective-permute-start.1 = (bf16[648,128]{1,0:T(8,128)(2,1)}, bf16[648,128]{1,0:T(8,128)(2,1)}, u32[]{:S(2)}, u32[]{:S(2)}) collective-permute-start(bf16[648,128]{1,0:T(8,128)(2,1)} %maximum_maximum_fusion.4), channel_id=1, source_target_pairs={{0,16},{1,17},{2,18},{3,19},{4,20},{5,21},{6,22},{7,23},{8,24},{9,... | collective-permute-start | bytes 497672 | tf_op jit(solution)/shard_map/ppermute | solution.py:631
  15.4 13.8 %collective-permute-start.2 = (bf16[648,128]{1,0:T(8,128)(2,1)}, bf16[648,128]{1,0:T(8,128)(2,1)}, u32[]{:S(2)}, u32[]{:S(2)}) collective-permute-start(bf16[648,128]{1,0:T(8,128)(2,1)} %maximum_maximum_fusion.4), channel_id=1, source_target_pairs={{0,24},{1,25},{2,26},{3,27},{4,28},{5,29},{6,30},{7,31},{8,16},{9,... | collective-permute-start | bytes 497672 | tf_op jit(solution)/shard_map/ppermute | solution.py:631
  18.1 18.8 %collective-permute-start.5 = (bf16[3,2,24,1152]{3,2,1,0:T(8,128)(2,1)}, bf16[3,2,24,1152]{3,2,1,0:T(8,128)(2,1)}, u32[]{:S(2)}, u32[]{:S(2)}) collective-permute-start(bf16[3,2,24,1152]{3,2,1,0:T(8,128)(2,1)} %pad_maximum_fusion.6), channel_id=1, source_target_pairs={{1,2},{5,6},{9,10},{13,14},{17,18},{21,22},{25,26},{29,30}} | collective-permute-start | bytes 995336 | tf_op jit(solution)/shard_map/ppermute | solution.py:638
  30.2 23.1 %collective-permute-start.3 = (bf16[2624,128]{1,0:T(8,128)(2,1)S(1)}, bf16[2624,128]{1,0:T(8,128)(2,1)S(1)}, u32[]{:S(2)}, u32[]{:S(2)}) collective-permute-start(bf16[2624,128]{1,0:T(8,128)(2,1)S(1)} %constant_dynamic-update-slice_fusion.refs_2_), channel_id=1, source_target_pairs={{0,1},{1,0},{2,3},{3,2},{4,5},{5,4},{6,7},{7,6},{8,9},{9,8},{10,11... | collective-permute-start | bytes 2015240 | tf_op jit(solution)/shard_map/ppermute | solution.py:631
  31.8 21.5 %collective-permute-start.4 = (bf16[2624,128]{1,0:T(8,128)(2,1)S(1)}, bf16[2624,128]{1,0:T(8,128)(2,1)S(1)}, u32[]{:S(2)}, u32[]{:S(2)}) collective-permute-start(bf16[2624,128]{1,0:T(8,128)(2,1)S(1)} %constant_dynamic-update-slice_fusion.refs_2_), channel_id=1, source_target_pairs={{0,2},{1,3},{2,0},{3,1},{4,6},{5,7},{6,4},{7,5},{8,10},{9,11},{10,... | collective-permute-start | bytes 2015240 | tf_op jit(solution)/shard_map/ppermute | solution.py:631
  33.3 52.4 %collective-permute-start.7 = (bf16[2624,128]{1,0:T(8,128)(2,1)S(1)}, bf16[2624,128]{1,0:T(8,128)(2,1)}, u32[]{:S(2)}, u32[]{:S(2)}) collective-permute-start(bf16[2624,128]{1,0:T(8,128)(2,1)S(1)} %constant_dynamic-update-slice_fusion.refs_2_), channel_id=1, source_target_pairs={{0,4},{1,5},{2,6},{3,7},{4,0},{5,1},{6,2},{7,3},{8,12},{9,13},{10,... | collective-permute-start | bytes 2015240 | tf_op jit(solution)/shard_map/ppermute | solution.py:631
  33.3 18.3 %collective-permute-start.11 = (bf16[144,1152]{1,0:T(8,128)(2,1)S(1)}, bf16[144,1152]{1,0:T(8,128)(2,1)S(1)}, u32[]{:S(2)}, u32[]{:S(2)}) collective-permute-start(bf16[144,1152]{1,0:T(8,128)(2,1)S(1)} %pad_maximum_fusion.7), channel_id=1, source_target_pairs={{0,16},{1,17},{2,18},{3,19},{4,20},{5,21},{6,22},{7,23},{8,24},{9,... | collective-permute-start | bytes 995336 | tf_op jit(solution)/shard_map/ppermute | solution.py:631
  52.5 17.0 %collective-permute-start.12 = (bf16[288,1152]{1,0:T(8,128)(2,1)}, bf16[288,1152]{1,0:T(8,128)(2,1)}, u32[]{:S(2)}, u32[]{:S(2)}) collective-permute-start(bf16[288,1152]{1,0:T(8,128)(2,1)} %pad_maximum_fusion.3), channel_id=1, source_target_pairs={{0,8},{1,9},{2,10},{3,11},{4,12},{5,13},{6,14},{7,15},{8,0},{9,1},... | collective-permute-start | bytes 1990664 | tf_op jit(solution)/shard_map/ppermute | solution.py:631
  65.7 16.9 %collective-permute-start.6 = (bf16[2624,128]{1,0:T(8,128)(2,1)S(1)}, bf16[2624,128]{1,0:T(8,128)(2,1)S(1)}, u32[]{:S(2)}, u32[]{:S(2)}) collective-permute-start(bf16[2624,128]{1,0:T(8,128)(2,1)S(1)} %copy-done.24), channel_id=1, source_target_pairs={{0,2},{1,3},{2,0},{3,1},{4,6},{5,7},{6,4},{7,5},{8,10},{9,11},{10,... | collective-permute-start | bytes 2015240 | tf_op jit(solution)/shard_map/ppermute | solution.py:631
  66.2 16.9 %collective-permute-start.8 = (bf16[2624,128]{1,0:T(8,128)(2,1)S(1)}, bf16[2624,128]{1,0:T(8,128)(2,1)S(1)}, u32[]{:S(2)}, u32[]{:S(2)}) collective-permute-start(bf16[2624,128]{1,0:T(8,128)(2,1)S(1)} %copy-done.24), channel_id=1, source_target_pairs={{0,4},{1,5},{2,6},{3,7},{4,0},{5,1},{6,2},{7,3},{8,12},{9,13},{10,... | collective-permute-start | bytes 2015240 | tf_op jit(solution)/shard_map/ppermute | solution.py:631
  66.2 17.5 %collective-permute-start.9 = (bf16[2624,128]{1,0:T(8,128)(2,1)S(1)}, bf16[2624,128]{1,0:T(8,128)(2,1)S(1)}, u32[]{:S(2)}, u32[]{:S(2)}) collective-permute-start(bf16[2624,128]{1,0:T(8,128)(2,1)S(1)} %copy-done.26), channel_id=1, source_target_pairs={{0,4},{1,5},{2,6},{3,7},{4,0},{5,1},{6,2},{7,3},{8,12},{9,13},{10,... | collective-permute-start | bytes 2015240 | tf_op jit(solution)/shard_map/ppermute | solution.py:631
  71.5 34.4 %collective-permute-start.13 = (bf16[576,1152]{1,0:T(8,128)(2,1)}, bf16[576,1152]{1,0:T(8,128)(2,1)S(1)}, u32[]{:S(2)}, u32[]{:S(2)}) collective-permute-start(bf16[576,1152]{1,0:T(8,128)(2,1)} %constant_dynamic-update-slice_fusion.7.refs_2_), channel_id=1, source_target_pairs={{0,4},{1,5},{2,6},{3,7},{4,0},{5,1},{6,2},{7,3},{8,12},{9,13},{10,... | collective-permute-start | bytes 3981320 | tf_op jit(solution)/shard_map/ppermute | solution.py:631
  82.6 30.3 %collective-permute-start.14 = (bf16[576,1152]{1,0:T(8,128)(2,1)}, bf16[576,1152]{1,0:T(8,128)(2,1)}, u32[]{:S(2)}, u32[]{:S(2)}) collective-permute-start(bf16[576,1152]{1,0:T(8,128)(2,1)} %constant_dynamic-update-slice_fusion.7.refs_2_), channel_id=1, source_target_pairs={{0,1},{1,0},{2,3},{3,2},{4,5},{5,4},{6,7},{7,6},{8,9},{9,8},{10,11... | collective-permute-start | bytes 3981320 | tf_op jit(solution)/shard_map/ppermute | solution.py:631
  83.2 34.3 %collective-permute-start.15 = (bf16[576,1152]{1,0:T(8,128)(2,1)}, bf16[576,1152]{1,0:T(8,128)(2,1)}, u32[]{:S(2)}, u32[]{:S(2)}) collective-permute-start(bf16[576,1152]{1,0:T(8,128)(2,1)} %constant_dynamic-update-slice_fusion.7.refs_2_), channel_id=1, source_target_pairs={{0,2},{1,3},{2,0},{3,1},{4,6},{5,7},{6,4},{7,5},{8,10},{9,11},{10,... | collective-permute-start | bytes 3981320 | tf_op jit(solution)/shard_map/ppermute | solution.py:631
  112.9 35.9 %collective-permute-start.16 = (bf16[576,1152]{1,0:T(8,128)(2,1)}, bf16[576,1152]{1,0:T(8,128)(2,1)}, u32[]{:S(2)}, u32[]{:S(2)}) collective-permute-start(bf16[576,1152]{1,0:T(8,128)(2,1)} %collective-permute-done.14.refs_3_), channel_id=1, source_target_pairs={{0,2},{1,3},{2,0},{3,1},{4,6},{5,7},{6,4},{7,5},{8,10},{9,11},{10,... | collective-permute-start | bytes 3981320 | tf_op jit(solution)/shard_map/ppermute | solution.py:631
  113.4 35.4 %collective-permute-start.17 = (bf16[576,1152]{1,0:T(8,128)(2,1)}, bf16[576,1152]{1,0:T(8,128)(2,1)}, u32[]{:S(2)}, u32[]{:S(2)}) collective-permute-start(bf16[576,1152]{1,0:T(8,128)(2,1)} %collective-permute-done.14.refs_3_), channel_id=1, source_target_pairs={{0,4},{1,5},{2,6},{3,7},{4,0},{5,1},{6,2},{7,3},{8,12},{9,13},{10,... | collective-permute-start | bytes 3981320 | tf_op jit(solution)/shard_map/ppermute | solution.py:631
  117.5 31.3 %collective-permute-start.18 = (bf16[576,1152]{1,0:T(8,128)(2,1)}, bf16[576,1152]{1,0:T(8,128)(2,1)}, u32[]{:S(2)}, u32[]{:S(2)}) collective-permute-start(bf16[576,1152]{1,0:T(8,128)(2,1)} %collective-permute-done.15.refs_4_), channel_id=1, source_target_pairs={{0,4},{1,5},{2,6},{3,7},{4,0},{5,1},{6,2},{7,3},{8,12},{9,13},{10,... | collective-permute-start | bytes 3981320 | tf_op jit(solution)/shard_map/ppermute | solution.py:631
  119.3 29.5 %collective-permute-start.19 = (bf16[1,544,1152]{2,1,0:T(8,128)(2,1)S(1)}, bf16[1,544,1152]{2,1,0:T(8,128)(2,1)S(1)}, u32[]{:S(2)}, u32[]{:S(2)}) collective-permute-start(bf16[1,544,1152]{2,1,0:T(8,128)(2,1)S(1)} %get-tuple-element.311), channel_id=1, source_target_pairs={{0,1},{1,0},{2,3},{3,2},{4,5},{5,4},{6,7},{7,6},{8,9},{9,8},{10,11... | collective-permute-start | bytes 3760136 | tf_op jit(solution)/shard_map/ppermute | solution.py:631
  119.9 17.4 %collective-permute-start.20 = (bf16[144,1152]{1,0:T(8,128)(2,1)S(1)}, bf16[144,1152]{1,0:T(8,128)(2,1)S(1)}, u32[]{:S(2)}, u32[]{:S(2)}) collective-permute-start(bf16[144,1152]{1,0:T(8,128)(2,1)S(1)} %copy-done.31), channel_id=1, source_target_pairs={{0,16},{1,17},{2,18},{3,19},{4,20},{5,21},{6,22},{7,23},{8,24},{9,... | collective-permute-start | bytes 995336 | tf_op jit(solution)/shard_map/ppermute | solution.py:631
  152.9 18.5 %collective-permute-start.23 = (bf16[1296,128]{1,0:T(8,128)(2,1)S(1)}, bf16[1296,128]{1,0:T(8,128)(2,1)}, u32[]{:S(2)}, u32[]{:S(2)}) collective-permute-start(bf16[1296,128]{1,0:T(8,128)(2,1)S(1)} %maximum_maximum_fusion.3), channel_id=1, source_target_pairs={{0,16},{1,17},{2,18},{3,19},{4,20},{5,21},{6,22},{7,23},{8,24},{9,... | collective-permute-start | bytes 995336 | tf_op jit(solution)/shard_map/ppermute | solution.py:631
  155.4 37.5 %collective-permute-start.24 = (bf16[1,544,1152]{2,1,0:T(8,128)(2,1)}, bf16[1,544,1152]{2,1,0:T(8,128)(2,1)}, u32[]{:S(2)}, u32[]{:S(2)}) collective-permute-start(bf16[1,544,1152]{2,1,0:T(8,128)(2,1)} %get-tuple-element.310), channel_id=1, source_target_pairs={{0,1},{1,0},{2,3},{3,2},{4,5},{5,4},{6,7},{7,6},{8,9},{9,8},{10,11... | collective-permute-start | bytes 3760136 | tf_op jit(solution)/shard_map/ppermute | solution.py:631
  155.9 24.0 %collective-permute-start.22 = (bf16[288,1152]{1,0:T(8,128)(2,1)S(1)}, bf16[288,1152]{1,0:T(8,128)(2,1)}, u32[]{:S(2)}, u32[]{:S(2)}) collective-permute-start(bf16[288,1152]{1,0:T(8,128)(2,1)S(1)} %constant_dynamic-update-slice_fusion.10), channel_id=1, source_target_pairs={{0,8},{1,9},{2,10},{3,11},{4,12},{5,13},{6,14},{7,15},{8,0},{9,1},... | collective-permute-start | bytes 1990664 | tf_op jit(solution)/shard_map/ppermute | solution.py:631
  172.4 25.7 %collective-permute-start.26 = (bf16[2592,128]{1,0:T(8,128)(2,1)S(1)}, bf16[2592,128]{1,0:T(8,128)(2,1)S(1)}, u32[]{:S(2)}, u32[]{:S(2)}) collective-permute-start(bf16[2592,128]{1,0:T(8,128)(2,1)S(1)} %constant_dynamic-update-slice_fusion.14), channel_id=1, source_target_pairs={{0,8},{1,9},{2,10},{3,11},{4,12},{5,13},{6,14},{7,15},{8,0},{9,1},... | collective-permute-start | bytes 1990664 | tf_op jit(solution)/shard_map/ppermute | solution.py:631
  181.9 21.9 %collective-permute-start.27 = (bf16[576,1152]{1,0:T(8,128)(2,1)}, bf16[576,1152]{1,0:T(8,128)(2,1)}, u32[]{:S(2)}, u32[]{:S(2)}) collective-permute-start(bf16[576,1152]{1,0:T(8,128)(2,1)} %constant_dynamic-update-slice_fusion.12.refs_1_), channel_id=1, source_target_pairs={{0,4},{1,5},{2,6},{3,7},{4,0},{5,1},{6,2},{7,3},{8,12},{9,13},{10,... | collective-permute-start | bytes 3981320 | tf_op jit(solution)/shard_map/ppermute | solution.py:631
  198.3 46.5 %collective-permute-start.30 = (bf16[5184,128]{1,0:T(8,128)(2,1)S(1)}, bf16[5184,128]{1,0:T(8,128)(2,1)}, u32[]{:S(2)}, u32[]{:S(2)}) collective-permute-start(bf16[5184,128]{1,0:T(8,128)(2,1)S(1)} %constant_dynamic-update-slice_fusion.16.refs_2_), channel_id=1, source_target_pairs={{0,2},{1,3},{2,0},{3,1},{4,6},{5,7},{6,4},{7,5},{8,10},{9,11},{10,... | collective-permute-start | bytes 3981320 | tf_op jit(solution)/shard_map/ppermute | solution.py:631
  201.3 45.0 %collective-permute-start.25 = (bf16[576,1152]{1,0:T(8,128)(2,1)}, bf16[576,1152]{1,0:T(8,128)(2,1)}, u32[]{:S(2)}, u32[]{:S(2)}) collective-permute-start(bf16[576,1152]{1,0:T(8,128)(2,1)} %constant_dynamic-update-slice_fusion.12.refs_1_), channel_id=1, source_target_pairs={{0,1},{1,0},{2,3},{3,2},{4,5},{5,4},{6,7},{7,6},{8,9},{9,8},{10,11... | collective-permute-start | bytes 3981320 | tf_op jit(solution)/shard_map/ppermute | solution.py:631
  202.8 56.0 %collective-permute-start.28 = (bf16[576,1152]{1,0:T(8,128)(2,1)}, bf16[576,1152]{1,0:T(8,128)(2,1)}, u32[]{:S(2)}, u32[]{:S(2)}) collective-permute-start(bf16[576,1152]{1,0:T(8,128)(2,1)} %constant_dynamic-update-slice_fusion.12.refs_1_), channel_id=1, source_target_pairs={{0,2},{1,3},{2,0},{3,1},{4,6},{5,7},{6,4},{7,5},{8,10},{9,11},{10,... | collective-permute-start | bytes 3981320 | tf_op jit(solution)/shard_map/ppermute | solution.py:631
  203.3 58.7 %collective-permute-start.29 = (bf16[5184,128]{1,0:T(8,128)(2,1)S(1)}, bf16[5184,128]{1,0:T(8,128)(2,1)}, u32[]{:S(2)}, u32[]{:S(2)}) collective-permute-start(bf16[5184,128]{1,0:T(8,128)(2,1)S(1)} %constant_dynamic-update-slice_fusion.16.refs_2_), channel_id=1, source_target_pairs={{0,1},{1,0},{2,3},{3,2},{4,5},{5,4},{6,7},{7,6},{8,9},{9,8},{10,11... | collective-permute-start | bytes 3981320 | tf_op jit(solution)/shard_map/ppermute | solution.py:631
  203.8 58.2 %collective-permute-start.31 = (bf16[5184,128]{1,0:T(8,128)(2,1)S(1)}, bf16[5184,128]{1,0:T(8,128)(2,1)S(1)}, u32[]{:S(2)}, u32[]{:S(2)}) collective-permute-start(bf16[5184,128]{1,0:T(8,128)(2,1)S(1)} %constant_dynamic-update-slice_fusion.16.refs_2_), channel_id=1, source_target_pairs={{0,4},{1,5},{2,6},{3,7},{4,0},{5,1},{6,2},{7,3},{8,12},{9,13},{10,... | collective-permute-start | bytes 3981320 | tf_op jit(solution)/shard_map/ppermute | solution.py:631
  244.8 58.5 %collective-permute-start.36 = (bf16[5184,128]{1,0:T(8,128)(2,1)}, bf16[5184,128]{1,0:T(8,128)(2,1)}, u32[]{:S(2)}, u32[]{:S(2)}) collective-permute-start(bf16[5184,128]{1,0:T(8,128)(2,1)} %collective-permute-done.30.refs_4_), channel_id=1, source_target_pairs={{0,1},{1,0},{2,3},{3,2},{4,5},{5,4},{6,7},{7,6},{8,9},{9,8},{10,11... | collective-permute-start | bytes 3981320 | tf_op jit(solution)/shard_map/ppermute | solution.py:631
  246.3 61.4 %collective-permute-start.32 = (bf16[576,1152]{1,0:T(8,128)(2,1)}, bf16[576,1152]{1,0:T(8,128)(2,1)}, u32[]{:S(2)}, u32[]{:S(2)}) collective-permute-start(bf16[576,1152]{1,0:T(8,128)(2,1)} %collective-permute-done.25.refs_2_), channel_id=1, source_target_pairs={{0,2},{1,3},{2,0},{3,1},{4,6},{5,7},{6,4},{7,5},{8,10},{9,11},{10,... | collective-permute-start | bytes 3981320 | tf_op jit(solution)/shard_map/ppermute | solution.py:631
  258.8 48.9 %collective-permute-start.33 = (bf16[576,1152]{1,0:T(8,128)(2,1)}, bf16[576,1152]{1,0:T(8,128)(2,1)}, u32[]{:S(2)}, u32[]{:S(2)}) collective-permute-start(bf16[576,1152]{1,0:T(8,128)(2,1)} %collective-permute-done.25.refs_2_), channel_id=1, source_target_pairs={{0,4},{1,5},{2,6},{3,7},{4,0},{5,1},{6,2},{7,3},{8,12},{9,13},{10,... | collective-permute-start | bytes 3981320 | tf_op jit(solution)/shard_map/ppermute | solution.py:631
  262.0 45.7 %collective-permute-start.34 = (bf16[576,1152]{1,0:T(8,128)(2,1)}, bf16[576,1152]{1,0:T(8,128)(2,1)}, u32[]{:S(2)}, u32[]{:S(2)}) collective-permute-start(bf16[576,1152]{1,0:T(8,128)(2,1)} %collective-permute-done.28.refs_3_), channel_id=1, source_target_pairs={{0,4},{1,5},{2,6},{3,7},{4,0},{5,1},{6,2},{7,3},{8,12},{9,13},{10,... | collective-permute-start | bytes 3981320 | tf_op jit(solution)/shard_map/ppermute | solution.py:631
  307.7 6.9 collective-permute-start.35
  308.7 14.8 %collective-permute-start.39 = (bf16[5184,128]{1,0:T(8,128)(2,1)}, bf16[5184,128]{1,0:T(8,128)(2,1)}, u32[]{:S(2)}, u32[]{:S(2)}) collective-permute-start(bf16[5184,128]{1,0:T(8,128)(2,1)} %collective-permute-done.36.refs_5_), channel_id=1, source_target_pairs={{0,4},{1,5},{2,6},{3,7},{4,0},{5,1},{6,2},{7,3},{8,12},{9,13},{10,... | collective-permute-start | bytes 3981320 | tf_op jit(solution)/shard_map/ppermute | solution.py:631
  444.5 21.5 %collective-permute-start.40 = (bf16[4,4,1296,128]{3,2,1,0:T(8,128)(2,1)}, bf16[4,4,1296,128]{3,2,1,0:T(8,128)(2,1)}, u32[]{:S(2)}, u32[]{:S(2)}) collective-permute-start(bf16[4,4,1296,128]{3,2,1,0:T(8,128)(2,1)} %get-tuple-element.145), channel_id=1, source_target_pairs={{0,4},{1,5},{2,6},{3,7},{4,0},{5,1},{6,2},{7,3},{8,12},{9,13},{10,... | collective-permute-start | bytes 15925256 | tf_op jit(solution)/shard_map/ppermute | solution.py:631
  465.6 9.3 %collective-permute-start.41 = (bf16[576,4608]{1,0:T(8,128)(2,1)}, bf16[576,4608]{1,0:T(8,128)(2,1)}, u32[]{:S(2)}, u32[]{:S(2)}) collective-permute-start(bf16[576,4608]{1,0:T(8,128)(2,1)} %get-tuple-element.150), channel_id=1, source_target_pairs={{0,4},{1,5},{2,6},{3,7},{4,0},{5,1},{6,2},{7,3},{8,12},{9,13},{10,... | collective-permute-start | bytes 15925256 | tf_op jit(solution)/shard_map/ppermute | solution.py:631
  473.3 59.9 %collective-permute-start.42 = (bf16[4,2,1296,128]{3,2,1,0:T(8,128)(2,1)}, bf16[4,2,1296,128]{3,2,1,0:T(8,128)(2,1)}, u32[]{:S(2)}, u32[]{:S(2)}) collective-permute-start(bf16[4,2,1296,128]{3,2,1,0:T(8,128)(2,1)} %get-tuple-element.299), channel_id=1, source_target_pairs={{0,1},{1,0},{2,3},{3,2},{4,5},{5,4},{6,7},{7,6},{8,9},{9,8},{10,11... | collective-permute-start | bytes 7962632 | tf_op jit(solution)/shard_map/ppermute | solution.py:631
  481.5 60.7 %collective-permute-start.43 = (bf16[4,144,2304]{2,1,0:T(8,128)(2,1)}, bf16[4,144,2304]{2,1,0:T(8,128)(2,1)}, u32[]{:S(2)}, u32[]{:S(2)}) collective-permute-start(bf16[4,144,2304]{2,1,0:T(8,128)(2,1)} %get-tuple-element.297), channel_id=1, source_target_pairs={{0,2},{1,3},{2,0},{3,1},{4,6},{5,7},{6,4},{7,5},{8,10},{9,11},{10,... | collective-permute-start | bytes 7962632 | tf_op jit(solution)/shard_map/ppermute | solution.py:631
  535.9 68.7 %collective-permute-start.44 = (bf16[4,1296,128]{2,1,0:T(8,128)(2,1)S(1)}, bf16[4,1296,128]{2,1,0:T(8,128)(2,1)}, u32[]{:S(2)}, u32[]{:S(2)}) collective-permute-start(bf16[4,1296,128]{2,1,0:T(8,128)(2,1)S(1)} %get-tuple-element.309), channel_id=1, source_target_pairs={{0,2},{1,3},{2,0},{3,1},{4,6},{5,7},{6,4},{7,5},{8,10},{9,11},{10,... | collective-permute-start | bytes 3981320 | tf_op jit(solution)/shard_map/ppermute | solution.py:631
  546.4 60.0 %collective-permute-start.45 = (bf16[4,144,1152]{2,1,0:T(8,128)(2,1)}, bf16[4,144,1152]{2,1,0:T(8,128)(2,1)}, u32[]{:S(2)}, u32[]{:S(2)}) collective-permute-start(bf16[4,144,1152]{2,1,0:T(8,128)(2,1)} %get-tuple-element.307), channel_id=1, source_target_pairs={{0,1},{1,0},{2,3},{3,2},{4,5},{5,4},{6,7},{7,6},{8,9},{9,8},{10,11... | collective-permute-start | bytes 3981320 | tf_op jit(solution)/shard_map/ppermute | solution.py:631
  554.1 54.0 %collective-permute-start.46 = (bf16[1,544,1152]{2,1,0:T(8,128)(2,1)}, bf16[1,544,1152]{2,1,0:T(8,128)(2,1)}, u32[]{:S(2)}, u32[]{:S(2)}) collective-permute-start(bf16[1,544,1152]{2,1,0:T(8,128)(2,1)} %fusion.11), channel_id=1, source_target_pairs={{0,1},{1,0},{2,3},{3,2},{4,5},{5,4},{6,7},{7,6},{8,9},{9,8},{10,11... | collective-permute-start | bytes 3760136 | tf_op jit(solution)/shard_map/ppermute | solution.py:631
  615.9 41.2 %collective-permute-start.47 = (bf16[1,544,1152]{2,1,0:T(8,128)(2,1)}, bf16[1,544,1152]{2,1,0:T(8,128)(2,1)}, u32[]{:S(2)}, u32[]{:S(2)}) collective-permute-start(bf16[1,544,1152]{2,1,0:T(8,128)(2,1)} %fusion.12), channel_id=1, source_target_pairs={{0,1},{1,0},{2,3},{3,2},{4,5},{5,4},{6,7},{7,6},{8,9},{9,8},{10,11... | collective-permute-start | bytes 3760136 | tf_op jit(solution)/shard_map/ppermute | solution.py:631
  657.0 19.5 %collective-permute-start.48 = (bf16[576,4608]{1,0:T(8,128)(2,1)}, bf16[576,4608]{1,0:T(8,128)(2,1)}, u32[]{:S(2)}, u32[]{:S(2)}) collective-permute-start(bf16[576,4608]{1,0:T(8,128)(2,1)} %get-tuple-element.169), channel_id=1, source_target_pairs={{0,4},{1,5},{2,6},{3,7},{4,0},{5,1},{6,2},{7,3},{8,12},{9,13},{10,... | collective-permute-start | bytes 15925256 | tf_op jit(solution)/shard_map/ppermute | solution.py:631
  672.9 46.9 %collective-permute-start.65 = (bf16[2,1296,128]{2,1,0:T(8,128)(2,1)}, bf16[2,1296,128]{2,1,0:T(8,128)(2,1)}, u32[]{:S(2)}, u32[]{:S(2)}) collective-permute-start(bf16[2,1296,128]{2,1,0:T(8,128)(2,1)} %get-tuple-element.315), channel_id=1, source_target_pairs={{0,16},{1,17},{2,18},{3,19},{4,20},{5,21},{6,22},{7,23},{8,24},{9,... | collective-permute-start | bytes 1990664 | tf_op jit(solution)/shard_map/ppermute | solution.py:631
  674.0 48.9 %collective-permute-start.63 = (bf16[2,144,1152]{2,1,0:T(8,128)(2,1)}, bf16[2,144,1152]{2,1,0:T(8,128)(2,1)}, u32[]{:S(2)}, u32[]{:S(2)}) collective-permute-start(bf16[2,144,1152]{2,1,0:T(8,128)(2,1)} %get-tuple-element.317), channel_id=1, source_target_pairs={{0,8},{1,9},{2,10},{3,11},{4,12},{5,13},{6,14},{7,15},{8,0},{9,1},... | collective-permute-start | bytes 1990664 | tf_op jit(solution)/shard_map/ppermute | solution.py:631
  685.8 43.5 %collective-permute-start.50 = (bf16[4,72,2304]{2,1,0:T(8,128)(2,1)}, bf16[4,72,2304]{2,1,0:T(8,128)(2,1)}, u32[]{:S(2)}, u32[]{:S(2)}) collective-permute-start(bf16[4,72,2304]{2,1,0:T(8,128)(2,1)} %pad_maximum_fusion.1), channel_id=1, source_target_pairs={{0,1},{1,0},{2,3},{3,2},{4,5},{5,4},{6,7},{7,6},{8,9},{9,8},{10,11... | collective-permute-start | bytes 3981320 | tf_op jit(solution)/shard_map/ppermute | solution.py:631
  686.3 46.1 %collective-permute-start.49 = (bf16[4,72,2304]{2,1,0:T(8,128)(2,1)}, bf16[4,72,2304]{2,1,0:T(8,128)(2,1)}, u32[]{:S(2)}, u32[]{:S(2)}) collective-permute-start(bf16[4,72,2304]{2,1,0:T(8,128)(2,1)} %get-tuple-element.305), channel_id=1, source_target_pairs={{0,2},{1,3},{2,0},{3,1},{4,6},{5,7},{6,4},{7,5},{8,10},{9,11},{10,... | collective-permute-start | bytes 3981320 | tf_op jit(solution)/shard_map/ppermute | solution.py:631
  711.2 24.7 %collective-permute-start.51 = (bf16[4,4,648,128]{3,2,1,0:T(8,128)(2,1)}, bf16[4,4,648,128]{3,2,1,0:T(8,128)(2,1)}, u32[]{:S(2)}, u32[]{:S(2)}) collective-permute-start(bf16[4,4,648,128]{3,2,1,0:T(8,128)(2,1)} %get-tuple-element.175), channel_id=1, source_target_pairs={{0,4},{1,5},{2,6},{3,7},{4,0},{5,1},{6,2},{7,3},{8,12},{9,13},{10,... | collective-permute-start | bytes 7962632 | tf_op jit(solution)/shard_map/ppermute | solution.py:631
  723.0 85.1 %collective-permute-start.66 = (bf16[1,1296,128]{2,1,0:T(8,128)(2,1)}, bf16[1,1296,128]{2,1,0:T(8,128)(2,1)}, u32[]{:S(2)}, u32[]{:S(2)}) collective-permute-start(bf16[1,1296,128]{2,1,0:T(8,128)(2,1)} %get-tuple-element.331), channel_id=1, source_target_pairs={{0,8},{1,9},{2,10},{3,11},{4,12},{5,13},{6,14},{7,15},{8,0},{9,1},... | collective-permute-start | bytes 995336 | tf_op jit(solution)/shard_map/ppermute | solution.py:631
  725.2 84.0 %collective-permute-start.64 = (bf16[1,144,1152]{2,1,0:T(8,128)(2,1)}, bf16[1,144,1152]{2,1,0:T(8,128)(2,1)}, u32[]{:S(2)}, u32[]{:S(2)}) collective-permute-start(bf16[1,144,1152]{2,1,0:T(8,128)(2,1)} %get-tuple-element.333), channel_id=1, source_target_pairs={{0,16},{1,17},{2,18},{3,19},{4,20},{5,21},{6,22},{7,23},{8,24},{9,... | collective-permute-start | bytes 995336 | tf_op jit(solution)/shard_map/ppermute | solution.py:631
  731.1 17.2 %collective-permute-start.54 = (bf16[4,72,1152]{2,1,0:T(8,128)(2,1)S(1)}, bf16[4,72,1152]{2,1,0:T(8,128)(2,1)S(1)}, u32[]{:S(2)}, u32[]{:S(2)}) collective-permute-start(bf16[4,72,1152]{2,1,0:T(8,128)(2,1)S(1)} %get-tuple-element.321), channel_id=1, source_target_pairs={{0,2},{1,3},{2,0},{3,1},{4,6},{5,7},{6,4},{7,5},{8,10},{9,11},{10,... | collective-permute-start | bytes 1990664 | tf_op jit(solution)/shard_map/ppermute | solution.py:631
  734.2 18.3 %collective-permute-start.53 = (bf16[4,72,1152]{2,1,0:T(8,128)(2,1)S(1)}, bf16[4,72,1152]{2,1,0:T(8,128)(2,1)S(1)}, u32[]{:S(2)}, u32[]{:S(2)}) collective-permute-start(bf16[4,72,1152]{2,1,0:T(8,128)(2,1)S(1)} %get-tuple-element.323), channel_id=1, source_target_pairs={{0,1},{1,0},{2,3},{3,2},{4,5},{5,4},{6,7},{7,6},{8,9},{9,8},{10,11... | collective-permute-start | bytes 1990664 | tf_op jit(solution)/shard_map/ppermute | solution.py:631
  739.0 48.9 %collective-permute-start.55 = (bf16[4,2,328,128]{3,2,0,1:T(8,128)(2,1)S(1)}, bf16[4,2,328,128]{3,2,0,1:T(8,128)(2,1)S(1)}, u32[]{:S(2)}, u32[]{:S(2)}) collective-permute-start(bf16[4,2,328,128]{3,2,0,1:T(8,128)(2,1)S(1)} %bitcast.226), channel_id=1, source_target_pairs={{0,1},{1,0},{2,3},{3,2},{4,5},{5,4},{6,7},{7,6},{8,9},{9,8},{10,11... | collective-permute-start | bytes 2015240 | tf_op jit(solution)/shard_map/ppermute | solution.py:631
  748.3 16.6 %collective-permute-start.57 = (bf16[4,2,320,128]{3,2,0,1:T(8,128)(2,1)S(1)}, bf16[4,2,320,128]{3,2,0,1:T(8,128)(2,1)S(1)}, u32[]{:S(2)}, u32[]{:S(2)}) collective-permute-start(bf16[4,2,320,128]{3,2,0,1:T(8,128)(2,1)S(1)} %bitcast.227), channel_id=1, source_target_pairs={{0,2},{1,3},{2,0},{3,1},{4,6},{5,7},{6,4},{7,5},{8,10},{9,11},{10,... | collective-permute-start | bytes 1966088 | tf_op jit(solution)/shard_map/ppermute | solution.py:631
  752.5 13.7 %collective-permute-start.52 = (f32[3,2,24,1152]{3,2,1,0:T(8,128)S(1)}, f32[3,2,24,1152]{3,2,1,0:T(8,128)S(1)}, u32[]{:S(2)}, u32[]{:S(2)}) collective-permute-start(f32[3,2,24,1152]{3,2,1,0:T(8,128)S(1)} %pad_maximum_fusion.4), channel_id=1, source_target_pairs={{2,1},{6,5},{10,9},{14,13},{18,17},{22,21},{26,25},{30,29}} | collective-permute-start | bytes 1990664 | tf_op jit(solution)/shard_map/ppermute | solution.py:638
  765.0 35.0 %collective-permute-start.59 = (bf16[2,144,1152]{2,1,0:T(8,128)(2,1)S(1)}, bf16[2,144,1152]{2,1,0:T(8,128)(2,1)S(1)}, u32[]{:S(2)}, u32[]{:S(2)}) collective-permute-start(bf16[2,144,1152]{2,1,0:T(8,128)(2,1)S(1)} %get-tuple-element.319), channel_id=1, source_target_pairs={{0,16},{1,17},{2,18},{3,19},{4,20},{5,21},{6,22},{7,23},{8,24},{9,... | collective-permute-start | bytes 1990664 | tf_op jit(solution)/shard_map/ppermute | solution.py:631
  766.2 27.0 %collective-permute-start.58 = (bf16[4,320,128]{2,1,0:T(8,128)(2,1)S(1)}, bf16[4,320,128]{2,1,0:T(8,128)(2,1)S(1)}, u32[]{:S(2)}, u32[]{:S(2)}) collective-permute-start(bf16[4,320,128]{2,1,0:T(8,128)(2,1)S(1)} %dynamic-slice_bitcast_fusion.9), channel_id=1, source_target_pairs={{0,1},{1,0},{2,3},{3,2},{4,5},{5,4},{6,7},{7,6},{8,9},{9,8},{10,11... | collective-permute-start | bytes 983048 | tf_op jit(solution)/shard_map/ppermute | solution.py:631
  788.1 8.1 collective-permute-start.56
  796.5 10.7 %collective-permute-start.60 = (bf16[2,648,128]{2,1,0:T(8,128)(2,1)S(1)}, bf16[2,648,128]{2,1,0:T(8,128)(2,1)S(1)}, u32[]{:S(2)}, u32[]{:S(2)}) collective-permute-start(bf16[2,648,128]{2,1,0:T(8,128)(2,1)S(1)} %get-tuple-element.337), channel_id=1, source_target_pairs={{0,8},{1,9},{2,10},{3,11},{4,12},{5,13},{6,14},{7,15},{8,0},{9,1},... | collective-permute-start | bytes 995336 | tf_op jit(solution)/shard_map/ppermute | solution.py:631
  800.3 14.4 %collective-permute-start.62 = (bf16[1,144,1152]{2,1,0:T(8,128)(2,1)S(1)}, bf16[1,144,1152]{2,1,0:T(8,128)(2,1)S(1)}, u32[]{:S(2)}, u32[]{:S(2)}) collective-permute-start(bf16[1,144,1152]{2,1,0:T(8,128)(2,1)S(1)} %get-tuple-element.335), channel_id=1, source_target_pairs={{0,8},{1,9},{2,10},{3,11},{4,12},{5,13},{6,14},{7,15},{8,0},{9,1},... | collective-permute-start | bytes 995336 | tf_op jit(solution)/shard_map/ppermute | solution.py:631
  808.1 12.4 %collective-permute-start.61 = (bf16[1,648,128]{2,1,0:T(8,128)(2,1)}, bf16[1,648,128]{2,1,0:T(8,128)(2,1)}, u32[]{:S(2)}, u32[]{:S(2)}) collective-permute-start(bf16[1,648,128]{2,1,0:T(8,128)(2,1)} %get-tuple-element.347), channel_id=1, source_target_pairs={{0,16},{1,17},{2,18},{3,19},{4,20},{5,21},{6,22},{7,23},{8,24},{9,... | collective-permute-start | bytes 497672 | tf_op jit(solution)/shard_map/ppermute | solution.py:631
  (82 other events, 1025.4 us)
Sparse Core Ops, SparseCore 0:
  728.5 73.3 all-gather.1

commit v4 on v3

--- a/solution.py
+++ b/solution.py
@@ -11,6 +11,7 @@
 epsilon = 1e-05
 masked_score = -1e30
 VMEM_BYTES = 60 * 1024 * 1024
+FORWARD_HEADS, BACKWARD_HEADS = 1, 2
 def nt_dot(left_side, right_side):
     return lax.dot_general(
         left_side, right_side, (((1,), (1,)), ((), ())), preferred_element_type=jnp.float32
@@ -50,8 +51,8 @@
     return jnp.concatenate([head_ref[head][:, :HEAD_DIM] for head in range(HEADS)], axis=1)
 
 
-def chunk_of(rows):
-    for count in (4, 2, 1):
+def chunk_of(rows, most=4):
+    for count in (most, 2, 1):
         if rows % (count * 16) == 0:
             return rows // count
     return rows
@@ -68,7 +69,7 @@
     scale = HEAD_DIM ** (-0.5)
     query_ids = qid_ref[0]
 
-    def one_head(head, carry):
+    def one_head(head, score, prob):
         query = qh[head]
         top = jnp.full((1, query.shape[0]), masked_score, jnp.float32)
         for start in range(0, key_rows, step):
@@ -84,9 +85,13 @@
         mixed = tn_dot(vh[head], prob[...]) / total
         qh[head] = mixed.T.astype(jnp.bfloat16)
         lse_ref[0, pl.ds(head, 1)] = top + jnp.log(total)
+
+    def some_heads(index, carry):
+        for lane in range(FORWARD_HEADS):
+            one_head(index * FORWARD_HEADS + lane, score.at[lane], prob.at[lane])
         return carry
 
-    lax.fori_loop(0, HEADS, one_head, 0)
+    lax.fori_loop(0, HEADS // FORWARD_HEADS, some_heads, 0)
     out_ref[0] = join_heads(qh)
 
 
@@ -118,8 +123,8 @@
             pltpu.VMEM((HEADS, width, LANES), jnp.bfloat16),
             pltpu.VMEM((HEADS, key_rows, LANES), jnp.bfloat16),
             pltpu.VMEM((HEADS, key_rows, LANES), jnp.bfloat16),
-            pltpu.VMEM((key_rows, width), jnp.float32),
-            pltpu.VMEM((key_rows, width), jnp.bfloat16),
+            pltpu.VMEM((FORWARD_HEADS, key_rows, width), jnp.float32),
+            pltpu.VMEM((FORWARD_HEADS, key_rows, width), jnp.bfloat16),
         ],
         input_output_aliases={5: 0, 6: 1} if old else {},
         compiler_params=pltpu.CompilerParams(vmem_limit_bytes=VMEM_BYTES),
@@ -142,11 +147,11 @@
     split_heads(o_ref[0], oh)
     split_heads(g_ref[0], gh)
     key_rows = kh.shape[1]
-    step = chunk_of(key_rows)
+    step = chunk_of(key_rows, 2)
     scale = HEAD_DIM ** (-0.5)
     query_ids = qid_ref[0]
 
-    def one_head(head, carry):
+    def one_head(head, prob, slope):
         query = qh[head]
         grad = gh[head]
         level = lse_ref[0, pl.ds(head, 1)]
@@ -165,9 +170,13 @@
         vh[head] = value_grad.astype(jnp.bfloat16)
         kh[head] = key_grad.astype(jnp.bfloat16)
         qh[head] = query_grad.T.astype(jnp.bfloat16)
+
+    def some_heads(index, carry):
+        for lane in range(BACKWARD_HEADS):
+            one_head(index * BACKWARD_HEADS + lane, prob.at[lane], slope.at[lane])
         return carry
 
-    lax.fori_loop(0, HEADS, one_head, 0)
+    lax.fori_loop(0, HEADS // BACKWARD_HEADS, some_heads, 0)
     dq_ref[0] = join_heads(qh)
     dkv_ref[0, :, :features] = join_heads(kh)
     dkv_ref[0, :, features:] = join_heads(vh)
@@ -210,8 +219,8 @@
             pltpu.VMEM((HEADS, key_rows, LANES), jnp.bfloat16),
             pltpu.VMEM((HEADS, width, LANES), jnp.bfloat16),
             pltpu.VMEM((HEADS, width, LANES), jnp.bfloat16),
-            pltpu.VMEM((key_rows, width), jnp.bfloat16),
-            pltpu.VMEM((key_rows, width), jnp.bfloat16),
+            pltpu.VMEM((BACKWARD_HEADS, key_rows, width), jnp.bfloat16),
+            pltpu.VMEM((BACKWARD_HEADS, key_rows, width), jnp.bfloat16),
         ],
         input_output_aliases={8: 0, 9: 1} if old else {},
         compiler_params=pltpu.CompilerParams(vmem_limit_bytes=VMEM_BYTES),
@@ -1099,7 +1108,7 @@
         mixed_piece = jnp.concatenate([qkv_weight, proj_weight], axis=1)
         mixed_way = Gather(grid, tie(mixed_piece, skip_way.column))
         mixed_way.first()
-        mixed_way.second()
+        mixed_way.second(skip_way.over_x, skip_way.over_y)
         mixed_way.last()
         mixed_way.spread()
         mixed_way.forward("y")
@@ -1125,8 +1134,8 @@
     ) = vectors
     joined_inputs = inputs
     if grid.square:
-        joined_inputs = tie(inputs, skip_way.over_x, skip_way.over_y)
-        segments = tie(segments, skip_way.over_x, skip_way.over_y)
+        joined_inputs = tie(inputs, skip_way.column)
+        segments = tie(segments, skip_way.column)
     items = Items(grid, segments, occupied, own_rows, all_rows)
     query_ids, used = items.of(grid.seq_index)
     key_ids = jnp.concatenate([query_ids, far_ids(grid, items)], axis=1)
@@ -1390,14 +1399,16 @@
 
     moved = items.moved[..., None] & (grid.seq_index == half - 1)
     results = [tie(output, skip_grad), input_grad, skip_grad]
-    tails = jnp.stack([value[:, own_rows:].astype(jnp.float32) for value in results])
+    edge = own_rows - 16
+    tails = jnp.stack([value[:, all_rows - 16 :].astype(jnp.float32) for value in results])
     tails = grid.shift(tails, half, half - 1)
+    if grid.square:
+        tails = tie(tails, skip_way.sent)
 
     def settle(place):
         own = results[place][:, :own_rows]
-        tail = own[:, own_rows - halo_rows :]
-        tail = jnp.where(moved, tails[place].astype(own.dtype), tail)
-        return lax.dynamic_update_slice_in_dim(own, tail, own_rows - halo_rows, 1)
+        tail = jnp.where(moved[:, -16:], tails[place].astype(own.dtype), own[:, edge:])
+        return lax.dynamic_update_slice_in_dim(own, tail, edge, 1)
 
     return (
         settle(0),

time: 841 us -> 819 us (0.974)
  starting transfers between devices: 71 us -> 53.6 us
    ppermute x65, starting transfers between devices: 68.6 us -> 51.5 us  [send(): return lax.ppermute(value, ('batch', 'seq'), pairs)]
    unnamed x182 -> x166, local copies, waits for them, and re-layouts: 19.8 us -> 19.4 us
  transfers between devices with their start and end apart: 68 -> 68, of which waited for: 23 -> 24; matrix products, arithmetic and copies ran while one was open for 24% -> 25% of each run, Pallas kernels for 32% -> 32%
where the time goes in v4:
time: 819 us; the launch traced here: 810 us
  Pallas kernels  382 us (47%)
  waiting for transfers between devices  139 us (17%)
  matrix products  81.8 us (10%)
  other arithmetic  78.7 us (10%)
  local copies, waits for them, and re-layouts  58.8 us (7%)
  starting transfers between devices  53.6 us (7%)
  between operations  16 us (2%)
    ppermute x65, waiting for transfers between devices, send(): return lax.ppermute(value, ('batch', 'seq'), pairs)  139 us
    pallas_call x2, Pallas kernels, attend_back(): pl.pallas_call(attend_back_kernel, grid=(1,), in_specs=[wide, pl.BlockSpe...  93.5 us
    pallas_call x1, Pallas kernels, middle_block(): pl.pallas_call(middle_kernel, grid=(blocks, steps), in_specs=[by_rows, by...  83.7 us
    pallas_call x2, Pallas kernels, attend(): pl.pallas_call(attend_kernel, grid=(1,), in_specs=[wide, pl.BlockSpec((1,...  66.5 us
    ppermute x65, starting transfers between devices, send(): return lax.ppermute(value, ('batch', 'seq'), pairs)  51.5 us
    dot_general x5, matrix products, dot_last(): lax.dot_general(left_side, right_side, (((2,), (0,)), ((), ())), preferre...  43.8 us
    pallas_call x2, Pallas kernels, tall_grad(): pl.pallas_call(lambda *refs: tall_grad_kernel(groups, *refs), grid_spec=p...  41 us
    pallas_call x1, Pallas kernels, mixed_grad(): pl.pallas_call(lambda *refs: mixed_grad_kernel(outer, *refs), grid_spec=p...  39.5 us
  transfers between devices with their start and end apart: 68, of which 24 were waited for; matrix products, arithmetic and copies ran while one was open for 25% of the time, Pallas kernels for 32%

profile of v4, /device:TPU:0, one launch (start us, length us, event | category | flops | bytes accessed | tf_op | source)
XLA Modules:
  0.0 810.3 jit_solution(5475510434009486907)
XLA Ops:
  10.6 3.0 collective-permute-start
  13.6 2.6 collective-permute-start.1
  25.7 3.4 collective-permute-done.1
  36.1 2.1 collective-permute-start.11
  41.4 8.1 maximum_maximum_fusion
  50.2 4.3 collective-permute-done.11
  58.0 13.1 %collective-permute-done.12 = bf16[288,1152]{1,0:T(8,128)(2,1)S(1)} collective-permute-done((bf16[288,1152]{1,0:T(8,128)(2,1)S(1)}, bf16[288,1152]{1,0:T(8,128)(2,1)S(1)}, u32[]{:S(2)}, u32[]{:S(2)}) %collective-permute-start.12) | collective-permute-done | bytes 663584 | tf_op jit(solution)/shard_map/ppermute | solution.py:640
  74.0 2.0 collective-permute-done.10.refs_9_
  76.9 7.5 join_skip.1
  84.3 11.6 %fusion.6 = f32[2,544,1152]{2,1,0:T(8,128)} fusion(bf16[2,544,2304]{2,1,0:T(8,128)(2,1)} %maximum_maximum_fusion, bf16[2304,1152]{1,0:T(8,128)(2,1)} %join_skip.1, f32[1152]{0:T(1024)S(1)} %reshape.366), kind=kOutput, calls=%fused_computation.22 | convolution fusion | flops 5776809984 | bytes 15340032 | tf_op jit(solution)/shard_map/dot_general | solution.py:590
  95.9 3.2 reduce_sum.90
  99.2 4.7 collective-permute-done.14.refs_3_
  104.3 3.1 multiply_reduce_fusion.2
  112.8 15.5 %collective-permute-done.20 = bf16[144,1152]{1,0:T(8,128)(2,1)S(1)} collective-permute-done((bf16[144,1152]{1,0:T(8,128)(2,1)S(1)}, bf16[144,1152]{1,0:T(8,128)(2,1)S(1)}, u32[]{:S(2)}, u32[]{:S(2)}) %collective-permute-start.20) | collective-permute-done | bytes 331808 | tf_op jit(solution)/shard_map/ppermute | solution.py:640
  128.3 11.5 %collective-permute-done.19 = bf16[1,544,1152]{2,1,0:T(8,128)(2,1)S(1)} collective-permute-done((bf16[1,544,1152]{2,1,0:T(8,128)(2,1)S(1)}, bf16[1,544,1152]{2,1,0:T(8,128)(2,1)S(1)}, u32[]{:S(2)}, u32[]{:S(2)}) %collective-permute-start.19) | collective-permute-done | bytes 1253408 | tf_op jit(solution)/shard_map/ppermute | solution.py:640
  143.9 2.3 collective-permute-start.23
  148.5 9.9 %join_mixed.1 = (bf16[1152,1152]{1,0:T(8,128)(2,1)}, bf16[1152,2304]{1,0:T(8,128)(2,1)}, bf16[1152,1152]{1,0:T(8,128)(2,1)}) custom-call(s32[4]{0:T(128)} %shift-right-arithmetic_or_fusion.refs_0_, s32[8]{0:T(128)} %xor_add_fusion.1.refs_1_, bf16[576,1152]{1,0:T(8,128)(2,1)} %constant_dynamic-update-slice_fusion.7.refs_2_, ...), custom_call_target="tpu_custom_call" | custom-call | bytes 21233664 | tf_op jit(solution)/shard_map/join_mixed/pallas_call | solution.py:726
  158.5 3.8 collective-permute-done.23
  164.5 6.7 collective-permute-done.22
  173.2 11.2 %convolution_convert_fusion.own_ref = bf16[2,544,2304]{2,1,0:T(8,128)(2,1)} fusion(bf16[2,544,1152]{2,1,0:T(8,128)(2,1)S(1)} %add_convert_fusion.7, bf16[1152,2304]{1,0:T(8,128)(2,1)} %get-tuple-element.125), kind=kOutput, calls=%fused_computation.3 | convolution fusion | flops 5778063360 | bytes 12828672 | tf_op jit(solution)/shard_map/dot_general | solution.py:590
  184.4 5.0 convolution_convert_fusion.3.q_ref
  195.1 7.8 fusion.9.far_ref
  202.8 33.4 %attend.2 = (bf16[2,544,1152]{2,1,0:T(8,128)(2,1)}, f32[2,16,544]{2,1,0:T(8,128)}) custom-call(bf16[2,544,1152]{2,1,0:T(8,128)(2,1)} %convolution_convert_fusion.3.q_ref, bf16[2,544,2304]{2,1,0:T(8,128)(2,1)} %convolution_convert_fusion.own_ref, bf16[1,544,2304]{2,1,0:T(8,128)(2,1)} %fusion.9.far_ref, s32[2,1,544]{2,1,0:T(1,128)} %add_select_fusion.qid_ref, ...), custom_call_target="tpu_custom_call" | custom-call | flops 4848615424 | bytes 7520256 | tf_op jit(solution)/shard_map/attend/pallas_call | solution.py:106
  239.0 11.1 %collective-permute-done.28.refs_3_ = bf16[576,1152]{1,0:T(8,128)(2,1)} collective-permute-done((bf16[576,1152]{1,0:T(8,128)(2,1)}, bf16[576,1152]{1,0:T(8,128)(2,1)}, u32[]{:S(2)}, u32[]{:S(2)}) %collective-permute-start.28) | collective-permute-done | bytes 1327136 | tf_op jit(solution)/shard_map/ppermute | solution.py:640
  250.1 3.0 collective-permute-done.29.refs_3_
  253.0 8.3 %fusion.10.far_ref = bf16[1,544,2304]{2,1,0:T(8,128)(2,1)} fusion(bf16[1152,2304]{1,0:T(8,128)(2,1)} %get-tuple-element.125, bf16[1,544,1152]{2,1,0:T(8,128)(2,1)} %collective-permute-done.24), kind=kOutput, calls=%fused_computation.28 | convolution fusion | flops 2889031680 | bytes 9068544 | tf_op jit(solution)/shard_map/dot_general | solution.py:590
  261.3 33.1 %attend.3 = (bf16[2,544,1152]{2,1,0:T(8,128)(2,1)}, f32[2,16,544]{2,1,0:T(8,128)}) custom-call(bf16[2,544,1152]{2,1,0:T(8,128)(2,1)} %convolution_convert_fusion.3.q_ref, bf16[2,544,2304]{2,1,0:T(8,128)(2,1)} %convolution_convert_fusion.own_ref, bf16[1,544,2304]{2,1,0:T(8,128)(2,1)} %fusion.10.far_ref, ...), custom_call_target="tpu_custom_call", output_to_operand_aliasing={{0}: (5, {}), {1}: (6, {})} | custom-call | flops 4848615424 | bytes 7520256 | tf_op jit(solution)/shard_map/attend/pallas_call | solution.py:106
  305.8 8.9 %place_blocks.1 = bf16[32,144,1152]{2,1,0:T(8,128)(2,1)} custom-call(s32[32]{0:T(128)} %xor_add_fusion.refs_0_, bf16[576,1152]{1,0:T(8,128)(2,1)} %constant_dynamic-update-slice_fusion.12.refs_1_, bf16[576,1152]{1,0:T(8,128)(2,1)} %collective-permute-done.25.refs_2_, bf16[576,1152]{1,0:T(8,128)(2,1)} %collective-permute-done.28.refs_3_, ...), custom_call_target="tpu_custom_call" | custom-call | bytes 21233664 | tf_op jit(solution)/shard_map/place_blocks/pallas_call | solution.py:774
  314.7 11.0 %join_down.1 = bf16[4608,1152]{1,0:T(8,128)(2,1)} custom-call(s32[4]{0:T(128)} %shift-right-arithmetic_or_fusion.refs_0_, s32[8]{0:T(128)} %xor_add_fusion.1.refs_1_, bf16[5184,128]{1,0:T(8,128)(2,1)} %copy-done.9, bf16[5184,128]{1,0:T(8,128)(2,1)} %collective-permute-done.29.refs_3_, bf16[5184,128]{1,0:T(8,128)(2,1)} %collective-permute-done.30.refs_4_, ...), custom_call_target="tpu_custom_call" | custom-call | bytes 21233664 | tf_op jit(solution)/shard_map/join_down/pallas_call | solution.py:726
  325.8 83.7 %middle_block.1 = (bf16[1088,1152]{1,0:T(8,128)(2,1)}, bf16[1088,1152]{1,0:T(8,128)(2,1)}, bf16[1088,4608]{1,0:T(8,128)(2,1)}, bf16[1088,4608]{1,0:T(8,128)(2,1)...) custom-call(f32[1088,1152]{1,0:T(8,128)} %bitcast.196, ...), custom_call_target="tpu_custom_call" | custom-call | flops 51980009472 | bytes 135069696 | tf_op jit(solution)/shard_map/middle_block/pallas_call | solution.py:497
  409.4 26.0 %down_weight_grad.1 = (bf16[4,4,1296,128]{3,2,1,0:T(8,128)(2,1)}, bf16[4,4,1296,128]{3,2,1,0:T(8,128)(2,1)}) custom-call(s32[1]{0:T(128)} %bitcast.26.refs_0_, bf16[1088,4608]{1,0:T(8,128)(2,1)} %get-tuple-element.147.refs_1_, bf16[1088,1152]{1,0:T(8,128)(2,1)} %broadcast_select_fusion.refs_2_), custom_call_target="tpu_custom_call" | custom-call | flops 11551113216 | bytes 20643840 | tf_op jit(solution)/shard_map/down_weight_grad/pallas_call | solution.py:308
  435.5 21.1 %hidden_weight_grad.1 = (bf16[576,4608]{1,0:T(8,128)(2,1)}, bf16[576,4608]{1,0:T(8,128)(2,1)}) custom-call(s32[1]{0:T(128)} %bitcast.26.refs_0_, bf16[1088,1152]{1,0:T(8,128)(2,1)} %get-tuple-element.149.refs_1_, bf16[1088,4608]{1,0:T(8,128)(2,1)} %get-tuple-element.150.refs_2_), custom_call_target="tpu_custom_call" | custom-call | flops 11551113216 | bytes 13123584 | tf_op jit(solution)/shard_map/hidden_weight_grad/pallas_call | solution.py:265
  457.1 5.5 add_convert_fusion.2
  466.0 3.8 add_convert_fusion.1
  469.8 2.7 constant_dynamic-slice_fusion.26
  473.7 46.7 %attend_back.2 = (bf16[2,544,1152]{2,1,0:T(8,128)(2,1)}, bf16[2,1088,2304]{2,1,0:T(8,128)(2,1)}) custom-call(bf16[2,544,1152]{2,1,0:T(8,128)(2,1)} %convolution_convert_fusion.3.q_ref, bf16[2,544,2304]{2,1,0:T(8,128)(2,1)} %convolution_convert_fusion.own_ref, bf16[1,544,2304]{2,1,0:T(8,128)(2,1)} %fusion.9.far_ref, ...), custom_call_target="tpu_custom_call" | custom-call | flops 12121538560 | bytes 15040512 | tf_op jit(solution)/shard_map/attend_back/pallas_call | solution.py:194
  520.3 3.9 collective-permute-done.42
  524.3 2.4 add_convert_fusion.5
  528.1 5.2 collective-permute-done.43
  533.3 2.5 add_convert_fusion.4
  539.0 6.2 fusion.11
  545.7 46.8 %attend_back.3 = (bf16[2,544,1152]{2,1,0:T(8,128)(2,1)}, bf16[2,1088,2304]{2,1,0:T(8,128)(2,1)}) custom-call(bf16[2,544,1152]{2,1,0:T(8,128)(2,1)} %convolution_convert_fusion.3.q_ref, bf16[2,544,2304]{2,1,0:T(8,128)(2,1)} %convolution_convert_fusion.own_ref, bf16[1,544,2304]{2,1,0:T(8,128)(2,1)} %fusion.10.far_ref, ...), custom_call_target="tpu_custom_call", output_to_operand_aliasing={{0}: (8, {}), {1}: (9, {})} | custom-call | flops 12121538560 | bytes 15040512 | tf_op jit(solution)/shard_map/attend_back/pallas_call | solution.py:194
  596.0 7.7 fusion.12
  605.2 39.5 %mixed_weight_grad.1 = (bf16[576,4608]{1,0:T(8,128)(2,1)}, bf16[576,4608]{1,0:T(8,128)(2,1)}) custom-call(s32[1]{0:T(128)} %bitcast.26.refs_0_, bf16[1088,1152]{1,0:T(8,128)(2,1)} %bitcast.206, bf16[544,1152]{1,0:T(8,128)(2,1)} %bitcast.239, bf16[544,1152]{1,0:T(8,128)(2,1)} %bitcast.17.refs_3_, bf16[1088,1152]{1,0:T(8,128)(2,1)} %bitcast.245, ...), custom_call_target="tpu_custom_call" | custom-call | flops 17326669824 | bytes 35684352 | tf_op jit(solution)/shard_map/mixed_weight_grad/pallas_call | solution.py:380
  645.3 10.3 %fusion = f32[2,544,1152]{2,1,0:T(8,128)S(1)} fusion(bf16[1152,2304]{1,0:T(8,128)(2,1)} %get-tuple-element.125, bf16[2,1088,2304]{2,1,0:T(8,128)(2,1)} %get-tuple-element.174), kind=kOutput, calls=%fused_computation.4 | convolution fusion | flops 5775556608 | bytes 15335424 | tf_op jit(solution)/shard_map/dot_general | solution.py:596
  655.6 3.8 convolution_add_fusion
  661.8 2.1 collective-permute-start.63
  663.9 5.4 add_convert_fusion
  674.8 4.8 multiply_reduce_fusion
  679.6 4.7 convert_reduce_fusion
  684.3 15.0 %skip_weight_grad.1 = (bf16[4,4,648,128]{3,2,1,0:T(8,128)(2,1)}, bf16[4,4,648,128]{3,2,1,0:T(8,128)(2,1)}) custom-call(s32[1]{0:T(128)} %bitcast.26.refs_0_, bf16[1088,2304]{1,0:T(8,128)(2,1)} %bitcast.215, bf16[1088,1152]{1,0:T(8,128)(2,1)} %bitcast.225), custom_call_target="tpu_custom_call" | custom-call | flops 5775556608 | bytes 10321920 | tf_op jit(solution)/shard_map/skip_weight_grad/pallas_call | solution.py:308
  699.4 6.3 fusion.14
  705.7 2.2 copy-done.5
  713.5 2.8 collective-permute-start.64
  724.1 2.6 add_convert_fusion.3
  728.9 3.8 fusion.13
  732.8 4.1 collective-permute-done.54
  738.0 2.8 collective-permute-done.53
  741.4 12.1 %collective-permute-done.57 = bf16[4,2,320,128]{3,2,0,1:T(8,128)(2,1)S(1)} collective-permute-done((bf16[4,2,320,128]{3,2,0,1:T(8,128)(2,1)S(1)}, bf16[4,2,320,128]{3,2,0,1:T(8,128)(2,1)S(1)}, u32[]{:S(2)}, u32[]{:S(2)}) %collective-permute-start.57) | collective-permute-done | bytes 655392 | tf_op jit(solution)/shard_map/ppermute | solution.py:640
  757.6 4.8 collective-permute-done.58
  765.1 7.8 collective-permute-done.59
  773.3 7.0 collective-permute-done.60
  783.6 2.8 add_bitcast_fusion
  786.6 8.9 %collective-permute-done.62 = bf16[1,144,1152]{2,1,0:T(8,128)(2,1)S(1)} collective-permute-done((bf16[1,144,1152]{2,1,0:T(8,128)(2,1)S(1)}, bf16[1,144,1152]{2,1,0:T(8,128)(2,1)S(1)}, u32[]{:S(2)}, u32[]{:S(2)}) %collective-permute-start.62) | collective-permute-done | bytes 331808 | tf_op jit(solution)/shard_map/ppermute | solution.py:640
  (425 shorter events, 125.7 us)
Async XLA Ops:
  7.3 791.1 %all-gather.2.cloned.1.call-start = ((), (), s32[]{:S(2)}) async-start(), calls=%async_computation | async-start | bytes 1757184 | tf_op jit(solution)/shard_map/all_gather | solution.py:992
  10.6 13.5 %collective-permute-start = (bf16[648,128]{1,0:T(8,128)(2,1)}, bf16[648,128]{1,0:T(8,128)(2,1)}, u32[]{:S(2)}, u32[]{:S(2)}) collective-permute-start(bf16[648,128]{1,0:T(8,128)(2,1)} %maximum_maximum_fusion.4), channel_id=1, source_target_pairs={{0,8},{1,9},{2,10},{3,11},{4,12},{5,13},{6,14},{7,15},{8,0},{9,1},... | collective-permute-start | bytes 497672 | tf_op jit(solution)/shard_map/ppermute | solution.py:640
  13.6 15.5 %collective-permute-start.1 = (bf16[648,128]{1,0:T(8,128)(2,1)}, bf16[648,128]{1,0:T(8,128)(2,1)}, u32[]{:S(2)}, u32[]{:S(2)}) collective-permute-start(bf16[648,128]{1,0:T(8,128)(2,1)} %maximum_maximum_fusion.4), channel_id=1, source_target_pairs={{0,16},{1,17},{2,18},{3,19},{4,20},{5,21},{6,22},{7,23},{8,24},{9,... | collective-permute-start | bytes 497672 | tf_op jit(solution)/shard_map/ppermute | solution.py:640
  16.2 14.5 %collective-permute-start.2 = (bf16[648,128]{1,0:T(8,128)(2,1)}, bf16[648,128]{1,0:T(8,128)(2,1)S(1)}, u32[]{:S(2)}, u32[]{:S(2)}) collective-permute-start(bf16[648,128]{1,0:T(8,128)(2,1)} %maximum_maximum_fusion.4), channel_id=1, source_target_pairs={{0,24},{1,25},{2,26},{3,27},{4,28},{5,29},{6,30},{7,31},{8,16},{9,... | collective-permute-start | bytes 497672 | tf_op jit(solution)/shard_map/ppermute | solution.py:640
  18.1 22.2 %collective-permute-start.3 = (bf16[3,2,24,1152]{3,2,1,0:T(8,128)(2,1)S(1)}, bf16[3,2,24,1152]{3,2,1,0:T(8,128)(2,1)}, u32[]{:S(2)}, u32[]{:S(2)}) collective-permute-start(bf16[3,2,24,1152]{3,2,1,0:T(8,128)(2,1)S(1)} %pad_maximum_fusion.6), channel_id=1, source_target_pairs={{1,2},{5,6},{9,10},{13,14},{17,18},{21,22},{25,26},{29,30}} | collective-permute-start | bytes 995336 | tf_op jit(solution)/shard_map/ppermute | solution.py:647
  32.0 17.5 %collective-permute-start.4 = (bf16[2624,128]{1,0:T(8,128)(2,1)}, bf16[2624,128]{1,0:T(8,128)(2,1)}, u32[]{:S(2)}, u32[]{:S(2)}) collective-permute-start(bf16[2624,128]{1,0:T(8,128)(2,1)} %constant_dynamic-update-slice_fusion.refs_2_), channel_id=1, source_target_pairs={{0,1},{1,0},{2,3},{3,2},{4,5},{5,4},{6,7},{7,6},{8,9},{9,8},{10,11... | collective-permute-start | bytes 2015240 | tf_op jit(solution)/shard_map/ppermute | solution.py:640
  33.5 16.7 %collective-permute-start.5 = (bf16[2624,128]{1,0:T(8,128)(2,1)}, bf16[2624,128]{1,0:T(8,128)(2,1)}, u32[]{:S(2)}, u32[]{:S(2)}) collective-permute-start(bf16[2624,128]{1,0:T(8,128)(2,1)} %constant_dynamic-update-slice_fusion.refs_2_), channel_id=1, source_target_pairs={{0,2},{1,3},{2,0},{3,1},{4,6},{5,7},{6,4},{7,5},{8,10},{9,11},{10,... | collective-permute-start | bytes 2015240 | tf_op jit(solution)/shard_map/ppermute | solution.py:640
  35.0 39.0 %collective-permute-start.7 = (bf16[2624,128]{1,0:T(8,128)(2,1)}, bf16[2624,128]{1,0:T(8,128)(2,1)}, u32[]{:S(2)}, u32[]{:S(2)}) collective-permute-start(bf16[2624,128]{1,0:T(8,128)(2,1)} %constant_dynamic-update-slice_fusion.refs_2_), channel_id=1, source_target_pairs={{0,4},{1,5},{2,6},{3,7},{4,0},{5,1},{6,2},{7,3},{8,12},{9,13},{10,... | collective-permute-start | bytes 2015240 | tf_op jit(solution)/shard_map/ppermute | solution.py:640
  36.1 18.3 %collective-permute-start.11 = (bf16[144,1152]{1,0:T(8,128)(2,1)S(1)}, bf16[144,1152]{1,0:T(8,128)(2,1)S(1)}, u32[]{:S(2)}, u32[]{:S(2)}) collective-permute-start(bf16[144,1152]{1,0:T(8,128)(2,1)S(1)} %pad_maximum_fusion.7), channel_id=1, source_target_pairs={{0,16},{1,17},{2,18},{3,19},{4,20},{5,21},{6,22},{7,23},{8,24},{9,... | collective-permute-start | bytes 995336 | tf_op jit(solution)/shard_map/ppermute | solution.py:640
  54.5 16.6 %collective-permute-start.12 = (bf16[288,1152]{1,0:T(8,128)(2,1)S(1)}, bf16[288,1152]{1,0:T(8,128)(2,1)S(1)}, u32[]{:S(2)}, u32[]{:S(2)}) collective-permute-start(bf16[288,1152]{1,0:T(8,128)(2,1)S(1)} %pad_maximum_fusion.3), channel_id=1, source_target_pairs={{0,8},{1,9},{2,10},{3,11},{4,12},{5,13},{6,14},{7,15},{8,0},{9,1},... | collective-permute-start | bytes 1990664 | tf_op jit(solution)/shard_map/ppermute | solution.py:640
  55.3 17.0 %collective-permute-start.6 = (bf16[2624,128]{1,0:T(8,128)(2,1)}, bf16[2624,128]{1,0:T(8,128)(2,1)S(1)}, u32[]{:S(2)}, u32[]{:S(2)}) collective-permute-start(bf16[2624,128]{1,0:T(8,128)(2,1)} %collective-permute-done.4.refs_3_), channel_id=1, source_target_pairs={{0,2},{1,3},{2,0},{3,1},{4,6},{5,7},{6,4},{7,5},{8,10},{9,11},{10,... | collective-permute-start | bytes 2015240 | tf_op jit(solution)/shard_map/ppermute | solution.py:640
  55.9 16.9 %collective-permute-start.8 = (bf16[2624,128]{1,0:T(8,128)(2,1)}, bf16[2624,128]{1,0:T(8,128)(2,1)S(1)}, u32[]{:S(2)}, u32[]{:S(2)}) collective-permute-start(bf16[2624,128]{1,0:T(8,128)(2,1)} %collective-permute-done.4.refs_3_), channel_id=1, source_target_pairs={{0,4},{1,5},{2,6},{3,7},{4,0},{5,1},{6,2},{7,3},{8,12},{9,13},{10,... | collective-permute-start | bytes 2015240 | tf_op jit(solution)/shard_map/ppermute | solution.py:640
  55.9 17.5 %collective-permute-start.9 = (bf16[2624,128]{1,0:T(8,128)(2,1)}, bf16[2624,128]{1,0:T(8,128)(2,1)}, u32[]{:S(2)}, u32[]{:S(2)}) collective-permute-start(bf16[2624,128]{1,0:T(8,128)(2,1)} %collective-permute-done.5.refs_4_), channel_id=1, source_target_pairs={{0,4},{1,5},{2,6},{3,7},{4,0},{5,1},{6,2},{7,3},{8,12},{9,13},{10,... | collective-permute-start | bytes 2015240 | tf_op jit(solution)/shard_map/ppermute | solution.py:640
  72.0 23.9 %collective-permute-start.13 = (bf16[576,1152]{1,0:T(8,128)(2,1)}, bf16[576,1152]{1,0:T(8,128)(2,1)S(1)}, u32[]{:S(2)}, u32[]{:S(2)}) collective-permute-start(bf16[576,1152]{1,0:T(8,128)(2,1)} %constant_dynamic-update-slice_fusion.7.refs_2_), channel_id=1, source_target_pairs={{0,4},{1,5},{2,6},{3,7},{4,0},{5,1},{6,2},{7,3},{8,12},{9,13},{10,... | collective-permute-start | bytes 3981320 | tf_op jit(solution)/shard_map/ppermute | solution.py:640
  72.3 31.6 %collective-permute-start.14 = (bf16[576,1152]{1,0:T(8,128)(2,1)}, bf16[576,1152]{1,0:T(8,128)(2,1)}, u32[]{:S(2)}, u32[]{:S(2)}) collective-permute-start(bf16[576,1152]{1,0:T(8,128)(2,1)} %constant_dynamic-update-slice_fusion.7.refs_2_), channel_id=1, source_target_pairs={{0,1},{1,0},{2,3},{3,2},{4,5},{5,4},{6,7},{7,6},{8,9},{9,8},{10,11... | collective-permute-start | bytes 3981320 | tf_op jit(solution)/shard_map/ppermute | solution.py:640
  72.9 35.5 %collective-permute-start.15 = (bf16[576,1152]{1,0:T(8,128)(2,1)}, bf16[576,1152]{1,0:T(8,128)(2,1)}, u32[]{:S(2)}, u32[]{:S(2)}) collective-permute-start(bf16[576,1152]{1,0:T(8,128)(2,1)} %constant_dynamic-update-slice_fusion.7.refs_2_), channel_id=1, source_target_pairs={{0,2},{1,3},{2,0},{3,1},{4,6},{5,7},{6,4},{7,5},{8,10},{9,11},{10,... | collective-permute-start | bytes 3981320 | tf_op jit(solution)/shard_map/ppermute | solution.py:640
  103.9 35.9 %collective-permute-start.16 = (bf16[576,1152]{1,0:T(8,128)(2,1)}, bf16[576,1152]{1,0:T(8,128)(2,1)}, u32[]{:S(2)}, u32[]{:S(2)}) collective-permute-start(bf16[576,1152]{1,0:T(8,128)(2,1)} %collective-permute-done.14.refs_3_), channel_id=1, source_target_pairs={{0,2},{1,3},{2,0},{3,1},{4,6},{5,7},{6,4},{7,5},{8,10},{9,11},{10,... | collective-permute-start | bytes 3981320 | tf_op jit(solution)/shard_map/ppermute | solution.py:640
  104.3 35.4 %collective-permute-start.17 = (bf16[576,1152]{1,0:T(8,128)(2,1)}, bf16[576,1152]{1,0:T(8,128)(2,1)}, u32[]{:S(2)}, u32[]{:S(2)}) collective-permute-start(bf16[576,1152]{1,0:T(8,128)(2,1)} %collective-permute-done.14.refs_3_), channel_id=1, source_target_pairs={{0,4},{1,5},{2,6},{3,7},{4,0},{5,1},{6,2},{7,3},{8,12},{9,13},{10,... | collective-permute-start | bytes 3981320 | tf_op jit(solution)/shard_map/ppermute | solution.py:640
  108.4 31.4 %collective-permute-start.18 = (bf16[576,1152]{1,0:T(8,128)(2,1)}, bf16[576,1152]{1,0:T(8,128)(2,1)}, u32[]{:S(2)}, u32[]{:S(2)}) collective-permute-start(bf16[576,1152]{1,0:T(8,128)(2,1)} %collective-permute-done.15.refs_4_), channel_id=1, source_target_pairs={{0,4},{1,5},{2,6},{3,7},{4,0},{5,1},{6,2},{7,3},{8,12},{9,13},{10,... | collective-permute-start | bytes 3981320 | tf_op jit(solution)/shard_map/ppermute | solution.py:640
  110.3 29.5 %collective-permute-start.19 = (bf16[1,544,1152]{2,1,0:T(8,128)(2,1)S(1)}, bf16[1,544,1152]{2,1,0:T(8,128)(2,1)S(1)}, u32[]{:S(2)}, u32[]{:S(2)}) collective-permute-start(bf16[1,544,1152]{2,1,0:T(8,128)(2,1)S(1)} %get-tuple-element.315), channel_id=1, source_target_pairs={{0,1},{1,0},{2,3},{3,2},{4,5},{5,4},{6,7},{7,6},{8,9},{9,8},{10,11... | collective-permute-start | bytes 3760136 | tf_op jit(solution)/shard_map/ppermute | solution.py:640
  110.8 17.4 %collective-permute-start.20 = (bf16[144,1152]{1,0:T(8,128)(2,1)S(1)}, bf16[144,1152]{1,0:T(8,128)(2,1)S(1)}, u32[]{:S(2)}, u32[]{:S(2)}) collective-permute-start(bf16[144,1152]{1,0:T(8,128)(2,1)S(1)} %copy-done.26), channel_id=1, source_target_pairs={{0,16},{1,17},{2,18},{3,19},{4,20},{5,21},{6,22},{7,23},{8,24},{9,... | collective-permute-start | bytes 995336 | tf_op jit(solution)/shard_map/ppermute | solution.py:640
  140.8 7.7 collective-permute-start.21
  143.9 18.5 %collective-permute-start.23 = (bf16[1296,128]{1,0:T(8,128)(2,1)S(1)}, bf16[1296,128]{1,0:T(8,128)(2,1)}, u32[]{:S(2)}, u32[]{:S(2)}) collective-permute-start(bf16[1296,128]{1,0:T(8,128)(2,1)S(1)} %maximum_maximum_fusion.3), channel_id=1, source_target_pairs={{0,16},{1,17},{2,18},{3,19},{4,20},{5,21},{6,22},{7,23},{8,24},{9,... | collective-permute-start | bytes 995336 | tf_op jit(solution)/shard_map/ppermute | solution.py:640
  146.7 37.7 %collective-permute-start.24 = (bf16[1,544,1152]{2,1,0:T(8,128)(2,1)}, bf16[1,544,1152]{2,1,0:T(8,128)(2,1)}, u32[]{:S(2)}, u32[]{:S(2)}) collective-permute-start(bf16[1,544,1152]{2,1,0:T(8,128)(2,1)} %get-tuple-element.314), channel_id=1, source_target_pairs={{0,1},{1,0},{2,3},{3,2},{4,5},{5,4},{6,7},{7,6},{8,9},{9,8},{10,11... | collective-permute-start | bytes 3760136 | tf_op jit(solution)/shard_map/ppermute | solution.py:640
  146.9 24.3 %collective-permute-start.22 = (bf16[288,1152]{1,0:T(8,128)(2,1)S(1)}, bf16[288,1152]{1,0:T(8,128)(2,1)}, u32[]{:S(2)}, u32[]{:S(2)}) collective-permute-start(bf16[288,1152]{1,0:T(8,128)(2,1)S(1)} %constant_dynamic-update-slice_fusion.10), channel_id=1, source_target_pairs={{0,8},{1,9},{2,10},{3,11},{4,12},{5,13},{6,14},{7,15},{8,0},{9,1},... | collective-permute-start | bytes 1990664 | tf_op jit(solution)/shard_map/ppermute | solution.py:640
  163.4 26.0 %collective-permute-start.26 = (bf16[2592,128]{1,0:T(8,128)(2,1)S(1)}, bf16[2592,128]{1,0:T(8,128)(2,1)S(1)}, u32[]{:S(2)}, u32[]{:S(2)}) collective-permute-start(bf16[2592,128]{1,0:T(8,128)(2,1)S(1)} %constant_dynamic-update-slice_fusion.14), channel_id=1, source_target_pairs={{0,8},{1,9},{2,10},{3,11},{4,12},{5,13},{6,14},{7,15},{8,0},{9,1},... | collective-permute-start | bytes 1990664 | tf_op jit(solution)/shard_map/ppermute | solution.py:640
  173.2 21.9 %collective-permute-start.27 = (bf16[576,1152]{1,0:T(8,128)(2,1)}, bf16[576,1152]{1,0:T(8,128)(2,1)}, u32[]{:S(2)}, u32[]{:S(2)}) collective-permute-start(bf16[576,1152]{1,0:T(8,128)(2,1)} %constant_dynamic-update-slice_fusion.12.refs_1_), channel_id=1, source_target_pairs={{0,4},{1,5},{2,6},{3,7},{4,0},{5,1},{6,2},{7,3},{8,12},{9,13},{10,... | collective-permute-start | bytes 3981320 | tf_op jit(solution)/shard_map/ppermute | solution.py:640
  189.5 46.7 %collective-permute-start.30 = (bf16[5184,128]{1,0:T(8,128)(2,1)S(1)}, bf16[5184,128]{1,0:T(8,128)(2,1)}, u32[]{:S(2)}, u32[]{:S(2)}) collective-permute-start(bf16[5184,128]{1,0:T(8,128)(2,1)S(1)} %constant_dynamic-update-slice_fusion.16.refs_2_), channel_id=1, source_target_pairs={{0,2},{1,3},{2,0},{3,1},{4,6},{5,7},{6,4},{7,5},{8,10},{9,11},{10,... | collective-permute-start | bytes 3981320 | tf_op jit(solution)/shard_map/ppermute | solution.py:640
  192.3 45.9 %collective-permute-start.25 = (bf16[576,1152]{1,0:T(8,128)(2,1)}, bf16[576,1152]{1,0:T(8,128)(2,1)}, u32[]{:S(2)}, u32[]{:S(2)}) collective-permute-start(bf16[576,1152]{1,0:T(8,128)(2,1)} %constant_dynamic-update-slice_fusion.12.refs_1_), channel_id=1, source_target_pairs={{0,1},{1,0},{2,3},{3,2},{4,5},{5,4},{6,7},{7,6},{8,9},{9,8},{10,11... | collective-permute-start | bytes 3981320 | tf_op jit(solution)/shard_map/ppermute | solution.py:640
  193.8 56.3 %collective-permute-start.28 = (bf16[576,1152]{1,0:T(8,128)(2,1)}, bf16[576,1152]{1,0:T(8,128)(2,1)}, u32[]{:S(2)}, u32[]{:S(2)}) collective-permute-start(bf16[576,1152]{1,0:T(8,128)(2,1)} %constant_dynamic-update-slice_fusion.12.refs_1_), channel_id=1, source_target_pairs={{0,2},{1,3},{2,0},{3,1},{4,6},{5,7},{6,4},{7,5},{8,10},{9,11},{10,... | collective-permute-start | bytes 3981320 | tf_op jit(solution)/shard_map/ppermute | solution.py:640
  195.0 58.0 %collective-permute-start.29 = (bf16[5184,128]{1,0:T(8,128)(2,1)S(1)}, bf16[5184,128]{1,0:T(8,128)(2,1)}, u32[]{:S(2)}, u32[]{:S(2)}) collective-permute-start(bf16[5184,128]{1,0:T(8,128)(2,1)S(1)} %constant_dynamic-update-slice_fusion.16.refs_2_), channel_id=1, source_target_pairs={{0,1},{1,0},{2,3},{3,2},{4,5},{5,4},{6,7},{7,6},{8,9},{9,8},{10,11... | collective-permute-start | bytes 3981320 | tf_op jit(solution)/shard_map/ppermute | solution.py:640
  195.1 58.0 %collective-permute-start.31 = (bf16[5184,128]{1,0:T(8,128)(2,1)S(1)}, bf16[5184,128]{1,0:T(8,128)(2,1)S(1)}, u32[]{:S(2)}, u32[]{:S(2)}) collective-permute-start(bf16[5184,128]{1,0:T(8,128)(2,1)S(1)} %constant_dynamic-update-slice_fusion.16.refs_2_), channel_id=1, source_target_pairs={{0,4},{1,5},{2,6},{3,7},{4,0},{5,1},{6,2},{7,3},{8,12},{9,13},{10,... | collective-permute-start | bytes 3981320 | tf_op jit(solution)/shard_map/ppermute | solution.py:640
  236.2 58.3 %collective-permute-start.36 = (bf16[5184,128]{1,0:T(8,128)(2,1)}, bf16[5184,128]{1,0:T(8,128)(2,1)}, u32[]{:S(2)}, u32[]{:S(2)}) collective-permute-start(bf16[5184,128]{1,0:T(8,128)(2,1)} %collective-permute-done.30.refs_4_), channel_id=1, source_target_pairs={{0,1},{1,0},{2,3},{3,2},{4,5},{5,4},{6,7},{7,6},{8,9},{9,8},{10,11... | collective-permute-start | bytes 3981320 | tf_op jit(solution)/shard_map/ppermute | solution.py:640
  238.2 60.4 %collective-permute-start.32 = (bf16[576,1152]{1,0:T(8,128)(2,1)}, bf16[576,1152]{1,0:T(8,128)(2,1)}, u32[]{:S(2)}, u32[]{:S(2)}) collective-permute-start(bf16[576,1152]{1,0:T(8,128)(2,1)} %collective-permute-done.25.refs_2_), channel_id=1, source_target_pairs={{0,2},{1,3},{2,0},{3,1},{4,6},{5,7},{6,4},{7,5},{8,10},{9,11},{10,... | collective-permute-start | bytes 3981320 | tf_op jit(solution)/shard_map/ppermute | solution.py:640
  250.1 48.5 %collective-permute-start.33 = (bf16[576,1152]{1,0:T(8,128)(2,1)}, bf16[576,1152]{1,0:T(8,128)(2,1)}, u32[]{:S(2)}, u32[]{:S(2)}) collective-permute-start(bf16[576,1152]{1,0:T(8,128)(2,1)} %collective-permute-done.25.refs_2_), channel_id=1, source_target_pairs={{0,4},{1,5},{2,6},{3,7},{4,0},{5,1},{6,2},{7,3},{8,12},{9,13},{10,... | collective-permute-start | bytes 3981320 | tf_op jit(solution)/shard_map/ppermute | solution.py:640
  253.0 45.6 %collective-permute-start.34 = (bf16[576,1152]{1,0:T(8,128)(2,1)}, bf16[576,1152]{1,0:T(8,128)(2,1)}, u32[]{:S(2)}, u32[]{:S(2)}) collective-permute-start(bf16[576,1152]{1,0:T(8,128)(2,1)} %collective-permute-done.28.refs_3_), channel_id=1, source_target_pairs={{0,4},{1,5},{2,6},{3,7},{4,0},{5,1},{6,2},{7,3},{8,12},{9,13},{10,... | collective-permute-start | bytes 3981320 | tf_op jit(solution)/shard_map/ppermute | solution.py:640
  299.9 14.8 %collective-permute-start.39 = (bf16[5184,128]{1,0:T(8,128)(2,1)}, bf16[5184,128]{1,0:T(8,128)(2,1)}, u32[]{:S(2)}, u32[]{:S(2)}) collective-permute-start(bf16[5184,128]{1,0:T(8,128)(2,1)} %collective-permute-done.36.refs_5_), channel_id=1, source_target_pairs={{0,4},{1,5},{2,6},{3,7},{4,0},{5,1},{6,2},{7,3},{8,12},{9,13},{10,... | collective-permute-start | bytes 3981320 | tf_op jit(solution)/shard_map/ppermute | solution.py:640
  435.4 21.7 %collective-permute-start.40 = (bf16[4,4,1296,128]{3,2,1,0:T(8,128)(2,1)}, bf16[4,4,1296,128]{3,2,1,0:T(8,128)(2,1)}, u32[]{:S(2)}, u32[]{:S(2)}) collective-permute-start(bf16[4,4,1296,128]{3,2,1,0:T(8,128)(2,1)} %get-tuple-element.148), channel_id=1, source_target_pairs={{0,4},{1,5},{2,6},{3,7},{4,0},{5,1},{6,2},{7,3},{8,12},{9,13},{10,... | collective-permute-start | bytes 15925256 | tf_op jit(solution)/shard_map/ppermute | solution.py:640
  456.6 9.3 %collective-permute-start.41 = (bf16[576,4608]{1,0:T(8,128)(2,1)}, bf16[576,4608]{1,0:T(8,128)(2,1)}, u32[]{:S(2)}, u32[]{:S(2)}) collective-permute-start(bf16[576,4608]{1,0:T(8,128)(2,1)} %get-tuple-element.153), channel_id=1, source_target_pairs={{0,4},{1,5},{2,6},{3,7},{4,0},{5,1},{6,2},{7,3},{8,12},{9,13},{10,... | collective-permute-start | bytes 15925256 | tf_op jit(solution)/shard_map/ppermute | solution.py:640
  464.4 59.9 %collective-permute-start.42 = (bf16[4,2,1296,128]{3,2,1,0:T(8,128)(2,1)}, bf16[4,2,1296,128]{3,2,1,0:T(8,128)(2,1)}, u32[]{:S(2)}, u32[]{:S(2)}) collective-permute-start(bf16[4,2,1296,128]{3,2,1,0:T(8,128)(2,1)} %get-tuple-element.303), channel_id=1, source_target_pairs={{0,1},{1,0},{2,3},{3,2},{4,5},{5,4},{6,7},{7,6},{8,9},{9,8},{10,11... | collective-permute-start | bytes 7962632 | tf_op jit(solution)/shard_map/ppermute | solution.py:640
  472.5 60.7 %collective-permute-start.43 = (bf16[4,144,2304]{2,1,0:T(8,128)(2,1)}, bf16[4,144,2304]{2,1,0:T(8,128)(2,1)}, u32[]{:S(2)}, u32[]{:S(2)}) collective-permute-start(bf16[4,144,2304]{2,1,0:T(8,128)(2,1)} %get-tuple-element.301), channel_id=1, source_target_pairs={{0,2},{1,3},{2,0},{3,1},{4,6},{5,7},{6,4},{7,5},{8,10},{9,11},{10,... | collective-permute-start | bytes 7962632 | tf_op jit(solution)/shard_map/ppermute | solution.py:640
  526.9 65.6 %collective-permute-start.44 = (bf16[4,1296,128]{2,1,0:T(8,128)(2,1)S(1)}, bf16[4,1296,128]{2,1,0:T(8,128)(2,1)}, u32[]{:S(2)}, u32[]{:S(2)}) collective-permute-start(bf16[4,1296,128]{2,1,0:T(8,128)(2,1)S(1)} %get-tuple-element.313), channel_id=1, source_target_pairs={{0,2},{1,3},{2,0},{3,1},{4,6},{5,7},{6,4},{7,5},{8,10},{9,11},{10,... | collective-permute-start | bytes 3981320 | tf_op jit(solution)/shard_map/ppermute | solution.py:640
  537.4 56.8 %collective-permute-start.45 = (bf16[4,144,1152]{2,1,0:T(8,128)(2,1)}, bf16[4,144,1152]{2,1,0:T(8,128)(2,1)}, u32[]{:S(2)}, u32[]{:S(2)}) collective-permute-start(bf16[4,144,1152]{2,1,0:T(8,128)(2,1)} %get-tuple-element.311), channel_id=1, source_target_pairs={{0,1},{1,0},{2,3},{3,2},{4,5},{5,4},{6,7},{7,6},{8,9},{9,8},{10,11... | collective-permute-start | bytes 3981320 | tf_op jit(solution)/shard_map/ppermute | solution.py:640
  545.1 50.8 %collective-permute-start.46 = (bf16[1,544,1152]{2,1,0:T(8,128)(2,1)}, bf16[1,544,1152]{2,1,0:T(8,128)(2,1)}, u32[]{:S(2)}, u32[]{:S(2)}) collective-permute-start(bf16[1,544,1152]{2,1,0:T(8,128)(2,1)} %fusion.11), channel_id=1, source_target_pairs={{0,1},{1,0},{2,3},{3,2},{4,5},{5,4},{6,7},{7,6},{8,9},{9,8},{10,11... | collective-permute-start | bytes 3760136 | tf_op jit(solution)/shard_map/ppermute | solution.py:640
  603.7 41.0 %collective-permute-start.47 = (bf16[1,544,1152]{2,1,0:T(8,128)(2,1)}, bf16[1,544,1152]{2,1,0:T(8,128)(2,1)}, u32[]{:S(2)}, u32[]{:S(2)}) collective-permute-start(bf16[1,544,1152]{2,1,0:T(8,128)(2,1)} %fusion.12), channel_id=1, source_target_pairs={{0,1},{1,0},{2,3},{3,2},{4,5},{5,4},{6,7},{7,6},{8,9},{9,8},{10,11... | collective-permute-start | bytes 3760136 | tf_op jit(solution)/shard_map/ppermute | solution.py:640
  644.7 19.2 %collective-permute-start.48 = (bf16[576,4608]{1,0:T(8,128)(2,1)}, bf16[576,4608]{1,0:T(8,128)(2,1)}, u32[]{:S(2)}, u32[]{:S(2)}) collective-permute-start(bf16[576,4608]{1,0:T(8,128)(2,1)} %get-tuple-element.172), channel_id=1, source_target_pairs={{0,4},{1,5},{2,6},{3,7},{4,0},{5,1},{6,2},{7,3},{8,12},{9,13},{10,... | collective-permute-start | bytes 15925256 | tf_op jit(solution)/shard_map/ppermute | solution.py:640
  660.6 47.4 %collective-permute-start.65 = (bf16[2,1296,128]{2,1,0:T(8,128)(2,1)}, bf16[2,1296,128]{2,1,0:T(8,128)(2,1)}, u32[]{:S(2)}, u32[]{:S(2)}) collective-permute-start(bf16[2,1296,128]{2,1,0:T(8,128)(2,1)} %get-tuple-element.319), channel_id=1, source_target_pairs={{0,16},{1,17},{2,18},{3,19},{4,20},{5,21},{6,22},{7,23},{8,24},{9,... | collective-permute-start | bytes 1990664 | tf_op jit(solution)/shard_map/ppermute | solution.py:640
  661.8 49.5 %collective-permute-start.63 = (bf16[2,144,1152]{2,1,0:T(8,128)(2,1)}, bf16[2,144,1152]{2,1,0:T(8,128)(2,1)}, u32[]{:S(2)}, u32[]{:S(2)}) collective-permute-start(bf16[2,144,1152]{2,1,0:T(8,128)(2,1)} %get-tuple-element.321), channel_id=1, source_target_pairs={{0,8},{1,9},{2,10},{3,11},{4,12},{5,13},{6,14},{7,15},{8,0},{9,1},... | collective-permute-start | bytes 1990664 | tf_op jit(solution)/shard_map/ppermute | solution.py:640
  673.2 44.7 %collective-permute-start.50 = (bf16[4,72,2304]{2,1,0:T(8,128)(2,1)}, bf16[4,72,2304]{2,1,0:T(8,128)(2,1)}, u32[]{:S(2)}, u32[]{:S(2)}) collective-permute-start(bf16[4,72,2304]{2,1,0:T(8,128)(2,1)} %pad_maximum_fusion.1), channel_id=1, source_target_pairs={{0,1},{1,0},{2,3},{3,2},{4,5},{5,4},{6,7},{7,6},{8,9},{9,8},{10,11... | collective-permute-start | bytes 3981320 | tf_op jit(solution)/shard_map/ppermute | solution.py:640
  673.7 47.0 %collective-permute-start.49 = (bf16[4,72,2304]{2,1,0:T(8,128)(2,1)}, bf16[4,72,2304]{2,1,0:T(8,128)(2,1)}, u32[]{:S(2)}, u32[]{:S(2)}) collective-permute-start(bf16[4,72,2304]{2,1,0:T(8,128)(2,1)} %get-tuple-element.309), channel_id=1, source_target_pairs={{0,2},{1,3},{2,0},{3,1},{4,6},{5,7},{6,4},{7,5},{8,10},{9,11},{10,... | collective-permute-start | bytes 3981320 | tf_op jit(solution)/shard_map/ppermute | solution.py:640
  699.3 24.7 %collective-permute-start.51 = (bf16[4,4,648,128]{3,2,1,0:T(8,128)(2,1)}, bf16[4,4,648,128]{3,2,1,0:T(8,128)(2,1)}, u32[]{:S(2)}, u32[]{:S(2)}) collective-permute-start(bf16[4,4,648,128]{3,2,1,0:T(8,128)(2,1)} %get-tuple-element.178), channel_id=1, source_target_pairs={{0,4},{1,5},{2,6},{3,7},{4,0},{5,1},{6,2},{7,3},{8,12},{9,13},{10,... | collective-permute-start | bytes 7962632 | tf_op jit(solution)/shard_map/ppermute | solution.py:640
  711.3 70.9 %collective-permute-start.66 = (bf16[1,1296,128]{2,1,0:T(8,128)(2,1)}, bf16[1,1296,128]{2,1,0:T(8,128)(2,1)}, u32[]{:S(2)}, u32[]{:S(2)}) collective-permute-start(bf16[1,1296,128]{2,1,0:T(8,128)(2,1)} %get-tuple-element.333), channel_id=1, source_target_pairs={{0,8},{1,9},{2,10},{3,11},{4,12},{5,13},{6,14},{7,15},{8,0},{9,1},... | collective-permute-start | bytes 995336 | tf_op jit(solution)/shard_map/ppermute | solution.py:640
  713.5 70.1 %collective-permute-start.64 = (bf16[1,144,1152]{2,1,0:T(8,128)(2,1)}, bf16[1,144,1152]{2,1,0:T(8,128)(2,1)}, u32[]{:S(2)}, u32[]{:S(2)}) collective-permute-start(bf16[1,144,1152]{2,1,0:T(8,128)(2,1)} %get-tuple-element.335), channel_id=1, source_target_pairs={{0,16},{1,17},{2,18},{3,19},{4,20},{5,21},{6,22},{7,23},{8,24},{9,... | collective-permute-start | bytes 995336 | tf_op jit(solution)/shard_map/ppermute | solution.py:640
  719.7 17.2 %collective-permute-start.54 = (bf16[4,72,1152]{2,1,0:T(8,128)(2,1)S(1)}, bf16[4,72,1152]{2,1,0:T(8,128)(2,1)S(1)}, u32[]{:S(2)}, u32[]{:S(2)}) collective-permute-start(bf16[4,72,1152]{2,1,0:T(8,128)(2,1)S(1)} %get-tuple-element.325), channel_id=1, source_target_pairs={{0,2},{1,3},{2,0},{3,1},{4,6},{5,7},{6,4},{7,5},{8,10},{9,11},{10,... | collective-permute-start | bytes 1990664 | tf_op jit(solution)/shard_map/ppermute | solution.py:640
  722.6 18.3 %collective-permute-start.53 = (bf16[4,72,1152]{2,1,0:T(8,128)(2,1)S(1)}, bf16[4,72,1152]{2,1,0:T(8,128)(2,1)S(1)}, u32[]{:S(2)}, u32[]{:S(2)}) collective-permute-start(bf16[4,72,1152]{2,1,0:T(8,128)(2,1)S(1)} %get-tuple-element.327), channel_id=1, source_target_pairs={{0,1},{1,0},{2,3},{3,2},{4,5},{5,4},{6,7},{7,6},{8,9},{9,8},{10,11... | collective-permute-start | bytes 1990664 | tf_op jit(solution)/shard_map/ppermute | solution.py:640
  727.3 28.8 %collective-permute-start.55 = (bf16[4,2,328,128]{3,2,0,1:T(8,128)(2,1)S(1)}, bf16[4,2,328,128]{3,2,0,1:T(8,128)(2,1)S(1)}, u32[]{:S(2)}, u32[]{:S(2)}) collective-permute-start(bf16[4,2,328,128]{3,2,0,1:T(8,128)(2,1)S(1)} %bitcast.226), channel_id=1, source_target_pairs={{0,1},{1,0},{2,3},{3,2},{4,5},{5,4},{6,7},{7,6},{8,9},{9,8},{10,11... | collective-permute-start | bytes 2015240 | tf_op jit(solution)/shard_map/ppermute | solution.py:640
  736.9 16.6 %collective-permute-start.57 = (bf16[4,2,320,128]{3,2,0,1:T(8,128)(2,1)S(1)}, bf16[4,2,320,128]{3,2,0,1:T(8,128)(2,1)S(1)}, u32[]{:S(2)}, u32[]{:S(2)}) collective-permute-start(bf16[4,2,320,128]{3,2,0,1:T(8,128)(2,1)S(1)} %bitcast.227), channel_id=1, source_target_pairs={{0,2},{1,3},{2,0},{3,1},{4,6},{5,7},{6,4},{7,5},{8,10},{9,11},{10,... | collective-permute-start | bytes 1966088 | tf_op jit(solution)/shard_map/ppermute | solution.py:640
  741.1 31.8 %collective-permute-start.59 = (bf16[2,144,1152]{2,1,0:T(8,128)(2,1)S(1)}, bf16[2,144,1152]{2,1,0:T(8,128)(2,1)S(1)}, u32[]{:S(2)}, u32[]{:S(2)}) collective-permute-start(bf16[2,144,1152]{2,1,0:T(8,128)(2,1)S(1)} %get-tuple-element.323), channel_id=1, source_target_pairs={{0,16},{1,17},{2,18},{3,19},{4,20},{5,21},{6,22},{7,23},{8,24},{9,... | collective-permute-start | bytes 1990664 | tf_op jit(solution)/shard_map/ppermute | solution.py:640
  753.7 8.7 %collective-permute-start.58 = (bf16[4,320,128]{2,1,0:T(8,128)(2,1)S(1)}, bf16[4,320,128]{2,1,0:T(8,128)(2,1)S(1)}, u32[]{:S(2)}, u32[]{:S(2)}) collective-permute-start(bf16[4,320,128]{2,1,0:T(8,128)(2,1)S(1)} %dynamic-slice_bitcast_fusion.9), channel_id=1, source_target_pairs={{0,1},{1,0},{2,3},{3,2},{4,5},{5,4},{6,7},{7,6},{8,9},{9,8},{10,11... | collective-permute-start | bytes 983048 | tf_op jit(solution)/shard_map/ppermute | solution.py:640
  756.3 8.1 %collective-permute-start.56 = (bf16[4,328,128]{2,1,0:T(8,128)(2,1)S(1)}, bf16[4,328,128]{2,1,0:T(8,128)(2,1)S(1)}, u32[]{:S(2)}, u32[]{:S(2)}) collective-permute-start(bf16[4,328,128]{2,1,0:T(8,128)(2,1)S(1)} %dynamic-slice_bitcast_fusion.6), channel_id=1, source_target_pairs={{0,2},{1,3},{2,0},{3,1},{4,6},{5,7},{6,4},{7,5},{8,10},{9,11},{10,... | collective-permute-start | bytes 1007624 | tf_op jit(solution)/shard_map/ppermute | solution.py:640
  762.4 18.6 %collective-permute-start.52 = (f32[3,2,16,1152]{3,2,1,0:T(8,128)S(1)}, f32[3,2,16,1152]{3,2,1,0:T(8,128)S(1)}, u32[]{:S(2)}, u32[]{:S(2)}) collective-permute-start(f32[3,2,16,1152]{3,2,1,0:T(8,128)S(1)} %pad_maximum_fusion.5), channel_id=1, source_target_pairs={{2,1},{6,5},{10,9},{14,13},{18,17},{22,21},{26,25},{30,29}} | collective-permute-start | bytes 1327112 | tf_op jit(solution)/shard_map/ppermute | solution.py:647
  764.6 15.6 %collective-permute-start.60 = (bf16[2,648,128]{2,1,0:T(8,128)(2,1)S(1)}, bf16[2,648,128]{2,1,0:T(8,128)(2,1)S(1)}, u32[]{:S(2)}, u32[]{:S(2)}) collective-permute-start(bf16[2,648,128]{2,1,0:T(8,128)(2,1)S(1)} %get-tuple-element.339), channel_id=1, source_target_pairs={{0,8},{1,9},{2,10},{3,11},{4,12},{5,13},{6,14},{7,15},{8,0},{9,1},... | collective-permute-start | bytes 995336 | tf_op jit(solution)/shard_map/ppermute | solution.py:640
  773.2 22.2 %collective-permute-start.62 = (bf16[1,144,1152]{2,1,0:T(8,128)(2,1)S(1)}, bf16[1,144,1152]{2,1,0:T(8,128)(2,1)S(1)}, u32[]{:S(2)}, u32[]{:S(2)}) collective-permute-start(bf16[1,144,1152]{2,1,0:T(8,128)(2,1)S(1)} %get-tuple-element.337), channel_id=1, source_target_pairs={{0,8},{1,9},{2,10},{3,11},{4,12},{5,13},{6,14},{7,15},{8,0},{9,1},... | collective-permute-start | bytes 995336 | tf_op jit(solution)/shard_map/ppermute | solution.py:640
  781.1 20.3 %collective-permute-start.61 = (bf16[1,648,128]{2,1,0:T(8,128)(2,1)}, bf16[1,648,128]{2,1,0:T(8,128)(2,1)}, u32[]{:S(2)}, u32[]{:S(2)}) collective-permute-start(bf16[1,648,128]{2,1,0:T(8,128)(2,1)} %get-tuple-element.351), channel_id=1, source_target_pairs={{0,16},{1,17},{2,18},{3,19},{4,20},{5,21},{6,22},{7,23},{8,24},{9,... | collective-permute-start | bytes 497672 | tf_op jit(solution)/shard_map/ppermute | solution.py:640
  (74 other events, 965.8 us)
Sparse Core Ops, SparseCore 0:
  717.1 79.1 all-gather.1

commit v5 on v4

--- a/solution.py
+++ b/solution.py
@@ -1160,7 +1160,7 @@
     if grid.square:
         hidden_way = Gather(grid, tie(hidden_weight, stream))
         hidden_way.first()
-        mixed_blocks = mixed_way.core(first_far[0], hidden_way.far)
+        mixed_blocks = mixed_way.core(hidden_way.far)
         hidden_way.second(mixed_way.blocks[3])
         down_way = Gather(grid, tie(pack_lanes(down_weight), hidden_way.pair))
         down_way.first()
@@ -1170,7 +1170,7 @@
         hidden_way.last(query_full)
         hidden_way.spread()
         down_way.second(query_full)
-        both_full = tie(both_full, hidden_way.column, down_way.pair)
+        both_full = tie(both_full, first_far[0], hidden_way.column, down_way.pair)
     own = dot_last(first_low, both_full).astype(jnp.bfloat16)
     if grid.square:
         query_full = tie(query_full, own, first_far[1])

time: 819 us -> 833 us (1.017)
  starting transfers between devices: 53.6 us -> 65.1 us
    ppermute x65, starting transfers between devices: 51.5 us -> 63 us  [send(): return lax.ppermute(value, ('batch', 'seq'), pairs)]
    unnamed x166 -> x140, local copies, waits for them, and re-layouts: 19.4 us -> 18.3 us
  transfers between devices with their start and end apart: 68 -> 68, of which waited for: 24 -> 25; matrix products, arithmetic and copies ran while one was open for 25% -> 25% of each run, Pallas kernels for 32% -> 32%
where the time goes in v5:
time: 833 us; the launch traced here: 822 us
  Pallas kernels  382 us (46%)
  waiting for transfers between devices  138 us (17%)
  matrix products  81.7 us (10%)
  other arithmetic  78 us (9%)
  starting transfers between devices  65.1 us (8%)
  local copies, waits for them, and re-layouts  61.4 us (7%)
  between operations  15.9 us (2%)
    ppermute x65, waiting for transfers between devices, send(): return lax.ppermute(value, ('batch', 'seq'), pairs)  138 us
    pallas_call x2, Pallas kernels, attend_back(): pl.pallas_call(attend_back_kernel, grid=(1,), in_specs=[wide, pl.BlockSpe...  93.5 us
    pallas_call x1, Pallas kernels, middle_block(): pl.pallas_call(middle_kernel, grid=(blocks, steps), in_specs=[by_rows, by...  83.6 us
    pallas_call x2, Pallas kernels, attend(): pl.pallas_call(attend_kernel, grid=(1,), in_specs=[wide, pl.BlockSpec((1,...  66.4 us
    ppermute x65, starting transfers between devices, send(): return lax.ppermute(value, ('batch', 'seq'), pairs)  63 us
    dot_general x5, matrix products, dot_last(): lax.dot_general(left_side, right_side, (((2,), (0,)), ((), ())), preferre...  43.7 us
    pallas_call x2, Pallas kernels, tall_grad(): pl.pallas_call(lambda *refs: tall_grad_kernel(groups, *refs), grid_spec=p...  40.9 us
    pallas_call x1, Pallas kernels, mixed_grad(): pl.pallas_call(lambda *refs: mixed_grad_kernel(outer, *refs), grid_spec=p...  39.5 us
  transfers between devices with their start and end apart: 68, of which 25 were waited for; matrix products, arithmetic and copies ran while one was open for 25% of the time, Pallas kernels for 32%

profile of v5, /device:TPU:0, one launch (start us, length us, event | category | flops | bytes accessed | tf_op | source)
XLA Modules:
  0.0 822.2 jit_solution(17971078044203710973)
XLA Ops:
  10.3 3.0 collective-permute-start
  13.4 2.6 collective-permute-start.1
  27.4 4.9 concatenate.126
  37.8 4.4 collective-permute-start.4
  47.1 8.1 maximum_maximum_fusion
  63.9 11.8 %collective-permute-done.12 = bf16[288,1152]{1,0:T(8,128)(2,1)S(1)} collective-permute-done((bf16[288,1152]{1,0:T(8,128)(2,1)S(1)}, bf16[288,1152]{1,0:T(8,128)(2,1)S(1)}, u32[]{:S(2)}, u32[]{:S(2)}) %collective-permute-start.12) | collective-permute-done | bytes 663584 | tf_op jit(solution)/shard_map/ppermute | solution.py:640
  81.1 2.9 collective-permute-done.10.refs_9_
  84.0 7.5 join_skip.1
  91.5 13.6 %collective-permute-done.14.refs_3_ = bf16[576,1152]{1,0:T(8,128)(2,1)S(1)} collective-permute-done((bf16[576,1152]{1,0:T(8,128)(2,1)S(1)}, bf16[576,1152]{1,0:T(8,128)(2,1)S(1)}, u32[]{:S(2)}, u32[]{:S(2)}) %collective-permute-start.14) | collective-permute-done | bytes 1327136 | tf_op jit(solution)/shard_map/ppermute | solution.py:640
  107.4 11.6 %fusion.6 = f32[2,544,1152]{2,1,0:T(8,128)} fusion(bf16[2,544,2304]{2,1,0:T(8,128)(2,1)} %maximum_maximum_fusion, bf16[2304,1152]{1,0:T(8,128)(2,1)} %join_skip.1, f32[1152]{0:T(1024)S(1)} %reshape.366), kind=kOutput, calls=%fused_computation.22 | convolution fusion | flops 5776809984 | bytes 15340032 | tf_op jit(solution)/shard_map/dot_general | solution.py:590
  119.0 3.8 collective-permute-start.19
  122.7 2.7 reduce_sum.90
  125.5 3.2 multiply_reduce_fusion.2
  128.7 9.1 %collective-permute-done.19 = bf16[144,1152]{1,0:T(8,128)(2,1)S(1)} collective-permute-done((bf16[144,1152]{1,0:T(8,128)(2,1)S(1)}, bf16[144,1152]{1,0:T(8,128)(2,1)S(1)}, u32[]{:S(2)}, u32[]{:S(2)}) %collective-permute-start.19) | collective-permute-done | bytes 331808 | tf_op jit(solution)/shard_map/ppermute | solution.py:640
  145.4 3.2 collective-permute-start.22
  148.6 9.9 %join_mixed.1 = (bf16[1152,1152]{1,0:T(8,128)(2,1)}, bf16[1152,2304]{1,0:T(8,128)(2,1)}, bf16[1152,1152]{1,0:T(8,128)(2,1)}) custom-call(s32[4]{0:T(128)} %shift-right-arithmetic_or_fusion.refs_0_, s32[8]{0:T(128)} %xor_add_fusion.1.refs_1_, bf16[576,1152]{1,0:T(8,128)(2,1)} %copy-done.19, bf16[576,1152]{1,0:T(8,128)(2,1)} %copy-done.24, ...), custom_call_target="tpu_custom_call" | custom-call | bytes 21233664 | tf_op jit(solution)/shard_map/join_mixed/pallas_call | solution.py:726
  161.7 9.2 %collective-permute-done.22 = bf16[288,1152]{1,0:T(8,128)(2,1)} collective-permute-done((bf16[288,1152]{1,0:T(8,128)(2,1)}, bf16[288,1152]{1,0:T(8,128)(2,1)}, u32[]{:S(2)}, u32[]{:S(2)}) %collective-permute-start.22) | collective-permute-done | bytes 663584 | tf_op jit(solution)/shard_map/ppermute | solution.py:640
  172.2 11.5 %convolution_convert_fusion.own_ref = bf16[2,544,2304]{2,1,0:T(8,128)(2,1)} fusion(bf16[2,544,1152]{2,1,0:T(8,128)(2,1)S(1)} %add_convert_fusion.7, bf16[1152,2304]{1,0:T(8,128)(2,1)} %get-tuple-element.125), kind=kOutput, calls=%fused_computation.3 | convolution fusion | flops 5778063360 | bytes 12828672 | tf_op jit(solution)/shard_map/dot_general | solution.py:590
  183.8 13.8 %collective-permute-done.24 = bf16[1,544,1152]{2,1,0:T(8,128)(2,1)} collective-permute-done((bf16[1,544,1152]{2,1,0:T(8,128)(2,1)}, bf16[1,544,1152]{2,1,0:T(8,128)(2,1)}, u32[]{:S(2)}, u32[]{:S(2)}) %collective-permute-start.24) | collective-permute-done | bytes 1253408 | tf_op jit(solution)/shard_map/ppermute | solution.py:640
  197.6 5.0 convolution_convert_fusion.3.q_ref
  208.3 7.7 fusion.9.far_ref
  216.0 33.4 %attend.2 = (bf16[2,544,1152]{2,1,0:T(8,128)(2,1)}, f32[2,16,544]{2,1,0:T(8,128)}) custom-call(bf16[2,544,1152]{2,1,0:T(8,128)(2,1)} %convolution_convert_fusion.3.q_ref, bf16[2,544,2304]{2,1,0:T(8,128)(2,1)} %convolution_convert_fusion.own_ref, bf16[1,544,2304]{2,1,0:T(8,128)(2,1)} %fusion.9.far_ref, s32[2,1,544]{2,1,0:T(1,128)} %add_select_fusion.qid_ref, ...), custom_call_target="tpu_custom_call" | custom-call | flops 4848615424 | bytes 7520256 | tf_op jit(solution)/shard_map/attend/pallas_call | solution.py:106
  251.5 11.9 %collective-permute-done.28.refs_3_ = bf16[576,1152]{1,0:T(8,128)(2,1)} collective-permute-done((bf16[576,1152]{1,0:T(8,128)(2,1)S(1)}, bf16[576,1152]{1,0:T(8,128)(2,1)}, u32[]{:S(2)}, u32[]{:S(2)}) %collective-permute-start.28) | collective-permute-done | bytes 1327136 | tf_op jit(solution)/shard_map/ppermute | solution.py:640
  265.2 7.8 fusion.10.far_ref
  273.0 33.1 %attend.3 = (bf16[2,544,1152]{2,1,0:T(8,128)(2,1)}, f32[2,16,544]{2,1,0:T(8,128)}) custom-call(bf16[2,544,1152]{2,1,0:T(8,128)(2,1)} %convolution_convert_fusion.3.q_ref, bf16[2,544,2304]{2,1,0:T(8,128)(2,1)} %convolution_convert_fusion.own_ref, bf16[1,544,2304]{2,1,0:T(8,128)(2,1)} %fusion.10.far_ref, ...), custom_call_target="tpu_custom_call", output_to_operand_aliasing={{0}: (5, {}), {1}: (6, {})} | custom-call | flops 4848615424 | bytes 7520256 | tf_op jit(solution)/shard_map/attend/pallas_call | solution.py:106
  312.0 2.0 broadcast_select_fusion.refs_2_
  317.5 8.9 %place_blocks.1 = bf16[32,144,1152]{2,1,0:T(8,128)(2,1)} custom-call(s32[32]{0:T(128)} %xor_add_fusion.refs_0_, bf16[576,1152]{1,0:T(8,128)(2,1)} %copy-done.9, bf16[576,1152]{1,0:T(8,128)(2,1)} %collective-permute-done.25.refs_2_, bf16[576,1152]{1,0:T(8,128)(2,1)} %collective-permute-done.28.refs_3_, bf16[576,1152]{1,0:T(8,128)(2,1)} %collective-permute-done.32.refs_4_, ...), custom_call_target="tpu_custom_call" | custom-call | bytes 21233664 | tf_op jit(solution)/shard_map/place_blocks/pallas_call | solution.py:774
  326.4 11.0 %join_down.1 = bf16[4608,1152]{1,0:T(8,128)(2,1)} custom-call(s32[4]{0:T(128)} %shift-right-arithmetic_or_fusion.refs_0_, s32[8]{0:T(128)} %xor_add_fusion.1.refs_1_, bf16[5184,128]{1,0:T(8,128)(2,1)} %copy-done.10, bf16[5184,128]{1,0:T(8,128)(2,1)} %collective-permute-done.29.refs_3_, bf16[5184,128]{1,0:T(8,128)(2,1)} %collective-permute-done.30.refs_4_, ...), custom_call_target="tpu_custom_call" | custom-call | bytes 21233664 | tf_op jit(solution)/shard_map/join_down/pallas_call | solution.py:726
  337.4 83.6 %middle_block.1 = (bf16[1088,1152]{1,0:T(8,128)(2,1)}, bf16[1088,1152]{1,0:T(8,128)(2,1)}, bf16[1088,4608]{1,0:T(8,128)(2,1)}, bf16[1088,4608]{1,0:T(8,128)(2,1)...) custom-call(f32[1088,1152]{1,0:T(8,128)} %bitcast.196, ...), custom_call_target="tpu_custom_call" | custom-call | flops 51980009472 | bytes 135069696 | tf_op jit(solution)/shard_map/middle_block/pallas_call | solution.py:497
  421.1 25.9 %down_weight_grad.1 = (bf16[4,4,1296,128]{3,2,1,0:T(8,128)(2,1)}, bf16[4,4,1296,128]{3,2,1,0:T(8,128)(2,1)}) custom-call(s32[1]{0:T(128)} %bitcast.26.refs_0_, bf16[1088,4608]{1,0:T(8,128)(2,1)} %get-tuple-element.147.refs_1_, bf16[1088,1152]{1,0:T(8,128)(2,1)} %broadcast_select_fusion.refs_2_), custom_call_target="tpu_custom_call" | custom-call | flops 11551113216 | bytes 20643840 | tf_op jit(solution)/shard_map/down_weight_grad/pallas_call | solution.py:308
  447.1 21.1 %hidden_weight_grad.1 = (bf16[576,4608]{1,0:T(8,128)(2,1)}, bf16[576,4608]{1,0:T(8,128)(2,1)}) custom-call(s32[1]{0:T(128)} %bitcast.26.refs_0_, bf16[1088,1152]{1,0:T(8,128)(2,1)} %get-tuple-element.149.refs_1_, bf16[1088,4608]{1,0:T(8,128)(2,1)} %get-tuple-element.150.refs_2_), custom_call_target="tpu_custom_call" | custom-call | flops 11551113216 | bytes 13123584 | tf_op jit(solution)/shard_map/hidden_weight_grad/pallas_call | solution.py:265
  468.6 5.5 add_convert_fusion.2
  477.7 3.8 add_convert_fusion.1
  481.6 2.8 constant_dynamic-slice_fusion.26
  485.8 46.7 %attend_back.2 = (bf16[2,544,1152]{2,1,0:T(8,128)(2,1)}, bf16[2,1088,2304]{2,1,0:T(8,128)(2,1)}) custom-call(bf16[2,544,1152]{2,1,0:T(8,128)(2,1)} %convolution_convert_fusion.3.q_ref, bf16[2,544,2304]{2,1,0:T(8,128)(2,1)} %convolution_convert_fusion.own_ref, bf16[1,544,2304]{2,1,0:T(8,128)(2,1)} %fusion.9.far_ref, ...), custom_call_target="tpu_custom_call" | custom-call | flops 12121538560 | bytes 15040512 | tf_op jit(solution)/shard_map/attend_back/pallas_call | solution.py:194
  532.4 3.5 collective-permute-done.42
  535.9 2.4 add_convert_fusion.5
  540.3 4.8 collective-permute-done.43
  545.1 2.5 add_convert_fusion.4
  550.8 6.2 fusion.11
  557.4 46.9 %attend_back.3 = (bf16[2,544,1152]{2,1,0:T(8,128)(2,1)}, bf16[2,1088,2304]{2,1,0:T(8,128)(2,1)}) custom-call(bf16[2,544,1152]{2,1,0:T(8,128)(2,1)} %convolution_convert_fusion.3.q_ref, bf16[2,544,2304]{2,1,0:T(8,128)(2,1)} %convolution_convert_fusion.own_ref, bf16[1,544,2304]{2,1,0:T(8,128)(2,1)} %fusion.10.far_ref, ...), custom_call_target="tpu_custom_call", output_to_operand_aliasing={{0}: (8, {}), {1}: (9, {})} | custom-call | flops 12121538560 | bytes 15040512 | tf_op jit(solution)/shard_map/attend_back/pallas_call | solution.py:194
  607.8 7.7 fusion.12
  617.1 39.5 %mixed_weight_grad.1 = (bf16[576,4608]{1,0:T(8,128)(2,1)}, bf16[576,4608]{1,0:T(8,128)(2,1)}) custom-call(s32[1]{0:T(128)} %bitcast.26.refs_0_, bf16[1088,1152]{1,0:T(8,128)(2,1)} %bitcast.206, bf16[544,1152]{1,0:T(8,128)(2,1)} %bitcast.15.refs_2_, bf16[544,1152]{1,0:T(8,128)(2,1)} %bitcast.17.refs_3_, bf16[1088,1152]{1,0:T(8,128)(2,1)} %bitcast.244, ...), custom_call_target="tpu_custom_call" | custom-call | flops 17326669824 | bytes 35684352 | tf_op jit(solution)/shard_map/mixed_weight_grad/pallas_call | solution.py:380
  657.2 10.3 %fusion = f32[2,544,1152]{2,1,0:T(8,128)S(1)} fusion(bf16[1152,2304]{1,0:T(8,128)(2,1)} %get-tuple-element.125, bf16[2,1088,2304]{2,1,0:T(8,128)(2,1)} %get-tuple-element.174), kind=kOutput, calls=%fused_computation.4 | convolution fusion | flops 5775556608 | bytes 15335424 | tf_op jit(solution)/shard_map/dot_general | solution.py:596
  667.5 3.8 convolution_add_fusion
  674.5 3.0 collective-permute-start.63
  677.5 5.4 add_convert_fusion
  689.0 4.3 multiply_reduce_fusion
  693.4 4.7 convert_reduce_fusion
  698.1 15.0 %skip_weight_grad.1 = (bf16[4,4,648,128]{3,2,1,0:T(8,128)(2,1)}, bf16[4,4,648,128]{3,2,1,0:T(8,128)(2,1)}) custom-call(s32[1]{0:T(128)} %bitcast.26.refs_0_, bf16[1088,2304]{1,0:T(8,128)(2,1)} %bitcast.215, bf16[1088,1152]{1,0:T(8,128)(2,1)} %bitcast.225), custom_call_target="tpu_custom_call" | custom-call | flops 5775556608 | bytes 10321920 | tf_op jit(solution)/shard_map/skip_weight_grad/pallas_call | solution.py:308
  713.2 6.3 fusion.14
  719.5 2.2 copy-done.5
  735.5 2.6 add_convert_fusion.3
  740.4 3.8 fusion.13
  744.3 4.5 collective-permute-done.54
  749.7 2.8 collective-permute-done.53
  752.8 2.0 collective-permute-start.59
  755.0 10.3 %collective-permute-done.57 = bf16[4,2,320,128]{3,2,0,1:T(8,128)(2,1)S(1)} collective-permute-done((bf16[4,2,320,128]{3,2,0,1:T(8,128)(2,1)S(1)}, bf16[4,2,320,128]{3,2,0,1:T(8,128)(2,1)S(1)}, u32[]{:S(2)}, u32[]{:S(2)}) %collective-permute-start.57) | collective-permute-done | bytes 655392 | tf_op jit(solution)/shard_map/ppermute | solution.py:640
  766.1 1.9 collective-permute-done.55
  769.8 4.4 collective-permute-done.58
  777.7 7.2 collective-permute-done.59
  785.3 6.8 collective-permute-done.60
  796.3 2.7 add_bitcast_fusion
  799.2 8.2 %collective-permute-done.62 = bf16[1,144,1152]{2,1,0:T(8,128)(2,1)S(1)} collective-permute-done((bf16[1,144,1152]{2,1,0:T(8,128)(2,1)S(1)}, bf16[1,144,1152]{2,1,0:T(8,128)(2,1)S(1)}, u32[]{:S(2)}, u32[]{:S(2)}) %collective-permute-start.62) | collective-permute-done | bytes 331808 | tf_op jit(solution)/shard_map/ppermute | solution.py:640
  (399 shorter events, 133.6 us)
Async XLA Ops:
  7.2 803.2 %all-gather.2.cloned.1.call-start = ((), (), s32[]{:S(2)}) async-start(), calls=%async_computation | async-start | bytes 1757184 | tf_op jit(solution)/shard_map/all_gather | solution.py:992
  10.3 22.1 %collective-permute-start = (bf16[648,128]{1,0:T(8,128)(2,1)}, bf16[648,128]{1,0:T(8,128)(2,1)}, u32[]{:S(2)}, u32[]{:S(2)}) collective-permute-start(bf16[648,128]{1,0:T(8,128)(2,1)} %maximum_maximum_fusion.4), channel_id=1, source_target_pairs={{0,8},{1,9},{2,10},{3,11},{4,12},{5,13},{6,14},{7,15},{8,0},{9,1},... | collective-permute-start | bytes 497672 | tf_op jit(solution)/shard_map/ppermute | solution.py:640
  13.4 20.6 %collective-permute-start.1 = (bf16[648,128]{1,0:T(8,128)(2,1)}, bf16[648,128]{1,0:T(8,128)(2,1)}, u32[]{:S(2)}, u32[]{:S(2)}) collective-permute-start(bf16[648,128]{1,0:T(8,128)(2,1)} %maximum_maximum_fusion.4), channel_id=1, source_target_pairs={{0,16},{1,17},{2,18},{3,19},{4,20},{5,21},{6,22},{7,23},{8,24},{9,... | collective-permute-start | bytes 497672 | tf_op jit(solution)/shard_map/ppermute | solution.py:640
  16.0 19.6 %collective-permute-start.2 = (bf16[648,128]{1,0:T(8,128)(2,1)}, bf16[648,128]{1,0:T(8,128)(2,1)}, u32[]{:S(2)}, u32[]{:S(2)}) collective-permute-start(bf16[648,128]{1,0:T(8,128)(2,1)} %maximum_maximum_fusion.4), channel_id=1, source_target_pairs={{0,24},{1,25},{2,26},{3,27},{4,28},{5,29},{6,30},{7,31},{8,16},{9,... | collective-permute-start | bytes 497672 | tf_op jit(solution)/shard_map/ppermute | solution.py:640
  17.9 28.1 %collective-permute-start.3 = (bf16[3,2,24,1152]{3,2,1,0:T(8,128)(2,1)S(1)}, bf16[3,2,24,1152]{3,2,1,0:T(8,128)(2,1)}, u32[]{:S(2)}, u32[]{:S(2)}) collective-permute-start(bf16[3,2,24,1152]{3,2,1,0:T(8,128)(2,1)S(1)} %pad_maximum_fusion.6), channel_id=1, source_target_pairs={{1,2},{5,6},{9,10},{13,14},{17,18},{21,22},{25,26},{29,30}} | collective-permute-start | bytes 995336 | tf_op jit(solution)/shard_map/ppermute | solution.py:647
  37.8 18.8 %collective-permute-start.4 = (bf16[2624,128]{1,0:T(8,128)(2,1)}, bf16[2624,128]{1,0:T(8,128)(2,1)}, u32[]{:S(2)}, u32[]{:S(2)}) collective-permute-start(bf16[2624,128]{1,0:T(8,128)(2,1)} %constant_dynamic-update-slice_fusion.refs_2_), channel_id=1, source_target_pairs={{0,1},{1,0},{2,3},{3,2},{4,5},{5,4},{6,7},{7,6},{8,9},{9,8},{10,11... | collective-permute-start | bytes 2015240 | tf_op jit(solution)/shard_map/ppermute | solution.py:640
  42.3 15.8 %collective-permute-start.5 = (bf16[2624,128]{1,0:T(8,128)(2,1)}, bf16[2624,128]{1,0:T(8,128)(2,1)}, u32[]{:S(2)}, u32[]{:S(2)}) collective-permute-start(bf16[2624,128]{1,0:T(8,128)(2,1)} %constant_dynamic-update-slice_fusion.refs_2_), channel_id=1, source_target_pairs={{0,2},{1,3},{2,0},{3,1},{4,6},{5,7},{6,4},{7,5},{8,10},{9,11},{10,... | collective-permute-start | bytes 2015240 | tf_op jit(solution)/shard_map/ppermute | solution.py:640
  43.4 16.3 %collective-permute-start.11 = (bf16[144,1152]{1,0:T(8,128)(2,1)S(1)}, bf16[144,1152]{1,0:T(8,128)(2,1)S(1)}, u32[]{:S(2)}, u32[]{:S(2)}) collective-permute-start(bf16[144,1152]{1,0:T(8,128)(2,1)S(1)} %pad_maximum_fusion.7), channel_id=1, source_target_pairs={{0,16},{1,17},{2,18},{3,19},{4,20},{5,21},{6,22},{7,23},{8,24},{9,... | collective-permute-start | bytes 995336 | tf_op jit(solution)/shard_map/ppermute | solution.py:640
  59.7 15.9 %collective-permute-start.12 = (bf16[288,1152]{1,0:T(8,128)(2,1)S(1)}, bf16[288,1152]{1,0:T(8,128)(2,1)S(1)}, u32[]{:S(2)}, u32[]{:S(2)}) collective-permute-start(bf16[288,1152]{1,0:T(8,128)(2,1)S(1)} %pad_maximum_fusion.3), channel_id=1, source_target_pairs={{0,8},{1,9},{2,10},{3,11},{4,12},{5,13},{6,14},{7,15},{8,0},{9,1},... | collective-permute-start | bytes 1990664 | tf_op jit(solution)/shard_map/ppermute | solution.py:640
  59.8 18.8 %collective-permute-start.6 = (bf16[2624,128]{1,0:T(8,128)(2,1)}, bf16[2624,128]{1,0:T(8,128)(2,1)}, u32[]{:S(2)}, u32[]{:S(2)}) collective-permute-start(bf16[2624,128]{1,0:T(8,128)(2,1)} %collective-permute-done.4.refs_3_), channel_id=1, source_target_pairs={{0,2},{1,3},{2,0},{3,1},{4,6},{5,7},{6,4},{7,5},{8,10},{9,11},{10,... | collective-permute-start | bytes 2015240 | tf_op jit(solution)/shard_map/ppermute | solution.py:640
  61.6 17.8 %collective-permute-start.8 = (bf16[2624,128]{1,0:T(8,128)(2,1)}, bf16[2624,128]{1,0:T(8,128)(2,1)}, u32[]{:S(2)}, u32[]{:S(2)}) collective-permute-start(bf16[2624,128]{1,0:T(8,128)(2,1)} %collective-permute-done.4.refs_3_), channel_id=1, source_target_pairs={{0,4},{1,5},{2,6},{3,7},{4,0},{5,1},{6,2},{7,3},{8,12},{9,13},{10,... | collective-permute-start | bytes 2015240 | tf_op jit(solution)/shard_map/ppermute | solution.py:640
  61.6 18.3 %collective-permute-start.9 = (bf16[2624,128]{1,0:T(8,128)(2,1)}, bf16[2624,128]{1,0:T(8,128)(2,1)}, u32[]{:S(2)}, u32[]{:S(2)}) collective-permute-start(bf16[2624,128]{1,0:T(8,128)(2,1)} %collective-permute-done.5.refs_4_), channel_id=1, source_target_pairs={{0,4},{1,5},{2,6},{3,7},{4,0},{5,1},{6,2},{7,3},{8,12},{9,13},{10,... | collective-permute-start | bytes 2015240 | tf_op jit(solution)/shard_map/ppermute | solution.py:640
  75.8 29.3 %collective-permute-start.14 = (bf16[576,1152]{1,0:T(8,128)(2,1)S(1)}, bf16[576,1152]{1,0:T(8,128)(2,1)S(1)}, u32[]{:S(2)}, u32[]{:S(2)}) collective-permute-start(bf16[576,1152]{1,0:T(8,128)(2,1)S(1)} %constant_dynamic-update-slice_fusion.7.refs_2_), channel_id=1, source_target_pairs={{0,1},{1,0},{2,3},{3,2},{4,5},{5,4},{6,7},{7,6},{8,9},{9,8},{10,11... | collective-permute-start | bytes 3981320 | tf_op jit(solution)/shard_map/ppermute | solution.py:640
  76.1 30.7 %collective-permute-start.15 = (bf16[576,1152]{1,0:T(8,128)(2,1)S(1)}, bf16[576,1152]{1,0:T(8,128)(2,1)}, u32[]{:S(2)}, u32[]{:S(2)}) collective-permute-start(bf16[576,1152]{1,0:T(8,128)(2,1)S(1)} %constant_dynamic-update-slice_fusion.7.refs_2_), channel_id=1, source_target_pairs={{0,2},{1,3},{2,0},{3,1},{4,6},{5,7},{6,4},{7,5},{8,10},{9,11},{10,... | collective-permute-start | bytes 3981320 | tf_op jit(solution)/shard_map/ppermute | solution.py:640
  79.4 39.5 %collective-permute-start.13 = (bf16[576,1152]{1,0:T(8,128)(2,1)S(1)}, bf16[576,1152]{1,0:T(8,128)(2,1)}, u32[]{:S(2)}, u32[]{:S(2)}) collective-permute-start(bf16[576,1152]{1,0:T(8,128)(2,1)S(1)} %constant_dynamic-update-slice_fusion.7.refs_2_), channel_id=1, source_target_pairs={{0,4},{1,5},{2,6},{3,7},{4,0},{5,1},{6,2},{7,3},{8,12},{9,13},{10,... | collective-permute-start | bytes 3981320 | tf_op jit(solution)/shard_map/ppermute | solution.py:640
  105.1 32.7 %collective-permute-start.16 = (bf16[576,1152]{1,0:T(8,128)(2,1)S(1)}, bf16[576,1152]{1,0:T(8,128)(2,1)}, u32[]{:S(2)}, u32[]{:S(2)}) collective-permute-start(bf16[576,1152]{1,0:T(8,128)(2,1)S(1)} %collective-permute-done.14.refs_3_), channel_id=1, source_target_pairs={{0,2},{1,3},{2,0},{3,1},{4,6},{5,7},{6,4},{7,5},{8,10},{9,11},{10,... | collective-permute-start | bytes 3981320 | tf_op jit(solution)/shard_map/ppermute | solution.py:640
  106.8 31.0 %collective-permute-start.17 = (bf16[576,1152]{1,0:T(8,128)(2,1)S(1)}, bf16[576,1152]{1,0:T(8,128)(2,1)}, u32[]{:S(2)}, u32[]{:S(2)}) collective-permute-start(bf16[576,1152]{1,0:T(8,128)(2,1)S(1)} %collective-permute-done.14.refs_3_), channel_id=1, source_target_pairs={{0,4},{1,5},{2,6},{3,7},{4,0},{5,1},{6,2},{7,3},{8,12},{9,13},{10,... | collective-permute-start | bytes 3981320 | tf_op jit(solution)/shard_map/ppermute | solution.py:640
  106.8 31.0 %collective-permute-start.18 = (bf16[576,1152]{1,0:T(8,128)(2,1)}, bf16[576,1152]{1,0:T(8,128)(2,1)}, u32[]{:S(2)}, u32[]{:S(2)}) collective-permute-start(bf16[576,1152]{1,0:T(8,128)(2,1)} %collective-permute-done.15.refs_4_), channel_id=1, source_target_pairs={{0,4},{1,5},{2,6},{3,7},{4,0},{5,1},{6,2},{7,3},{8,12},{9,13},{10,... | collective-permute-start | bytes 3981320 | tf_op jit(solution)/shard_map/ppermute | solution.py:640
  119.0 18.8 %collective-permute-start.19 = (bf16[144,1152]{1,0:T(8,128)(2,1)S(1)}, bf16[144,1152]{1,0:T(8,128)(2,1)S(1)}, u32[]{:S(2)}, u32[]{:S(2)}) collective-permute-start(bf16[144,1152]{1,0:T(8,128)(2,1)S(1)} %copy-done.25), channel_id=1, source_target_pairs={{0,16},{1,17},{2,18},{3,19},{4,20},{5,21},{6,22},{7,23},{8,24},{9,... | collective-permute-start | bytes 995336 | tf_op jit(solution)/shard_map/ppermute | solution.py:640
  137.8 10.8 %collective-permute-start.20 = (bf16[576,1152]{1,0:T(8,128)(2,1)}, bf16[576,1152]{1,0:T(8,128)(2,1)}, u32[]{:S(2)}, u32[]{:S(2)}) collective-permute-start(bf16[576,1152]{1,0:T(8,128)(2,1)} %collective-permute-done.16.refs_5_), channel_id=1, source_target_pairs={{0,4},{1,5},{2,6},{3,7},{4,0},{5,1},{6,2},{7,3},{8,12},{9,13},{10,... | collective-permute-start | bytes 3981320 | tf_op jit(solution)/shard_map/ppermute | solution.py:640
  140.5 31.7 %collective-permute-start.21 = (bf16[1,544,1152]{2,1,0:T(8,128)(2,1)}, bf16[1,544,1152]{2,1,0:T(8,128)(2,1)}, u32[]{:S(2)}, u32[]{:S(2)}) collective-permute-start(bf16[1,544,1152]{2,1,0:T(8,128)(2,1)} %get-tuple-element.315), channel_id=1, source_target_pairs={{0,1},{1,0},{2,3},{3,2},{4,5},{5,4},{6,7},{7,6},{8,9},{9,8},{10,11... | collective-permute-start | bytes 3760136 | tf_op jit(solution)/shard_map/ppermute | solution.py:640
  142.4 18.0 %collective-permute-start.23 = (bf16[1296,128]{1,0:T(8,128)(2,1)S(1)}, bf16[1296,128]{1,0:T(8,128)(2,1)S(1)}, u32[]{:S(2)}, u32[]{:S(2)}) collective-permute-start(bf16[1296,128]{1,0:T(8,128)(2,1)S(1)} %copy-done.20), channel_id=1, source_target_pairs={{0,16},{1,17},{2,18},{3,19},{4,20},{5,21},{6,22},{7,23},{8,24},{9,... | collective-permute-start | bytes 995336 | tf_op jit(solution)/shard_map/ppermute | solution.py:640
  143.7 53.9 %collective-permute-start.24 = (bf16[1,544,1152]{2,1,0:T(8,128)(2,1)}, bf16[1,544,1152]{2,1,0:T(8,128)(2,1)}, u32[]{:S(2)}, u32[]{:S(2)}) collective-permute-start(bf16[1,544,1152]{2,1,0:T(8,128)(2,1)} %get-tuple-element.314), channel_id=1, source_target_pairs={{0,1},{1,0},{2,3},{3,2},{4,5},{5,4},{6,7},{7,6},{8,9},{9,8},{10,11... | collective-permute-start | bytes 3760136 | tf_op jit(solution)/shard_map/ppermute | solution.py:640
  145.4 25.6 %collective-permute-start.22 = (bf16[288,1152]{1,0:T(8,128)(2,1)}, bf16[288,1152]{1,0:T(8,128)(2,1)}, u32[]{:S(2)}, u32[]{:S(2)}) collective-permute-start(bf16[288,1152]{1,0:T(8,128)(2,1)} %constant_dynamic-update-slice_fusion.10), channel_id=1, source_target_pairs={{0,8},{1,9},{2,10},{3,11},{4,12},{5,13},{6,14},{7,15},{8,0},{9,1},... | collective-permute-start | bytes 1990664 | tf_op jit(solution)/shard_map/ppermute | solution.py:640
  160.5 42.2 %collective-permute-start.26 = (bf16[2592,128]{1,0:T(8,128)(2,1)S(1)}, bf16[2592,128]{1,0:T(8,128)(2,1)S(1)}, u32[]{:S(2)}, u32[]{:S(2)}) collective-permute-start(bf16[2592,128]{1,0:T(8,128)(2,1)S(1)} %constant_dynamic-update-slice_fusion.14), channel_id=1, source_target_pairs={{0,8},{1,9},{2,10},{3,11},{4,12},{5,13},{6,14},{7,15},{8,0},{9,1},... | collective-permute-start | bytes 1990664 | tf_op jit(solution)/shard_map/ppermute | solution.py:640
  172.1 36.1 %collective-permute-start.27 = (bf16[576,1152]{1,0:T(8,128)(2,1)S(1)}, bf16[576,1152]{1,0:T(8,128)(2,1)}, u32[]{:S(2)}, u32[]{:S(2)}) collective-permute-start(bf16[576,1152]{1,0:T(8,128)(2,1)S(1)} %constant_dynamic-update-slice_fusion.12.refs_1_), channel_id=1, source_target_pairs={{0,4},{1,5},{2,6},{3,7},{4,0},{5,1},{6,2},{7,3},{8,12},{9,13},{10,... | collective-permute-start | bytes 3981320 | tf_op jit(solution)/shard_map/ppermute | solution.py:640
  202.8 46.6 %collective-permute-start.30 = (bf16[5184,128]{1,0:T(8,128)(2,1)S(1)}, bf16[5184,128]{1,0:T(8,128)(2,1)}, u32[]{:S(2)}, u32[]{:S(2)}) collective-permute-start(bf16[5184,128]{1,0:T(8,128)(2,1)S(1)} %constant_dynamic-update-slice_fusion.16.refs_2_), channel_id=1, source_target_pairs={{0,2},{1,3},{2,0},{3,1},{4,6},{5,7},{6,4},{7,5},{8,10},{9,11},{10,... | collective-permute-start | bytes 3981320 | tf_op jit(solution)/shard_map/ppermute | solution.py:640
  204.6 45.1 %collective-permute-start.25 = (bf16[576,1152]{1,0:T(8,128)(2,1)S(1)}, bf16[576,1152]{1,0:T(8,128)(2,1)}, u32[]{:S(2)}, u32[]{:S(2)}) collective-permute-start(bf16[576,1152]{1,0:T(8,128)(2,1)S(1)} %constant_dynamic-update-slice_fusion.12.refs_1_), channel_id=1, source_target_pairs={{0,1},{1,0},{2,3},{3,2},{4,5},{5,4},{6,7},{7,6},{8,9},{9,8},{10,11... | collective-permute-start | bytes 3981320 | tf_op jit(solution)/shard_map/ppermute | solution.py:640
  206.4 57.0 %collective-permute-start.28 = (bf16[576,1152]{1,0:T(8,128)(2,1)S(1)}, bf16[576,1152]{1,0:T(8,128)(2,1)}, u32[]{:S(2)}, u32[]{:S(2)}) collective-permute-start(bf16[576,1152]{1,0:T(8,128)(2,1)S(1)} %constant_dynamic-update-slice_fusion.12.refs_1_), channel_id=1, source_target_pairs={{0,2},{1,3},{2,0},{3,1},{4,6},{5,7},{6,4},{7,5},{8,10},{9,11},{10,... | collective-permute-start | bytes 3981320 | tf_op jit(solution)/shard_map/ppermute | solution.py:640
  206.7 58.6 %collective-permute-start.29 = (bf16[5184,128]{1,0:T(8,128)(2,1)S(1)}, bf16[5184,128]{1,0:T(8,128)(2,1)}, u32[]{:S(2)}, u32[]{:S(2)}) collective-permute-start(bf16[5184,128]{1,0:T(8,128)(2,1)S(1)} %constant_dynamic-update-slice_fusion.16.refs_2_), channel_id=1, source_target_pairs={{0,1},{1,0},{2,3},{3,2},{4,5},{5,4},{6,7},{7,6},{8,9},{9,8},{10,11... | collective-permute-start | bytes 3981320 | tf_op jit(solution)/shard_map/ppermute | solution.py:640
  208.3 57.0 %collective-permute-start.31 = (bf16[5184,128]{1,0:T(8,128)(2,1)S(1)}, bf16[5184,128]{1,0:T(8,128)(2,1)}, u32[]{:S(2)}, u32[]{:S(2)}) collective-permute-start(bf16[5184,128]{1,0:T(8,128)(2,1)S(1)} %constant_dynamic-update-slice_fusion.16.refs_2_), channel_id=1, source_target_pairs={{0,4},{1,5},{2,6},{3,7},{4,0},{5,1},{6,2},{7,3},{8,12},{9,13},{10,... | collective-permute-start | bytes 3981320 | tf_op jit(solution)/shard_map/ppermute | solution.py:640
  249.4 56.8 %collective-permute-start.36 = (bf16[5184,128]{1,0:T(8,128)(2,1)}, bf16[5184,128]{1,0:T(8,128)(2,1)}, u32[]{:S(2)}, u32[]{:S(2)}) collective-permute-start(bf16[5184,128]{1,0:T(8,128)(2,1)} %collective-permute-done.30.refs_4_), channel_id=1, source_target_pairs={{0,1},{1,0},{2,3},{3,2},{4,5},{5,4},{6,7},{7,6},{8,9},{9,8},{10,11... | collective-permute-start | bytes 3981320 | tf_op jit(solution)/shard_map/ppermute | solution.py:640
  249.8 60.5 %collective-permute-start.32 = (bf16[576,1152]{1,0:T(8,128)(2,1)}, bf16[576,1152]{1,0:T(8,128)(2,1)}, u32[]{:S(2)}, u32[]{:S(2)}) collective-permute-start(bf16[576,1152]{1,0:T(8,128)(2,1)} %collective-permute-done.25.refs_2_), channel_id=1, source_target_pairs={{0,2},{1,3},{2,0},{3,1},{4,6},{5,7},{6,4},{7,5},{8,10},{9,11},{10,... | collective-permute-start | bytes 3981320 | tf_op jit(solution)/shard_map/ppermute | solution.py:640
  263.4 46.9 %collective-permute-start.33 = (bf16[576,1152]{1,0:T(8,128)(2,1)}, bf16[576,1152]{1,0:T(8,128)(2,1)}, u32[]{:S(2)}, u32[]{:S(2)}) collective-permute-start(bf16[576,1152]{1,0:T(8,128)(2,1)} %collective-permute-done.25.refs_2_), channel_id=1, source_target_pairs={{0,4},{1,5},{2,6},{3,7},{4,0},{5,1},{6,2},{7,3},{8,12},{9,13},{10,... | collective-permute-start | bytes 3981320 | tf_op jit(solution)/shard_map/ppermute | solution.py:640
  265.2 45.1 %collective-permute-start.34 = (bf16[576,1152]{1,0:T(8,128)(2,1)}, bf16[576,1152]{1,0:T(8,128)(2,1)}, u32[]{:S(2)}, u32[]{:S(2)}) collective-permute-start(bf16[576,1152]{1,0:T(8,128)(2,1)} %collective-permute-done.28.refs_3_), channel_id=1, source_target_pairs={{0,4},{1,5},{2,6},{3,7},{4,0},{5,1},{6,2},{7,3},{8,12},{9,13},{10,... | collective-permute-start | bytes 3981320 | tf_op jit(solution)/shard_map/ppermute | solution.py:640
  310.3 7.2 collective-permute-start.35
  311.6 14.8 %collective-permute-start.39 = (bf16[5184,128]{1,0:T(8,128)(2,1)}, bf16[5184,128]{1,0:T(8,128)(2,1)}, u32[]{:S(2)}, u32[]{:S(2)}) collective-permute-start(bf16[5184,128]{1,0:T(8,128)(2,1)} %collective-permute-done.36.refs_5_), channel_id=1, source_target_pairs={{0,4},{1,5},{2,6},{3,7},{4,0},{5,1},{6,2},{7,3},{8,12},{9,13},{10,... | collective-permute-start | bytes 3981320 | tf_op jit(solution)/shard_map/ppermute | solution.py:640
  447.0 21.6 %collective-permute-start.40 = (bf16[4,4,1296,128]{3,2,1,0:T(8,128)(2,1)}, bf16[4,4,1296,128]{3,2,1,0:T(8,128)(2,1)}, u32[]{:S(2)}, u32[]{:S(2)}) collective-permute-start(bf16[4,4,1296,128]{3,2,1,0:T(8,128)(2,1)} %get-tuple-element.148), channel_id=1, source_target_pairs={{0,4},{1,5},{2,6},{3,7},{4,0},{5,1},{6,2},{7,3},{8,12},{9,13},{10,... | collective-permute-start | bytes 15925256 | tf_op jit(solution)/shard_map/ppermute | solution.py:640
  468.2 9.5 %collective-permute-start.41 = (bf16[576,4608]{1,0:T(8,128)(2,1)}, bf16[576,4608]{1,0:T(8,128)(2,1)}, u32[]{:S(2)}, u32[]{:S(2)}) collective-permute-start(bf16[576,4608]{1,0:T(8,128)(2,1)} %get-tuple-element.153), channel_id=1, source_target_pairs={{0,4},{1,5},{2,6},{3,7},{4,0},{5,1},{6,2},{7,3},{8,12},{9,13},{10,... | collective-permute-start | bytes 15925256 | tf_op jit(solution)/shard_map/ppermute | solution.py:640
  475.9 60.0 %collective-permute-start.42 = (bf16[4,2,1296,128]{3,2,1,0:T(8,128)(2,1)}, bf16[4,2,1296,128]{3,2,1,0:T(8,128)(2,1)}, u32[]{:S(2)}, u32[]{:S(2)}) collective-permute-start(bf16[4,2,1296,128]{3,2,1,0:T(8,128)(2,1)} %get-tuple-element.303), channel_id=1, source_target_pairs={{0,1},{1,0},{2,3},{3,2},{4,5},{5,4},{6,7},{7,6},{8,9},{9,8},{10,11... | collective-permute-start | bytes 7962632 | tf_op jit(solution)/shard_map/ppermute | solution.py:640
  484.3 60.8 %collective-permute-start.43 = (bf16[4,144,2304]{2,1,0:T(8,128)(2,1)}, bf16[4,144,2304]{2,1,0:T(8,128)(2,1)}, u32[]{:S(2)}, u32[]{:S(2)}) collective-permute-start(bf16[4,144,2304]{2,1,0:T(8,128)(2,1)} %get-tuple-element.301), channel_id=1, source_target_pairs={{0,2},{1,3},{2,0},{3,1},{4,6},{5,7},{6,4},{7,5},{8,10},{9,11},{10,... | collective-permute-start | bytes 7962632 | tf_op jit(solution)/shard_map/ppermute | solution.py:640
  538.6 65.7 %collective-permute-start.44 = (bf16[4,1296,128]{2,1,0:T(8,128)(2,1)S(1)}, bf16[4,1296,128]{2,1,0:T(8,128)(2,1)}, u32[]{:S(2)}, u32[]{:S(2)}) collective-permute-start(bf16[4,1296,128]{2,1,0:T(8,128)(2,1)S(1)} %get-tuple-element.313), channel_id=1, source_target_pairs={{0,2},{1,3},{2,0},{3,1},{4,6},{5,7},{6,4},{7,5},{8,10},{9,11},{10,... | collective-permute-start | bytes 3981320 | tf_op jit(solution)/shard_map/ppermute | solution.py:640
  549.2 56.8 %collective-permute-start.45 = (bf16[4,144,1152]{2,1,0:T(8,128)(2,1)}, bf16[4,144,1152]{2,1,0:T(8,128)(2,1)}, u32[]{:S(2)}, u32[]{:S(2)}) collective-permute-start(bf16[4,144,1152]{2,1,0:T(8,128)(2,1)} %get-tuple-element.311), channel_id=1, source_target_pairs={{0,1},{1,0},{2,3},{3,2},{4,5},{5,4},{6,7},{7,6},{8,9},{9,8},{10,11... | collective-permute-start | bytes 3981320 | tf_op jit(solution)/shard_map/ppermute | solution.py:640
  557.0 50.8 %collective-permute-start.46 = (bf16[1,544,1152]{2,1,0:T(8,128)(2,1)}, bf16[1,544,1152]{2,1,0:T(8,128)(2,1)}, u32[]{:S(2)}, u32[]{:S(2)}) collective-permute-start(bf16[1,544,1152]{2,1,0:T(8,128)(2,1)} %fusion.11), channel_id=1, source_target_pairs={{0,1},{1,0},{2,3},{3,2},{4,5},{5,4},{6,7},{7,6},{8,9},{9,8},{10,11... | collective-permute-start | bytes 3760136 | tf_op jit(solution)/shard_map/ppermute | solution.py:640
  615.5 41.1 %collective-permute-start.47 = (bf16[1,544,1152]{2,1,0:T(8,128)(2,1)}, bf16[1,544,1152]{2,1,0:T(8,128)(2,1)}, u32[]{:S(2)}, u32[]{:S(2)}) collective-permute-start(bf16[1,544,1152]{2,1,0:T(8,128)(2,1)} %fusion.12), channel_id=1, source_target_pairs={{0,1},{1,0},{2,3},{3,2},{4,5},{5,4},{6,7},{7,6},{8,9},{9,8},{10,11... | collective-permute-start | bytes 3760136 | tf_op jit(solution)/shard_map/ppermute | solution.py:640
  656.6 20.9 %collective-permute-start.48 = (bf16[576,4608]{1,0:T(8,128)(2,1)}, bf16[576,4608]{1,0:T(8,128)(2,1)}, u32[]{:S(2)}, u32[]{:S(2)}) collective-permute-start(bf16[576,4608]{1,0:T(8,128)(2,1)} %get-tuple-element.172), channel_id=1, source_target_pairs={{0,4},{1,5},{2,6},{3,7},{4,0},{5,1},{6,2},{7,3},{8,12},{9,13},{10,... | collective-permute-start | bytes 15925256 | tf_op jit(solution)/shard_map/ppermute | solution.py:640
  672.5 49.3 %collective-permute-start.65 = (bf16[2,1296,128]{2,1,0:T(8,128)(2,1)}, bf16[2,1296,128]{2,1,0:T(8,128)(2,1)}, u32[]{:S(2)}, u32[]{:S(2)}) collective-permute-start(bf16[2,1296,128]{2,1,0:T(8,128)(2,1)} %get-tuple-element.319), channel_id=1, source_target_pairs={{0,16},{1,17},{2,18},{3,19},{4,20},{5,21},{6,22},{7,23},{8,24},{9,... | collective-permute-start | bytes 1990664 | tf_op jit(solution)/shard_map/ppermute | solution.py:640
  674.5 50.5 %collective-permute-start.63 = (bf16[2,144,1152]{2,1,0:T(8,128)(2,1)}, bf16[2,144,1152]{2,1,0:T(8,128)(2,1)}, u32[]{:S(2)}, u32[]{:S(2)}) collective-permute-start(bf16[2,144,1152]{2,1,0:T(8,128)(2,1)} %get-tuple-element.321), channel_id=1, source_target_pairs={{0,8},{1,9},{2,10},{3,11},{4,12},{5,13},{6,14},{7,15},{8,0},{9,1},... | collective-permute-start | bytes 1990664 | tf_op jit(solution)/shard_map/ppermute | solution.py:640
  686.8 42.9 %collective-permute-start.50 = (bf16[4,72,2304]{2,1,0:T(8,128)(2,1)}, bf16[4,72,2304]{2,1,0:T(8,128)(2,1)}, u32[]{:S(2)}, u32[]{:S(2)}) collective-permute-start(bf16[4,72,2304]{2,1,0:T(8,128)(2,1)} %pad_maximum_fusion.1), channel_id=1, source_target_pairs={{0,1},{1,0},{2,3},{3,2},{4,5},{5,4},{6,7},{7,6},{8,9},{9,8},{10,11... | collective-permute-start | bytes 3981320 | tf_op jit(solution)/shard_map/ppermute | solution.py:640
  687.3 45.2 %collective-permute-start.49 = (bf16[4,72,2304]{2,1,0:T(8,128)(2,1)}, bf16[4,72,2304]{2,1,0:T(8,128)(2,1)}, u32[]{:S(2)}, u32[]{:S(2)}) collective-permute-start(bf16[4,72,2304]{2,1,0:T(8,128)(2,1)} %get-tuple-element.309), channel_id=1, source_target_pairs={{0,2},{1,3},{2,0},{3,1},{4,6},{5,7},{6,4},{7,5},{8,10},{9,11},{10,... | collective-permute-start | bytes 3981320 | tf_op jit(solution)/shard_map/ppermute | solution.py:640
  713.1 22.4 %collective-permute-start.51 = (bf16[4,4,648,128]{3,2,1,0:T(8,128)(2,1)}, bf16[4,4,648,128]{3,2,1,0:T(8,128)(2,1)}, u32[]{:S(2)}, u32[]{:S(2)}) collective-permute-start(bf16[4,4,648,128]{3,2,1,0:T(8,128)(2,1)} %get-tuple-element.178), channel_id=1, source_target_pairs={{0,4},{1,5},{2,6},{3,7},{4,0},{5,1},{6,2},{7,3},{8,12},{9,13},{10,... | collective-permute-start | bytes 7962632 | tf_op jit(solution)/shard_map/ppermute | solution.py:640
  725.0 69.8 %collective-permute-start.66 = (bf16[1,1296,128]{2,1,0:T(8,128)(2,1)}, bf16[1,1296,128]{2,1,0:T(8,128)(2,1)}, u32[]{:S(2)}, u32[]{:S(2)}) collective-permute-start(bf16[1,1296,128]{2,1,0:T(8,128)(2,1)} %get-tuple-element.333), channel_id=1, source_target_pairs={{0,8},{1,9},{2,10},{3,11},{4,12},{5,13},{6,14},{7,15},{8,0},{9,1},... | collective-permute-start | bytes 995336 | tf_op jit(solution)/shard_map/ppermute | solution.py:640
  727.2 69.0 %collective-permute-start.64 = (bf16[1,144,1152]{2,1,0:T(8,128)(2,1)}, bf16[1,144,1152]{2,1,0:T(8,128)(2,1)}, u32[]{:S(2)}, u32[]{:S(2)}) collective-permute-start(bf16[1,144,1152]{2,1,0:T(8,128)(2,1)} %get-tuple-element.335), channel_id=1, source_target_pairs={{0,16},{1,17},{2,18},{3,19},{4,20},{5,21},{6,22},{7,23},{8,24},{9,... | collective-permute-start | bytes 995336 | tf_op jit(solution)/shard_map/ppermute | solution.py:640
  731.6 17.2 %collective-permute-start.54 = (bf16[4,72,1152]{2,1,0:T(8,128)(2,1)S(1)}, bf16[4,72,1152]{2,1,0:T(8,128)(2,1)S(1)}, u32[]{:S(2)}, u32[]{:S(2)}) collective-permute-start(bf16[4,72,1152]{2,1,0:T(8,128)(2,1)S(1)} %get-tuple-element.325), channel_id=1, source_target_pairs={{0,2},{1,3},{2,0},{3,1},{4,6},{5,7},{6,4},{7,5},{8,10},{9,11},{10,... | collective-permute-start | bytes 1990664 | tf_op jit(solution)/shard_map/ppermute | solution.py:640
  734.3 18.3 %collective-permute-start.53 = (bf16[4,72,1152]{2,1,0:T(8,128)(2,1)S(1)}, bf16[4,72,1152]{2,1,0:T(8,128)(2,1)S(1)}, u32[]{:S(2)}, u32[]{:S(2)}) collective-permute-start(bf16[4,72,1152]{2,1,0:T(8,128)(2,1)S(1)} %get-tuple-element.327), channel_id=1, source_target_pairs={{0,1},{1,0},{2,3},{3,2},{4,5},{5,4},{6,7},{7,6},{8,9},{9,8},{10,11... | collective-permute-start | bytes 1990664 | tf_op jit(solution)/shard_map/ppermute | solution.py:640
  738.8 29.3 %collective-permute-start.55 = (bf16[4,2,328,128]{3,2,0,1:T(8,128)(2,1)S(1)}, bf16[4,2,328,128]{3,2,0,1:T(8,128)(2,1)S(1)}, u32[]{:S(2)}, u32[]{:S(2)}) collective-permute-start(bf16[4,2,328,128]{3,2,0,1:T(8,128)(2,1)S(1)} %bitcast.226), channel_id=1, source_target_pairs={{0,1},{1,0},{2,3},{3,2},{4,5},{5,4},{6,7},{7,6},{8,9},{9,8},{10,11... | collective-permute-start | bytes 2015240 | tf_op jit(solution)/shard_map/ppermute | solution.py:640
  748.7 16.5 %collective-permute-start.57 = (bf16[4,2,320,128]{3,2,0,1:T(8,128)(2,1)S(1)}, bf16[4,2,320,128]{3,2,0,1:T(8,128)(2,1)S(1)}, u32[]{:S(2)}, u32[]{:S(2)}) collective-permute-start(bf16[4,2,320,128]{3,2,0,1:T(8,128)(2,1)S(1)} %bitcast.227), channel_id=1, source_target_pairs={{0,2},{1,3},{2,0},{3,1},{4,6},{5,7},{6,4},{7,5},{8,10},{9,11},{10,... | collective-permute-start | bytes 1966088 | tf_op jit(solution)/shard_map/ppermute | solution.py:640
  752.8 32.1 %collective-permute-start.59 = (bf16[2,144,1152]{2,1,0:T(8,128)(2,1)S(1)}, bf16[2,144,1152]{2,1,0:T(8,128)(2,1)S(1)}, u32[]{:S(2)}, u32[]{:S(2)}) collective-permute-start(bf16[2,144,1152]{2,1,0:T(8,128)(2,1)S(1)} %get-tuple-element.323), channel_id=1, source_target_pairs={{0,16},{1,17},{2,18},{3,19},{4,20},{5,21},{6,22},{7,23},{8,24},{9,... | collective-permute-start | bytes 1990664 | tf_op jit(solution)/shard_map/ppermute | solution.py:640
  765.4 8.8 %collective-permute-start.58 = (bf16[4,320,128]{2,1,0:T(8,128)(2,1)S(1)}, bf16[4,320,128]{2,1,0:T(8,128)(2,1)S(1)}, u32[]{:S(2)}, u32[]{:S(2)}) collective-permute-start(bf16[4,320,128]{2,1,0:T(8,128)(2,1)S(1)} %dynamic-slice_bitcast_fusion.9), channel_id=1, source_target_pairs={{0,1},{1,0},{2,3},{3,2},{4,5},{5,4},{6,7},{7,6},{8,9},{9,8},{10,11... | collective-permute-start | bytes 983048 | tf_op jit(solution)/shard_map/ppermute | solution.py:640
  768.3 8.1 collective-permute-start.56
  774.3 19.5 %collective-permute-start.52 = (f32[3,2,16,1152]{3,2,1,0:T(8,128)S(1)}, f32[3,2,16,1152]{3,2,1,0:T(8,128)S(1)}, u32[]{:S(2)}, u32[]{:S(2)}) collective-permute-start(f32[3,2,16,1152]{3,2,1,0:T(8,128)S(1)} %pad_maximum_fusion.5), channel_id=1, source_target_pairs={{2,1},{6,5},{10,9},{14,13},{18,17},{22,21},{26,25},{30,29}} | collective-permute-start | bytes 1327112 | tf_op jit(solution)/shard_map/ppermute | solution.py:647
  776.6 15.5 %collective-permute-start.60 = (bf16[2,648,128]{2,1,0:T(8,128)(2,1)S(1)}, bf16[2,648,128]{2,1,0:T(8,128)(2,1)S(1)}, u32[]{:S(2)}, u32[]{:S(2)}) collective-permute-start(bf16[2,648,128]{2,1,0:T(8,128)(2,1)S(1)} %get-tuple-element.339), channel_id=1, source_target_pairs={{0,8},{1,9},{2,10},{3,11},{4,12},{5,13},{6,14},{7,15},{8,0},{9,1},... | collective-permute-start | bytes 995336 | tf_op jit(solution)/shard_map/ppermute | solution.py:640
  785.2 22.2 %collective-permute-start.62 = (bf16[1,144,1152]{2,1,0:T(8,128)(2,1)S(1)}, bf16[1,144,1152]{2,1,0:T(8,128)(2,1)S(1)}, u32[]{:S(2)}, u32[]{:S(2)}) collective-permute-start(bf16[1,144,1152]{2,1,0:T(8,128)(2,1)S(1)} %get-tuple-element.337), channel_id=1, source_target_pairs={{0,8},{1,9},{2,10},{3,11},{4,12},{5,13},{6,14},{7,15},{8,0},{9,1},... | collective-permute-start | bytes 995336 | tf_op jit(solution)/shard_map/ppermute | solution.py:640
  792.9 20.4 %collective-permute-start.61 = (bf16[1,648,128]{2,1,0:T(8,128)(2,1)}, bf16[1,648,128]{2,1,0:T(8,128)(2,1)}, u32[]{:S(2)}, u32[]{:S(2)}) collective-permute-start(bf16[1,648,128]{2,1,0:T(8,128)(2,1)} %get-tuple-element.351), channel_id=1, source_target_pairs={{0,16},{1,17},{2,18},{3,19},{4,20},{5,21},{6,22},{7,23},{8,24},{9,... | collective-permute-start | bytes 497672 | tf_op jit(solution)/shard_map/ppermute | solution.py:640
  (61 other events, 829.3 us)
Sparse Core Ops, SparseCore 0:
  728.9 79.6 all-gather.1
